TPU v7x, 32 devices: a whole 2x2x4 slice. The times are simulated.
32 devices in a mesh: phase: 4 (over y, x), dp: 8 (over z, core).
Axes of the slice: x: 2, y: 2, z: 4, core: 2. Of those that a mesh axis runs over, the one named last changes fastest.
Arguments:
- tap_tokens: bfloat16 [4, 4096, 4096], P('phase', 'dp'), may hold values from -6 to 6
- project_weight: bfloat16 [4, 4096, 256], P('phase'), may hold values from -0.09375 to 0.09375
- expand_four: bfloat16 [256, 4096], replicated, may hold values from -0.375 to 0.375
- expand_two: bfloat16 [256, 1024], replicated, may hold values from -0.375 to 0.375
- shrink_weight: bfloat16 [1024, 256], replicated, may hold values from -0.1875 to 0.1875
- refine_filters: bfloat16 [4, 2, 2304, 256], P(None, None, 'dp'), may hold values from -0.125 to 0.125
- head_matrix: bfloat16 [256, 128], replicated, may hold values from -0.375 to 0.375
- head_vector: float32 [128], replicated, may hold values from -0.5 to 0.5
- tile_slot: int32 [8, 4, 8], replicated, may hold values from 0 to 191, as said below
Outputs:
- scene_depth: float32 [192, 256], P(('phase', 'dp'))
Inputs may be any that keep to these rules, and one draw needn't show every extreme that they name: tile_slot[d, s, j] is the slot of tile (d, s, j); it lies among the slots s * 48 to (s + 1) * 48 - 1, and every slot receives at least one tile.
All inputs are finite; a program needn't handle non-finite values.
Results may differ from a plain program's by a relative error of at most 0.015.
Values may be sent and summed in bfloat16 or wider, within the bound.
No kernel may reach another device: no remote copies, remote signals or barrier semaphores. Data moves between devices by JAX's collectives and lax.ppermute only.
A program may use at most 128 MiB of HBM per device.

v0:
```python
import jax
import jax.numpy as jnp
from jax import lax
from jax.sharding import PartitionSpec as P

G = 32
TILES_DEV = 8
SLOT_DEV = 6


def padded_2(block, sides, width):
    for axis, dim in sides:
        count = lax.axis_size(axis)
        forward = [(i, i + 1) for i in range(count - 1)]
        backward = [(target, source) for source, target in forward]
        low = lax.ppermute(
            lax.slice_in_dim(block, block.shape[dim] - width, None, axis=dim), axis, forward
        )
        high = lax.ppermute(lax.slice_in_dim(block, 0, width, axis=dim), axis, backward)
        block = jnp.concatenate([low, block, high], axis=dim)
    return block


def from_partner(block, axis, bit):
    count = lax.axis_size(axis)
    route = []
    for low in range(count):
        high = low | 1 << bit
        if high != low and high < count:
            route += [(low, high), (high, low)]
    return lax.ppermute(block, axis, route)


def expand(feature, matrix, factor):
    height, breadth, channels = feature.shape
    flattened = jnp.dot(
        feature.reshape(height * breadth, channels), matrix, preferred_element_type=jnp.float32
    ).astype(jnp.bfloat16)
    arranged = flattened.reshape(height, breadth, factor, factor, channels).transpose(0, 2, 1, 3, 4)
    return arranged.reshape(height * factor, breadth * factor, channels)


def shrink(feature, matrix):
    height, breadth, channels = feature.shape
    blocks = feature.reshape(height // 2, 2, breadth // 2, 2, channels).transpose(0, 2, 1, 3, 4)
    blocks = blocks.reshape(height // 2 * (breadth // 2), 4 * channels)
    result = jnp.dot(blocks, matrix, preferred_element_type=jnp.float32).astype(jnp.bfloat16)
    return result.reshape(height // 2, breadth // 2, channels)


def upsample(feature):
    height, breadth, channels = feature.shape
    widened = jnp.broadcast_to(feature[:, None, :, None, :], (height, 2, breadth, 2, channels))
    return widened.reshape(2 * height, 2 * breadth, channels)


def extend(feature):
    widened = padded_2(feature, (("phase", 1),), 1)
    parity = lax.axis_index("dp") % 2
    boundary = jnp.where(parity == 0, widened[-1], widened[0])
    partner = from_partner(boundary, "dp", 0)
    zeroed = jnp.zeros_like(partner)
    upper_row = jnp.where(parity == 1, partner, zeroed)
    lower_row = jnp.where(parity == 0, partner, zeroed)
    return jnp.concatenate([upper_row[None], widened, lower_row[None]], axis=0)


def convolve(feature, matrix):
    height, breadth, channels = feature.shape
    padded = extend(feature)
    patches = jnp.concatenate(
        [
            padded[row_shift : row_shift + height, col_shift : col_shift + breadth]
            for row_shift in range(3)
            for col_shift in range(3)
        ],
        axis=-1,
    )
    patches = patches.reshape(height * breadth, 9 * channels)
    result = jnp.dot(patches, matrix, preferred_element_type=jnp.float32)
    return result.reshape(height, breadth, channels)


def refine(summed, first_matrix, second_matrix):
    inner_map = convolve(jax.nn.relu(summed).astype(jnp.bfloat16), first_matrix)
    branch = convolve(jax.nn.relu(inner_map).astype(jnp.bfloat16), second_matrix)
    return (summed + branch).astype(jnp.bfloat16)


def per_device(
    tap_tokens,
    project_weight,
    expand_four,
    expand_two,
    shrink_weight,
    refine_filters,
    head_matrix,
    head_vector,
    tile_slot,
):
    token_rows = tap_tokens.shape[1] // G
    channels = project_weight.shape[2]
    projected = jnp.dot(
        tap_tokens[0], project_weight[0], preferred_element_type=jnp.float32
    ).astype(jnp.bfloat16)
    projected = projected.reshape(1, token_rows, G, channels)
    quarters = lax.all_to_all(projected, "phase", split_axis=2, concat_axis=0, tiled=True)
    filter_set = lax.all_gather(refine_filters, "dp", axis=2, tiled=True)
    inputs = [
        expand(quarters[0], expand_four, 4),
        expand(quarters[1], expand_two, 2),
        quarters[2],
        shrink(quarters[3], shrink_weight),
    ]
    joined_map = refine(inputs[3].astype(jnp.float32), filter_set[3, 0], filter_set[3, 1])
    for level_id in (2, 1, 0):
        summed = inputs[level_id].astype(jnp.float32) + upsample(joined_map).astype(jnp.float32)
        joined_map = refine(summed, filter_set[level_id, 0], filter_set[level_id, 1])
    hidden = jax.nn.relu(
        jnp.dot(joined_map.reshape(-1, channels), head_matrix, preferred_element_type=jnp.float32)
    )
    depth_map = jnp.dot(hidden, head_vector, precision=lax.Precision.HIGHEST)
    depth_tiles = depth_map.reshape(TILES_DEV, -1)
    phase_id = lax.axis_index("phase")
    dp_id = lax.axis_index("dp")
    dp_count = lax.axis_size("dp")
    owned_slots = (phase_id * dp_count + dp_id) * SLOT_DEV + jnp.arange(SLOT_DEV, dtype=jnp.int32)
    portion = lax.all_gather(depth_tiles[None], "dp", axis=0, tiled=True)
    targets = lax.dynamic_index_in_dim(tile_slot, phase_id, 1, keepdims=False).reshape(-1)
    matches = (owned_slots[:, None] == targets[None, :]).astype(jnp.float32)
    return jnp.dot(matches, portion.reshape(-1, portion.shape[-1]), precision=lax.Precision.HIGHEST)


def solution(mesh):
    in_specs = (
        P("phase", "dp", None),
        P("phase", None, None),
        P(),
        P(),
        P(),
        P(None, None, "dp", None),
        P(),
        P(),
        P(),
    )
    out_specs = P(("phase", "dp"), None)
    return jax.shard_map(
        per_device, mesh=mesh, in_specs=in_specs, out_specs=out_specs, check_vma=False
    )
```

profile of v0, /device:TPU:0, one launch (start us, length us, event | category | flops | bytes accessed | tf_op | source)
XLA Modules:
  0.0 244.1 jit_solution(18260867389084024488)
XLA Ops:
  7.3 4.2 %fusion.6 = bf16[512,256]{1,0:T(8,128)(2,1)S(1)} fusion(bf16[1,4096,256]{2,1,0:T(8,128)(2,1)} %param.10, bf16[1,512,4096]{2,1,0:T(8,128)(2,1)} %param.9), kind=kOutput, calls=%fused_computation.18 | convolution fusion | flops 1073872896 | bytes 6553600 | tf_op jit(solution)/shard_map/dot_general | solution.py:103
  11.6 10.7 %all_to_all.15 = bf16[1,16,32,256]{3,1,0,2:T(8,128)(2,1)S(1)} all-to-all(bf16[1,16,32,256]{3,1,0,2:T(8,128)(2,1)S(1)} %copy.93), channel_id=1, replica_groups=mesh['phase'=4,'dp'=8] {'phase'}, dimensions={2} | all-to-all | bytes 524288 | tf_op jit(solution)/shard_map/all_to_all | solution.py:107
  22.8 2.8 %collective-permute-start = (bf16[8,1,256]{2,0,1:T(8,128)(2,1)S(1)}, bf16[8,1,256]{2,0,1:T(8,128)(2,1)S(1)}, u32[]{:S(2)}, u32[]{:S(2)}) collective-permute-start(bf16[8,1,256]{2,0,1:T(8,128)(2,1)S(1)} %get-tuple-element.41), channel_id=1, source_target_pairs={{0,8},{8,16},{16,24},{1,9},{9,17},{17,25},{2,10},{10,18},{18,26},{... | collective-permute-start | bytes 12296 | tf_op jit(solution)/shard_map/ppermute | solution.py:16
  27.0 4.2 %collective-permute-done.1 = bf16[8,1,256]{2,0,1:T(8,128)(2,1)S(1)} collective-permute-done((bf16[8,1,256]{2,0,1:T(8,128)(2,1)S(1)}, bf16[8,1,256]{2,0,1:T(8,128)(2,1)S(1)}, u32[]{:S(2)}, u32[]{:S(2)}) %collective-permute-start.1) | collective-permute-done | bytes 4128 | tf_op jit(solution)/shard_map/ppermute | solution.py:19
  32.6 69.8 %all-gather.2.cloned.1.call-done = bf16[4,2,2304,256]{3,2,1,0:T(8,128)(2,1)} async-done(((bf16[4,2,288,256]{3,2,1,0:T(8,128)(2,1)}), bf16[4,2,2304,256]{3,2,1,0:T(8,128)(2,1)}) %all-gather.2.cloned.1.call-update) | async-done | bytes 9437200 | tf_op jit(solution)/shard_map/all_gather | solution.py:108
  104.0 3.4 %collective-permute-start.3 = (bf16[8,1,256]{2,0,1:T(8,128)(2,1)S(1)}, bf16[8,1,256]{2,0,1:T(8,128)(2,1)S(1)}, u32[]{:S(2)}, u32[]{:S(2)}) collective-permute-start(bf16[8,1,256]{2,0,1:T(8,128)(2,1)S(1)} %get-tuple-element.39), channel_id=1, source_target_pairs={{0,8},{8,16},{16,24},{1,9},{9,17},{17,25},{2,10},{10,18},{18,26},{... | collective-permute-start | bytes 12296 | tf_op jit(solution)/shard_map/ppermute | solution.py:16
  108.7 4.2 %collective-permute-done.4 = bf16[8,1,256]{2,0,1:T(8,128)(2,1)S(1)} collective-permute-done((bf16[8,1,256]{2,0,1:T(8,128)(2,1)S(1)}, bf16[8,1,256]{2,0,1:T(8,128)(2,1)S(1)}, u32[]{:S(2)}, u32[]{:S(2)}) %collective-permute-start.4) | collective-permute-done | bytes 4128 | tf_op jit(solution)/shard_map/ppermute | solution.py:19
  116.1 4.3 %collective-permute-start.6 = (bf16[16,1,256]{2,1,0:T(2,128)(2,1)S(1)}, bf16[16,1,256]{2,1,0:T(2,128)(2,1)S(1)}, u32[]{:S(2)}, u32[]{:S(2)}) collective-permute-start(bf16[16,1,256]{2,1,0:T(2,128)(2,1)S(1)} %get-tuple-element.29), channel_id=1, source_target_pairs={{0,8},{8,16},{16,24},{1,9},{9,17},{17,25},{2,10},{10,18},{18,26},{... | collective-permute-start | bytes 24584 | tf_op jit(solution)/shard_map/ppermute | solution.py:16
  121.8 4.2 %collective-permute-done.7 = bf16[16,1,256]{2,1,0:T(2,128)(2,1)S(1)} collective-permute-done((bf16[16,1,256]{2,1,0:T(2,128)(2,1)S(1)}, bf16[16,1,256]{2,1,0:T(2,128)(2,1)S(1)}, u32[]{:S(2)}, u32[]{:S(2)}) %collective-permute-start.7) | collective-permute-done | bytes 8224 | tf_op jit(solution)/shard_map/ppermute | solution.py:19
  129.3 3.4 %collective-permute-start.9 = (bf16[16,1,256]{2,1,0:T(2,128)(2,1)S(1)}, bf16[16,1,256]{2,1,0:T(2,128)(2,1)S(1)}, u32[]{:S(2)}, u32[]{:S(2)}) collective-permute-start(bf16[16,1,256]{2,1,0:T(2,128)(2,1)S(1)} %get-tuple-element.27), channel_id=1, source_target_pairs={{0,8},{8,16},{16,24},{1,9},{9,17},{17,25},{2,10},{10,18},{18,26},{... | collective-permute-start | bytes 24584 | tf_op jit(solution)/shard_map/ppermute | solution.py:16
  134.2 4.2 %collective-permute-done.10 = bf16[16,1,256]{2,1,0:T(2,128)(2,1)S(1)} collective-permute-done((bf16[16,1,256]{2,1,0:T(2,128)(2,1)S(1)}, bf16[16,1,256]{2,1,0:T(2,128)(2,1)S(1)}, u32[]{:S(2)}, u32[]{:S(2)}) %collective-permute-start.10) | collective-permute-done | bytes 8224 | tf_op jit(solution)/shard_map/ppermute | solution.py:19
  140.0 1.6 fusion.18
  142.5 2.8 %collective-permute-start.12 = (bf16[32,1,256]{2,1,0:T(2,128)(2,1)S(1)}, bf16[32,1,256]{2,1,0:T(2,128)(2,1)S(1)}, u32[]{:S(2)}, u32[]{:S(2)}) collective-permute-start(bf16[32,1,256]{2,1,0:T(2,128)(2,1)S(1)} %get-tuple-element.21), channel_id=1, source_target_pairs={{0,8},{8,16},{16,24},{1,9},{9,17},{17,25},{2,10},{10,18},{18,26},{... | collective-permute-start | bytes 49160 | tf_op jit(solution)/shard_map/ppermute | solution.py:16
  146.9 4.2 %collective-permute-done.13 = bf16[32,1,256]{2,1,0:T(2,128)(2,1)S(1)} collective-permute-done((bf16[32,1,256]{2,1,0:T(2,128)(2,1)S(1)}, bf16[32,1,256]{2,1,0:T(2,128)(2,1)S(1)}, u32[]{:S(2)}, u32[]{:S(2)}) %collective-permute-start.13) | collective-permute-done | bytes 16416 | tf_op jit(solution)/shard_map/ppermute | solution.py:19
  153.4 2.0 fusion.3
  155.5 2.8 %collective-permute-start.15 = (bf16[32,1,256]{2,1,0:T(2,128)(2,1)S(1)}, bf16[32,1,256]{2,1,0:T(2,128)(2,1)S(1)}, u32[]{:S(2)}, u32[]{:S(2)}) collective-permute-start(bf16[32,1,256]{2,1,0:T(2,128)(2,1)S(1)} %get-tuple-element.19), channel_id=1, source_target_pairs={{0,8},{8,16},{16,24},{1,9},{9,17},{17,25},{2,10},{10,18},{18,26},{... | collective-permute-start | bytes 49160 | tf_op jit(solution)/shard_map/ppermute | solution.py:16
  161.2 3.0 %collective-permute-done.16 = bf16[32,1,256]{2,1,0:T(2,128)(2,1)S(1)} collective-permute-done((bf16[32,1,256]{2,1,0:T(2,128)(2,1)S(1)}, bf16[32,1,256]{2,1,0:T(2,128)(2,1)S(1)}, u32[]{:S(2)}, u32[]{:S(2)}) %collective-permute-start.16) | collective-permute-done | bytes 16416 | tf_op jit(solution)/shard_map/ppermute | solution.py:19
  164.5 2.2 copy.96
  166.8 2.0 reshape.106
  169.8 2.0 fusion.5
  171.9 2.3 broadcast_in_dim.81
  174.2 3.7 %convert_element_type.127 = f32[64,32,256]{2,1,0:T(8,128)} reshape(f32[32,2,16,2,256]{4,3,2,1,0:T(2,128)} %broadcast_in_dim.81) | data formatting | bytes 4194304 | tf_op jit(solution)/shard_map/convert_element_type | solution.py:117
  177.8 3.5 %maximum_convert_fusion.1 = (bf16[64,32,256]{2,1,0:T(8,128)(2,1)S(1)}, f32[64,32,256]{2,1,0:T(8,128)}) fusion(f32[64,32,256]{2,1,0:T(8,128)S(1)} %reshape.106, f32[64,32,256]{2,1,0:T(8,128)} %convert_element_type.127), kind=kLoop, calls=%fused_computation.8 | loop fusion | flops 1572864 | bytes 7340032 | tf_op jit(solution)/shard_map/convert_element_type | solution.py:85
  181.4 2.8 %collective-permute-start.18 = (bf16[64,1,256]{2,1,0:T(2,128)(2,1)S(1)}, bf16[64,1,256]{2,1,0:T(2,128)(2,1)S(1)}, u32[]{:S(2)}, u32[]{:S(2)}) collective-permute-start(bf16[64,1,256]{2,1,0:T(2,128)(2,1)S(1)} %get-tuple-element.13), channel_id=1, source_target_pairs={{0,8},{8,16},{16,24},{1,9},{9,17},{17,25},{2,10},{10,18},{18,26},{... | collective-permute-start | bytes 98312 | tf_op jit(solution)/shard_map/ppermute | solution.py:16
  186.2 4.2 %collective-permute-done.19 = bf16[64,1,256]{2,1,0:T(2,128)(2,1)S(1)} collective-permute-done((bf16[64,1,256]{2,1,0:T(2,128)(2,1)S(1)}, bf16[64,1,256]{2,1,0:T(2,128)(2,1)S(1)}, u32[]{:S(2)}, u32[]{:S(2)}) %collective-permute-start.19) | collective-permute-done | bytes 32800 | tf_op jit(solution)/shard_map/ppermute | solution.py:19
  191.7 1.6 pad_maximum_fusion
  196.7 3.9 %maximum_convert_fusion = bf16[64,32,256]{2,1,0:T(8,128)(2,1)S(1)} fusion(bf16[64,32,2304]{2,1,0:T(8,128)(2,1)S(1)} %slice_dynamic-update-slice_fusion.6, bf16[4,2,2304,256]{3,2,1,0:T(8,128)(2,1)} %all-gather.2.cloned.1.call-done), kind=kOutput, calls=%fused_computation.7 | convolution fusion | flops 2416967680 | bytes 11665408 | tf_op jit(solution)/shard_map/dot_general | solution.py:80
  200.7 3.0 %collective-permute-start.21 = (bf16[64,1,256]{2,1,0:T(2,128)(2,1)S(1)}, bf16[64,1,256]{2,1,0:T(2,128)(2,1)S(1)}, u32[]{:S(2)}, u32[]{:S(2)}) collective-permute-start(bf16[64,1,256]{2,1,0:T(2,128)(2,1)S(1)} %get-tuple-element.11), channel_id=1, source_target_pairs={{0,8},{8,16},{16,24},{1,9},{9,17},{17,25},{2,10},{10,18},{18,26},{... | collective-permute-start | bytes 98312 | tf_op jit(solution)/shard_map/ppermute | solution.py:16
  205.6 4.3 %collective-permute-done.22 = bf16[64,1,256]{2,1,0:T(2,128)(2,1)S(1)} collective-permute-done((bf16[64,1,256]{2,1,0:T(2,128)(2,1)S(1)}, bf16[64,1,256]{2,1,0:T(2,128)(2,1)S(1)}, u32[]{:S(2)}, u32[]{:S(2)}) %collective-permute-start.22) | collective-permute-done | bytes 32800 | tf_op jit(solution)/shard_map/ppermute | solution.py:19
  211.2 1.6 pad_maximum_fusion.1
  216.8 4.2 %add_convert_fusion = bf16[64,32,256]{2,1,0:T(8,128)(2,1)S(1)} fusion(f32[64,32,256]{2,1,0:T(8,128)S(1)} %copy-done.2, bf16[64,32,2304]{2,1,0:T(8,128)(2,1)S(1)} %slice_dynamic-update-slice_fusion, bf16[4,2,2304,256]{3,2,1,0:T(8,128)(2,1)} %all-gather.2.cloned.1.call-done), kind=kOutput, calls=%fused_computation.6 | convolution fusion | flops 2416967680 | bytes 13762560 | tf_op jit(solution)/shard_map/dot_general | solution.py:80
  222.4 14.0 %all_gather.7 = f32[8,8,256]{2,1,0:T(8,128)S(1)} all-gather(f32[1,8,256]{2,1,0:T(8,128)S(1)} %broadcast_in_dim_reshape.4), channel_id=1, replica_groups=mesh['phase'=4,'dp'=8] {'dp'}, dimensions={0}, use_global_device_ids=true | all-gather | bytes 73728 | tf_op jit(solution)/shard_map/all_gather | solution.py:128
  (188 shorter events, 42.3 us)
Async XLA Ops:
  6.5 153.3 %copy-start = (bf16[256,4096]{1,0:T(8,128)(2,1)S(1)}, bf16[256,4096]{1,0:T(8,128)(2,1)}, u32[]{:S(2)}) copy-start(bf16[256,4096]{1,0:T(8,128)(2,1)} %param.11) | copy-start | bytes 6291460
  6.5 95.9 %all-gather.2.cloned.1.call-start = ((), (), s32[]{:S(2)}) async-start(), calls=%async_computation.1 | async-start | bytes 10616832 | tf_op jit(solution)/shard_map/all_gather | solution.py:108
  7.3 15.3 %copy-start.4 = (bf16[1024,256]{1,0:T(8,128)(2,1)S(1)}, bf16[1024,256]{1,0:T(8,128)(2,1)}, u32[]{:S(2)}) copy-start(bf16[1024,256]{1,0:T(8,128)(2,1)} %param.13) | copy-start | bytes 1572868
  22.4 117.6 %copy-start.3 = (bf16[1,16,4,8,256]{4,3,1,0,2:T(8,128)(2,1)}, bf16[1,16,4,8,256]{4,3,1,0,2:T(8,128)(2,1)S(1)}, u32[]{:S(2)}) copy-start(bf16[1,16,4,8,256]{4,3,1,0,2:T(8,128)(2,1)S(1)} %copy.118) | copy-start | bytes 786436
  22.8 4.1 %collective-permute-start = (bf16[8,1,256]{2,0,1:T(8,128)(2,1)S(1)}, bf16[8,1,256]{2,0,1:T(8,128)(2,1)S(1)}, u32[]{:S(2)}, u32[]{:S(2)}) collective-permute-start(bf16[8,1,256]{2,0,1:T(8,128)(2,1)S(1)} %get-tuple-element.41), channel_id=1, source_target_pairs={{0,8},{8,16},{16,24},{1,9},{9,17},{17,25},{2,10},{10,18},{18,26},{... | collective-permute-start | bytes 12296 | tf_op jit(solution)/shard_map/ppermute | solution.py:16
  25.6 5.5 %collective-permute-start.1 = (bf16[8,1,256]{2,0,1:T(8,128)(2,1)S(1)}, bf16[8,1,256]{2,0,1:T(8,128)(2,1)S(1)}, u32[]{:S(2)}, u32[]{:S(2)}) collective-permute-start(bf16[8,1,256]{2,0,1:T(8,128)(2,1)S(1)} %get-tuple-element.42), channel_id=1, source_target_pairs={{8,0},{16,8},{24,16},{9,1},{17,9},{25,17},{10,2},{18,10},{26,18},{... | collective-permute-start | bytes 12296 | tf_op jit(solution)/shard_map/ppermute | solution.py:19
  31.2 1.2 collective-permute-start.2
  104.0 4.7 %collective-permute-start.3 = (bf16[8,1,256]{2,0,1:T(8,128)(2,1)S(1)}, bf16[8,1,256]{2,0,1:T(8,128)(2,1)S(1)}, u32[]{:S(2)}, u32[]{:S(2)}) collective-permute-start(bf16[8,1,256]{2,0,1:T(8,128)(2,1)S(1)} %get-tuple-element.39), channel_id=1, source_target_pairs={{0,8},{8,16},{16,24},{1,9},{9,17},{17,25},{2,10},{10,18},{18,26},{... | collective-permute-start | bytes 12296 | tf_op jit(solution)/shard_map/ppermute | solution.py:16
  107.4 5.5 %collective-permute-start.4 = (bf16[8,1,256]{2,0,1:T(8,128)(2,1)S(1)}, bf16[8,1,256]{2,0,1:T(8,128)(2,1)S(1)}, u32[]{:S(2)}, u32[]{:S(2)}) collective-permute-start(bf16[8,1,256]{2,0,1:T(8,128)(2,1)S(1)} %get-tuple-element.40), channel_id=1, source_target_pairs={{8,0},{16,8},{24,16},{9,1},{17,9},{25,17},{10,2},{18,10},{26,18},{... | collective-permute-start | bytes 12296 | tf_op jit(solution)/shard_map/ppermute | solution.py:19
  112.9 1.2 collective-permute-start.5
  115.9 22.6 %copy-start.5 = (bf16[256,1024]{1,0:T(8,128)(2,1)S(1)}, bf16[256,1024]{1,0:T(8,128)(2,1)}, u32[]{:S(2)}) copy-start(bf16[256,1024]{1,0:T(8,128)(2,1)} %param.12) | copy-start | bytes 1572868
  116.1 5.7 %collective-permute-start.6 = (bf16[16,1,256]{2,1,0:T(2,128)(2,1)S(1)}, bf16[16,1,256]{2,1,0:T(2,128)(2,1)S(1)}, u32[]{:S(2)}, u32[]{:S(2)}) collective-permute-start(bf16[16,1,256]{2,1,0:T(2,128)(2,1)S(1)} %get-tuple-element.29), channel_id=1, source_target_pairs={{0,8},{8,16},{16,24},{1,9},{9,17},{17,25},{2,10},{10,18},{18,26},{... | collective-permute-start | bytes 24584 | tf_op jit(solution)/shard_map/ppermute | solution.py:16
  120.4 5.6 %collective-permute-start.7 = (bf16[16,1,256]{2,1,0:T(2,128)(2,1)S(1)}, bf16[16,1,256]{2,1,0:T(2,128)(2,1)S(1)}, u32[]{:S(2)}, u32[]{:S(2)}) collective-permute-start(bf16[16,1,256]{2,1,0:T(2,128)(2,1)S(1)} %get-tuple-element.30), channel_id=1, source_target_pairs={{8,0},{16,8},{24,16},{9,1},{17,9},{25,17},{10,2},{18,10},{26,18},{... | collective-permute-start | bytes 24584 | tf_op jit(solution)/shard_map/ppermute | solution.py:19
  126.1 1.2 collective-permute-start.8
  129.3 4.8 %collective-permute-start.9 = (bf16[16,1,256]{2,1,0:T(2,128)(2,1)S(1)}, bf16[16,1,256]{2,1,0:T(2,128)(2,1)S(1)}, u32[]{:S(2)}, u32[]{:S(2)}) collective-permute-start(bf16[16,1,256]{2,1,0:T(2,128)(2,1)S(1)} %get-tuple-element.27), channel_id=1, source_target_pairs={{0,8},{8,16},{16,24},{1,9},{9,17},{17,25},{2,10},{10,18},{18,26},{... | collective-permute-start | bytes 24584 | tf_op jit(solution)/shard_map/ppermute | solution.py:16
  132.7 5.6 %collective-permute-start.10 = (bf16[16,1,256]{2,1,0:T(2,128)(2,1)S(1)}, bf16[16,1,256]{2,1,0:T(2,128)(2,1)S(1)}, u32[]{:S(2)}, u32[]{:S(2)}) collective-permute-start(bf16[16,1,256]{2,1,0:T(2,128)(2,1)S(1)} %get-tuple-element.28), channel_id=1, source_target_pairs={{8,0},{16,8},{24,16},{9,1},{17,9},{25,17},{10,2},{18,10},{26,18},{... | collective-permute-start | bytes 24584 | tf_op jit(solution)/shard_map/ppermute | solution.py:19
  138.4 1.2 collective-permute-start.11
  142.5 4.4 %collective-permute-start.12 = (bf16[32,1,256]{2,1,0:T(2,128)(2,1)S(1)}, bf16[32,1,256]{2,1,0:T(2,128)(2,1)S(1)}, u32[]{:S(2)}, u32[]{:S(2)}) collective-permute-start(bf16[32,1,256]{2,1,0:T(2,128)(2,1)S(1)} %get-tuple-element.21), channel_id=1, source_target_pairs={{0,8},{8,16},{16,24},{1,9},{9,17},{17,25},{2,10},{10,18},{18,26},{... | collective-permute-start | bytes 49160 | tf_op jit(solution)/shard_map/ppermute | solution.py:16
  145.3 5.8 %collective-permute-start.13 = (bf16[32,1,256]{2,1,0:T(2,128)(2,1)S(1)}, bf16[32,1,256]{2,1,0:T(2,128)(2,1)S(1)}, u32[]{:S(2)}, u32[]{:S(2)}) collective-permute-start(bf16[32,1,256]{2,1,0:T(2,128)(2,1)S(1)} %get-tuple-element.22), channel_id=1, source_target_pairs={{8,0},{16,8},{24,16},{9,1},{17,9},{25,17},{10,2},{18,10},{26,18},{... | collective-permute-start | bytes 49160 | tf_op jit(solution)/shard_map/ppermute | solution.py:19
  151.1 1.2 collective-permute-start.14
  155.5 5.6 %collective-permute-start.15 = (bf16[32,1,256]{2,1,0:T(2,128)(2,1)S(1)}, bf16[32,1,256]{2,1,0:T(2,128)(2,1)S(1)}, u32[]{:S(2)}, u32[]{:S(2)}) collective-permute-start(bf16[32,1,256]{2,1,0:T(2,128)(2,1)S(1)} %get-tuple-element.19), channel_id=1, source_target_pairs={{0,8},{8,16},{16,24},{1,9},{9,17},{17,25},{2,10},{10,18},{18,26},{... | collective-permute-start | bytes 49160 | tf_op jit(solution)/shard_map/ppermute | solution.py:16
  158.4 5.8 %collective-permute-start.16 = (bf16[32,1,256]{2,1,0:T(2,128)(2,1)S(1)}, bf16[32,1,256]{2,1,0:T(2,128)(2,1)S(1)}, u32[]{:S(2)}, u32[]{:S(2)}) collective-permute-start(bf16[32,1,256]{2,1,0:T(2,128)(2,1)S(1)} %get-tuple-element.20), channel_id=1, source_target_pairs={{8,0},{16,8},{24,16},{9,1},{17,9},{25,17},{10,2},{18,10},{26,18},{... | collective-permute-start | bytes 49160 | tf_op jit(solution)/shard_map/ppermute | solution.py:19
  164.2 4.6 %collective-permute-start.17 = (bf16[18,256]{1,0:T(8,128)(2,1)S(1)}, bf16[18,256]{1,0:T(8,128)(2,1)S(1)}, u32[]{:S(2)}, u32[]{:S(2)}) collective-permute-start(bf16[18,256]{1,0:T(8,128)(2,1)S(1)} %fusion.42), channel_id=1, source_target_pairs={{0,1},{1,0},{2,3},{3,2},{4,5},{5,4},{6,7},{7,6},{8,9},{9,8},{10,11... | collective-permute-start | bytes 27656 | tf_op jit(solution)/shard_map/ppermute | solution.py:31
  181.4 4.8 %collective-permute-start.18 = (bf16[64,1,256]{2,1,0:T(2,128)(2,1)S(1)}, bf16[64,1,256]{2,1,0:T(2,128)(2,1)S(1)}, u32[]{:S(2)}, u32[]{:S(2)}) collective-permute-start(bf16[64,1,256]{2,1,0:T(2,128)(2,1)S(1)} %get-tuple-element.13), channel_id=1, source_target_pairs={{0,8},{8,16},{16,24},{1,9},{9,17},{17,25},{2,10},{10,18},{18,26},{... | collective-permute-start | bytes 98312 | tf_op jit(solution)/shard_map/ppermute | solution.py:16
  184.3 6.2 %collective-permute-start.19 = (bf16[64,1,256]{2,1,0:T(2,128)(2,1)S(1)}, bf16[64,1,256]{2,1,0:T(2,128)(2,1)S(1)}, u32[]{:S(2)}, u32[]{:S(2)}) collective-permute-start(bf16[64,1,256]{2,1,0:T(2,128)(2,1)S(1)} %get-tuple-element.14), channel_id=1, source_target_pairs={{8,0},{16,8},{24,16},{9,1},{17,9},{25,17},{10,2},{18,10},{26,18},{... | collective-permute-start | bytes 98312 | tf_op jit(solution)/shard_map/ppermute | solution.py:19
  190.4 1.3 collective-permute-start.20
  200.7 4.9 %collective-permute-start.21 = (bf16[64,1,256]{2,1,0:T(2,128)(2,1)S(1)}, bf16[64,1,256]{2,1,0:T(2,128)(2,1)S(1)}, u32[]{:S(2)}, u32[]{:S(2)}) collective-permute-start(bf16[64,1,256]{2,1,0:T(2,128)(2,1)S(1)} %get-tuple-element.11), channel_id=1, source_target_pairs={{0,8},{8,16},{16,24},{1,9},{9,17},{17,25},{2,10},{10,18},{18,26},{... | collective-permute-start | bytes 98312 | tf_op jit(solution)/shard_map/ppermute | solution.py:16
  203.7 6.2 %collective-permute-start.22 = (bf16[64,1,256]{2,1,0:T(2,128)(2,1)S(1)}, bf16[64,1,256]{2,1,0:T(2,128)(2,1)S(1)}, u32[]{:S(2)}, u32[]{:S(2)}) collective-permute-start(bf16[64,1,256]{2,1,0:T(2,128)(2,1)S(1)} %get-tuple-element.12), channel_id=1, source_target_pairs={{8,0},{16,8},{24,16},{9,1},{17,9},{25,17},{10,2},{18,10},{26,18},{... | collective-permute-start | bytes 98312 | tf_op jit(solution)/shard_map/ppermute | solution.py:19
  209.9 1.3 collective-permute-start.23
  216.8 4.2 %copy-start.6 = (bf16[256,128]{1,0:T(8,128)(2,1)S(1)}, bf16[256,128]{1,0:T(8,128)(2,1)}, u32[]{:S(2)}) copy-start(bf16[256,128]{1,0:T(8,128)(2,1)} %param.15) | copy-start | bytes 196612
  216.8 4.6 %copy-start.7 = (f32[128]{0:T(128)S(1)}, f32[128]{0:T(128)}, u32[]{:S(2)}) copy-start(f32[128]{0:T(128)} %param.16) | copy-start | bytes 1540
  216.8 20.4 %copy-start.1 = (bf16[256,4096]{1,0:T(8,128)(2,1)S(1)}, bf16[256,4096]{1,0:T(8,128)(2,1)}, u32[]{:S(2)}) copy-start(bf16[256,4096]{1,0:T(8,128)(2,1)} %param.11) | copy-start | bytes 6291460
  (1 other events, 1.6 us)
Sparse Core Ops, SparseCore 0:
  8.9 93.4 all-gather.1
where the time goes:
time: 245 us; the launch traced here: 244 us
  waiting for transfers between devices  111 us (45%)
  starting transfers between devices  36.9 us (15%)
  matrix products  26.5 us (11%)
  blocking collectives  24.7 us (10%)
  local copies, waits for them, and re-layouts  18.7 us (8%)
  between operations  14.6 us (6%)
  other arithmetic  11.2 us (5%)
    all_gather x1, waiting for transfers between devices, per_device(): filter_set = lax.all_gather(refine_filters, 'dp', axis=2, tiled=True)  69.8 us
    ppermute x8, waiting for transfers between devices, padded_2(): lax.ppermute(lax.slice_in_dim(block, 0, width, axis=dim), axis, backward)  32.5 us
    ppermute x8, starting transfers between devices, padded_2(): lax.ppermute(lax.slice_in_dim(block, block.shape[dim] - width, None, axis...  25.3 us
    dot_general x8, matrix products, convolve(): result = jnp.dot(patches, matrix, preferred_element_type=jnp.float32)  18.5 us
    all_gather x1, blocking collectives, per_device(): portion = lax.all_gather(depth_tiles[None], 'dp', axis=0, tiled=True)  14 us
    ppermute x8, starting transfers between devices, padded_2(): lax.ppermute(lax.slice_in_dim(block, 0, width, axis=dim), axis, backward)  11 us
    all_to_all x1, blocking collectives, per_device(): lax.all_to_all(projected, 'phase', split_axis=2, concat_axis=0, tiled=True)  10.7 us
    ppermute x8, waiting for transfers between devices, from_partner(): return lax.ppermute(block, axis, route)  7.05 us
  transfers between devices with their start and end apart: 25, of which 21 were waited for; matrix products, arithmetic and copies ran while one was open for 5% of the time, Pallas kernels for 0%

commit v1 on v0

v1 whole, which is shorter than its diff:
```python
import functools

import jax
import jax.numpy as jnp
from jax import lax
from jax.experimental import pallas as pl
from jax.experimental.pallas import tpu as pltpu
from jax.sharding import PartitionSpec as P

G = 32
TILES_DEV = 8
SLOT_DEV = 6
LEVELS = 4
F32 = jnp.float32
BF16 = jnp.bfloat16
VMEM_LIMIT = 60 * 1024 * 1024


LANES = 128


def take(ref, *at):
    return jnp.concatenate([ref[(i,) + at] for i in range(ref.shape[0])], axis=-1)


def put(ref, value, *at):
    for i in range(ref.shape[0]):
        ref[(i,) + at] = value[..., i * LANES : (i + 1) * LANES]


def dot(lhs, rhs):
    return jnp.dot(lhs, rhs, preferred_element_type=F32)


class Plan:
    def __init__(self, phases, channels):
        self.ch = channels
        self.half = G // 2
        self.block = G // phases
        self.sent = 2 * self.block
        self.rows1 = 3 * G // 4
        self.cols1 = self.block + self.block // 2
        self.cols0 = self.block + 2
        self.conv_cols = 4 * self.block + 4
        self.conv_rows = 4 * self.half + 16

    def sent_start(self, s):
        return jnp.clip(s * self.block - self.block // 2, 0, G - self.sent)

    def start1(self, s):
        return jnp.clip(s * self.block - self.block // 4, 0, G - self.cols1)

    def start0(self, s):
        return jnp.clip(s * self.block - 1, 0, G - self.cols0)


def project_kernel(plan, phases, where, tokens, weight, shrink, *refs):
    outs, acc_lo, acc_hi = refs[:phases], refs[phases], refs[phases + 1]
    step = pl.program_id(0)
    part = dot(tokens[0], weight[0])
    lanes = acc_lo.shape[1]

    @pl.when(step == 0)
    def _():
        acc_lo[...] = part[:, :lanes]
        acc_hi[...] = part[:, lanes:]

    @pl.when(step > 0)
    def _():
        acc_lo[...] += part[:, :lanes]
        acc_hi[...] += part[:, lanes:]

    last = step == pl.num_programs(0) - 1
    phase = where[0]

    def column(start, size, stride):
        where_rows = pl.ds(start, size, stride=stride)
        return jnp.concatenate([acc_lo[where_rows, :], acc_hi[where_rows, :]], axis=1)

    @pl.when(last & (phase < LEVELS - 1))
    def _():
        for k in range(phases):
            start = plan.sent_start(phase ^ k)
            for j in range(plan.sent):
                outs[k][j * plan.half : (j + 1) * plan.half, :] = column(
                    start + j, plan.half, G
                ).astype(BF16)

    @pl.when(last & (phase == LEVELS - 1))
    def _():
        total = jnp.zeros((plan.half * plan.half // 2, plan.ch), F32)
        for a in range(2):
            for b in range(2):
                tall = jnp.concatenate(
                    [column(a * G + 2 * j + b, plan.half // 2, 2 * G) for j in range(G // 2)],
                    axis=0,
                )
                total += dot(
                    tall.astype(BF16), shrink[(2 * a + b) * plan.ch : (2 * a + b + 1) * plan.ch, :]
                )
        for k in range(phases):
            outs[k][: total.shape[0], :] = total.astype(BF16)
            outs[k][total.shape[0] :, :] = jnp.zeros(
                (outs[k].shape[0] - total.shape[0], plan.ch), BF16
            )


def project(plan, phases, where, tokens, weight, shrink):
    rows, depth = tokens.shape[1:]
    block = min(depth, 512)
    pixels = plan.sent * plan.half
    out = jax.ShapeDtypeStruct((pixels, plan.ch), BF16)
    return pl.pallas_call(
        functools.partial(project_kernel, plan, phases),
        grid_spec=pltpu.PrefetchScalarGridSpec(
            num_scalar_prefetch=1,
            grid=(depth // block,),
            in_specs=[
                pl.BlockSpec((1, rows, block), lambda i, w: (0, 0, i)),
                pl.BlockSpec((1, block, plan.ch), lambda i, w: (0, i, 0)),
                pl.BlockSpec(shrink.shape, lambda i, w: (0, 0)),
            ],
            out_specs=[pl.BlockSpec((pixels, plan.ch), lambda i, w: (0, 0))] * phases,
            scratch_shapes=[pltpu.VMEM((rows, plan.ch // 2), F32)] * 2,
        ),
        out_shape=[out] * phases,
        compiler_params=pltpu.CompilerParams(vmem_limit_bytes=VMEM_LIMIT),
        cost_estimate=pl.CostEstimate(
            flops=2 * rows * depth * plan.ch,
            bytes_accessed=2 * depth * (rows + plan.ch),
            transcendentals=0,
        ),
        name="project",
    )(where, tokens, weight, shrink)


def put_shifted(shifted, col, value):
    count, rows, _ = value.shape
    value = jnp.maximum(value, 0.0)
    at = lax.broadcasted_iota(jnp.int32, value.shape, 1)
    above = jnp.where(at == 0, 0.0, pltpu.roll(value, 1, 1))
    below = jnp.where(at == rows - 1, 0.0, pltpu.roll(value, rows - 1, 1))
    for p, moved in enumerate((above, value, below)):
        shifted[p, pl.ds(col + 1, count)] = moved.astype(BF16)


def clear_edges(shifted):
    shape = shifted.shape
    zeros = jnp.zeros((shape[0], 1) + shape[2:], BF16)
    shifted[:, 0:1] = zeros
    shifted[:, shape[1] - 1 : shape[1]] = zeros


def conv_block(shifted, weight, col, count, rows):
    channels = shifted.shape[3]
    start, size = rows
    patches = [
        shifted[p, pl.ds(col + q, count), pl.ds(start, size), :].reshape(count * size, channels)
        for p in range(3)
        for q in range(3)
    ]
    return dot(jnp.concatenate(patches, axis=1), weight[...]).reshape(count, size, -1)


def loop(count, body):
    if count == 1:
        body(0)
    else:
        lax.fori_loop(0, count, lambda i, c: (body(i), c)[1], 0)


def refine(source, weights, first, second, chunk, out_col, out_count, out_chunk, emit):
    cols, rows = first.shape[1] - 2, first.shape[2]
    clear_edges(first)
    clear_edges(second)
    loop(cols // chunk, lambda i: put_shifted(first, i * chunk, source(i * chunk, chunk)))

    def inner(i):
        put_shifted(second, i * chunk, conv_block(first, weights[0], i * chunk, chunk, (0, rows)))

    loop(cols // chunk, inner)

    def outer(i):
        col = out_col + i * out_chunk
        branch = conv_block(second, weights[1], col, out_chunk, (0, rows))
        emit(i * out_chunk, source(col, out_chunk) + branch)

    loop(out_count // out_chunk, outer)


def start_filters(filters, level, weights, sems):
    copies = []
    for m in range(2):
        copy = pltpu.make_async_copy(filters.at[level, m], weights.at[m], sems.at[m])
        copy.start()
        copies.append(copy)
    return copies


def pyramid_kernel(
    plan,
    where,
    mine,
    other,
    expand_four,
    expand_two,
    filters,
    summed0,
    weight3,
    weight2,
    weight1,
    sems,
    out_sem,
    patch,
    map3,
    joined3,
    map2,
    joined2,
    map1,
    joined1,
    map0,
    first3,
    second3,
    first2,
    second2,
    first1,
    second1,
):
    ch = plan.ch
    phase, side = where[0], where[1]
    copies = {}
    for level, weights in ((3, weight3), (2, weight2), (1, weight1)):
        copies[level] = start_filters(filters, level, weights, sems.at[level])

    def load_patches(level):
        k = phase ^ level
        for ref, at in ((mine, side), (other, 1 - side)):
            patch[:, pl.ds(pl.multiple_of(at * plan.half, plan.half), plan.half), :] = (
                ref[k].astype(F32).reshape(plan.sent, plan.half, ch)
            )

    def wait(level):
        for copy in copies[level]:
            copy.wait()

    size3 = G // 2
    quarter = plan.half // 2
    k3 = phase ^ 3
    for ref, at in ((mine, side), (other, 1 - side)):
        map3[:, pl.ds(pl.multiple_of(at * quarter, quarter), quarter), :] = (
            ref[k3, : size3 * quarter, :].astype(F32).reshape(size3, quarter, ch)
        )
    wait(3)

    def keep3(col, value):
        joined3[pl.ds(col, value.shape[0])] = value.astype(BF16).astype(F32)

    refine(
        lambda col, n: map3[pl.ds(col, n)], weight3, first3, second3, size3, 0, size3, size3, keep3
    )

    load_patches(2)
    from3 = plan.sent_start(phase) // 2
    tall = joined3[pl.ds(from3, plan.sent // 2)]
    for b in range(2):
        for a in range(2):
            put(map2, tall, slice(None), b, pl.ds(a, size3, stride=2), slice(None))
    for j in range(plan.sent):
        at = (j // 2, j % 2)
        put(map2, take(map2, *at) + patch[j], *at)
    wait(2)

    def source2(col, n):
        return take(map2, pl.ds(col // 2, n // 2)).reshape(n, G, ch)

    def keep2(col, value):
        joined2[pl.ds(col, value.shape[0])] = value.astype(BF16).astype(F32)

    refine(source2, weight2, first2, second2, plan.block, 0, plan.sent, plan.block, keep2)

    load_patches(1)
    row1 = pl.multiple_of(side * (G - plan.rows1), 8)
    off1 = plan.start1(phase) - plan.sent_start(phase)
    tall = patch[pl.ds(off1, plan.cols1), pl.ds(row1, plan.rows1), :]
    lhs = tall.reshape(plan.cols1 * plan.rows1, ch).astype(BF16)
    below = joined2[pl.ds(off1, plan.cols1), pl.ds(row1, plan.rows1), :]
    for a in range(2):
        for b in range(2):
            n = 2 * a + b
            grown = dot(lhs, expand_two[:, n * ch : (n + 1) * ch])
            put(
                map1,
                grown.reshape(plan.cols1, plan.rows1, ch) + below,
                slice(None),
                b,
                pl.ds(a, plan.rows1, stride=2),
                slice(None),
            )
    wait(1)
    off0 = 2 * (plan.start0(phase) - plan.start1(phase))

    def source1(col, n):
        return take(map1, pl.ds(col // 2, n // 2)).reshape(n, 2 * plan.rows1, ch)

    def keep1(col, value):
        at = pl.ds(col // 2, value.shape[0] // 2)
        value = value.astype(BF16).astype(F32)
        put(joined1, value.reshape(value.shape[0] // 2, 2, 2 * plan.rows1, ch), at)

    refine(
        source1, weight1, first1, second1, plan.block, off0, 2 * plan.cols0, 4, keep1
    )

    load_patches(0)
    off = plan.start0(phase) - plan.sent_start(phase)
    tall = patch[pl.ds(off, plan.cols0), pl.ds(row1, plan.rows1), :]
    lhs = tall.reshape(plan.cols0 * plan.rows1, ch).astype(BF16)
    for a in range(4):
        for b in range(4):
            n = 4 * a + b
            grown = dot(lhs, expand_four[:, n * ch : (n + 1) * ch])
            below = take(
                joined1, slice(None), b // 2, pl.ds(a // 2, plan.rows1, stride=2), slice(None)
            )
            put(
                map0,
                grown.reshape(plan.cols0, plan.rows1, ch) + below,
                slice(None),
                b,
                pl.ds(a, plan.rows1, stride=4),
                slice(None),
            )
    own0 = 4 * (phase * plan.block - plan.start0(phase))
    conv0 = jnp.clip(own0 - 2, 0, 4 * plan.cols0 - plan.conv_cols) // 2
    out = pltpu.make_async_copy(
        map0.reshape(ch // LANES, 2 * plan.cols0, 2, 4 * plan.rows1, LANES).at[
            :,
            pl.ds(conv0, plan.conv_cols // 2),
            :,
            pl.ds(pl.multiple_of(side * 16, 16), plan.conv_rows),
            :,
        ],
        summed0,
        out_sem,
    )
    out.start()
    out.wait()


def pyramid(plan, where, mine, other, expand_four, expand_two, filters):
    ch = plan.ch
    depth = filters.shape[2]
    vmem = pl.BlockSpec(memory_space=pltpu.VMEM)
    any_space = pl.BlockSpec(memory_space=pl.ANY)
    weights = pltpu.VMEM((2, depth, ch), BF16)
    size3 = G // 2
    slabs = ch // LANES

    def maps(cols, rows):
        return [pltpu.VMEM((3, cols + 2, rows, ch), BF16)] * 2

    return pl.pallas_call(
        functools.partial(pyramid_kernel, plan),
        out_shape=jax.ShapeDtypeStruct(
            (ch // LANES, plan.conv_cols // 2, 2, plan.conv_rows, LANES), F32
        ),
        in_specs=[pl.BlockSpec(memory_space=pltpu.SMEM), vmem, vmem, vmem, vmem, any_space],
        out_specs=any_space,
        scratch_shapes=[
            weights,
            weights,
            weights,
            pltpu.SemaphoreType.DMA((LEVELS, 2)),
            pltpu.SemaphoreType.DMA,
            pltpu.VMEM((plan.sent, G, ch), F32),
            pltpu.VMEM((size3, size3, ch), F32),
            pltpu.VMEM((size3, size3, ch), F32),
            pltpu.VMEM((slabs, plan.sent // 2, 2, G, LANES), F32),
            pltpu.VMEM((plan.sent, G, ch), F32),
            pltpu.VMEM((slabs, plan.cols1, 2, 2 * plan.rows1, LANES), F32),
            pltpu.VMEM((slabs, plan.cols0, 2, 2 * plan.rows1, LANES), F32),
            pltpu.VMEM((slabs, plan.cols0, 4, 4 * plan.rows1, LANES), F32),
        ]
        + maps(size3, size3)
        + maps(plan.sent, G)
        + maps(2 * plan.cols1, 2 * plan.rows1),
        compiler_params=pltpu.CompilerParams(vmem_limit_bytes=VMEM_LIMIT),
        cost_estimate=pl.CostEstimate(
            flops=5_000_000_000, bytes_accessed=20_000_000, transcendentals=0
        ),
        name="pyramid",
    )(where, mine, other, expand_four, expand_two, filters)


def finest_kernel(plan, where, summed, head, vector, filters, depth, weights, sems, first, second):
    ch = plan.ch
    phase, side = where[0], where[1]
    copies = start_filters(filters, 0, weights, sems)
    cols, rows = plan.conv_cols, plan.conv_rows
    own_rows = 4 * plan.half
    start0 = 4 * plan.start0(phase)
    own0 = 4 * phase * plan.block - start0
    own = own0 - jnp.clip(own0 - 2, 0, 4 * plan.cols0 - cols)
    row = pl.multiple_of(side * 16, 16)
    clear_edges(first)
    clear_edges(second)
    chunk = 4

    def source(col, n):
        return take(summed, pl.ds(col // 2, n // 2)).reshape(n, rows, ch)

    loop(cols // chunk, lambda i: put_shifted(first, i * chunk, source(i * chunk, chunk)))
    copies[0].wait()

    def inner(i):
        put_shifted(
            second, i * chunk, conv_block(first, weights.at[0], i * chunk, chunk, (0, rows))
        )

    loop(cols // chunk, inner)
    copies[1].wait()

    def outer(i):
        col = own + i * chunk
        branch = conv_block(second, weights.at[1], col, chunk, (row, own_rows))
        at = (pl.ds(col // 2, chunk // 2), slice(None), pl.ds(row, own_rows))
        joined = (take(summed, *at).reshape(branch.shape) + branch).astype(BF16)
        hidden = dot(joined.reshape(chunk * own_rows, ch), head[...])
        hidden = jnp.maximum(hidden, 0.0)
        depth[i] = lax.dot_general(
            vector[...],
            hidden,
            (((1,), (1,)), ((), ())),
            precision=lax.Precision.HIGHEST,
            preferred_element_type=F32,
        )

    loop(4 * plan.block // chunk, outer)


def finest(plan, where, summed, head, vector, filters):
    ch = plan.ch
    vmem = pl.BlockSpec(memory_space=pltpu.VMEM)
    own_cols, own_rows = 4 * plan.block, 4 * plan.half
    chunk = 4
    maps = pltpu.VMEM((3, plan.conv_cols + 2, plan.conv_rows, ch), BF16)
    vector = jnp.broadcast_to(vector[None, :], (8, vector.shape[0]))
    return pl.pallas_call(
        functools.partial(finest_kernel, plan),
        out_shape=jax.ShapeDtypeStruct((own_cols // chunk, 8, chunk * own_rows), F32),
        in_specs=[
            pl.BlockSpec(memory_space=pltpu.SMEM),
            vmem,
            vmem,
            vmem,
            pl.BlockSpec(memory_space=pl.ANY),
        ],
        out_specs=vmem,
        scratch_shapes=[
            pltpu.VMEM((2,) + filters.shape[2:], BF16),
            pltpu.SemaphoreType.DMA((2,)),
            maps,
            maps,
        ],
        compiler_params=pltpu.CompilerParams(vmem_limit_bytes=VMEM_LIMIT),
        cost_estimate=pl.CostEstimate(
            flops=6_000_000_000, bytes_accessed=6_000_000, transcendentals=0
        ),
        name="finest",
    )(where, summed, head, vector, filters)


def per_device(
    phases,
    dp_count,
    tap_tokens,
    project_weight,
    expand_four,
    expand_two,
    shrink_weight,
    refine_filters,
    head_matrix,
    head_vector,
    tile_slot,
):
    plan = Plan(phases, project_weight.shape[2])
    phase_id = lax.axis_index("phase")
    dp_id = lax.axis_index("dp")
    where = jnp.stack([phase_id, dp_id % 2]).astype(jnp.int32)
    filters = lax.all_gather(refine_filters, "dp", axis=2, tiled=True)
    sent = project(plan, phases, where, tap_tokens, project_weight, shrink_weight)
    arrived = [sent[0]] + [
        lax.ppermute(sent[k], "phase", [(s, s ^ k) for s in range(phases)])
        for k in range(1, phases)
    ]
    mine = jnp.stack(arrived)
    other = lax.ppermute(mine, "dp", [(d, d ^ 1) for d in range(dp_count)])
    summed = pyramid(plan, where, mine, other, expand_four, expand_two, filters)
    depth = finest(plan, where, summed, head_matrix, head_vector, filters)
    depth = depth[:, 0].reshape(4 * plan.block, TILES_DEV, -1)
    depth_tiles = depth.transpose(1, 2, 0).reshape(TILES_DEV, -1)
    slots = phase_id * dp_count * SLOT_DEV + jnp.arange(dp_count * SLOT_DEV, dtype=jnp.int32)
    targets = lax.dynamic_slice(tile_slot, (dp_id, phase_id, 0), (1, 1, TILES_DEV)).reshape(-1)
    matches = (slots[:, None] == targets[None, :]).astype(F32)
    partial = jnp.dot(matches, depth_tiles, precision=lax.Precision.HIGHEST)
    partial = partial.reshape(dp_count, SLOT_DEV, -1)
    portions = lax.all_to_all(partial, "dp", split_axis=0, concat_axis=0, tiled=True)
    return portions.sum(axis=0)


def solution(mesh):
    in_specs = (
        P("phase", "dp", None),
        P("phase", None, None),
        P(),
        P(),
        P(),
        P(None, None, "dp", None),
        P(),
        P(),
        P(),
    )
    out_specs = P(("phase", "dp"), None)
    body = functools.partial(per_device, mesh.shape["phase"], mesh.shape["dp"])
    return jax.shard_map(
        body, mesh=mesh, in_specs=in_specs, out_specs=out_specs, check_vma=False
    )
```

time: 245 us -> 152 us (0.62)
  Pallas kernels: 0 us -> 40.2 us
  starting transfers between devices: 36.9 us -> 4.54 us
  waiting for transfers between devices: 111 us -> 80.9 us
  matrix products: 26.5 us -> 0.18 us
  local copies, waits for them, and re-layouts: 18.7 us -> 1.76 us
  blocking collectives: 24.7 us -> 8.3 us
  other arithmetic: 11.2 us -> 2.23 us
    pallas_call x0 -> x3, Pallas kernels: none -> 40.2 us  [the longest x1 17.2 us: finest(): pl.pallas_call(functools.partial(finest_kernel, plan), out_shape=jax.Shap...]
    ppermute x24 -> x4, waiting for transfers between devices: 40.9 us -> 8.26 us  [the longest x3 6.48 us: per_device(): lax.ppermute(sent[k], 'phase', [(s, s ^ k) for s in range(phases)])]
    ppermute x24 -> x4, starting transfers between devices: 36.9 us -> 4.54 us  [the longest x3 4.47 us: per_device(): lax.ppermute(sent[k], 'phase', [(s, s ^ k) for s in range(phases)])]
    dot_general x15 -> x1, matrix products: 26.5 us -> 0.18 us  [per_device(): partial = jnp.dot(matches, depth_tiles, precision=lax.Precision.HIGHEST)]
    all_gather x1 -> x0, blocking collectives: 14 us -> none  [per_device(): portion = lax.all_gather(depth_tiles[None], 'dp', axis=0, tiled=True)]
    convert_element_type x6 -> x0, local copies, waits for them, and re-layouts: 8.01 us -> none  [the longest x2 4.22 us: per_device(): inputs[level_id].astype(jnp.float32)]
    unnamed x64 -> x8, local copies, waits for them, and re-layouts: 4.95 us -> 0.02 us
    concatenate x8 -> x0, other arithmetic: 4.24 us -> none  [extend(): return jnp.concatenate([upper_row[None], widened, lower_row[None]], axis=0)]
  transfers between devices with their start and end apart: 25 -> 5, of which waited for: 21 -> 4; matrix products, arithmetic and copies ran while one was open for 5% -> 1% of each run, Pallas kernels for 0% -> 6%
where the time goes in v1:
time: 152 us
  waiting for transfers between devices  80.9 us (53%)
  Pallas kernels  40.2 us (26%)
  between operations  13.5 us (9%)
  blocking collectives  8.3 us (5%)
  starting transfers between devices  4.54 us (3%)
  other arithmetic  2.23 us (1%)
  local copies, waits for them, and re-layouts  1.76 us (1%)
    all_gather x1, waiting for transfers between devices, per_device(): filters = lax.all_gather(refine_filters, 'dp', axis=2, tiled=True)  71.9 us
    pallas_call x1, Pallas kernels, finest(): pl.pallas_call(functools.partial(finest_kernel, plan), out_shape=jax.Shap...  17.2 us
    pallas_call x1, Pallas kernels, pyramid(): pl.pallas_call(functools.partial(pyramid_kernel, plan), out_shape=jax.Sha...  14.3 us
    pallas_call x1, Pallas kernels, project(): pl.pallas_call(functools.partial(project_kernel, plan, phases), grid_spec...  8.7 us
    all_to_all x1, blocking collectives, per_device(): lax.all_to_all(partial, 'dp', split_axis=0, concat_axis=0, tiled=True)  8.3 us
    ppermute x3, waiting for transfers between devices, per_device(): lax.ppermute(sent[k], 'phase', [(s, s ^ k) for s in range(phases)])  6.48 us
    ppermute x3, starting transfers between devices, per_device(): lax.ppermute(sent[k], 'phase', [(s, s ^ k) for s in range(phases)])  4.47 us
  transfers between devices with their start and end apart: 5, of which 4 were waited for; matrix products, arithmetic and copies ran while one was open for 1% of the time, Pallas kernels for 6%

profile of v1, /device:TPU:0, one launch (start us, length us, event | category | flops | bytes accessed | tf_op | source)
XLA Modules:
  0.0 151.6 jit_solution(5506314909399673812)
XLA Ops:
  6.5 0.0 copy-start
  6.5 0.0 all-gather.2.cloned.1.call-start
  6.5 0.7 all-gather.2.cloned.1.call-update
  7.3 0.6 pad_add_fusion.where
  7.8 8.7 %project.1 = (bf16[256,256]{1,0:T(8,128)(2,1)}, bf16[256,256]{1,0:T(8,128)(2,1)}, bf16[256,256]{1,0:T(8,128)(2,1)}, bf16[256,256]{1,0:T(8,128)(2,1)}) custom-call(s32[2]{0:T(128)} %pad_add_fusion.where, bf16[1,512,4096]{2,1,0:T(8,128)(2,1)} %tokens.1, bf16[1,4096,256]{2,1,0:T(8,128)(2,1)} %weight.1, bf16[1024,256]{1,0:T(8,128)(2,1)} %shrink.1), custom_call_target="tpu_custom_call" | custom-call | flops 1073741824 | bytes 6291456 | tf_op jit(solution)/shard_map/project/pallas_call | solution.py:113
  16.5 3.0 %collective-permute-start = (bf16[256,256]{1,0:T(8,128)(2,1)}, bf16[256,256]{1,0:T(8,128)(2,1)S(1)}, u32[]{:S(2)}, u32[]{:S(2)}) collective-permute-start(bf16[256,256]{1,0:T(8,128)(2,1)} %get-tuple-element.10), channel_id=1, source_target_pairs={{0,8},{8,0},{16,24},{24,16},{1,9},{9,1},{17,25},{25,17},{2,10},{10... | collective-permute-start | bytes 393224 | tf_op jit(solution)/shard_map/ppermute | solution.py:493
  19.5 1.4 collective-permute-start.1
  20.9 0.1 collective-permute-start.2
  21.0 2.7 %collective-permute-done = bf16[256,256]{1,0:T(8,128)(2,1)S(1)} collective-permute-done((bf16[256,256]{1,0:T(8,128)(2,1)}, bf16[256,256]{1,0:T(8,128)(2,1)S(1)}, u32[]{:S(2)}, u32[]{:S(2)}) %collective-permute-start) | collective-permute-done | bytes 131104 | tf_op jit(solution)/shard_map/ppermute | solution.py:493
  23.7 3.8 %collective-permute-done.1 = bf16[256,256]{1,0:T(8,128)(2,1)S(1)} collective-permute-done((bf16[256,256]{1,0:T(8,128)(2,1)}, bf16[256,256]{1,0:T(8,128)(2,1)S(1)}, u32[]{:S(2)}, u32[]{:S(2)}) %collective-permute-start.1) | collective-permute-done | bytes 131104 | tf_op jit(solution)/shard_map/ppermute | solution.py:493
  27.5 0.0 collective-permute-done.2
  27.5 1.0 pad_maximum_fusion.mine
  28.5 0.0 copy-start.1
  28.5 0.1 collective-permute-start.3
  28.6 0.0 copy-done
  28.6 0.1 broadcast_compare_fusion
  28.7 0.0 copy-start.2
  28.7 1.8 %collective-permute-done.3.other = bf16[4,256,256]{2,1,0:T(8,128)(2,1)S(1)} collective-permute-done((bf16[4,256,256]{2,1,0:T(8,128)(2,1)S(1)}, bf16[4,256,256]{2,1,0:T(8,128)(2,1)S(1)}, u32[]{:S(2)}, u32[]{:S(2)}) %collective-permute-start.3) | collective-permute-done | bytes 524320 | tf_op jit(solution)/shard_map/ppermute | solution.py:497
  30.5 71.9 %all-gather.2.cloned.1.call-done.filters = bf16[4,2,2304,256]{3,2,1,0:T(8,128)(2,1)} async-done(((bf16[4,2,288,256]{3,2,1,0:T(8,128)(2,1)}), bf16[4,2,2304,256]{3,2,1,0:T(8,128)(2,1)}) %all-gather.2.cloned.1.call-update) | async-done | bytes 9437200 | tf_op jit(solution)/shard_map/all_gather | solution.py:490
  102.4 0.0 copy-done.1
  102.4 0.0 copy-done.3
  102.4 14.3 %pyramid.1.summed = f32[2,18,2,80,128]{4,3,2,1,0:T(8,128)} custom-call(s32[2]{0:T(128)} %pad_add_fusion.where, bf16[4,256,256]{2,1,0:T(8,128)(2,1)} %copy-done.1, bf16[4,256,256]{2,1,0:T(8,128)(2,1)} %copy-done.3, bf16[256,4096]{1,0:T(8,128)(2,1)} %expand_four.1, bf16[256,1024]{1,0:T(8,128)(2,1)} %expand_two.1, ...), custom_call_target="tpu_custom_call" | custom-call | flops 5000000000 | bytes 20000000 | tf_op jit(solution)/shard_map/pyramid/pallas_call | solution.py:362
  116.7 0.0 copy-done.2
  116.7 0.6 broadcast_in_dim.2.vector
  117.3 17.2 %finest.1 = f32[8,8,256]{2,1,0:T(8,128)} custom-call(s32[2]{0:T(128)} %pad_add_fusion.where, f32[2,18,2,80,128]{4,3,2,1,0:T(8,128)} %pyramid.1.summed, bf16[256,128]{1,0:T(8,128)(2,1)} %head.1, f32[8,128]{1,0:T(8,128)} %broadcast_in_dim.2.vector, bf16[4,2,2304,256]{3,2,1,0:T(8,128)(2,1)} %all-gather.2.cloned.1.call-done.filters), custom_call_target="tpu_custom_call" | custom-call | flops 6000000000 | bytes 6000000 | tf_op jit(solution)/shard_map/finest/pallas_call | solution.py:448
  134.5 0.9 slice_reduce_fusion
  135.4 0.1 reshape_squeeze.3
  135.5 0.1 copy.12
  135.6 0.1 reshape.25
  135.6 0.2 fusion
  135.8 8.3 %all_to_all.5 = f32[8,6,256]{2,1,0:T(8,128)S(1)} all-to-all(f32[8,6,256]{2,1,0:T(8,128)S(1)} %fusion), channel_id=1, replica_groups=mesh['phase'=4,'dp'=8] {'dp'}, dimensions={0} | all-to-all | bytes 98304 | tf_op jit(solution)/shard_map/all_to_all | solution.py:507
  144.1 0.6 reduce_sum.9
  (3 shorter events, 0.0 us)
Async XLA Ops:
  6.5 22.0 %copy-start = (s32[8,4,8]{2,1,0:T(4,128)S(1)}, s32[8,4,8]{2,1,0:T(4,128)}, u32[]{:S(2)}) copy-start(s32[8,4,8]{2,1,0:T(4,128)} %param.17) | copy-start | bytes 3076
  6.5 95.9 %all-gather.2.cloned.1.call-start = ((), (), s32[]{:S(2)}) async-start(), calls=%async_computation.1 | async-start | bytes 10616832 | tf_op jit(solution)/shard_map/all_gather | solution.py:490
  16.5 7.2 %collective-permute-start = (bf16[256,256]{1,0:T(8,128)(2,1)}, bf16[256,256]{1,0:T(8,128)(2,1)S(1)}, u32[]{:S(2)}, u32[]{:S(2)}) collective-permute-start(bf16[256,256]{1,0:T(8,128)(2,1)} %get-tuple-element.10), channel_id=1, source_target_pairs={{0,8},{8,0},{16,24},{24,16},{1,9},{9,1},{17,25},{25,17},{2,10},{10... | collective-permute-start | bytes 393224 | tf_op jit(solution)/shard_map/ppermute | solution.py:493
  19.5 8.0 %collective-permute-start.1 = (bf16[256,256]{1,0:T(8,128)(2,1)}, bf16[256,256]{1,0:T(8,128)(2,1)S(1)}, u32[]{:S(2)}, u32[]{:S(2)}) collective-permute-start(bf16[256,256]{1,0:T(8,128)(2,1)} %get-tuple-element.11), channel_id=1, source_target_pairs={{0,16},{8,24},{16,0},{24,8},{1,17},{9,25},{17,1},{25,9},{2,18},{10... | collective-permute-start | bytes 393224 | tf_op jit(solution)/shard_map/ppermute | solution.py:493
  20.9 6.6 %collective-permute-start.2 = (bf16[256,256]{1,0:T(8,128)(2,1)}, bf16[256,256]{1,0:T(8,128)(2,1)S(1)}, u32[]{:S(2)}, u32[]{:S(2)}) collective-permute-start(bf16[256,256]{1,0:T(8,128)(2,1)} %get-tuple-element.12), channel_id=1, source_target_pairs={{0,24},{8,16},{16,8},{24,0},{1,25},{9,17},{17,9},{25,1},{2,26},{10... | collective-permute-start | bytes 393224 | tf_op jit(solution)/shard_map/ppermute | solution.py:493
  28.5 73.9 %copy-start.1 = (bf16[4,256,256]{2,1,0:T(8,128)(2,1)}, bf16[4,256,256]{2,1,0:T(8,128)(2,1)S(1)}, u32[]{:S(2)}) copy-start(bf16[4,256,256]{2,1,0:T(8,128)(2,1)S(1)} %pad_maximum_fusion.mine) | copy-start | bytes 1572868
  28.5 2.0 %collective-permute-start.3 = (bf16[4,256,256]{2,1,0:T(8,128)(2,1)S(1)}, bf16[4,256,256]{2,1,0:T(8,128)(2,1)S(1)}, u32[]{:S(2)}, u32[]{:S(2)}) collective-permute-start(bf16[4,256,256]{2,1,0:T(8,128)(2,1)S(1)} %pad_maximum_fusion.mine), channel_id=1, source_target_pairs={{0,1},{1,0},{2,3},{3,2},{4,5},{5,4},{6,7},{7,6},{8,9},{9,8},{10,11... | collective-permute-start | bytes 1572872 | tf_op jit(solution)/shard_map/ppermute | solution.py:497
  28.7 88.0 %copy-start.2 = (f32[128]{0:T(128)S(1)}, f32[128]{0:T(128)}, u32[]{:S(2)}) copy-start(f32[128]{0:T(128)} %param.16) | copy-start | bytes 1540
  30.5 72.0 %copy-start.3 = (bf16[4,256,256]{2,1,0:T(8,128)(2,1)}, bf16[4,256,256]{2,1,0:T(8,128)(2,1)S(1)}, u32[]{:S(2)}) copy-start(bf16[4,256,256]{2,1,0:T(8,128)(2,1)S(1)} %collective-permute-done.3.other) | copy-start | bytes 1572868
Sparse Core Ops, SparseCore 0:
  8.9 93.4 all-gather.1

commit v2 on v1

--- a/solution.py
+++ b/solution.py
@@ -30,6 +30,10 @@
 
 def dot(lhs, rhs):
     return jnp.dot(lhs, rhs, preferred_element_type=F32)
+
+
+CHIP_ORDER = (2, 1, 3)
+GROUPS = ((1, 2, 3), (0,))
 
 
 class Plan:
@@ -43,6 +47,14 @@
         self.cols0 = self.block + 2
         self.conv_cols = 4 * self.block + 4
         self.conv_rows = 4 * self.half + 16
+
+    def slot_of(self, level):
+        return next(g.index(level) for g in GROUPS if level in g)
+
+    def pieces_of(self, level, filters):
+        groups = GROUPS[:1] if level else GROUPS[1:]
+        n = next(i for i, g in enumerate(groups) if level in g)
+        return filters[2 + 8 * n : 10 + 8 * n]
 
     def sent_start(self, s):
         return jnp.clip(s * self.block - self.block // 2, 0, G - self.sent)
@@ -188,16 +200,52 @@
     loop(out_count // out_chunk, outer)
 
 
-def start_filters(filters, level, weights, sems):
-    copies = []
-    for m in range(2):
-        copy = pltpu.make_async_copy(filters.at[level, m], weights.at[m], sems.at[m])
-        copy.start()
-        copies.append(copy)
-    return copies
+def start_filters(plan, where, filters, level, weights, sem):
+    if len(filters) == 1:
+        pltpu.make_async_copy(filters[0].at[level], weights, sem).start()
+        return
+    phase, side, chip = where[0], where[1], where[2]
+    own, swapped = filters[:2]
+    rows = own.shape[2]
+    part = rows // 2
+    for ref, core in ((own, side), (swapped, 1 - side)):
+        at = pl.ds(pl.multiple_of((2 * chip + core) * rows, 16), rows)
+        pltpu.make_async_copy(ref.at[level], weights.at[:, at], sem).start()
+    at_level = plan.slot_of(level)
+    pieces = plan.pieces_of(level, filters)
+    for refs, core in ((pieces[:4], side), (pieces[4:], 1 - side)):
+        for ref, moved in zip(refs, (0, 1 + core, 2 - core, 3)):
+            quarter = phase ^ moved
+            for i, away in enumerate(CHIP_ORDER):
+                start = (2 * (chip ^ away) + core) * rows + (quarter % 2) * part
+                at = pl.ds(pl.multiple_of(start, 16), part)
+                pltpu.make_async_copy(
+                    ref.at[i, at_level], weights.at[quarter // 2, at], sem
+                ).start()
+
+
+def wait_filters(weights, sem):
+    pltpu.make_async_copy(weights, weights, sem).wait()
 
 
 def pyramid_kernel(
+    plan,
+    where,
+    mine,
+    other,
+    expand_four,
+    expand_two,
+    *refs,
+):
+    count = len(refs) - PYRAMID_SCRATCH
+    filters, refs = refs[:count], refs[count:]
+    pyramid_body(plan, where, mine, other, expand_four, expand_two, filters, *refs)
+
+
+PYRAMID_SCRATCH = 20
+
+
+def pyramid_body(
     plan,
     where,
     mine,
@@ -228,9 +276,9 @@
 ):
     ch = plan.ch
     phase, side = where[0], where[1]
-    copies = {}
-    for level, weights in ((3, weight3), (2, weight2), (1, weight1)):
-        copies[level] = start_filters(filters, level, weights, sems.at[level])
+    weights_of = {3: weight3, 2: weight2, 1: weight1}
+    for level, weights in weights_of.items():
+        start_filters(plan, where, filters, level, weights, sems.at[level])
 
     def load_patches(level):
         k = phase ^ level
@@ -240,8 +288,7 @@
             )
 
     def wait(level):
-        for copy in copies[level]:
-            copy.wait()
+        wait_filters(weights_of[level], sems.at[level])
 
     size3 = G // 2
     quarter = plan.half // 2
@@ -349,7 +396,7 @@
 
 def pyramid(plan, where, mine, other, expand_four, expand_two, filters):
     ch = plan.ch
-    depth = filters.shape[2]
+    depth = 9 * ch
     vmem = pl.BlockSpec(memory_space=pltpu.VMEM)
     any_space = pl.BlockSpec(memory_space=pl.ANY)
     weights = pltpu.VMEM((2, depth, ch), BF16)
@@ -364,13 +411,14 @@
         out_shape=jax.ShapeDtypeStruct(
             (ch // LANES, plan.conv_cols // 2, 2, plan.conv_rows, LANES), F32
         ),
-        in_specs=[pl.BlockSpec(memory_space=pltpu.SMEM), vmem, vmem, vmem, vmem, any_space],
+        in_specs=[pl.BlockSpec(memory_space=pltpu.SMEM), vmem, vmem, vmem, vmem]
+        + [any_space] * len(filters),
         out_specs=any_space,
         scratch_shapes=[
             weights,
             weights,
             weights,
-            pltpu.SemaphoreType.DMA((LEVELS, 2)),
+            pltpu.SemaphoreType.DMA((LEVELS,)),
             pltpu.SemaphoreType.DMA,
             pltpu.VMEM((plan.sent, G, ch), F32),
             pltpu.VMEM((size3, size3, ch), F32),
@@ -389,13 +437,15 @@
             flops=5_000_000_000, bytes_accessed=20_000_000, transcendentals=0
         ),
         name="pyramid",
-    )(where, mine, other, expand_four, expand_two, filters)
-
-
-def finest_kernel(plan, where, summed, head, vector, filters, depth, weights, sems, first, second):
+    )(where, mine, other, expand_four, expand_two, *filters)
+
+
+def finest_kernel(plan, where, summed, head, vector, *refs):
+    filters, refs = refs[:-5], refs[-5:]
+    depth, weights, sem, first, second = refs
     ch = plan.ch
     phase, side = where[0], where[1]
-    copies = start_filters(filters, 0, weights, sems)
+    start_filters(plan, where, filters, 0, weights, sem)
     cols, rows = plan.conv_cols, plan.conv_rows
     own_rows = 4 * plan.half
     start0 = 4 * plan.start0(phase)
@@ -410,7 +460,7 @@
         return take(summed, pl.ds(col // 2, n // 2)).reshape(n, rows, ch)
 
     loop(cols // chunk, lambda i: put_shifted(first, i * chunk, source(i * chunk, chunk)))
-    copies[0].wait()
+    wait_filters(weights, sem)
 
     def inner(i):
         put_shifted(
@@ -418,7 +468,6 @@
         )
 
     loop(cols // chunk, inner)
-    copies[1].wait()
 
     def outer(i):
         col = own + i * chunk
@@ -453,12 +502,12 @@
             vmem,
             vmem,
             vmem,
-            pl.BlockSpec(memory_space=pl.ANY),
-        ],
+        ]
+        + [pl.BlockSpec(memory_space=pl.ANY)] * len(filters),
         out_specs=vmem,
         scratch_shapes=[
-            pltpu.VMEM((2,) + filters.shape[2:], BF16),
-            pltpu.SemaphoreType.DMA((2,)),
+            pltpu.VMEM((2, 9 * ch, ch), BF16),
+            pltpu.SemaphoreType.DMA,
             maps,
             maps,
         ],
@@ -467,7 +516,48 @@
             flops=6_000_000_000, bytes_accessed=6_000_000, transcendentals=0
         ),
         name="finest",
-    )(where, summed, head, vector, filters)
+    )(where, summed, head, vector, *filters)
+
+
+def gather_filters(filters, phases, dp_count):
+    axes = ("phase", "dp")
+    phase_id = lax.axis_index("phase")
+    chips = dp_count // 2
+
+    def move(value, to):
+        route = []
+        for p in range(phases):
+            for z in range(chips):
+                for c in range(2):
+                    q, y, d = to(p, z, c)
+                    route.append((p * dp_count + 2 * z + c, q * dp_count + 2 * y + d))
+        return lax.ppermute(value, axes, route)
+
+    def across(value, bit):
+        return move(value, lambda p, z, c: (p, z ^ bit, c))
+
+    def first(value):
+        return move(value, lambda p, z, c: (p ^ (1 + c), z, c))
+
+    def second(value):
+        return move(value, lambda p, z, c: (p ^ (2 - c), z, c))
+
+    def swap(value):
+        return move(value, lambda p, z, c: (p, z, c ^ 1))
+
+    levels, convs, rows, channels = filters.shape
+    quarters = filters.reshape(levels, phases, convs * rows // phases, channels)
+    swapped = swap(filters)
+    gathered = []
+    for group in GROUPS:
+        part = lax.slice_in_dim(quarters, group[0], group[-1] + 1, axis=0)
+        own = lax.dynamic_index_in_dim(part, phase_id, 1, keepdims=False)
+        far = across(own, 2)
+        column = jnp.stack([far, across(own, 1), across(far, 1)])
+        one = first(column)
+        pieces = [column, one, second(column), second(one)]
+        gathered.append(pieces + [swap(piece) for piece in pieces])
+    return [filters, swapped], gathered
 
 
 def per_device(
@@ -486,8 +576,12 @@
     plan = Plan(phases, project_weight.shape[2])
     phase_id = lax.axis_index("phase")
     dp_id = lax.axis_index("dp")
-    where = jnp.stack([phase_id, dp_id % 2]).astype(jnp.int32)
-    filters = lax.all_gather(refine_filters, "dp", axis=2, tiled=True)
+    where = jnp.stack([phase_id, dp_id % 2, dp_id // 2]).astype(jnp.int32)
+    if phases == 4 and dp_count == 8 and refine_filters.shape[2] % 32 == 0:
+        base, gathered = gather_filters(refine_filters, phases, dp_count)
+        upper, finer = base + gathered[0], base + gathered[1]
+    else:
+        upper = finer = [lax.all_gather(refine_filters, "dp", axis=2, tiled=True)]
     sent = project(plan, phases, where, tap_tokens, project_weight, shrink_weight)
     arrived = [sent[0]] + [
         lax.ppermute(sent[k], "phase", [(s, s ^ k) for s in range(phases)])
@@ -495,8 +589,8 @@
     ]
     mine = jnp.stack(arrived)
     other = lax.ppermute(mine, "dp", [(d, d ^ 1) for d in range(dp_count)])
-    summed = pyramid(plan, where, mine, other, expand_four, expand_two, filters)
-    depth = finest(plan, where, summed, head_matrix, head_vector, filters)
+    summed = pyramid(plan, where, mine, other, expand_four, expand_two, upper)
+    depth = finest(plan, where, summed, head_matrix, head_vector, finer)
     depth = depth[:, 0].reshape(4 * plan.block, TILES_DEV, -1)
     depth_tiles = depth.transpose(1, 2, 0).reshape(TILES_DEV, -1)
     slots = phase_id * dp_count * SLOT_DEV + jnp.arange(dp_count * SLOT_DEV, dtype=jnp.int32)

time: 152 us -> 124 us (0.82)
  waiting for transfers between devices: 80.9 us -> 41.2 us
  starting transfers between devices: 4.54 us -> 25.6 us
  between operations: 13.5 us -> 0.24 us
  blocking collectives: 8.3 us -> 10.4 us
  local copies, waits for them, and re-layouts: 1.76 us -> 3.64 us
    all_gather x1 -> x0, waiting for transfers between devices: 71.9 us -> none  [per_device(): filters = lax.all_gather(refine_filters, 'dp', axis=2, tiled=True)]
    ppermute x0 -> x21, waiting for transfers between devices: none -> 38 us  [move(): return lax.ppermute(value, axes, route)]
    ppermute x0 -> x21, starting transfers between devices: none -> 22.1 us  [move(): return lax.ppermute(value, axes, route)]
    ppermute x3, waiting for transfers between devices: 6.48 us -> 3.16 us  [per_device(): lax.ppermute(sent[k], 'phase', [(s, s ^ k) for s in range(phases)])]
    all_to_all x1, blocking collectives: 8.3 us -> 10.4 us  [per_device(): lax.all_to_all(partial, 'dp', split_axis=0, concat_axis=0, tiled=True)]
    ppermute x1, waiting for transfers between devices: 1.77 us -> 0.01 us  [per_device(): other = lax.ppermute(mine, 'dp', [(d, d ^ 1) for d in range(dp_count)])]
  transfers between devices with their start and end apart: 5 -> 25, of which waited for: 4 -> 13; matrix products, arithmetic and copies ran while one was open for 1% -> 1% of each run, Pallas kernels for 6% -> 18%
where the time goes in v2:
time: 124 us
  waiting for transfers between devices  41.2 us (33%)
  Pallas kernels  40.4 us (33%)
  starting transfers between devices  25.6 us (21%)
  blocking collectives  10.4 us (8%)
  local copies, waits for them, and re-layouts  3.64 us (3%)
  other arithmetic  2.43 us (2%)
    ppermute x21, waiting for transfers between devices, move(): return lax.ppermute(value, axes, route)  38 us
    ppermute x21, starting transfers between devices, move(): return lax.ppermute(value, axes, route)  22.1 us
    pallas_call x1, Pallas kernels, finest(): pl.pallas_call(functools.partial(finest_kernel, plan), out_shape=jax.Shap...  17.5 us
    pallas_call x1, Pallas kernels, pyramid(): pl.pallas_call(functools.partial(pyramid_kernel, plan), out_shape=jax.Sha...  14.2 us
    all_to_all x1, blocking collectives, per_device(): lax.all_to_all(partial, 'dp', split_axis=0, concat_axis=0, tiled=True)  10.4 us
    pallas_call x1, Pallas kernels, project(): pl.pallas_call(functools.partial(project_kernel, plan, phases), grid_spec...  8.69 us
    ppermute x3, starting transfers between devices, per_device(): lax.ppermute(sent[k], 'phase', [(s, s ^ k) for s in range(phases)])  3.49 us
    ppermute x3, waiting for transfers between devices, per_device(): lax.ppermute(sent[k], 'phase', [(s, s ^ k) for s in range(phases)])  3.16 us
  transfers between devices with their start and end apart: 25, of which 13 were waited for; matrix products, arithmetic and copies ran while one was open for 1% of the time, Pallas kernels for 18%

profile of v2, /device:TPU:0, one launch (start us, length us, event | category | flops | bytes accessed | tf_op | source)
XLA Modules:
  0.0 124.0 jit_solution(690012639756968999)
XLA Ops:
  0.0 1.3 %slice.15 = bf16[3,2,288,256]{3,2,1,0:T(8,128)(2,1)S(1)} slice(bf16[4,2,288,256]{3,2,1,0:T(8,128)(2,1)} %refs_0_.3), slice={[1:4], [0:2], [0:288], [0:256]} | slice | bytes 1769472 | tf_op jit(solution)/shard_map/slice | solution.py:553
  1.3 4.1 %collective-permute-start.5 = (bf16[3,144,256]{2,1,0:T(8,128)(2,1)S(1)}, bf16[3,144,256]{2,1,0:T(8,128)(2,1)S(1)}, u32[]{:S(2)}, u32[]{:S(2)}) collective-permute-start(bf16[3,144,256]{2,1,0:T(8,128)(2,1)S(1)} %dynamic-slice_bitcast_fusion), channel_id=1, source_target_pairs={{0,4},{1,5},{2,6},{3,7},{4,0},{5,1},{6,2},{7,3},{8,12},{9,13},{10,... | collective-permute-start | bytes 663560 | tf_op jit(solution)/shard_map/ppermute | solution.py:534
  5.4 1.6 %collective-permute-start.6 = (bf16[3,144,256]{2,1,0:T(8,128)(2,1)S(1)}, bf16[3,144,256]{2,1,0:T(8,128)(2,1)S(1)}, u32[]{:S(2)}, u32[]{:S(2)}) collective-permute-start(bf16[3,144,256]{2,1,0:T(8,128)(2,1)S(1)} %dynamic-slice_bitcast_fusion), channel_id=1, source_target_pairs={{0,2},{1,3},{2,0},{3,1},{4,6},{5,7},{6,4},{7,5},{8,10},{9,11},{10,... | collective-permute-start | bytes 663560 | tf_op jit(solution)/shard_map/ppermute | solution.py:534
  7.0 8.7 %collective-permute-done.5 = bf16[3,144,256]{2,1,0:T(8,128)(2,1)S(1)} collective-permute-done((bf16[3,144,256]{2,1,0:T(8,128)(2,1)S(1)}, bf16[3,144,256]{2,1,0:T(8,128)(2,1)S(1)}, u32[]{:S(2)}, u32[]{:S(2)}) %collective-permute-start.5) | collective-permute-done | bytes 221216 | tf_op jit(solution)/shard_map/ppermute | solution.py:534
  15.7 0.6 collective-permute-start.7
  16.3 5.9 %collective-permute-done.7 = bf16[3,144,256]{2,1,0:T(8,128)(2,1)S(1)} collective-permute-done((bf16[3,144,256]{2,1,0:T(8,128)(2,1)S(1)}, bf16[3,144,256]{2,1,0:T(8,128)(2,1)S(1)}, u32[]{:S(2)}, u32[]{:S(2)}) %collective-permute-start.7) | collective-permute-done | bytes 221216 | tf_op jit(solution)/shard_map/ppermute | solution.py:534
  22.3 1.3 %collective-permute-start.8 = (bf16[3,3,144,256]{3,2,1,0:T(8,128)(2,1)S(1)}, bf16[3,3,144,256]{3,2,1,0:T(8,128)(2,1)S(1)}, u32[]{:S(2)}, u32[]{:S(2)}) collective-permute-start(bf16[3,3,144,256]{3,2,1,0:T(8,128)(2,1)S(1)} %pad_maximum_fusion.refs_2_), channel_id=1, source_target_pairs={{0,8},{1,17},{2,10},{3,19},{4,12},{5,21},{6,14},{7,23},{8,0},{9,25... | collective-permute-start | bytes 1990664 | tf_op jit(solution)/shard_map/ppermute | solution.py:534
  23.7 3.3 %collective-permute-start.15 = (bf16[1,144,256]{2,1,0:T(8,128)(2,1)S(1)}, bf16[1,144,256]{2,1,0:T(8,128)(2,1)S(1)}, u32[]{:S(2)}, u32[]{:S(2)}) collective-permute-start(bf16[1,144,256]{2,1,0:T(8,128)(2,1)S(1)} %dynamic-slice_bitcast_fusion.1), channel_id=1, source_target_pairs={{0,4},{1,5},{2,6},{3,7},{4,0},{5,1},{6,2},{7,3},{8,12},{9,13},{10,... | collective-permute-start | bytes 221192 | tf_op jit(solution)/shard_map/ppermute | solution.py:534
  27.0 1.7 %collective-permute-start.16 = (bf16[1,144,256]{2,1,0:T(8,128)(2,1)S(1)}, bf16[1,144,256]{2,1,0:T(8,128)(2,1)S(1)}, u32[]{:S(2)}, u32[]{:S(2)}) collective-permute-start(bf16[1,144,256]{2,1,0:T(8,128)(2,1)S(1)} %dynamic-slice_bitcast_fusion.1), channel_id=1, source_target_pairs={{0,2},{1,3},{2,0},{3,1},{4,6},{5,7},{6,4},{7,5},{8,10},{9,11},{10,... | collective-permute-start | bytes 221192 | tf_op jit(solution)/shard_map/ppermute | solution.py:534
  28.8 0.7 pad_add_fusion.where
  29.7 1.6 %collective-permute-start.17 = (bf16[1,144,256]{2,1,0:T(8,128)(2,1)S(1)}, bf16[1,144,256]{2,1,0:T(8,128)(2,1)S(1)}, u32[]{:S(2)}, u32[]{:S(2)}) collective-permute-start(bf16[1,144,256]{2,1,0:T(8,128)(2,1)S(1)} %collective-permute-done.15), channel_id=1, source_target_pairs={{0,2},{1,3},{2,0},{3,1},{4,6},{5,7},{6,4},{7,5},{8,10},{9,11},{10,... | collective-permute-start | bytes 221192 | tf_op jit(solution)/shard_map/ppermute | solution.py:534
  31.3 8.7 %project.1 = (bf16[256,256]{1,0:T(8,128)(2,1)}, bf16[256,256]{1,0:T(8,128)(2,1)}, bf16[256,256]{1,0:T(8,128)(2,1)}, bf16[256,256]{1,0:T(8,128)(2,1)}) custom-call(s32[3]{0:T(128)} %pad_add_fusion.where, bf16[1,512,4096]{2,1,0:T(8,128)(2,1)} %tokens.1, bf16[1,4096,256]{2,1,0:T(8,128)(2,1)} %weight.1, bf16[1024,256]{1,0:T(8,128)(2,1)} %shrink.1), custom_call_target="tpu_custom_call" | custom-call | flops 1073741824 | bytes 6291456 | tf_op jit(solution)/shard_map/project/pallas_call | solution.py:125
  40.0 1.2 collective-permute-start
  41.1 0.7 collective-permute-start.1
  41.9 1.6 %collective-permute-start.2 = (bf16[256,256]{1,0:T(8,128)(2,1)}, bf16[256,256]{1,0:T(8,128)(2,1)S(1)}, u32[]{:S(2)}, u32[]{:S(2)}) collective-permute-start(bf16[256,256]{1,0:T(8,128)(2,1)} %get-tuple-element.12), channel_id=1, source_target_pairs={{0,24},{8,16},{16,8},{24,0},{1,25},{9,17},{17,9},{25,1},{2,26},{10... | collective-permute-start | bytes 393224 | tf_op jit(solution)/shard_map/ppermute | solution.py:587
  43.5 1.2 collective-permute-start.18
  44.8 1.0 collective-permute-done
  45.7 2.2 %collective-permute-start.9 = (bf16[3,3,144,256]{3,2,1,0:T(8,128)(2,1)S(1)}, bf16[3,3,144,256]{3,2,1,0:T(8,128)(2,1)}, u32[]{:S(2)}, u32[]{:S(2)}) collective-permute-start(bf16[3,3,144,256]{3,2,1,0:T(8,128)(2,1)S(1)} %pad_maximum_fusion.refs_2_), channel_id=1, source_target_pairs={{0,16},{1,9},{2,18},{3,11},{4,20},{5,13},{6,22},{7,15},{8,24},{9,1... | collective-permute-start | bytes 1990664 | tf_op jit(solution)/shard_map/ppermute | solution.py:534
  48.1 1.9 %collective-permute-done.1 = bf16[256,256]{1,0:T(8,128)(2,1)S(1)} collective-permute-done((bf16[256,256]{1,0:T(8,128)(2,1)}, bf16[256,256]{1,0:T(8,128)(2,1)S(1)}, u32[]{:S(2)}, u32[]{:S(2)}) %collective-permute-start.1) | collective-permute-done | bytes 131104 | tf_op jit(solution)/shard_map/ppermute | solution.py:587
  50.2 1.0 pad_maximum_fusion.1.mine
  51.8 2.2 %collective-permute-done.18.refs_3_ = bf16[3,1,144,256]{3,2,1,0:T(8,128)(2,1)S(1)} collective-permute-done((bf16[3,1,144,256]{3,2,1,0:T(8,128)(2,1)S(1)}, bf16[3,1,144,256]{3,2,1,0:T(8,128)(2,1)S(1)}, u32[]{:S(2)}, u32[]{:S(2)}) %collective-permute-start.18) | collective-permute-done | bytes 221216 | tf_op jit(solution)/shard_map/ppermute | solution.py:534
  54.0 1.6 %collective-permute-start.19 = (bf16[3,1,144,256]{3,2,1,0:T(8,128)(2,1)S(1)}, bf16[3,1,144,256]{3,2,1,0:T(8,128)(2,1)S(1)}, u32[]{:S(2)}, u32[]{:S(2)}) collective-permute-start(bf16[3,1,144,256]{3,2,1,0:T(8,128)(2,1)S(1)} %pad_maximum_fusion.2.refs_2_), channel_id=1, source_target_pairs={{0,16},{1,9},{2,18},{3,11},{4,20},{5,13},{6,22},{7,15},{8,24},{9,1... | collective-permute-start | bytes 663560 | tf_op jit(solution)/shard_map/ppermute | solution.py:534
  55.5 12.5 %collective-permute-done.19.refs_4_ = bf16[3,1,144,256]{3,2,1,0:T(8,128)(2,1)S(1)} collective-permute-done((bf16[3,1,144,256]{3,2,1,0:T(8,128)(2,1)S(1)}, bf16[3,1,144,256]{3,2,1,0:T(8,128)(2,1)S(1)}, u32[]{:S(2)}, u32[]{:S(2)}) %collective-permute-start.19) | collective-permute-done | bytes 221216 | tf_op jit(solution)/shard_map/ppermute | solution.py:534
  68.3 5.7 %collective-permute-done.20.refs_5_ = bf16[3,1,144,256]{3,2,1,0:T(8,128)(2,1)S(1)} collective-permute-done((bf16[3,1,144,256]{3,2,1,0:T(8,128)(2,1)S(1)}, bf16[3,1,144,256]{3,2,1,0:T(8,128)(2,1)S(1)}, u32[]{:S(2)}, u32[]{:S(2)}) %collective-permute-start.20) | collective-permute-done | bytes 221216 | tf_op jit(solution)/shard_map/ppermute | solution.py:534
  75.4 0.8 collective-permute-done.11.refs_6_
  77.3 0.8 collective-permute-done.13.refs_8_
  78.2 0.8 collective-permute-done.14.refs_9_
  79.0 14.2 %pyramid.1.summed = f32[2,18,2,80,128]{4,3,2,1,0:T(8,128)} custom-call(s32[3]{0:T(128)} %pad_add_fusion.where, bf16[4,256,256]{2,1,0:T(8,128)(2,1)} %copy-done.3, bf16[4,256,256]{2,1,0:T(8,128)(2,1)} %copy-done.7, bf16[256,4096]{1,0:T(8,128)(2,1)} %expand_four.1, bf16[256,1024]{1,0:T(8,128)(2,1)} %expand_two.1, bf16[4,2,288,256]{3,2,1,0:T(8,128)(2,1)} %refs_0_.3, ...), custom_call_target="tpu_custom_call" | custom-call | flops 5000000000 | bytes 20000000 | tf_op jit(solution)/shard_map/pyramid/pallas_call | solution.py:409
  93.4 0.7 broadcast_in_dim.2.vector
  94.3 17.5 %finest.1 = f32[8,8,256]{2,1,0:T(8,128)} custom-call(s32[3]{0:T(128)} %pad_add_fusion.where, f32[2,18,2,80,128]{4,3,2,1,0:T(8,128)} %pyramid.1.summed, bf16[256,128]{1,0:T(8,128)(2,1)} %head.1, f32[8,128]{1,0:T(8,128)} %broadcast_in_dim.2.vector, bf16[4,2,288,256]{3,2,1,0:T(8,128)(2,1)} %refs_0_.3, bf16[4,2,288,256]{3,2,1,0:T(8,128)(2,1)} %collective-permute-done.4.refs_1_, ...), custom_call_target="tpu_custom_call" | custom-call | flops 6000000000 | bytes 6000000 | tf_op jit(solution)/shard_map/finest/pallas_call | solution.py:497
  111.7 0.9 slice_reduce_fusion
  113.1 10.4 %all_to_all.5 = f32[8,6,256]{2,1,0:T(8,128)S(1)} all-to-all(f32[8,6,256]{2,1,0:T(8,128)S(1)} %fusion), channel_id=1, replica_groups=mesh['phase'=4,'dp'=8] {'dp'}, dimensions={0} | all-to-all | bytes 98304 | tf_op jit(solution)/shard_map/all_to_all | solution.py:601
  (71 shorter events, 5.5 us)
Async XLA Ops:
  0.0 75.3 %copy-start = (s32[8,4,8]{2,1,0:T(4,128)S(1)}, s32[8,4,8]{2,1,0:T(4,128)}, u32[]{:S(2)}) copy-start(s32[8,4,8]{2,1,0:T(4,128)} %param.17) | copy-start | bytes 3076
  0.0 23.7 %slice-start = ((bf16[4,2,288,256]{3,2,1,0:T(8,128)(2,1)}), bf16[1,2,288,256]{3,2,1,0:T(8,128)(2,1)S(1)}, s32[]{:S(2)}) async-start(bf16[4,2,288,256]{3,2,1,0:T(8,128)(2,1)} %refs_0_.3), calls=%async_computation.1 | async-start | bytes 589824 | tf_op jit(solution)/shard_map/slice | solution.py:553
  1.3 14.4 %collective-permute-start.5 = (bf16[3,144,256]{2,1,0:T(8,128)(2,1)S(1)}, bf16[3,144,256]{2,1,0:T(8,128)(2,1)S(1)}, u32[]{:S(2)}, u32[]{:S(2)}) collective-permute-start(bf16[3,144,256]{2,1,0:T(8,128)(2,1)S(1)} %dynamic-slice_bitcast_fusion), channel_id=1, source_target_pairs={{0,4},{1,5},{2,6},{3,7},{4,0},{5,1},{6,2},{7,3},{8,12},{9,13},{10,... | collective-permute-start | bytes 663560 | tf_op jit(solution)/shard_map/ppermute | solution.py:534
  5.4 10.9 %collective-permute-start.6 = (bf16[3,144,256]{2,1,0:T(8,128)(2,1)S(1)}, bf16[3,144,256]{2,1,0:T(8,128)(2,1)S(1)}, u32[]{:S(2)}, u32[]{:S(2)}) collective-permute-start(bf16[3,144,256]{2,1,0:T(8,128)(2,1)S(1)} %dynamic-slice_bitcast_fusion), channel_id=1, source_target_pairs={{0,2},{1,3},{2,0},{3,1},{4,6},{5,7},{6,4},{7,5},{8,10},{9,11},{10,... | collective-permute-start | bytes 663560 | tf_op jit(solution)/shard_map/ppermute | solution.py:534
  15.7 6.5 %collective-permute-start.7 = (bf16[3,144,256]{2,1,0:T(8,128)(2,1)S(1)}, bf16[3,144,256]{2,1,0:T(8,128)(2,1)S(1)}, u32[]{:S(2)}, u32[]{:S(2)}) collective-permute-start(bf16[3,144,256]{2,1,0:T(8,128)(2,1)S(1)} %collective-permute-done.5), channel_id=1, source_target_pairs={{0,2},{1,3},{2,0},{3,1},{4,6},{5,7},{6,4},{7,5},{8,10},{9,11},{10,... | collective-permute-start | bytes 663560 | tf_op jit(solution)/shard_map/ppermute | solution.py:534
  22.3 51.6 %copy-start.2 = (bf16[3,3,144,256]{3,2,1,0:T(8,128)(2,1)}, bf16[3,3,144,256]{3,2,1,0:T(8,128)(2,1)S(1)}, u32[]{:S(2)}) copy-start(bf16[3,3,144,256]{3,2,1,0:T(8,128)(2,1)S(1)} %pad_maximum_fusion.refs_2_) | copy-start | bytes 1990660
  22.3 25.7 %collective-permute-start.8 = (bf16[3,3,144,256]{3,2,1,0:T(8,128)(2,1)S(1)}, bf16[3,3,144,256]{3,2,1,0:T(8,128)(2,1)S(1)}, u32[]{:S(2)}, u32[]{:S(2)}) collective-permute-start(bf16[3,3,144,256]{3,2,1,0:T(8,128)(2,1)S(1)} %pad_maximum_fusion.refs_2_), channel_id=1, source_target_pairs={{0,8},{1,17},{2,10},{3,19},{4,12},{5,21},{6,14},{7,23},{8,0},{9,25... | collective-permute-start | bytes 1990664 | tf_op jit(solution)/shard_map/ppermute | solution.py:534
  23.7 6.0 %collective-permute-start.15 = (bf16[1,144,256]{2,1,0:T(8,128)(2,1)S(1)}, bf16[1,144,256]{2,1,0:T(8,128)(2,1)S(1)}, u32[]{:S(2)}, u32[]{:S(2)}) collective-permute-start(bf16[1,144,256]{2,1,0:T(8,128)(2,1)S(1)} %dynamic-slice_bitcast_fusion.1), channel_id=1, source_target_pairs={{0,4},{1,5},{2,6},{3,7},{4,0},{5,1},{6,2},{7,3},{8,12},{9,13},{10,... | collective-permute-start | bytes 221192 | tf_op jit(solution)/shard_map/ppermute | solution.py:534
  27.0 14.8 %collective-permute-start.16 = (bf16[1,144,256]{2,1,0:T(8,128)(2,1)S(1)}, bf16[1,144,256]{2,1,0:T(8,128)(2,1)S(1)}, u32[]{:S(2)}, u32[]{:S(2)}) collective-permute-start(bf16[1,144,256]{2,1,0:T(8,128)(2,1)S(1)} %dynamic-slice_bitcast_fusion.1), channel_id=1, source_target_pairs={{0,2},{1,3},{2,0},{3,1},{4,6},{5,7},{6,4},{7,5},{8,10},{9,11},{10,... | collective-permute-start | bytes 221192 | tf_op jit(solution)/shard_map/ppermute | solution.py:534
  29.7 13.8 %collective-permute-start.17 = (bf16[1,144,256]{2,1,0:T(8,128)(2,1)S(1)}, bf16[1,144,256]{2,1,0:T(8,128)(2,1)S(1)}, u32[]{:S(2)}, u32[]{:S(2)}) collective-permute-start(bf16[1,144,256]{2,1,0:T(8,128)(2,1)S(1)} %collective-permute-done.15), channel_id=1, source_target_pairs={{0,2},{1,3},{2,0},{3,1},{4,6},{5,7},{6,4},{7,5},{8,10},{9,11},{10,... | collective-permute-start | bytes 221192 | tf_op jit(solution)/shard_map/ppermute | solution.py:534
  40.0 5.7 %collective-permute-start = (bf16[256,256]{1,0:T(8,128)(2,1)}, bf16[256,256]{1,0:T(8,128)(2,1)S(1)}, u32[]{:S(2)}, u32[]{:S(2)}) collective-permute-start(bf16[256,256]{1,0:T(8,128)(2,1)} %get-tuple-element.10), channel_id=1, source_target_pairs={{0,8},{8,0},{16,24},{24,16},{1,9},{9,1},{17,25},{25,17},{2,10},{10... | collective-permute-start | bytes 393224 | tf_op jit(solution)/shard_map/ppermute | solution.py:587
  41.1 8.8 %collective-permute-start.1 = (bf16[256,256]{1,0:T(8,128)(2,1)}, bf16[256,256]{1,0:T(8,128)(2,1)S(1)}, u32[]{:S(2)}, u32[]{:S(2)}) collective-permute-start(bf16[256,256]{1,0:T(8,128)(2,1)} %get-tuple-element.11), channel_id=1, source_target_pairs={{0,16},{8,24},{16,0},{24,8},{1,17},{9,25},{17,1},{25,9},{2,18},{10... | collective-permute-start | bytes 393224 | tf_op jit(solution)/shard_map/ppermute | solution.py:587
  41.9 8.3 %collective-permute-start.2 = (bf16[256,256]{1,0:T(8,128)(2,1)}, bf16[256,256]{1,0:T(8,128)(2,1)S(1)}, u32[]{:S(2)}, u32[]{:S(2)}) collective-permute-start(bf16[256,256]{1,0:T(8,128)(2,1)} %get-tuple-element.12), channel_id=1, source_target_pairs={{0,24},{8,16},{16,8},{24,0},{1,25},{9,17},{17,9},{25,1},{2,26},{10... | collective-permute-start | bytes 393224 | tf_op jit(solution)/shard_map/ppermute | solution.py:587
  43.5 49.8 %copy-start.4 = (bf16[3,1,144,256]{3,2,1,0:T(8,128)(2,1)}, bf16[3,1,144,256]{3,2,1,0:T(8,128)(2,1)S(1)}, u32[]{:S(2)}) copy-start(bf16[3,1,144,256]{3,2,1,0:T(8,128)(2,1)S(1)} %pad_maximum_fusion.2.refs_2_) | copy-start | bytes 663556
  43.5 10.4 %collective-permute-start.18 = (bf16[3,1,144,256]{3,2,1,0:T(8,128)(2,1)S(1)}, bf16[3,1,144,256]{3,2,1,0:T(8,128)(2,1)S(1)}, u32[]{:S(2)}, u32[]{:S(2)}) collective-permute-start(bf16[3,1,144,256]{3,2,1,0:T(8,128)(2,1)S(1)} %pad_maximum_fusion.2.refs_2_), channel_id=1, source_target_pairs={{0,8},{1,17},{2,10},{3,19},{4,12},{5,21},{6,14},{7,23},{8,0},{9,25... | collective-permute-start | bytes 663560 | tf_op jit(solution)/shard_map/ppermute | solution.py:534
  45.7 28.7 %collective-permute-start.9 = (bf16[3,3,144,256]{3,2,1,0:T(8,128)(2,1)S(1)}, bf16[3,3,144,256]{3,2,1,0:T(8,128)(2,1)}, u32[]{:S(2)}, u32[]{:S(2)}) collective-permute-start(bf16[3,3,144,256]{3,2,1,0:T(8,128)(2,1)S(1)} %pad_maximum_fusion.refs_2_), channel_id=1, source_target_pairs={{0,16},{1,9},{2,18},{3,11},{4,20},{5,13},{6,22},{7,15},{8,24},{9,1... | collective-permute-start | bytes 1990664 | tf_op jit(solution)/shard_map/ppermute | solution.py:534
  48.0 31.0 %copy-start.6 = (bf16[3,3,144,256]{3,2,1,0:T(8,128)(2,1)}, bf16[3,3,144,256]{3,2,1,0:T(8,128)(2,1)S(1)}, u32[]{:S(2)}) copy-start(bf16[3,3,144,256]{3,2,1,0:T(8,128)(2,1)S(1)} %collective-permute-done.8.refs_3_) | copy-start | bytes 1990660
  48.0 26.5 %collective-permute-start.10 = (bf16[3,3,144,256]{3,2,1,0:T(8,128)(2,1)S(1)}, bf16[3,3,144,256]{3,2,1,0:T(8,128)(2,1)}, u32[]{:S(2)}, u32[]{:S(2)}) collective-permute-start(bf16[3,3,144,256]{3,2,1,0:T(8,128)(2,1)S(1)} %collective-permute-done.8.refs_3_), channel_id=1, source_target_pairs={{0,16},{1,9},{2,18},{3,11},{4,20},{5,13},{6,22},{7,15},{8,24},{9,1... | collective-permute-start | bytes 1990664 | tf_op jit(solution)/shard_map/ppermute | solution.py:534
  51.2 27.8 %copy-start.3 = (bf16[4,256,256]{2,1,0:T(8,128)(2,1)}, bf16[4,256,256]{2,1,0:T(8,128)(2,1)S(1)}, u32[]{:S(2)}) copy-start(bf16[4,256,256]{2,1,0:T(8,128)(2,1)S(1)} %pad_maximum_fusion.1.mine) | copy-start | bytes 1572868
  51.2 22.7 %collective-permute-start.3 = (bf16[4,256,256]{2,1,0:T(8,128)(2,1)S(1)}, bf16[4,256,256]{2,1,0:T(8,128)(2,1)S(1)}, u32[]{:S(2)}, u32[]{:S(2)}) collective-permute-start(bf16[4,256,256]{2,1,0:T(8,128)(2,1)S(1)} %pad_maximum_fusion.1.mine), channel_id=1, source_target_pairs={{0,1},{1,0},{2,3},{3,2},{4,5},{5,4},{6,7},{7,6},{8,9},{9,8},{10,11... | collective-permute-start | bytes 1572872 | tf_op jit(solution)/shard_map/ppermute | solution.py:591
  51.3 25.0 %collective-permute-start.4 = (bf16[4,2,288,256]{3,2,1,0:T(8,128)(2,1)S(1)}, bf16[4,2,288,256]{3,2,1,0:T(8,128)(2,1)}, u32[]{:S(2)}, u32[]{:S(2)}) collective-permute-start(bf16[4,2,288,256]{3,2,1,0:T(8,128)(2,1)S(1)} %copy-done.1), channel_id=1, source_target_pairs={{0,1},{1,0},{2,3},{3,2},{4,5},{5,4},{6,7},{7,6},{8,9},{9,8},{10,11... | collective-permute-start | bytes 3538952 | tf_op jit(solution)/shard_map/ppermute | solution.py:534
  54.0 39.3 %copy-start.8 = (bf16[3,1,144,256]{3,2,1,0:T(8,128)(2,1)}, bf16[3,1,144,256]{3,2,1,0:T(8,128)(2,1)S(1)}, u32[]{:S(2)}) copy-start(bf16[3,1,144,256]{3,2,1,0:T(8,128)(2,1)S(1)} %collective-permute-done.18.refs_3_) | copy-start | bytes 663556
  54.0 14.0 %collective-permute-start.19 = (bf16[3,1,144,256]{3,2,1,0:T(8,128)(2,1)S(1)}, bf16[3,1,144,256]{3,2,1,0:T(8,128)(2,1)S(1)}, u32[]{:S(2)}, u32[]{:S(2)}) collective-permute-start(bf16[3,1,144,256]{3,2,1,0:T(8,128)(2,1)S(1)} %pad_maximum_fusion.2.refs_2_), channel_id=1, source_target_pairs={{0,16},{1,9},{2,18},{3,11},{4,20},{5,13},{6,22},{7,15},{8,24},{9,1... | collective-permute-start | bytes 663560 | tf_op jit(solution)/shard_map/ppermute | solution.py:534
  68.0 5.9 %collective-permute-start.20 = (bf16[3,1,144,256]{3,2,1,0:T(8,128)(2,1)S(1)}, bf16[3,1,144,256]{3,2,1,0:T(8,128)(2,1)S(1)}, u32[]{:S(2)}, u32[]{:S(2)}) collective-permute-start(bf16[3,1,144,256]{3,2,1,0:T(8,128)(2,1)S(1)} %collective-permute-done.18.refs_3_), channel_id=1, source_target_pairs={{0,16},{1,9},{2,18},{3,11},{4,20},{5,13},{6,22},{7,15},{8,24},{9,1... | collective-permute-start | bytes 663560 | tf_op jit(solution)/shard_map/ppermute | solution.py:534
  73.9 2.2 %collective-permute-start.11 = (bf16[3,3,144,256]{3,2,1,0:T(8,128)(2,1)S(1)}, bf16[3,3,144,256]{3,2,1,0:T(8,128)(2,1)}, u32[]{:S(2)}, u32[]{:S(2)}) collective-permute-start(bf16[3,3,144,256]{3,2,1,0:T(8,128)(2,1)S(1)} %pad_maximum_fusion.refs_2_), channel_id=1, source_target_pairs={{0,1},{1,0},{2,3},{3,2},{4,5},{5,4},{6,7},{7,6},{8,9},{9,8},{10,11... | collective-permute-start | bytes 1990664 | tf_op jit(solution)/shard_map/ppermute | solution.py:534
  74.0 3.2 %collective-permute-start.12 = (bf16[3,3,144,256]{3,2,1,0:T(8,128)(2,1)S(1)}, bf16[3,3,144,256]{3,2,1,0:T(8,128)(2,1)}, u32[]{:S(2)}, u32[]{:S(2)}) collective-permute-start(bf16[3,3,144,256]{3,2,1,0:T(8,128)(2,1)S(1)} %collective-permute-done.8.refs_3_), channel_id=1, source_target_pairs={{0,1},{1,0},{2,3},{3,2},{4,5},{5,4},{6,7},{7,6},{8,9},{9,8},{10,11... | collective-permute-start | bytes 1990664 | tf_op jit(solution)/shard_map/ppermute | solution.py:534
  74.5 3.6 %collective-permute-start.13 = (bf16[3,3,144,256]{3,2,1,0:T(8,128)(2,1)}, bf16[3,3,144,256]{3,2,1,0:T(8,128)(2,1)}, u32[]{:S(2)}, u32[]{:S(2)}) collective-permute-start(bf16[3,3,144,256]{3,2,1,0:T(8,128)(2,1)} %collective-permute-done.9.refs_4_), channel_id=1, source_target_pairs={{0,1},{1,0},{2,3},{3,2},{4,5},{5,4},{6,7},{7,6},{8,9},{9,8},{10,11... | collective-permute-start | bytes 1990664 | tf_op jit(solution)/shard_map/ppermute | solution.py:534
  74.8 4.2 %collective-permute-start.14 = (bf16[3,3,144,256]{3,2,1,0:T(8,128)(2,1)}, bf16[3,3,144,256]{3,2,1,0:T(8,128)(2,1)}, u32[]{:S(2)}, u32[]{:S(2)}) collective-permute-start(bf16[3,3,144,256]{3,2,1,0:T(8,128)(2,1)} %collective-permute-done.10.refs_5_), channel_id=1, source_target_pairs={{0,1},{1,0},{2,3},{3,2},{4,5},{5,4},{6,7},{7,6},{8,9},{9,8},{10,11... | collective-permute-start | bytes 1990664 | tf_op jit(solution)/shard_map/ppermute | solution.py:534
  76.2 17.1 %collective-permute-start.21 = (bf16[3,1,144,256]{3,2,1,0:T(8,128)(2,1)S(1)}, bf16[3,1,144,256]{3,2,1,0:T(8,128)(2,1)S(1)}, u32[]{:S(2)}, u32[]{:S(2)}) collective-permute-start(bf16[3,1,144,256]{3,2,1,0:T(8,128)(2,1)S(1)} %pad_maximum_fusion.2.refs_2_), channel_id=1, source_target_pairs={{0,1},{1,0},{2,3},{3,2},{4,5},{5,4},{6,7},{7,6},{8,9},{9,8},{10,11... | collective-permute-start | bytes 663560 | tf_op jit(solution)/shard_map/ppermute | solution.py:534
  76.3 17.0 %collective-permute-start.22 = (bf16[3,1,144,256]{3,2,1,0:T(8,128)(2,1)S(1)}, bf16[3,1,144,256]{3,2,1,0:T(8,128)(2,1)S(1)}, u32[]{:S(2)}, u32[]{:S(2)}) collective-permute-start(bf16[3,1,144,256]{3,2,1,0:T(8,128)(2,1)S(1)} %collective-permute-done.18.refs_3_), channel_id=1, source_target_pairs={{0,1},{1,0},{2,3},{3,2},{4,5},{5,4},{6,7},{7,6},{8,9},{9,8},{10,11... | collective-permute-start | bytes 663560 | tf_op jit(solution)/shard_map/ppermute | solution.py:534
  77.1 16.2 %collective-permute-start.23 = (bf16[3,1,144,256]{3,2,1,0:T(8,128)(2,1)}, bf16[3,1,144,256]{3,2,1,0:T(8,128)(2,1)S(1)}, u32[]{:S(2)}, u32[]{:S(2)}) collective-permute-start(bf16[3,1,144,256]{3,2,1,0:T(8,128)(2,1)} %copy-done.9), channel_id=1, source_target_pairs={{0,1},{1,0},{2,3},{3,2},{4,5},{5,4},{6,7},{7,6},{8,9},{9,8},{10,11... | collective-permute-start | bytes 663560 | tf_op jit(solution)/shard_map/ppermute | solution.py:534
  78.1 15.3 %collective-permute-start.24 = (bf16[3,1,144,256]{3,2,1,0:T(8,128)(2,1)}, bf16[3,1,144,256]{3,2,1,0:T(8,128)(2,1)S(1)}, u32[]{:S(2)}, u32[]{:S(2)}) collective-permute-start(bf16[3,1,144,256]{3,2,1,0:T(8,128)(2,1)} %copy-done.10), channel_id=1, source_target_pairs={{0,1},{1,0},{2,3},{3,2},{4,5},{5,4},{6,7},{7,6},{8,9},{9,8},{10,11... | collective-permute-start | bytes 663560 | tf_op jit(solution)/shard_map/ppermute | solution.py:534
  (9 other events, 51.2 us)

commit v3 on v2

v3 whole, which is shorter than its diff:
```python
import functools

import jax
import jax.numpy as jnp
from jax import lax
from jax.experimental import pallas as pl
from jax.experimental.pallas import tpu as pltpu
from jax.sharding import PartitionSpec as P

G = 32
TILES_DEV = 8
SLOT_DEV = 6
LEVELS = 4
F32 = jnp.float32
BF16 = jnp.bfloat16
PROJECT_VMEM = 16 * 1024 * 1024
COARSE_VMEM = 32 * 1024 * 1024
FINE_VMEM = 48 * 1024 * 1024


LANES = 128


def take(ref, *at):
    return jnp.concatenate([ref[(i,) + at] for i in range(ref.shape[0])], axis=-1)


def put(ref, value, *at):
    for i in range(ref.shape[0]):
        ref[(i,) + at] = value[..., i * LANES : (i + 1) * LANES]


def dot(lhs, rhs):
    return jnp.dot(lhs, rhs, preferred_element_type=F32)


CHIP_ORDER = (2, 1, 3)
GROUPS = ((2, 3), (0, 1))


class Plan:
    def __init__(self, phases, channels):
        self.phases = phases
        self.ch = channels
        self.half = G // 2
        self.block = G // phases
        self.sent = 2 * self.block
        self.rows1 = 3 * G // 4
        self.cols1 = self.block + self.block // 2
        self.cols0 = self.block + 2
        self.conv_cols = 4 * self.block + 4
        self.conv_rows = 4 * self.half + 16

    def slot_of(self, level):
        return next(g.index(level) for g in GROUPS if level in g)

    def sent_start(self, s):
        return jnp.clip(s * self.block - self.block // 2, 0, G - self.sent)

    def start1(self, s):
        return jnp.clip(s * self.block - self.block // 4, 0, G - self.cols1)

    def start0(self, s):
        return jnp.clip(s * self.block - 1, 0, G - self.cols0)


def project_kernel(plan, phases, where, tokens, weight, shrink, *refs):
    outs, acc_lo, acc_hi = refs[:phases], refs[phases], refs[phases + 1]
    step = pl.program_id(0)
    part = dot(tokens[0], weight[0])
    lanes = acc_lo.shape[1]

    @pl.when(step == 0)
    def _():
        acc_lo[...] = part[:, :lanes]
        acc_hi[...] = part[:, lanes:]

    @pl.when(step > 0)
    def _():
        acc_lo[...] += part[:, :lanes]
        acc_hi[...] += part[:, lanes:]

    last = step == pl.num_programs(0) - 1
    phase = where[0]

    def column(start, size, stride):
        where_rows = pl.ds(start, size, stride=stride)
        return jnp.concatenate([acc_lo[where_rows, :], acc_hi[where_rows, :]], axis=1)

    @pl.when(last & (phase < LEVELS - 1))
    def _():
        for k in range(phases):
            start = plan.sent_start(phase ^ k)
            for j in range(plan.sent):
                outs[k][j * plan.half : (j + 1) * plan.half, :] = column(
                    start + j, plan.half, G
                ).astype(BF16)

    @pl.when(last & (phase == LEVELS - 1))
    def _():
        total = jnp.zeros((plan.half * plan.half // 2, plan.ch), F32)
        for a in range(2):
            for b in range(2):
                tall = jnp.concatenate(
                    [column(a * G + 2 * j + b, plan.half // 2, 2 * G) for j in range(G // 2)],
                    axis=0,
                )
                total += dot(
                    tall.astype(BF16), shrink[(2 * a + b) * plan.ch : (2 * a + b + 1) * plan.ch, :]
                )
        for k in range(phases):
            outs[k][: total.shape[0], :] = total.astype(BF16)
            outs[k][total.shape[0] :, :] = jnp.zeros(
                (outs[k].shape[0] - total.shape[0], plan.ch), BF16
            )


def project(plan, phases, where, tokens, weight, shrink):
    rows, depth = tokens.shape[1:]
    block = min(depth, 512)
    pixels = plan.sent * plan.half
    out = jax.ShapeDtypeStruct((pixels, plan.ch), BF16)
    return pl.pallas_call(
        functools.partial(project_kernel, plan, phases),
        grid_spec=pltpu.PrefetchScalarGridSpec(
            num_scalar_prefetch=1,
            grid=(depth // block,),
            in_specs=[
                pl.BlockSpec((1, rows, block), lambda i, w: (0, 0, i)),
                pl.BlockSpec((1, block, plan.ch), lambda i, w: (0, i, 0)),
                pl.BlockSpec(shrink.shape, lambda i, w: (0, 0)),
            ],
            out_specs=[pl.BlockSpec((pixels, plan.ch), lambda i, w: (0, 0))] * phases,
            scratch_shapes=[pltpu.VMEM((rows, plan.ch // 2), F32)] * 2,
        ),
        out_shape=[out] * phases,
        compiler_params=pltpu.CompilerParams(vmem_limit_bytes=PROJECT_VMEM),
        cost_estimate=pl.CostEstimate(
            flops=2 * rows * depth * plan.ch,
            bytes_accessed=2 * depth * (rows + plan.ch),
            transcendentals=0,
        ),
        name="project",
    )(where, tokens, weight, shrink)


def put_shifted(shifted, col, value):
    count, rows, _ = value.shape
    value = jnp.maximum(value, 0.0)
    at = lax.broadcasted_iota(jnp.int32, value.shape, 1)
    above = jnp.where(at == 0, 0.0, pltpu.roll(value, 1, 1))
    below = jnp.where(at == rows - 1, 0.0, pltpu.roll(value, rows - 1, 1))
    for p, moved in enumerate((above, value, below)):
        shifted[p, pl.ds(col + 1, count)] = moved.astype(BF16)


def clear_edges(shifted):
    shape = shifted.shape
    zeros = jnp.zeros((shape[0], 1) + shape[2:], BF16)
    shifted[:, 0:1] = zeros
    shifted[:, shape[1] - 1 : shape[1]] = zeros


def conv_block(shifted, weight, col, count, rows):
    channels = shifted.shape[3]
    start, size = rows
    patches = [
        shifted[p, pl.ds(col + q, count), pl.ds(start, size), :].reshape(count * size, channels)
        for p in range(3)
        for q in range(3)
    ]
    return dot(jnp.concatenate(patches, axis=1), weight[...]).reshape(count, size, -1)


def loop(count, body):
    if count == 1:
        body(0)
    else:
        lax.fori_loop(0, count, lambda i, c: (body(i), c)[1], 0)


def refine(source, weights, sems, first, second, chunk, out_col, out_count, out_chunk, emit):
    cols, rows = first.shape[1] - 2, first.shape[2]
    clear_edges(first)
    clear_edges(second)
    loop(cols // chunk, lambda i: put_shifted(first, i * chunk, source(i * chunk, chunk)))

    wait_filters(weights, sems, 0)

    def inner(i):
        put_shifted(second, i * chunk, conv_block(first, weights.at[0], i * chunk, chunk, (0, rows)))

    loop(cols // chunk, inner)

    wait_filters(weights, sems, 1)

    def outer(i):
        col = out_col + i * out_chunk
        branch = conv_block(second, weights.at[1], col, out_chunk, (0, rows))
        emit(i * out_chunk, source(col, out_chunk) + branch)

    loop(out_count // out_chunk, outer)


def start_filters(plan, where, filters, level, weights, sems):
    if len(filters) == 1:
        for m in range(2):
            pltpu.make_async_copy(filters[0].at[level, m], weights.at[m], sems.at[m]).start()
        return
    phase, side, chip = where[0], where[1], where[2]
    own, swapped = filters[:2]
    rows = own.shape[2]
    part = rows // 2
    slot = plan.slot_of(level)
    for m in range(2):
        for ref, core in ((own, side), (swapped, 1 - side)):
            at = pl.ds(pl.multiple_of((2 * chip + core) * rows, 16), rows)
            pltpu.make_async_copy(ref.at[level, m], weights.at[m, at], sems.at[m]).start()

    def start_pieces(p):
        for m in range(2):
            for half in range(2):
                quarter = 2 * m + half
                for i, away in enumerate(CHIP_ORDER):
                    for refs, core in ((filters[2:6], side), (filters[6:10], 1 - side)):
                        start = (2 * (chip ^ away) + core) * rows + half * part
                        at = pl.ds(pl.multiple_of(start, 16), part)
                        moved = p ^ quarter
                        if moved in (0, 3):
                            pltpu.make_async_copy(
                                refs[moved].at[i, slot], weights.at[m, at], sems.at[m]
                            ).start()
                            continue
                        for c in range(2):
                            k = moved if c == 0 else 3 - moved

                            @pl.when(core == c)
                            def _(ref=refs[k], at=at, i=i, m=m):
                                pltpu.make_async_copy(
                                    ref.at[i, slot], weights.at[m, at], sems.at[m]
                                ).start()

    for p in range(plan.phases):

        @pl.when(phase == p)
        def _(p=p):
            start_pieces(p)


def wait_filters(weights, sems, m):
    pltpu.make_async_copy(weights.at[m], weights.at[m], sems.at[m]).wait()


def load_patches(plan, patch, mine, other, k, side):
    for ref, at in ((mine, side), (other, 1 - side)):
        patch[:, pl.ds(pl.multiple_of(at * plan.half, plan.half), plan.half), :] = (
            ref[k].astype(F32).reshape(plan.sent, plan.half, plan.ch)
        )


def rounded(value):
    return value.astype(BF16).astype(F32)


COARSE_SCRATCH = 14


def coarse_kernel(plan, where, mine, other, expand_two, *refs):
    count = len(refs) - COARSE_SCRATCH
    filters = refs[:count]
    (
        summed1,
        patch0,
        weight3,
        weight2,
        sems,
        patch,
        map3,
        joined3,
        map2,
        joined2,
        first3,
        second3,
        first2,
        second2,
    ) = refs[count:]
    ch = plan.ch
    phase, side = where[0], where[1]
    for level, weights in ((3, weight3), (2, weight2)):
        start_filters(plan, where, filters, level, weights, sems.at[level])

    row1 = pl.multiple_of(side * (G - plan.rows1), 8)
    load_patches(plan, patch, mine, other, phase, side)
    off = plan.start0(phase) - plan.sent_start(phase)
    tall = patch[pl.ds(off, plan.cols0), pl.ds(row1, plan.rows1), :]
    patch0[...] = tall.reshape(patch0.shape).astype(BF16)

    size3 = G // 2
    quarter = plan.half // 2
    k3 = phase ^ 3
    for ref, at in ((mine, side), (other, 1 - side)):
        map3[:, pl.ds(pl.multiple_of(at * quarter, quarter), quarter), :] = (
            ref[k3, : size3 * quarter, :].astype(F32).reshape(size3, quarter, ch)
        )

    def keep3(col, value):
        joined3[pl.ds(col, value.shape[0])] = rounded(value)

    refine(
        lambda col, n: map3[pl.ds(col, n)],
        weight3,
        sems.at[3],
        first3,
        second3,
        size3,
        0,
        size3,
        size3,
        keep3,
    )

    load_patches(plan, patch, mine, other, phase ^ 2, side)
    from3 = plan.sent_start(phase) // 2
    tall = joined3[pl.ds(from3, plan.sent // 2)]
    for b in range(2):
        for a in range(2):
            put(map2, tall, slice(None), b, pl.ds(a, size3, stride=2), slice(None))
    for j in range(plan.sent):
        at = (j // 2, j % 2)
        put(map2, take(map2, *at) + patch[j], *at)

    def source2(col, n):
        return take(map2, pl.ds(col // 2, n // 2)).reshape(n, G, ch)

    def keep2(col, value):
        joined2[pl.ds(col, value.shape[0])] = rounded(value)

    refine(
        source2, weight2, sems.at[2], first2, second2, plan.sent, 0, plan.sent, plan.sent, keep2
    )

    load_patches(plan, patch, mine, other, phase ^ 1, side)
    off1 = plan.start1(phase) - plan.sent_start(phase)
    tall = patch[pl.ds(off1, plan.cols1), pl.ds(row1, plan.rows1), :]
    lhs = tall.reshape(plan.cols1 * plan.rows1, ch).astype(BF16)
    below = joined2[pl.ds(off1, plan.cols1), pl.ds(row1, plan.rows1), :]
    for a in range(2):
        for b in range(2):
            n = 2 * a + b
            grown = dot(lhs, expand_two[:, n * ch : (n + 1) * ch])
            put(
                summed1,
                grown.reshape(plan.cols1, plan.rows1, ch) + below,
                slice(None),
                b,
                pl.ds(a, plan.rows1, stride=2),
                slice(None),
            )


def shifted_maps(cols, rows, ch):
    return [pltpu.VMEM((3, cols + 2, rows, ch), BF16)] * 2


def coarse(plan, where, mine, other, expand_two, filters):
    ch = plan.ch
    vmem = pl.BlockSpec(memory_space=pltpu.VMEM)
    weights = pltpu.VMEM((2, 9 * ch, ch), BF16)
    size3 = G // 2
    slabs = ch // LANES
    return pl.pallas_call(
        functools.partial(coarse_kernel, plan),
        out_shape=[
            jax.ShapeDtypeStruct((slabs, plan.cols1, 2, 2 * plan.rows1, LANES), F32),
            jax.ShapeDtypeStruct((plan.cols0 * plan.rows1, ch), BF16),
        ],
        in_specs=[pl.BlockSpec(memory_space=pltpu.SMEM), vmem, vmem, vmem]
        + [pl.BlockSpec(memory_space=pl.ANY)] * len(filters),
        out_specs=[vmem, vmem],
        scratch_shapes=[
            weights,
            weights,
            pltpu.SemaphoreType.DMA((LEVELS, 2)),
            pltpu.VMEM((plan.sent, G, ch), F32),
            pltpu.VMEM((size3, size3, ch), F32),
            pltpu.VMEM((size3, size3, ch), F32),
            pltpu.VMEM((slabs, plan.sent // 2, 2, G, LANES), F32),
            pltpu.VMEM((plan.sent, G, ch), F32),
        ]
        + shifted_maps(size3, size3, ch)
        + shifted_maps(plan.sent, G, ch),
        compiler_params=pltpu.CompilerParams(vmem_limit_bytes=COARSE_VMEM),
        cost_estimate=pl.CostEstimate(
            flops=2_000_000_000, bytes_accessed=8_000_000, transcendentals=0
        ),
        name="coarse",
    )(where, mine, other, expand_two, *filters)


FINE_SCRATCH = 12


def fine_kernel(plan, where, summed1, patch0, head, vector, expand_four, *refs):
    count = len(refs) - FINE_SCRATCH
    filters = refs[:count]
    (
        depth,
        weight1,
        weight0,
        sems,
        grow,
        grow_sem,
        joined1,
        map0,
        first1,
        second1,
        first,
        second,
    ) = refs[count:]
    ch = plan.ch
    phase, side = where[0], where[1]
    start_filters(plan, where, filters, 1, weight1, sems.at[1])
    grow_copy = pltpu.make_async_copy(expand_four, grow, grow_sem)
    grow_copy.start()
    start_filters(plan, where, filters, 0, weight0, sems.at[0])

    off0 = 2 * (plan.start0(phase) - plan.start1(phase))

    def source1(col, n):
        return take(summed1, pl.ds(col // 2, n // 2)).reshape(n, 2 * plan.rows1, ch)

    def keep1(col, value):
        value = rounded(value)
        put(
            joined1,
            value.reshape(value.shape[0] // 2, 2, 2 * plan.rows1, ch),
            pl.ds(col // 2, value.shape[0] // 2),
        )

    refine(
        source1,
        weight1,
        sems.at[1],
        first1,
        second1,
        plan.cols1,
        off0,
        2 * plan.cols0,
        plan.cols0,
        keep1,
    )

    grow_copy.wait()
    for a in range(4):
        for b in range(4):
            n = 4 * a + b
            grown = dot(patch0[...], grow[:, n * ch : (n + 1) * ch])
            below = take(
                joined1, slice(None), b // 2, pl.ds(a // 2, plan.rows1, stride=2), slice(None)
            )
            put(
                map0,
                grown.reshape(plan.cols0, plan.rows1, ch) + below,
                slice(None),
                b,
                pl.ds(a, plan.rows1, stride=4),
                slice(None),
            )
    cols, rows, own_rows = plan.conv_cols, plan.conv_rows, 4 * plan.half
    own0 = 4 * (phase * plan.block - plan.start0(phase))
    conv0 = jnp.clip(own0 - 2, 0, 4 * plan.cols0 - cols)
    own = own0 - conv0
    row = pl.multiple_of(side * 16, 16)
    pairs = map0.reshape(ch // LANES, 2 * plan.cols0, 2, 4 * plan.rows1, LANES)
    chunk = cols // 2

    def source0(col, n, start, size):
        at = (pl.ds((conv0 + col) // 2, n // 2), slice(None), pl.ds(start, size), slice(None))
        return take(pairs, *at).reshape(n, size, ch)

    clear_edges(first)
    clear_edges(second)
    loop(9, lambda i: put_shifted(first, i * 4, source0(i * 4, 4, row, rows)))
    wait_filters(weight0, sems.at[0], 0)

    def inner(i):
        put_shifted(
            second, i * chunk, conv_block(first, weight0.at[0], i * chunk, chunk, (0, rows))
        )

    loop(cols // chunk, inner)
    wait_filters(weight0, sems.at[0], 1)
    half_cols = 2 * plan.block

    def outer(i):
        col = own + i * half_cols
        branch = conv_block(second, weight0.at[1], col, half_cols, (row, own_rows))
        summed = source0(col, half_cols, pl.multiple_of(2 * row, 16), own_rows)
        joined = (summed + branch).astype(BF16)
        hidden = lax.dot_general(
            head[...],
            joined.reshape(half_cols * own_rows, ch),
            (((1,), (1,)), ((), ())),
            preferred_element_type=F32,
        )
        hidden = jnp.maximum(hidden, 0.0) * vector[...]
        depth[i] = jnp.broadcast_to(hidden.sum(axis=0, keepdims=True), depth.shape[1:])

    loop(2, outer)


def fine(plan, where, summed1, patch0, head, vector, expand_four, filters):
    ch = plan.ch
    vmem = pl.BlockSpec(memory_space=pltpu.VMEM)
    any_space = pl.BlockSpec(memory_space=pl.ANY)
    own_rows = 4 * plan.half
    slabs = ch // LANES
    weights = pltpu.VMEM((2, 9 * ch, ch), BF16)
    return pl.pallas_call(
        functools.partial(fine_kernel, plan),
        out_shape=jax.ShapeDtypeStruct((2, 8, 2 * plan.block * own_rows), F32),
        in_specs=[pl.BlockSpec(memory_space=pltpu.SMEM), vmem, vmem, vmem, vmem, any_space]
        + [any_space] * len(filters),
        out_specs=vmem,
        scratch_shapes=[
            weights,
            weights,
            pltpu.SemaphoreType.DMA((LEVELS, 2)),
            pltpu.VMEM(expand_four.shape, BF16),
            pltpu.SemaphoreType.DMA,
            pltpu.VMEM((slabs, plan.cols0, 2, 2 * plan.rows1, LANES), F32),
            pltpu.VMEM((slabs, plan.cols0, 4, 4 * plan.rows1, LANES), F32),
        ]
        + shifted_maps(2 * plan.cols1, 2 * plan.rows1, ch)
        + shifted_maps(plan.conv_cols, plan.conv_rows, ch),
        compiler_params=pltpu.CompilerParams(vmem_limit_bytes=FINE_VMEM),
        cost_estimate=pl.CostEstimate(
            flops=8_000_000_000, bytes_accessed=10_000_000, transcendentals=0
        ),
        name="fine",
    )(where, summed1, patch0, head.T, vector[:, None], expand_four, *filters)


def gather_filters(filters, phases, dp_count):
    axes = ("phase", "dp")
    phase_id = lax.axis_index("phase")
    chips = dp_count // 2

    def move(value, to):
        route = []
        for p in range(phases):
            for z in range(chips):
                for c in range(2):
                    q, y, d = to(p, z, c)
                    route.append((p * dp_count + 2 * z + c, q * dp_count + 2 * y + d))
        return lax.ppermute(value, axes, route)

    def across(value, bit):
        return move(value, lambda p, z, c: (p, z ^ bit, c))

    def first(value):
        return move(value, lambda p, z, c: (p ^ (1 + c), z, c))

    def second(value):
        return move(value, lambda p, z, c: (p ^ (2 - c), z, c))

    def swap(value):
        return move(value, lambda p, z, c: (p, z, c ^ 1))

    levels, convs, rows, channels = filters.shape
    quarters = filters.reshape(levels, phases, convs * rows // phases, channels)
    swapped = swap(filters)
    gathered = []
    for group in GROUPS:
        part = lax.slice_in_dim(quarters, group[0], group[-1] + 1, axis=0)
        own = lax.dynamic_index_in_dim(part, phase_id, 1, keepdims=False)
        far = across(own, 2)
        column = jnp.stack([far, across(own, 1), across(far, 1)])
        one = first(column)
        pieces = [column, one, second(column), second(one)]
        gathered.append(pieces + [swap(piece) for piece in pieces])
    return [filters, swapped], gathered


def per_device(
    phases,
    dp_count,
    tap_tokens,
    project_weight,
    expand_four,
    expand_two,
    shrink_weight,
    refine_filters,
    head_matrix,
    head_vector,
    tile_slot,
):
    plan = Plan(phases, project_weight.shape[2])
    phase_id = lax.axis_index("phase")
    dp_id = lax.axis_index("dp")
    where = jnp.stack([phase_id, dp_id % 2, dp_id // 2]).astype(jnp.int32)
    if phases == 4 and dp_count == 8 and refine_filters.shape[2] % 32 == 0:
        base, gathered = gather_filters(refine_filters, phases, dp_count)
        upper, finer = base + gathered[0], base + gathered[1]
    else:
        upper = finer = [lax.all_gather(refine_filters, "dp", axis=2, tiled=True)]
    sent = project(plan, phases, where, tap_tokens, project_weight, shrink_weight)
    arrived = [sent[0]] + [
        lax.ppermute(sent[k], "phase", [(s, s ^ k) for s in range(phases)])
        for k in range(1, phases)
    ]
    mine = jnp.stack(arrived)
    other = lax.ppermute(mine, "dp", [(d, d ^ 1) for d in range(dp_count)])
    summed1, patch0 = coarse(plan, where, mine, other, expand_two, upper)
    depth = fine(plan, where, summed1, patch0, head_matrix, head_vector, expand_four, finer)
    depth = depth[:, 0].reshape(4 * plan.block, TILES_DEV, -1)
    depth_tiles = depth.transpose(1, 2, 0).reshape(TILES_DEV, -1)
    slots = phase_id * dp_count * SLOT_DEV + jnp.arange(dp_count * SLOT_DEV, dtype=jnp.int32)
    targets = lax.dynamic_slice(tile_slot, (dp_id, phase_id, 0), (1, 1, TILES_DEV)).reshape(-1)
    matches = (slots[:, None] == targets[None, :]).astype(F32)
    partial = jnp.dot(matches, depth_tiles, precision=lax.Precision.HIGHEST)
    partial = partial.reshape(dp_count, SLOT_DEV, -1)
    portions = lax.all_to_all(partial, "dp", split_axis=0, concat_axis=0, tiled=True)
    return portions.sum(axis=0)


def solution(mesh):
    in_specs = (
        P("phase", "dp", None),
        P("phase", None, None),
        P(),
        P(),
        P(),
        P(None, None, "dp", None),
        P(),
        P(),
        P(),
    )
    out_specs = P(("phase", "dp"), None)
    body = functools.partial(per_device, mesh.shape["phase"], mesh.shape["dp"])
    return jax.shard_map(
        body, mesh=mesh, in_specs=in_specs, out_specs=out_specs, check_vma=False
    )
```

time: 124 us -> 104 us (0.84)
  waiting for transfers between devices: 41.2 us -> 28.3 us
  Pallas kernels: 40.4 us -> 28.6 us
  local copies, waits for them, and re-layouts: 3.64 us -> 12.1 us
  starting transfers between devices: 25.6 us -> 22.7 us
  other arithmetic: 2.43 us -> 0.94 us
    ppermute x21, waiting for transfers between devices: 38 us -> 24.6 us  [move(): return lax.ppermute(value, axes, route)]
    pallas_call x2, Pallas kernels: 31.7 us -> 24.2 us  [the longest x1 15.6 us: fine(): pl.pallas_call(functools.partial(fine_kernel, plan), out_shape=jax.ShapeD...]
    unnamed x30 -> x35, local copies, waits for them, and re-layouts: 0.5 us -> 7.85 us
    pallas_call x1, Pallas kernels: 8.69 us -> 4.36 us  [project(): pl.pallas_call(functools.partial(project_kernel, plan, phases), grid_spec...]
    ppermute x21, starting transfers between devices: 22.1 us -> 19.1 us  [move(): return lax.ppermute(value, axes, route)]
    squeeze x2, local copies, waits for them, and re-layouts: 0.03 us -> 1.58 us  [gather_filters(): own = lax.dynamic_index_in_dim(part, phase_id, 1, keepdims=False)]
  transfers between devices with their start and end apart: 25 -> 25, of which waited for: 13 -> 10; matrix products, arithmetic and copies ran while one was open for 1% -> 1% of each run, Pallas kernels for 18% -> 13%
where the time goes in v3:
time: 104 us; the launch traced here: 103 us
  Pallas kernels  28.6 us (28%)
  waiting for transfers between devices  28.3 us (27%)
  starting transfers between devices  22.7 us (22%)
  local copies, waits for them, and re-layouts  12.1 us (12%)
  blocking collectives  10.3 us (10%)
    ppermute x21, waiting for transfers between devices, move(): return lax.ppermute(value, axes, route)  24.6 us
    ppermute x21, starting transfers between devices, move(): return lax.ppermute(value, axes, route)  19.1 us
    pallas_call x1, Pallas kernels, fine(): pl.pallas_call(functools.partial(fine_kernel, plan), out_shape=jax.ShapeD...  15.6 us
    all_to_all x1, blocking collectives, per_device(): lax.all_to_all(partial, 'dp', split_axis=0, concat_axis=0, tiled=True)  10.3 us
    pallas_call x1, Pallas kernels, coarse(): pl.pallas_call(functools.partial(coarse_kernel, plan), out_shape=[jax.Sha...  8.59 us
    unnamed x35, local copies, waits for them, and re-layouts  7.85 us
    pallas_call x1, Pallas kernels, project(): pl.pallas_call(functools.partial(project_kernel, plan, phases), grid_spec...  4.36 us
    ppermute x3, waiting for transfers between devices, per_device(): lax.ppermute(sent[k], 'phase', [(s, s ^ k) for s in range(phases)])  3.75 us
  transfers between devices with their start and end apart: 25, of which 10 were waited for; matrix products, arithmetic and copies ran while one was open for 1% of the time, Pallas kernels for 13%

profile of v3, /device:TPU:0, one launch (start us, length us, event | category | flops | bytes accessed | tf_op | source)
XLA Modules:
  0.0 103.4 jit_solution(9209768134354501001)
XLA Ops:
  0.0 2.3 %fusion.3 = (bf16[2,2,288,256]{3,2,1,0:T(8,128)(2,1)}, bf16[2,2,288,256]{3,2,1,0:T(8,128)(2,1)S(1)}) fusion(bf16[4,2,288,256]{3,2,1,0:T(8,128)(2,1)} %refs_0_.3), kind=kLoop, calls=%fused_computation.13 | loop fusion | bytes 2359296 | tf_op jit(solution)/shard_map/slice | solution.py:575
  3.0 4.1 %collective-permute-start.5 = (bf16[2,144,256]{2,1,0:T(8,128)(2,1)}, bf16[2,144,256]{2,1,0:T(8,128)(2,1)S(1)}, u32[]{:S(2)}, u32[]{:S(2)}) collective-permute-start(bf16[2,144,256]{2,1,0:T(8,128)(2,1)} %dynamic-slice_bitcast_fusion.1), channel_id=1, source_target_pairs={{0,4},{1,5},{2,6},{3,7},{4,0},{5,1},{6,2},{7,3},{8,12},{9,13},{10,... | collective-permute-start | bytes 442376 | tf_op jit(solution)/shard_map/ppermute | solution.py:556
  7.1 2.2 %copy-done.2 = bf16[1,512,4096]{2,1,0:T(8,128)(2,1)S(1)} copy-done((bf16[1,512,4096]{2,1,0:T(8,128)(2,1)S(1)}, bf16[1,512,4096]{2,1,0:T(8,128)(2,1)}, u32[]{:S(2)}) %copy-start.2) | copy-done | bytes 4194328
  9.3 4.4 %project.1 = (bf16[256,256]{1,0:T(8,128)(2,1)S(1)}, bf16[256,256]{1,0:T(8,128)(2,1)S(1)}, bf16[256,256]{1,0:T(8,128)(2,1)S(1)}, bf16[256,256]{1,0:T(8,128)(2,1)S(1)}) custom-call(s32[3]{0:T(128)S(1)} %pad_add_fusion.where, bf16[1,512,4096]{2,1,0:T(8,128)(2,1)S(1)} %copy-done.2, bf16[1,4096,256]{2,1,0:T(8,128)(2,1)S(1)} %copy-done.3, ...), custom_call_target="tpu_custom_call" | custom-call | flops 1073741824 | bytes 6291456 | tf_op jit(solution)/shard_map/project/pallas_call | solution.py:123
  13.7 1.6 %collective-permute-start = (bf16[256,256]{1,0:T(8,128)(2,1)S(1)}, bf16[256,256]{1,0:T(8,128)(2,1)S(1)}, u32[]{:S(2)}, u32[]{:S(2)}) collective-permute-start(bf16[256,256]{1,0:T(8,128)(2,1)S(1)} %get-tuple-element.12), channel_id=1, source_target_pairs={{0,8},{8,0},{16,24},{24,16},{1,9},{9,1},{17,25},{25,17},{2,10},{10... | collective-permute-start | bytes 393224 | tf_op jit(solution)/shard_map/ppermute | solution.py:609
  15.2 1.3 %collective-permute-start.1 = (bf16[256,256]{1,0:T(8,128)(2,1)S(1)}, bf16[256,256]{1,0:T(8,128)(2,1)S(1)}, u32[]{:S(2)}, u32[]{:S(2)}) collective-permute-start(bf16[256,256]{1,0:T(8,128)(2,1)S(1)} %get-tuple-element.13), channel_id=1, source_target_pairs={{0,16},{8,24},{16,0},{24,8},{1,17},{9,25},{17,1},{25,9},{2,18},{10... | collective-permute-start | bytes 393224 | tf_op jit(solution)/shard_map/ppermute | solution.py:609
  17.2 1.6 %collective-permute-start.6 = (bf16[2,144,256]{2,1,0:T(8,128)(2,1)}, bf16[2,144,256]{2,1,0:T(8,128)(2,1)S(1)}, u32[]{:S(2)}, u32[]{:S(2)}) collective-permute-start(bf16[2,144,256]{2,1,0:T(8,128)(2,1)} %dynamic-slice_bitcast_fusion.1), channel_id=1, source_target_pairs={{0,2},{1,3},{2,0},{3,1},{4,6},{5,7},{6,4},{7,5},{8,10},{9,11},{10,... | collective-permute-start | bytes 442376 | tf_op jit(solution)/shard_map/ppermute | solution.py:556
  19.3 3.7 %collective-permute-done.1 = bf16[256,256]{1,0:T(8,128)(2,1)S(1)} collective-permute-done((bf16[256,256]{1,0:T(8,128)(2,1)S(1)}, bf16[256,256]{1,0:T(8,128)(2,1)S(1)}, u32[]{:S(2)}, u32[]{:S(2)}) %collective-permute-start.1) | collective-permute-done | bytes 131104 | tf_op jit(solution)/shard_map/ppermute | solution.py:609
  23.5 1.6 %collective-permute-done.7 = bf16[2,144,256]{2,1,0:T(8,128)(2,1)S(1)} collective-permute-done((bf16[2,144,256]{2,1,0:T(8,128)(2,1)S(1)}, bf16[2,144,256]{2,1,0:T(8,128)(2,1)S(1)}, u32[]{:S(2)}, u32[]{:S(2)}) %collective-permute-start.7) | collective-permute-done | bytes 147488 | tf_op jit(solution)/shard_map/ppermute | solution.py:556
  25.1 1.6 %collective-permute-start.8 = (bf16[3,2,144,256]{3,2,1,0:T(8,128)(2,1)S(1)}, bf16[3,2,144,256]{3,2,1,0:T(8,128)(2,1)}, u32[]{:S(2)}, u32[]{:S(2)}) collective-permute-start(bf16[3,2,144,256]{3,2,1,0:T(8,128)(2,1)S(1)} %pad_maximum_fusion.1.refs_2_), channel_id=1, source_target_pairs={{0,8},{1,17},{2,10},{3,19},{4,12},{5,21},{6,14},{7,23},{8,0},{9,25... | collective-permute-start | bytes 1327112 | tf_op jit(solution)/shard_map/ppermute | solution.py:556
  26.7 0.9 dynamic-slice_bitcast_fusion
  28.0 1.6 %collective-permute-start.16 = (bf16[2,144,256]{2,1,0:T(8,128)(2,1)S(1)}, bf16[2,144,256]{2,1,0:T(8,128)(2,1)S(1)}, u32[]{:S(2)}, u32[]{:S(2)}) collective-permute-start(bf16[2,144,256]{2,1,0:T(8,128)(2,1)S(1)} %dynamic-slice_bitcast_fusion), channel_id=1, source_target_pairs={{0,2},{1,3},{2,0},{3,1},{4,6},{5,7},{6,4},{7,5},{8,10},{9,11},{10,... | collective-permute-start | bytes 442376 | tf_op jit(solution)/shard_map/ppermute | solution.py:556
  29.6 5.2 %collective-permute-done.15 = bf16[2,144,256]{2,1,0:T(8,128)(2,1)S(1)} collective-permute-done((bf16[2,144,256]{2,1,0:T(8,128)(2,1)S(1)}, bf16[2,144,256]{2,1,0:T(8,128)(2,1)S(1)}, u32[]{:S(2)}, u32[]{:S(2)}) %collective-permute-start.15) | collective-permute-done | bytes 147488 | tf_op jit(solution)/shard_map/ppermute | solution.py:556
  34.7 2.1 %collective-permute-start.17 = (bf16[2,144,256]{2,1,0:T(8,128)(2,1)S(1)}, bf16[2,144,256]{2,1,0:T(8,128)(2,1)S(1)}, u32[]{:S(2)}, u32[]{:S(2)}) collective-permute-start(bf16[2,144,256]{2,1,0:T(8,128)(2,1)S(1)} %collective-permute-done.15), channel_id=1, source_target_pairs={{0,2},{1,3},{2,0},{3,1},{4,6},{5,7},{6,4},{7,5},{8,10},{9,11},{10,... | collective-permute-start | bytes 442376 | tf_op jit(solution)/shard_map/ppermute | solution.py:556
  36.9 1.3 %collective-permute-start.9 = (bf16[3,2,144,256]{3,2,1,0:T(8,128)(2,1)S(1)}, bf16[3,2,144,256]{3,2,1,0:T(8,128)(2,1)}, u32[]{:S(2)}, u32[]{:S(2)}) collective-permute-start(bf16[3,2,144,256]{3,2,1,0:T(8,128)(2,1)S(1)} %pad_maximum_fusion.1.refs_2_), channel_id=1, source_target_pairs={{0,16},{1,9},{2,18},{3,11},{4,20},{5,13},{6,22},{7,15},{8,24},{9,1... | collective-permute-start | bytes 1327112 | tf_op jit(solution)/shard_map/ppermute | solution.py:556
  38.2 1.8 %collective-permute-done.17 = bf16[2,144,256]{2,1,0:T(8,128)(2,1)S(1)} collective-permute-done((bf16[2,144,256]{2,1,0:T(8,128)(2,1)S(1)}, bf16[2,144,256]{2,1,0:T(8,128)(2,1)S(1)}, u32[]{:S(2)}, u32[]{:S(2)}) %collective-permute-start.17) | collective-permute-done | bytes 147488 | tf_op jit(solution)/shard_map/ppermute | solution.py:556
  40.1 0.8 copy-done.6
  40.9 1.1 %collective-permute-start.18 = (bf16[3,2,144,256]{3,2,1,0:T(8,128)(2,1)S(1)}, bf16[3,2,144,256]{3,2,1,0:T(8,128)(2,1)}, u32[]{:S(2)}, u32[]{:S(2)}) collective-permute-start(bf16[3,2,144,256]{3,2,1,0:T(8,128)(2,1)S(1)} %pad_maximum_fusion.2.refs_2_), channel_id=1, source_target_pairs={{0,8},{1,17},{2,10},{3,19},{4,12},{5,21},{6,14},{7,23},{8,0},{9,25... | collective-permute-start | bytes 1327112 | tf_op jit(solution)/shard_map/ppermute | solution.py:556
  42.0 0.9 collective-permute-start.19
  43.0 3.5 %collective-permute-done.9.refs_4_ = bf16[3,2,144,256]{3,2,1,0:T(8,128)(2,1)} collective-permute-done((bf16[3,2,144,256]{3,2,1,0:T(8,128)(2,1)S(1)}, bf16[3,2,144,256]{3,2,1,0:T(8,128)(2,1)}, u32[]{:S(2)}, u32[]{:S(2)}) %collective-permute-start.9) | collective-permute-done | bytes 442400 | tf_op jit(solution)/shard_map/ppermute | solution.py:556
  46.4 1.3 %collective-permute-start.10 = (bf16[3,2,144,256]{3,2,1,0:T(8,128)(2,1)}, bf16[3,2,144,256]{3,2,1,0:T(8,128)(2,1)}, u32[]{:S(2)}, u32[]{:S(2)}) collective-permute-start(bf16[3,2,144,256]{3,2,1,0:T(8,128)(2,1)} %collective-permute-done.8.refs_3_), channel_id=1, source_target_pairs={{0,16},{1,9},{2,18},{3,11},{4,20},{5,13},{6,22},{7,15},{8,24},{9,1... | collective-permute-start | bytes 1327112 | tf_op jit(solution)/shard_map/ppermute | solution.py:556
  48.6 4.8 %collective-permute-done.18.refs_3_ = bf16[3,2,144,256]{3,2,1,0:T(8,128)(2,1)} collective-permute-done((bf16[3,2,144,256]{3,2,1,0:T(8,128)(2,1)S(1)}, bf16[3,2,144,256]{3,2,1,0:T(8,128)(2,1)}, u32[]{:S(2)}, u32[]{:S(2)}) %collective-permute-start.18) | collective-permute-done | bytes 442400 | tf_op jit(solution)/shard_map/ppermute | solution.py:556
  53.6 1.1 %collective-permute-done.19.refs_4_ = bf16[3,2,144,256]{3,2,1,0:T(8,128)(2,1)S(1)} collective-permute-done((bf16[3,2,144,256]{3,2,1,0:T(8,128)(2,1)S(1)}, bf16[3,2,144,256]{3,2,1,0:T(8,128)(2,1)S(1)}, u32[]{:S(2)}, u32[]{:S(2)}) %collective-permute-start.19) | collective-permute-done | bytes 442400 | tf_op jit(solution)/shard_map/ppermute | solution.py:556
  55.4 1.3 %collective-permute-start.20 = (bf16[3,2,144,256]{3,2,1,0:T(8,128)(2,1)}, bf16[3,2,144,256]{3,2,1,0:T(8,128)(2,1)}, u32[]{:S(2)}, u32[]{:S(2)}) collective-permute-start(bf16[3,2,144,256]{3,2,1,0:T(8,128)(2,1)} %collective-permute-done.18.refs_3_), channel_id=1, source_target_pairs={{0,16},{1,9},{2,18},{3,11},{4,20},{5,13},{6,22},{7,15},{8,24},{9,1... | collective-permute-start | bytes 1327112 | tf_op jit(solution)/shard_map/ppermute | solution.py:556
  56.8 2.7 %collective-permute-done.10.refs_5_ = bf16[3,2,144,256]{3,2,1,0:T(8,128)(2,1)} collective-permute-done((bf16[3,2,144,256]{3,2,1,0:T(8,128)(2,1)}, bf16[3,2,144,256]{3,2,1,0:T(8,128)(2,1)}, u32[]{:S(2)}, u32[]{:S(2)}) %collective-permute-start.10) | collective-permute-done | bytes 442400 | tf_op jit(solution)/shard_map/ppermute | solution.py:556
  60.6 3.6 %collective-permute-done.20.refs_5_ = bf16[3,2,144,256]{3,2,1,0:T(8,128)(2,1)} collective-permute-done((bf16[3,2,144,256]{3,2,1,0:T(8,128)(2,1)}, bf16[3,2,144,256]{3,2,1,0:T(8,128)(2,1)}, u32[]{:S(2)}, u32[]{:S(2)}) %collective-permute-start.20) | collective-permute-done | bytes 442400 | tf_op jit(solution)/shard_map/ppermute | solution.py:556
  64.6 1.0 copy-done.5
  65.6 1.0 %copy-done.7 = bf16[4,256,256]{2,1,0:T(8,128)(2,1)S(1)} copy-done((bf16[4,256,256]{2,1,0:T(8,128)(2,1)S(1)}, bf16[4,256,256]{2,1,0:T(8,128)(2,1)}, u32[]{:S(2)}) %copy-start.7) | copy-done | bytes 524312
  66.7 1.0 copy-done.12
  67.7 8.6 %coarse.1 = (f32[2,12,2,48,128]{4,3,2,1,0:T(8,128)S(1)}, bf16[240,256]{1,0:T(8,128)(2,1)S(1)}) custom-call(s32[3]{0:T(128)S(1)} %pad_add_fusion.where, bf16[4,256,256]{2,1,0:T(8,128)(2,1)S(1)} %pad_maximum_fusion.mine, bf16[4,256,256]{2,1,0:T(8,128)(2,1)S(1)} %copy-done.7, bf16[256,1024]{1,0:T(8,128)(2,1)S(1)} %copy-done.5, ...), custom_call_target="tpu_custom_call" | custom-call | flops 2000000000 | bytes 8000000 | tf_op jit(solution)/shard_map/coarse/pallas_call | solution.py:371
  76.4 15.6 %fine.1 = f32[2,8,1024]{2,1,0:T(8,128)S(1)} custom-call(s32[3]{0:T(128)S(1)} %pad_add_fusion.where, f32[2,12,2,48,128]{4,3,2,1,0:T(8,128)S(1)} %get-tuple-element.15.summed1, bf16[240,256]{1,0:T(8,128)(2,1)S(1)} %get-tuple-element.16.patch0, bf16[128,256]{1,0:T(8,128)(2,1)S(1)} %bitcast.30, f32[128,1]{1,0:T(8,128)S(1)} %copy.23.vector, ...), custom_call_target="tpu_custom_call" | custom-call | flops 8000000000 | bytes 10000000 | tf_op jit(solution)/shard_map/fine/pallas_call | solution.py:519
  92.5 10.3 %all_to_all.5 = f32[8,6,256]{2,1,0:T(8,128)S(1)} all-to-all(f32[8,6,256]{2,1,0:T(8,128)S(1)} %fusion), channel_id=1, replica_groups=mesh['phase'=4,'dp'=8] {'dp'}, dimensions={0} | all-to-all | bytes 98304 | tf_op jit(solution)/shard_map/all_to_all | solution.py:623
  (74 shorter events, 7.1 us)
Async XLA Ops:
  0.0 64.2 %copy-start = (s32[8,4,8]{2,1,0:T(4,128)S(1)}, s32[8,4,8]{2,1,0:T(4,128)}, u32[]{:S(2)}) copy-start(s32[8,4,8]{2,1,0:T(4,128)} %param.17) | copy-start | bytes 3076
  3.0 15.9 %collective-permute-start.5 = (bf16[2,144,256]{2,1,0:T(8,128)(2,1)}, bf16[2,144,256]{2,1,0:T(8,128)(2,1)S(1)}, u32[]{:S(2)}, u32[]{:S(2)}) collective-permute-start(bf16[2,144,256]{2,1,0:T(8,128)(2,1)} %dynamic-slice_bitcast_fusion.1), channel_id=1, source_target_pairs={{0,4},{1,5},{2,6},{3,7},{4,0},{5,1},{6,2},{7,3},{8,12},{9,13},{10,... | collective-permute-start | bytes 442376 | tf_op jit(solution)/shard_map/ppermute | solution.py:556
  13.7 14.3 %copy-start.1 = (bf16[4,2,288,256]{3,2,1,0:T(8,128)(2,1)S(1)}, bf16[4,2,288,256]{3,2,1,0:T(8,128)(2,1)}, u32[]{:S(2)}) copy-start(bf16[4,2,288,256]{3,2,1,0:T(8,128)(2,1)} %refs_0_.3) | copy-start | bytes 3538948
  13.7 5.6 %collective-permute-start = (bf16[256,256]{1,0:T(8,128)(2,1)S(1)}, bf16[256,256]{1,0:T(8,128)(2,1)S(1)}, u32[]{:S(2)}, u32[]{:S(2)}) collective-permute-start(bf16[256,256]{1,0:T(8,128)(2,1)S(1)} %get-tuple-element.12), channel_id=1, source_target_pairs={{0,8},{8,0},{16,24},{24,16},{1,9},{9,1},{17,25},{25,17},{2,10},{10... | collective-permute-start | bytes 393224 | tf_op jit(solution)/shard_map/ppermute | solution.py:609
  15.2 7.8 %collective-permute-start.1 = (bf16[256,256]{1,0:T(8,128)(2,1)S(1)}, bf16[256,256]{1,0:T(8,128)(2,1)S(1)}, u32[]{:S(2)}, u32[]{:S(2)}) collective-permute-start(bf16[256,256]{1,0:T(8,128)(2,1)S(1)} %get-tuple-element.13), channel_id=1, source_target_pairs={{0,16},{8,24},{16,0},{24,8},{1,17},{9,25},{17,1},{25,9},{2,18},{10... | collective-permute-start | bytes 393224 | tf_op jit(solution)/shard_map/ppermute | solution.py:609
  16.6 6.4 %collective-permute-start.2 = (bf16[256,256]{1,0:T(8,128)(2,1)S(1)}, bf16[256,256]{1,0:T(8,128)(2,1)S(1)}, u32[]{:S(2)}, u32[]{:S(2)}) collective-permute-start(bf16[256,256]{1,0:T(8,128)(2,1)S(1)} %get-tuple-element.14), channel_id=1, source_target_pairs={{0,24},{8,16},{16,8},{24,0},{1,25},{9,17},{17,9},{25,1},{2,26},{10... | collective-permute-start | bytes 393224 | tf_op jit(solution)/shard_map/ppermute | solution.py:609
  17.2 6.3 %collective-permute-start.6 = (bf16[2,144,256]{2,1,0:T(8,128)(2,1)}, bf16[2,144,256]{2,1,0:T(8,128)(2,1)S(1)}, u32[]{:S(2)}, u32[]{:S(2)}) collective-permute-start(bf16[2,144,256]{2,1,0:T(8,128)(2,1)} %dynamic-slice_bitcast_fusion.1), channel_id=1, source_target_pairs={{0,2},{1,3},{2,0},{3,1},{4,6},{5,7},{6,4},{7,5},{8,10},{9,11},{10,... | collective-permute-start | bytes 442376 | tf_op jit(solution)/shard_map/ppermute | solution.py:556
  18.8 6.3 %collective-permute-start.7 = (bf16[2,144,256]{2,1,0:T(8,128)(2,1)S(1)}, bf16[2,144,256]{2,1,0:T(8,128)(2,1)S(1)}, u32[]{:S(2)}, u32[]{:S(2)}) collective-permute-start(bf16[2,144,256]{2,1,0:T(8,128)(2,1)S(1)} %collective-permute-done.5), channel_id=1, source_target_pairs={{0,2},{1,3},{2,0},{3,1},{4,6},{5,7},{6,4},{7,5},{8,10},{9,11},{10,... | collective-permute-start | bytes 442376 | tf_op jit(solution)/shard_map/ppermute | solution.py:556
  23.1 41.2 %copy-start.15 = (bf16[256,128]{1,0:T(8,128)(2,1)S(1)}, bf16[256,128]{1,0:T(8,128)(2,1)}, u32[]{:S(2)}) copy-start(bf16[256,128]{1,0:T(8,128)(2,1)} %param.15) | copy-start | bytes 196612
  23.1 41.3 %copy-start.16 = (f32[128]{0:T(128)S(1)}, f32[128]{0:T(128)}, u32[]{:S(2)}) copy-start(f32[128]{0:T(128)} %param.16) | copy-start | bytes 1540
  23.1 17.0 %collective-permute-start.3 = (bf16[4,256,256]{2,1,0:T(8,128)(2,1)S(1)}, bf16[4,256,256]{2,1,0:T(8,128)(2,1)S(1)}, u32[]{:S(2)}, u32[]{:S(2)}) collective-permute-start(bf16[4,256,256]{2,1,0:T(8,128)(2,1)S(1)} %pad_maximum_fusion.mine), channel_id=1, source_target_pairs={{0,1},{1,0},{2,3},{3,2},{4,5},{5,4},{6,7},{7,6},{8,9},{9,8},{10,11... | collective-permute-start | bytes 1572872 | tf_op jit(solution)/shard_map/ppermute | solution.py:613
  25.1 16.9 %collective-permute-start.8 = (bf16[3,2,144,256]{3,2,1,0:T(8,128)(2,1)S(1)}, bf16[3,2,144,256]{3,2,1,0:T(8,128)(2,1)}, u32[]{:S(2)}, u32[]{:S(2)}) collective-permute-start(bf16[3,2,144,256]{3,2,1,0:T(8,128)(2,1)S(1)} %pad_maximum_fusion.1.refs_2_), channel_id=1, source_target_pairs={{0,8},{1,17},{2,10},{3,19},{4,12},{5,21},{6,14},{7,23},{8,0},{9,25... | collective-permute-start | bytes 1327112 | tf_op jit(solution)/shard_map/ppermute | solution.py:556
  27.6 7.1 %collective-permute-start.15 = (bf16[2,144,256]{2,1,0:T(8,128)(2,1)S(1)}, bf16[2,144,256]{2,1,0:T(8,128)(2,1)S(1)}, u32[]{:S(2)}, u32[]{:S(2)}) collective-permute-start(bf16[2,144,256]{2,1,0:T(8,128)(2,1)S(1)} %dynamic-slice_bitcast_fusion), channel_id=1, source_target_pairs={{0,4},{1,5},{2,6},{3,7},{4,0},{5,1},{6,2},{7,3},{8,12},{9,13},{10,... | collective-permute-start | bytes 442376 | tf_op jit(solution)/shard_map/ppermute | solution.py:556
  28.0 32.2 %collective-permute-start.4 = (bf16[4,2,288,256]{3,2,1,0:T(8,128)(2,1)S(1)}, bf16[4,2,288,256]{3,2,1,0:T(8,128)(2,1)S(1)}, u32[]{:S(2)}, u32[]{:S(2)}) collective-permute-start(bf16[4,2,288,256]{3,2,1,0:T(8,128)(2,1)S(1)} %copy-done.1), channel_id=1, source_target_pairs={{0,1},{1,0},{2,3},{3,2},{4,5},{5,4},{6,7},{7,6},{8,9},{9,8},{10,11... | collective-permute-start | bytes 3538952 | tf_op jit(solution)/shard_map/ppermute | solution.py:556
  28.0 8.9 %collective-permute-start.16 = (bf16[2,144,256]{2,1,0:T(8,128)(2,1)S(1)}, bf16[2,144,256]{2,1,0:T(8,128)(2,1)S(1)}, u32[]{:S(2)}, u32[]{:S(2)}) collective-permute-start(bf16[2,144,256]{2,1,0:T(8,128)(2,1)S(1)} %dynamic-slice_bitcast_fusion), channel_id=1, source_target_pairs={{0,2},{1,3},{2,0},{3,1},{4,6},{5,7},{6,4},{7,5},{8,10},{9,11},{10,... | collective-permute-start | bytes 442376 | tf_op jit(solution)/shard_map/ppermute | solution.py:556
  34.7 5.2 %collective-permute-start.17 = (bf16[2,144,256]{2,1,0:T(8,128)(2,1)S(1)}, bf16[2,144,256]{2,1,0:T(8,128)(2,1)S(1)}, u32[]{:S(2)}, u32[]{:S(2)}) collective-permute-start(bf16[2,144,256]{2,1,0:T(8,128)(2,1)S(1)} %collective-permute-done.15), channel_id=1, source_target_pairs={{0,2},{1,3},{2,0},{3,1},{4,6},{5,7},{6,4},{7,5},{8,10},{9,11},{10,... | collective-permute-start | bytes 442376 | tf_op jit(solution)/shard_map/ppermute | solution.py:556
  36.9 9.6 %collective-permute-start.9 = (bf16[3,2,144,256]{3,2,1,0:T(8,128)(2,1)S(1)}, bf16[3,2,144,256]{3,2,1,0:T(8,128)(2,1)}, u32[]{:S(2)}, u32[]{:S(2)}) collective-permute-start(bf16[3,2,144,256]{3,2,1,0:T(8,128)(2,1)S(1)} %pad_maximum_fusion.1.refs_2_), channel_id=1, source_target_pairs={{0,16},{1,9},{2,18},{3,11},{4,20},{5,13},{6,22},{7,15},{8,24},{9,1... | collective-permute-start | bytes 1327112 | tf_op jit(solution)/shard_map/ppermute | solution.py:556
  40.0 7.8 %collective-permute-start.11 = (bf16[3,2,144,256]{3,2,1,0:T(8,128)(2,1)S(1)}, bf16[3,2,144,256]{3,2,1,0:T(8,128)(2,1)S(1)}, u32[]{:S(2)}, u32[]{:S(2)}) collective-permute-start(bf16[3,2,144,256]{3,2,1,0:T(8,128)(2,1)S(1)} %pad_maximum_fusion.1.refs_2_), channel_id=1, source_target_pairs={{0,1},{1,0},{2,3},{3,2},{4,5},{5,4},{6,7},{7,6},{8,9},{9,8},{10,11... | collective-permute-start | bytes 1327112 | tf_op jit(solution)/shard_map/ppermute | solution.py:556
  40.9 12.5 %collective-permute-start.18 = (bf16[3,2,144,256]{3,2,1,0:T(8,128)(2,1)S(1)}, bf16[3,2,144,256]{3,2,1,0:T(8,128)(2,1)}, u32[]{:S(2)}, u32[]{:S(2)}) collective-permute-start(bf16[3,2,144,256]{3,2,1,0:T(8,128)(2,1)S(1)} %pad_maximum_fusion.2.refs_2_), channel_id=1, source_target_pairs={{0,8},{1,17},{2,10},{3,19},{4,12},{5,21},{6,14},{7,23},{8,0},{9,25... | collective-permute-start | bytes 1327112 | tf_op jit(solution)/shard_map/ppermute | solution.py:556
  42.0 12.6 %collective-permute-start.19 = (bf16[3,2,144,256]{3,2,1,0:T(8,128)(2,1)S(1)}, bf16[3,2,144,256]{3,2,1,0:T(8,128)(2,1)S(1)}, u32[]{:S(2)}, u32[]{:S(2)}) collective-permute-start(bf16[3,2,144,256]{3,2,1,0:T(8,128)(2,1)S(1)} %pad_maximum_fusion.2.refs_2_), channel_id=1, source_target_pairs={{0,16},{1,9},{2,18},{3,11},{4,20},{5,13},{6,22},{7,15},{8,24},{9,1... | collective-permute-start | bytes 1327112 | tf_op jit(solution)/shard_map/ppermute | solution.py:556
  46.4 13.1 %collective-permute-start.10 = (bf16[3,2,144,256]{3,2,1,0:T(8,128)(2,1)}, bf16[3,2,144,256]{3,2,1,0:T(8,128)(2,1)}, u32[]{:S(2)}, u32[]{:S(2)}) collective-permute-start(bf16[3,2,144,256]{3,2,1,0:T(8,128)(2,1)} %collective-permute-done.8.refs_3_), channel_id=1, source_target_pairs={{0,16},{1,9},{2,18},{3,11},{4,20},{5,13},{6,22},{7,15},{8,24},{9,1... | collective-permute-start | bytes 1327112 | tf_op jit(solution)/shard_map/ppermute | solution.py:556
  48.6 10.9 %collective-permute-start.12 = (bf16[3,2,144,256]{3,2,1,0:T(8,128)(2,1)}, bf16[3,2,144,256]{3,2,1,0:T(8,128)(2,1)}, u32[]{:S(2)}, u32[]{:S(2)}) collective-permute-start(bf16[3,2,144,256]{3,2,1,0:T(8,128)(2,1)} %collective-permute-done.8.refs_3_), channel_id=1, source_target_pairs={{0,1},{1,0},{2,3},{3,2},{4,5},{5,4},{6,7},{7,6},{8,9},{9,8},{10,11... | collective-permute-start | bytes 1327112 | tf_op jit(solution)/shard_map/ppermute | solution.py:556
  53.4 6.6 %collective-permute-start.13 = (bf16[3,2,144,256]{3,2,1,0:T(8,128)(2,1)}, bf16[3,2,144,256]{3,2,1,0:T(8,128)(2,1)}, u32[]{:S(2)}, u32[]{:S(2)}) collective-permute-start(bf16[3,2,144,256]{3,2,1,0:T(8,128)(2,1)} %collective-permute-done.9.refs_4_), channel_id=1, source_target_pairs={{0,1},{1,0},{2,3},{3,2},{4,5},{5,4},{6,7},{7,6},{8,9},{9,8},{10,11... | collective-permute-start | bytes 1327112 | tf_op jit(solution)/shard_map/ppermute | solution.py:556
  55.4 8.8 %collective-permute-start.20 = (bf16[3,2,144,256]{3,2,1,0:T(8,128)(2,1)}, bf16[3,2,144,256]{3,2,1,0:T(8,128)(2,1)}, u32[]{:S(2)}, u32[]{:S(2)}) collective-permute-start(bf16[3,2,144,256]{3,2,1,0:T(8,128)(2,1)} %collective-permute-done.18.refs_3_), channel_id=1, source_target_pairs={{0,16},{1,9},{2,18},{3,11},{4,20},{5,13},{6,22},{7,15},{8,24},{9,1... | collective-permute-start | bytes 1327112 | tf_op jit(solution)/shard_map/ppermute | solution.py:556
  59.5 5.1 %collective-permute-start.14 = (bf16[3,2,144,256]{3,2,1,0:T(8,128)(2,1)}, bf16[3,2,144,256]{3,2,1,0:T(8,128)(2,1)}, u32[]{:S(2)}, u32[]{:S(2)}) collective-permute-start(bf16[3,2,144,256]{3,2,1,0:T(8,128)(2,1)} %collective-permute-done.10.refs_5_), channel_id=1, source_target_pairs={{0,1},{1,0},{2,3},{3,2},{4,5},{5,4},{6,7},{7,6},{8,9},{9,8},{10,11... | collective-permute-start | bytes 1327112 | tf_op jit(solution)/shard_map/ppermute | solution.py:556
  59.5 16.8 %collective-permute-start.21 = (bf16[3,2,144,256]{3,2,1,0:T(8,128)(2,1)}, bf16[3,2,144,256]{3,2,1,0:T(8,128)(2,1)}, u32[]{:S(2)}, u32[]{:S(2)}) collective-permute-start(bf16[3,2,144,256]{3,2,1,0:T(8,128)(2,1)} %copy-done.9), channel_id=1, source_target_pairs={{0,1},{1,0},{2,3},{3,2},{4,5},{5,4},{6,7},{7,6},{8,9},{9,8},{10,11... | collective-permute-start | bytes 1327112 | tf_op jit(solution)/shard_map/ppermute | solution.py:556
  60.1 16.2 %collective-permute-start.22 = (bf16[3,2,144,256]{3,2,1,0:T(8,128)(2,1)}, bf16[3,2,144,256]{3,2,1,0:T(8,128)(2,1)}, u32[]{:S(2)}, u32[]{:S(2)}) collective-permute-start(bf16[3,2,144,256]{3,2,1,0:T(8,128)(2,1)} %collective-permute-done.18.refs_3_), channel_id=1, source_target_pairs={{0,1},{1,0},{2,3},{3,2},{4,5},{5,4},{6,7},{7,6},{8,9},{9,8},{10,11... | collective-permute-start | bytes 1327112 | tf_op jit(solution)/shard_map/ppermute | solution.py:556
  60.2 16.1 %copy-start.4 = (bf16[4,2,288,256]{3,2,1,0:T(8,128)(2,1)}, bf16[4,2,288,256]{3,2,1,0:T(8,128)(2,1)S(1)}, u32[]{:S(2)}) copy-start(bf16[4,2,288,256]{3,2,1,0:T(8,128)(2,1)S(1)} %collective-permute-done.4.refs_1_) | copy-start | bytes 3538948
  60.2 16.1 %collective-permute-start.23 = (bf16[3,2,144,256]{3,2,1,0:T(8,128)(2,1)}, bf16[3,2,144,256]{3,2,1,0:T(8,128)(2,1)}, u32[]{:S(2)}, u32[]{:S(2)}) collective-permute-start(bf16[3,2,144,256]{3,2,1,0:T(8,128)(2,1)} %copy-done.13), channel_id=1, source_target_pairs={{0,1},{1,0},{2,3},{3,2},{4,5},{5,4},{6,7},{7,6},{8,9},{9,8},{10,11... | collective-permute-start | bytes 1327112 | tf_op jit(solution)/shard_map/ppermute | solution.py:556
  64.2 12.1 %collective-permute-start.24 = (bf16[3,2,144,256]{3,2,1,0:T(8,128)(2,1)}, bf16[3,2,144,256]{3,2,1,0:T(8,128)(2,1)}, u32[]{:S(2)}, u32[]{:S(2)}) collective-permute-start(bf16[3,2,144,256]{3,2,1,0:T(8,128)(2,1)} %collective-permute-done.20.refs_5_), channel_id=1, source_target_pairs={{0,1},{1,0},{2,3},{3,2},{4,5},{5,4},{6,7},{7,6},{8,9},{9,8},{10,11... | collective-permute-start | bytes 1327112 | tf_op jit(solution)/shard_map/ppermute | solution.py:556
  67.7 8.7 %copy-start.10 = (bf16[3,2,144,256]{3,2,1,0:T(8,128)(2,1)S(1)}, bf16[3,2,144,256]{3,2,1,0:T(8,128)(2,1)}, u32[]{:S(2)}) copy-start(bf16[3,2,144,256]{3,2,1,0:T(8,128)(2,1)} %copy-done.9) | copy-start | bytes 1327108
  67.7 8.7 %copy-start.14 = (bf16[3,2,144,256]{3,2,1,0:T(8,128)(2,1)S(1)}, bf16[3,2,144,256]{3,2,1,0:T(8,128)(2,1)}, u32[]{:S(2)}) copy-start(bf16[3,2,144,256]{3,2,1,0:T(8,128)(2,1)} %copy-done.13) | copy-start | bytes 1327108
  (10 other events, 29.7 us)

commit v4 on v3

--- a/solution.py
+++ b/solution.py
@@ -14,8 +14,8 @@
 F32 = jnp.float32
 BF16 = jnp.bfloat16
 PROJECT_VMEM = 16 * 1024 * 1024
-COARSE_VMEM = 32 * 1024 * 1024
-FINE_VMEM = 48 * 1024 * 1024
+COARSE_VMEM = 16 * 1024 * 1024
+FINE_VMEM = 36 * 1024 * 1024
 
 
 LANES = 128
@@ -568,18 +568,25 @@
         return move(value, lambda p, z, c: (p, z, c ^ 1))
 
     levels, convs, rows, channels = filters.shape
-    quarters = filters.reshape(levels, phases, convs * rows // phases, channels)
+    part = convs * rows // phases
+    quarters = filters.reshape(levels, phases, part, channels)
     swapped = swap(filters)
     gathered = []
     for group in GROUPS:
-        part = lax.slice_in_dim(quarters, group[0], group[-1] + 1, axis=0)
-        own = lax.dynamic_index_in_dim(part, phase_id, 1, keepdims=False)
+        own = lax.dynamic_slice(
+            quarters, (group[0], phase_id, 0, 0), (len(group), 1, part, channels)
+        )[:, 0]
         far = across(own, 2)
-        column = jnp.stack([far, across(own, 1), across(far, 1)])
+        near = across(own, 1)
+        column = jnp.stack([far, near, across(far, 1)])
         one = first(column)
         pieces = [column, one, second(column), second(one)]
-        gathered.append(pieces + [swap(piece) for piece in pieces])
+        gathered.append(pieces + [swap(v) for v in pieces])
     return [filters, swapped], gathered
+
+
+def by_permutes(phases, dp_count):
+    return phases == 4 and dp_count == 8
 
 
 def per_device(
@@ -599,16 +606,15 @@
     phase_id = lax.axis_index("phase")
     dp_id = lax.axis_index("dp")
     where = jnp.stack([phase_id, dp_id % 2, dp_id // 2]).astype(jnp.int32)
-    if phases == 4 and dp_count == 8 and refine_filters.shape[2] % 32 == 0:
+    if by_permutes(phases, dp_count):
         base, gathered = gather_filters(refine_filters, phases, dp_count)
         upper, finer = base + gathered[0], base + gathered[1]
     else:
         upper = finer = [lax.all_gather(refine_filters, "dp", axis=2, tiled=True)]
     sent = project(plan, phases, where, tap_tokens, project_weight, shrink_weight)
-    arrived = [sent[0]] + [
-        lax.ppermute(sent[k], "phase", [(s, s ^ k) for s in range(phases)])
-        for k in range(1, phases)
-    ]
+    arrived = [sent[0]]
+    for k in range(1, phases):
+        arrived.append(lax.ppermute(sent[k], "phase", [(s, s ^ k) for s in range(phases)]))
     mine = jnp.stack(arrived)
     other = lax.ppermute(mine, "dp", [(d, d ^ 1) for d in range(dp_count)])
     summed1, patch0 = coarse(plan, where, mine, other, expand_two, upper)
@@ -637,7 +643,11 @@
         P(),
     )
     out_specs = P(("phase", "dp"), None)
-    body = functools.partial(per_device, mesh.shape["phase"], mesh.shape["dp"])
+    phases, dp_count = mesh.shape["phase"], mesh.shape["dp"]
+
+    def body(*args):
+        return per_device(phases, dp_count, *args)
+
     return jax.shard_map(
         body, mesh=mesh, in_specs=in_specs, out_specs=out_specs, check_vma=False
     )

time: 104 us -> 105 us (level)
    unnamed x35 -> x33, local copies, waits for them, and re-layouts: 7.85 us -> 11.3 us
    slice x1 -> x0, local copies, waits for them, and re-layouts: 2.29 us -> none  [gather_filters(): part = lax.slice_in_dim(quarters, group[0], group[-1] + 1, axis=0)]
  transfers between devices with their start and end apart: 25 -> 25, of which waited for: 10 -> 10; matrix products, arithmetic and copies ran while one was open for 1% -> 1% of each run, Pallas kernels for 13% -> 12%
where the time goes in v4:
time: 105 us
  Pallas kernels  29.4 us (28%)
  waiting for transfers between devices  28.7 us (27%)
  starting transfers between devices  22.2 us (21%)
  local copies, waits for them, and re-layouts  12.7 us (12%)
  blocking collectives  10.2 us (10%)
    ppermute x21, waiting for transfers between devices, move(): return lax.ppermute(value, axes, route)  24.9 us
    ppermute x21, starting transfers between devices, move(): return lax.ppermute(value, axes, route)  18.6 us
    pallas_call x1, Pallas kernels, fine(): pl.pallas_call(functools.partial(fine_kernel, plan), out_shape=jax.ShapeD...  16.5 us
    unnamed x33, local copies, waits for them, and re-layouts  11.3 us
    all_to_all x1, blocking collectives, per_device(): lax.all_to_all(partial, 'dp', split_axis=0, concat_axis=0, tiled=True)  10.2 us
    pallas_call x1, Pallas kernels, coarse(): pl.pallas_call(functools.partial(coarse_kernel, plan), out_shape=[jax.Sha...  8.58 us
    pallas_call x1, Pallas kernels, project(): pl.pallas_call(functools.partial(project_kernel, plan, phases), grid_spec...  4.35 us
    ppermute x3, waiting for transfers between devices, per_device(): lax.ppermute(sent[k], 'phase', [(s, s ^ k) for s in range(phases)])  3.76 us
  transfers between devices with their start and end apart: 25, of which 10 were waited for; matrix products, arithmetic and copies ran while one was open for 1% of the time, Pallas kernels for 12%

profile of v4, /device:TPU:0, one launch (start us, length us, event | category | flops | bytes accessed | tf_op | source)
XLA Modules:
  0.0 104.5 jit_solution(1070691647540796202)
XLA Ops:
  0.0 1.0 dynamic-slice_bitcast_fusion
  1.0 4.1 %collective-permute-start.5 = (bf16[2,144,256]{2,1,0:T(8,128)(2,1)S(1)}, bf16[2,144,256]{2,1,0:T(8,128)(2,1)S(1)}, u32[]{:S(2)}, u32[]{:S(2)}) collective-permute-start(bf16[2,144,256]{2,1,0:T(8,128)(2,1)S(1)} %get-tuple-element.18), channel_id=1, source_target_pairs={{0,4},{1,5},{2,6},{3,7},{4,0},{5,1},{6,2},{7,3},{8,12},{9,13},{10,... | collective-permute-start | bytes 442376 | tf_op jit(solution)/shard_map/ppermute | solution.py:556
  5.2 2.2 %copy-done.1 = bf16[1,512,4096]{2,1,0:T(8,128)(2,1)S(1)} copy-done((bf16[1,512,4096]{2,1,0:T(8,128)(2,1)S(1)}, bf16[1,512,4096]{2,1,0:T(8,128)(2,1)}, u32[]{:S(2)}) %copy-start.1) | copy-done | bytes 4194328
  7.4 1.6 %copy-done.2 = bf16[1,4096,256]{2,1,0:T(8,128)(2,1)S(1)} copy-done((bf16[1,4096,256]{2,1,0:T(8,128)(2,1)S(1)}, bf16[1,4096,256]{2,1,0:T(8,128)(2,1)}, u32[]{:S(2)}) %copy-start.2) | copy-done | bytes 2097176
  9.0 1.0 copy-done.7
  10.1 4.4 %project.1 = (bf16[256,256]{1,0:T(8,128)(2,1)S(1)}, bf16[256,256]{1,0:T(8,128)(2,1)S(1)}, bf16[256,256]{1,0:T(8,128)(2,1)S(1)}, bf16[256,256]{1,0:T(8,128)(2,1)S(1)}) custom-call(s32[3]{0:T(128)S(1)} %pad_add_fusion.where, bf16[1,512,4096]{2,1,0:T(8,128)(2,1)S(1)} %copy-done.1, bf16[1,4096,256]{2,1,0:T(8,128)(2,1)S(1)} %copy-done.2, ...), custom_call_target="tpu_custom_call" | custom-call | flops 1073741824 | bytes 6291456 | tf_op jit(solution)/shard_map/project/pallas_call | solution.py:123
  14.4 1.6 %collective-permute-start = (bf16[256,256]{1,0:T(8,128)(2,1)S(1)}, bf16[256,256]{1,0:T(8,128)(2,1)S(1)}, u32[]{:S(2)}, u32[]{:S(2)}) collective-permute-start(bf16[256,256]{1,0:T(8,128)(2,1)S(1)} %get-tuple-element.12), channel_id=1, source_target_pairs={{0,8},{8,0},{16,24},{24,16},{1,9},{9,1},{17,25},{25,17},{2,10},{10... | collective-permute-start | bytes 393224 | tf_op jit(solution)/shard_map/ppermute | solution.py:617
  16.0 1.4 %collective-permute-start.1 = (bf16[256,256]{1,0:T(8,128)(2,1)S(1)}, bf16[256,256]{1,0:T(8,128)(2,1)S(1)}, u32[]{:S(2)}, u32[]{:S(2)}) collective-permute-start(bf16[256,256]{1,0:T(8,128)(2,1)S(1)} %get-tuple-element.13), channel_id=1, source_target_pairs={{0,16},{8,24},{16,0},{24,8},{1,17},{9,25},{17,1},{25,9},{2,18},{10... | collective-permute-start | bytes 393224 | tf_op jit(solution)/shard_map/ppermute | solution.py:617
  18.0 1.6 %collective-permute-start.6 = (bf16[2,144,256]{2,1,0:T(8,128)(2,1)S(1)}, bf16[2,144,256]{2,1,0:T(8,128)(2,1)S(1)}, u32[]{:S(2)}, u32[]{:S(2)}) collective-permute-start(bf16[2,144,256]{2,1,0:T(8,128)(2,1)S(1)} %get-tuple-element.18), channel_id=1, source_target_pairs={{0,2},{1,3},{2,0},{3,1},{4,6},{5,7},{6,4},{7,5},{8,10},{9,11},{10,... | collective-permute-start | bytes 442376 | tf_op jit(solution)/shard_map/ppermute | solution.py:556
  20.0 3.8 %collective-permute-done.1 = bf16[256,256]{1,0:T(8,128)(2,1)S(1)} collective-permute-done((bf16[256,256]{1,0:T(8,128)(2,1)S(1)}, bf16[256,256]{1,0:T(8,128)(2,1)S(1)}, u32[]{:S(2)}, u32[]{:S(2)}) %collective-permute-start.1) | collective-permute-done | bytes 131104 | tf_op jit(solution)/shard_map/ppermute | solution.py:617
  24.0 1.6 %collective-permute-done.7 = bf16[2,144,256]{2,1,0:T(8,128)(2,1)S(1)} collective-permute-done((bf16[2,144,256]{2,1,0:T(8,128)(2,1)S(1)}, bf16[2,144,256]{2,1,0:T(8,128)(2,1)S(1)}, u32[]{:S(2)}, u32[]{:S(2)}) %collective-permute-start.7) | collective-permute-done | bytes 147488 | tf_op jit(solution)/shard_map/ppermute | solution.py:556
  25.7 1.6 %collective-permute-start.8 = (bf16[3,2,144,256]{3,2,1,0:T(8,128)(2,1)S(1)}, bf16[3,2,144,256]{3,2,1,0:T(8,128)(2,1)}, u32[]{:S(2)}, u32[]{:S(2)}) collective-permute-start(bf16[3,2,144,256]{3,2,1,0:T(8,128)(2,1)S(1)} %pad_maximum_fusion.1.refs_2_), channel_id=1, source_target_pairs={{0,8},{1,17},{2,10},{3,19},{4,12},{5,21},{6,14},{7,23},{8,0},{9,25... | collective-permute-start | bytes 1327112 | tf_op jit(solution)/shard_map/ppermute | solution.py:556
  27.6 1.6 %collective-permute-start.16 = (bf16[2,144,256]{2,1,0:T(8,128)(2,1)S(1)}, bf16[2,144,256]{2,1,0:T(8,128)(2,1)S(1)}, u32[]{:S(2)}, u32[]{:S(2)}) collective-permute-start(bf16[2,144,256]{2,1,0:T(8,128)(2,1)S(1)} %get-tuple-element.17), channel_id=1, source_target_pairs={{0,2},{1,3},{2,0},{3,1},{4,6},{5,7},{6,4},{7,5},{8,10},{9,11},{10,... | collective-permute-start | bytes 442376 | tf_op jit(solution)/shard_map/ppermute | solution.py:556
  29.1 5.6 %collective-permute-done.15 = bf16[2,144,256]{2,1,0:T(8,128)(2,1)S(1)} collective-permute-done((bf16[2,144,256]{2,1,0:T(8,128)(2,1)S(1)}, bf16[2,144,256]{2,1,0:T(8,128)(2,1)S(1)}, u32[]{:S(2)}, u32[]{:S(2)}) %collective-permute-start.15) | collective-permute-done | bytes 147488 | tf_op jit(solution)/shard_map/ppermute | solution.py:556
  34.7 1.7 %collective-permute-start.17 = (bf16[2,144,256]{2,1,0:T(8,128)(2,1)S(1)}, bf16[2,144,256]{2,1,0:T(8,128)(2,1)S(1)}, u32[]{:S(2)}, u32[]{:S(2)}) collective-permute-start(bf16[2,144,256]{2,1,0:T(8,128)(2,1)S(1)} %collective-permute-done.15), channel_id=1, source_target_pairs={{0,2},{1,3},{2,0},{3,1},{4,6},{5,7},{6,4},{7,5},{8,10},{9,11},{10,... | collective-permute-start | bytes 442376 | tf_op jit(solution)/shard_map/ppermute | solution.py:556
  36.4 1.4 %collective-permute-start.9 = (bf16[3,2,144,256]{3,2,1,0:T(8,128)(2,1)S(1)}, bf16[3,2,144,256]{3,2,1,0:T(8,128)(2,1)}, u32[]{:S(2)}, u32[]{:S(2)}) collective-permute-start(bf16[3,2,144,256]{3,2,1,0:T(8,128)(2,1)S(1)} %pad_maximum_fusion.1.refs_2_), channel_id=1, source_target_pairs={{0,16},{1,9},{2,18},{3,11},{4,20},{5,13},{6,22},{7,15},{8,24},{9,1... | collective-permute-start | bytes 1327112 | tf_op jit(solution)/shard_map/ppermute | solution.py:556
  37.8 2.1 %collective-permute-done.17 = bf16[2,144,256]{2,1,0:T(8,128)(2,1)S(1)} collective-permute-done((bf16[2,144,256]{2,1,0:T(8,128)(2,1)S(1)}, bf16[2,144,256]{2,1,0:T(8,128)(2,1)S(1)}, u32[]{:S(2)}, u32[]{:S(2)}) %collective-permute-start.17) | collective-permute-done | bytes 147488 | tf_op jit(solution)/shard_map/ppermute | solution.py:556
  39.9 0.8 copy-done.5
  41.6 0.9 collective-permute-start.19
  42.5 3.2 %collective-permute-done.9.refs_4_ = bf16[3,2,144,256]{3,2,1,0:T(8,128)(2,1)} collective-permute-done((bf16[3,2,144,256]{3,2,1,0:T(8,128)(2,1)S(1)}, bf16[3,2,144,256]{3,2,1,0:T(8,128)(2,1)}, u32[]{:S(2)}, u32[]{:S(2)}) %collective-permute-start.9) | collective-permute-done | bytes 442400 | tf_op jit(solution)/shard_map/ppermute | solution.py:556
  45.7 1.7 %collective-permute-start.10 = (bf16[3,2,144,256]{3,2,1,0:T(8,128)(2,1)}, bf16[3,2,144,256]{3,2,1,0:T(8,128)(2,1)}, u32[]{:S(2)}, u32[]{:S(2)}) collective-permute-start(bf16[3,2,144,256]{3,2,1,0:T(8,128)(2,1)} %collective-permute-done.8.refs_3_), channel_id=1, source_target_pairs={{0,16},{1,9},{2,18},{3,11},{4,20},{5,13},{6,22},{7,15},{8,24},{9,1... | collective-permute-start | bytes 1327112 | tf_op jit(solution)/shard_map/ppermute | solution.py:556
  48.1 5.4 %collective-permute-done.18.refs_3_ = bf16[3,2,144,256]{3,2,1,0:T(8,128)(2,1)} collective-permute-done((bf16[3,2,144,256]{3,2,1,0:T(8,128)(2,1)S(1)}, bf16[3,2,144,256]{3,2,1,0:T(8,128)(2,1)}, u32[]{:S(2)}, u32[]{:S(2)}) %collective-permute-start.18) | collective-permute-done | bytes 442400 | tf_op jit(solution)/shard_map/ppermute | solution.py:556
  55.0 1.4 %collective-permute-start.20 = (bf16[3,2,144,256]{3,2,1,0:T(8,128)(2,1)}, bf16[3,2,144,256]{3,2,1,0:T(8,128)(2,1)}, u32[]{:S(2)}, u32[]{:S(2)}) collective-permute-start(bf16[3,2,144,256]{3,2,1,0:T(8,128)(2,1)} %collective-permute-done.18.refs_3_), channel_id=1, source_target_pairs={{0,16},{1,9},{2,18},{3,11},{4,20},{5,13},{6,22},{7,15},{8,24},{9,1... | collective-permute-start | bytes 1327112 | tf_op jit(solution)/shard_map/ppermute | solution.py:556
  56.3 2.7 %collective-permute-done.10.refs_5_ = bf16[3,2,144,256]{3,2,1,0:T(8,128)(2,1)} collective-permute-done((bf16[3,2,144,256]{3,2,1,0:T(8,128)(2,1)}, bf16[3,2,144,256]{3,2,1,0:T(8,128)(2,1)}, u32[]{:S(2)}, u32[]{:S(2)}) %collective-permute-start.10) | collective-permute-done | bytes 442400 | tf_op jit(solution)/shard_map/ppermute | solution.py:556
  60.1 3.6 %collective-permute-done.20.refs_5_ = bf16[3,2,144,256]{3,2,1,0:T(8,128)(2,1)} collective-permute-done((bf16[3,2,144,256]{3,2,1,0:T(8,128)(2,1)}, bf16[3,2,144,256]{3,2,1,0:T(8,128)(2,1)}, u32[]{:S(2)}, u32[]{:S(2)}) %collective-permute-start.20) | collective-permute-done | bytes 442400 | tf_op jit(solution)/shard_map/ppermute | solution.py:556
  63.8 0.9 copy.21
  65.0 1.0 copy-done.4
  66.0 1.0 copy-done.6
  67.0 1.0 copy-done.11
  68.1 8.6 %coarse.1 = (f32[2,12,2,48,128]{4,3,2,1,0:T(8,128)S(1)}, bf16[240,256]{1,0:T(8,128)(2,1)S(1)}) custom-call(s32[3]{0:T(128)S(1)} %pad_add_fusion.where, bf16[4,256,256]{2,1,0:T(8,128)(2,1)S(1)} %pad_maximum_fusion.mine, bf16[4,256,256]{2,1,0:T(8,128)(2,1)S(1)} %copy-done.6, bf16[256,1024]{1,0:T(8,128)(2,1)S(1)} %copy-done.4, ...), custom_call_target="tpu_custom_call" | custom-call | flops 2000000000 | bytes 8000000 | tf_op jit(solution)/shard_map/coarse/pallas_call | solution.py:371
  76.7 16.5 %fine.1 = f32[2,8,1024]{2,1,0:T(8,128)S(1)} custom-call(s32[3]{0:T(128)S(1)} %pad_add_fusion.where, f32[2,12,2,48,128]{4,3,2,1,0:T(8,128)S(1)} %get-tuple-element.15.summed1, bf16[240,256]{1,0:T(8,128)(2,1)S(1)} %get-tuple-element.16.patch0, bf16[128,256]{1,0:T(8,128)(2,1)S(1)} %bitcast.30, f32[128,1]{1,0:T(8,128)S(1)} %copy.23.vector, ...), custom_call_target="tpu_custom_call" | custom-call | flops 8000000000 | bytes 10000000 | tf_op jit(solution)/shard_map/fine/pallas_call | solution.py:519
  93.7 10.2 %all_to_all.5 = f32[8,6,256]{2,1,0:T(8,128)S(1)} all-to-all(f32[8,6,256]{2,1,0:T(8,128)S(1)} %fusion), channel_id=1, replica_groups=mesh['phase'=4,'dp'=8] {'dp'}, dimensions={0} | all-to-all | bytes 98304 | tf_op jit(solution)/shard_map/all_to_all | solution.py:629
  (70 shorter events, 7.3 us)
Async XLA Ops:
  0.0 63.8 %copy-start = (s32[8,4,8]{2,1,0:T(4,128)S(1)}, s32[8,4,8]{2,1,0:T(4,128)}, u32[]{:S(2)}) copy-start(s32[8,4,8]{2,1,0:T(4,128)} %param.17) | copy-start | bytes 3076
  1.0 18.5 %collective-permute-start.5 = (bf16[2,144,256]{2,1,0:T(8,128)(2,1)S(1)}, bf16[2,144,256]{2,1,0:T(8,128)(2,1)S(1)}, u32[]{:S(2)}, u32[]{:S(2)}) collective-permute-start(bf16[2,144,256]{2,1,0:T(8,128)(2,1)S(1)} %get-tuple-element.18), channel_id=1, source_target_pairs={{0,4},{1,5},{2,6},{3,7},{4,0},{5,1},{6,2},{7,3},{8,12},{9,13},{10,... | collective-permute-start | bytes 442376 | tf_op jit(solution)/shard_map/ppermute | solution.py:556
  14.4 13.1 %copy-start.3 = (bf16[4,2,288,256]{3,2,1,0:T(8,128)(2,1)S(1)}, bf16[4,2,288,256]{3,2,1,0:T(8,128)(2,1)}, u32[]{:S(2)}) copy-start(bf16[4,2,288,256]{3,2,1,0:T(8,128)(2,1)} %refs_0_.3) | copy-start | bytes 3538948
  14.4 5.6 %collective-permute-start = (bf16[256,256]{1,0:T(8,128)(2,1)S(1)}, bf16[256,256]{1,0:T(8,128)(2,1)S(1)}, u32[]{:S(2)}, u32[]{:S(2)}) collective-permute-start(bf16[256,256]{1,0:T(8,128)(2,1)S(1)} %get-tuple-element.12), channel_id=1, source_target_pairs={{0,8},{8,0},{16,24},{24,16},{1,9},{9,1},{17,25},{25,17},{2,10},{10... | collective-permute-start | bytes 393224 | tf_op jit(solution)/shard_map/ppermute | solution.py:617
  16.0 7.8 %collective-permute-start.1 = (bf16[256,256]{1,0:T(8,128)(2,1)S(1)}, bf16[256,256]{1,0:T(8,128)(2,1)S(1)}, u32[]{:S(2)}, u32[]{:S(2)}) collective-permute-start(bf16[256,256]{1,0:T(8,128)(2,1)S(1)} %get-tuple-element.13), channel_id=1, source_target_pairs={{0,16},{8,24},{16,0},{24,8},{1,17},{9,25},{17,1},{25,9},{2,18},{10... | collective-permute-start | bytes 393224 | tf_op jit(solution)/shard_map/ppermute | solution.py:617
  17.3 6.4 %collective-permute-start.2 = (bf16[256,256]{1,0:T(8,128)(2,1)S(1)}, bf16[256,256]{1,0:T(8,128)(2,1)S(1)}, u32[]{:S(2)}, u32[]{:S(2)}) collective-permute-start(bf16[256,256]{1,0:T(8,128)(2,1)S(1)} %get-tuple-element.14), channel_id=1, source_target_pairs={{0,24},{8,16},{16,8},{24,0},{1,25},{9,17},{17,9},{25,1},{2,26},{10... | collective-permute-start | bytes 393224 | tf_op jit(solution)/shard_map/ppermute | solution.py:617
  18.0 6.1 %collective-permute-start.6 = (bf16[2,144,256]{2,1,0:T(8,128)(2,1)S(1)}, bf16[2,144,256]{2,1,0:T(8,128)(2,1)S(1)}, u32[]{:S(2)}, u32[]{:S(2)}) collective-permute-start(bf16[2,144,256]{2,1,0:T(8,128)(2,1)S(1)} %get-tuple-element.18), channel_id=1, source_target_pairs={{0,2},{1,3},{2,0},{3,1},{4,6},{5,7},{6,4},{7,5},{8,10},{9,11},{10,... | collective-permute-start | bytes 442376 | tf_op jit(solution)/shard_map/ppermute | solution.py:556
  19.6 6.1 %collective-permute-start.7 = (bf16[2,144,256]{2,1,0:T(8,128)(2,1)S(1)}, bf16[2,144,256]{2,1,0:T(8,128)(2,1)S(1)}, u32[]{:S(2)}, u32[]{:S(2)}) collective-permute-start(bf16[2,144,256]{2,1,0:T(8,128)(2,1)S(1)} %collective-permute-done.5), channel_id=1, source_target_pairs={{0,2},{1,3},{2,0},{3,1},{4,6},{5,7},{6,4},{7,5},{8,10},{9,11},{10,... | collective-permute-start | bytes 442376 | tf_op jit(solution)/shard_map/ppermute | solution.py:556
  23.8 40.9 %copy-start.15 = (f32[128]{0:T(128)S(1)}, f32[128]{0:T(128)}, u32[]{:S(2)}) copy-start(f32[128]{0:T(128)} %param.16) | copy-start | bytes 1540
  23.9 16.1 %collective-permute-start.3 = (bf16[4,256,256]{2,1,0:T(8,128)(2,1)S(1)}, bf16[4,256,256]{2,1,0:T(8,128)(2,1)S(1)}, u32[]{:S(2)}, u32[]{:S(2)}) collective-permute-start(bf16[4,256,256]{2,1,0:T(8,128)(2,1)S(1)} %pad_maximum_fusion.mine), channel_id=1, source_target_pairs={{0,1},{1,0},{2,3},{3,2},{4,5},{5,4},{6,7},{7,6},{8,9},{9,8},{10,11... | collective-permute-start | bytes 1572872 | tf_op jit(solution)/shard_map/ppermute | solution.py:619
  25.7 15.9 %collective-permute-start.8 = (bf16[3,2,144,256]{3,2,1,0:T(8,128)(2,1)S(1)}, bf16[3,2,144,256]{3,2,1,0:T(8,128)(2,1)}, u32[]{:S(2)}, u32[]{:S(2)}) collective-permute-start(bf16[3,2,144,256]{3,2,1,0:T(8,128)(2,1)S(1)} %pad_maximum_fusion.1.refs_2_), channel_id=1, source_target_pairs={{0,8},{1,17},{2,10},{3,19},{4,12},{5,21},{6,14},{7,23},{8,0},{9,25... | collective-permute-start | bytes 1327112 | tf_op jit(solution)/shard_map/ppermute | solution.py:556
  27.2 7.5 %collective-permute-start.15 = (bf16[2,144,256]{2,1,0:T(8,128)(2,1)S(1)}, bf16[2,144,256]{2,1,0:T(8,128)(2,1)S(1)}, u32[]{:S(2)}, u32[]{:S(2)}) collective-permute-start(bf16[2,144,256]{2,1,0:T(8,128)(2,1)S(1)} %get-tuple-element.17), channel_id=1, source_target_pairs={{0,4},{1,5},{2,6},{3,7},{4,0},{5,1},{6,2},{7,3},{8,12},{9,13},{10,... | collective-permute-start | bytes 442376 | tf_op jit(solution)/shard_map/ppermute | solution.py:556
  27.6 32.2 %collective-permute-start.4 = (bf16[4,2,288,256]{3,2,1,0:T(8,128)(2,1)S(1)}, bf16[4,2,288,256]{3,2,1,0:T(8,128)(2,1)S(1)}, u32[]{:S(2)}, u32[]{:S(2)}) collective-permute-start(bf16[4,2,288,256]{3,2,1,0:T(8,128)(2,1)S(1)} %copy-done.3), channel_id=1, source_target_pairs={{0,1},{1,0},{2,3},{3,2},{4,5},{5,4},{6,7},{7,6},{8,9},{9,8},{10,11... | collective-permute-start | bytes 3538952 | tf_op jit(solution)/shard_map/ppermute | solution.py:556
  27.6 8.9 %collective-permute-start.16 = (bf16[2,144,256]{2,1,0:T(8,128)(2,1)S(1)}, bf16[2,144,256]{2,1,0:T(8,128)(2,1)S(1)}, u32[]{:S(2)}, u32[]{:S(2)}) collective-permute-start(bf16[2,144,256]{2,1,0:T(8,128)(2,1)S(1)} %get-tuple-element.17), channel_id=1, source_target_pairs={{0,2},{1,3},{2,0},{3,1},{4,6},{5,7},{6,4},{7,5},{8,10},{9,11},{10,... | collective-permute-start | bytes 442376 | tf_op jit(solution)/shard_map/ppermute | solution.py:556
  34.7 5.1 %collective-permute-start.17 = (bf16[2,144,256]{2,1,0:T(8,128)(2,1)S(1)}, bf16[2,144,256]{2,1,0:T(8,128)(2,1)S(1)}, u32[]{:S(2)}, u32[]{:S(2)}) collective-permute-start(bf16[2,144,256]{2,1,0:T(8,128)(2,1)S(1)} %collective-permute-done.15), channel_id=1, source_target_pairs={{0,2},{1,3},{2,0},{3,1},{4,6},{5,7},{6,4},{7,5},{8,10},{9,11},{10,... | collective-permute-start | bytes 442376 | tf_op jit(solution)/shard_map/ppermute | solution.py:556
  36.4 9.3 %collective-permute-start.9 = (bf16[3,2,144,256]{3,2,1,0:T(8,128)(2,1)S(1)}, bf16[3,2,144,256]{3,2,1,0:T(8,128)(2,1)}, u32[]{:S(2)}, u32[]{:S(2)}) collective-permute-start(bf16[3,2,144,256]{3,2,1,0:T(8,128)(2,1)S(1)} %pad_maximum_fusion.1.refs_2_), channel_id=1, source_target_pairs={{0,16},{1,9},{2,18},{3,11},{4,20},{5,13},{6,22},{7,15},{8,24},{9,1... | collective-permute-start | bytes 1327112 | tf_op jit(solution)/shard_map/ppermute | solution.py:556
  39.8 7.5 %collective-permute-start.11 = (bf16[3,2,144,256]{3,2,1,0:T(8,128)(2,1)S(1)}, bf16[3,2,144,256]{3,2,1,0:T(8,128)(2,1)S(1)}, u32[]{:S(2)}, u32[]{:S(2)}) collective-permute-start(bf16[3,2,144,256]{3,2,1,0:T(8,128)(2,1)S(1)} %pad_maximum_fusion.1.refs_2_), channel_id=1, source_target_pairs={{0,1},{1,0},{2,3},{3,2},{4,5},{5,4},{6,7},{7,6},{8,9},{9,8},{10,11... | collective-permute-start | bytes 1327112 | tf_op jit(solution)/shard_map/ppermute | solution.py:556
  39.9 7.5 %copy-start.8 = (bf16[3,2,144,256]{3,2,1,0:T(8,128)(2,1)}, bf16[3,2,144,256]{3,2,1,0:T(8,128)(2,1)S(1)}, u32[]{:S(2)}) copy-start(bf16[3,2,144,256]{3,2,1,0:T(8,128)(2,1)S(1)} %pad_maximum_fusion.2.refs_2_) | copy-start | bytes 1327108
  40.8 12.8 %collective-permute-start.18 = (bf16[3,2,144,256]{3,2,1,0:T(8,128)(2,1)S(1)}, bf16[3,2,144,256]{3,2,1,0:T(8,128)(2,1)}, u32[]{:S(2)}, u32[]{:S(2)}) collective-permute-start(bf16[3,2,144,256]{3,2,1,0:T(8,128)(2,1)S(1)} %pad_maximum_fusion.2.refs_2_), channel_id=1, source_target_pairs={{0,8},{1,17},{2,10},{3,19},{4,12},{5,21},{6,14},{7,23},{8,0},{9,25... | collective-permute-start | bytes 1327112 | tf_op jit(solution)/shard_map/ppermute | solution.py:556
  41.6 12.6 %collective-permute-start.19 = (bf16[3,2,144,256]{3,2,1,0:T(8,128)(2,1)S(1)}, bf16[3,2,144,256]{3,2,1,0:T(8,128)(2,1)S(1)}, u32[]{:S(2)}, u32[]{:S(2)}) collective-permute-start(bf16[3,2,144,256]{3,2,1,0:T(8,128)(2,1)S(1)} %pad_maximum_fusion.2.refs_2_), channel_id=1, source_target_pairs={{0,16},{1,9},{2,18},{3,11},{4,20},{5,13},{6,22},{7,15},{8,24},{9,1... | collective-permute-start | bytes 1327112 | tf_op jit(solution)/shard_map/ppermute | solution.py:556
  45.7 13.4 %collective-permute-start.10 = (bf16[3,2,144,256]{3,2,1,0:T(8,128)(2,1)}, bf16[3,2,144,256]{3,2,1,0:T(8,128)(2,1)}, u32[]{:S(2)}, u32[]{:S(2)}) collective-permute-start(bf16[3,2,144,256]{3,2,1,0:T(8,128)(2,1)} %collective-permute-done.8.refs_3_), channel_id=1, source_target_pairs={{0,16},{1,9},{2,18},{3,11},{4,20},{5,13},{6,22},{7,15},{8,24},{9,1... | collective-permute-start | bytes 1327112 | tf_op jit(solution)/shard_map/ppermute | solution.py:556
  48.1 10.9 %collective-permute-start.12 = (bf16[3,2,144,256]{3,2,1,0:T(8,128)(2,1)}, bf16[3,2,144,256]{3,2,1,0:T(8,128)(2,1)}, u32[]{:S(2)}, u32[]{:S(2)}) collective-permute-start(bf16[3,2,144,256]{3,2,1,0:T(8,128)(2,1)} %collective-permute-done.8.refs_3_), channel_id=1, source_target_pairs={{0,1},{1,0},{2,3},{3,2},{4,5},{5,4},{6,7},{7,6},{8,9},{9,8},{10,11... | collective-permute-start | bytes 1327112 | tf_op jit(solution)/shard_map/ppermute | solution.py:556
  53.6 6.0 %collective-permute-start.13 = (bf16[3,2,144,256]{3,2,1,0:T(8,128)(2,1)}, bf16[3,2,144,256]{3,2,1,0:T(8,128)(2,1)}, u32[]{:S(2)}, u32[]{:S(2)}) collective-permute-start(bf16[3,2,144,256]{3,2,1,0:T(8,128)(2,1)} %collective-permute-done.9.refs_4_), channel_id=1, source_target_pairs={{0,1},{1,0},{2,3},{3,2},{4,5},{5,4},{6,7},{7,6},{8,9},{9,8},{10,11... | collective-permute-start | bytes 1327112 | tf_op jit(solution)/shard_map/ppermute | solution.py:556
  55.0 8.8 %collective-permute-start.20 = (bf16[3,2,144,256]{3,2,1,0:T(8,128)(2,1)}, bf16[3,2,144,256]{3,2,1,0:T(8,128)(2,1)}, u32[]{:S(2)}, u32[]{:S(2)}) collective-permute-start(bf16[3,2,144,256]{3,2,1,0:T(8,128)(2,1)} %collective-permute-done.18.refs_3_), channel_id=1, source_target_pairs={{0,16},{1,9},{2,18},{3,11},{4,20},{5,13},{6,22},{7,15},{8,24},{9,1... | collective-permute-start | bytes 1327112 | tf_op jit(solution)/shard_map/ppermute | solution.py:556
  59.0 5.9 %collective-permute-start.14 = (bf16[3,2,144,256]{3,2,1,0:T(8,128)(2,1)}, bf16[3,2,144,256]{3,2,1,0:T(8,128)(2,1)}, u32[]{:S(2)}, u32[]{:S(2)}) collective-permute-start(bf16[3,2,144,256]{3,2,1,0:T(8,128)(2,1)} %collective-permute-done.10.refs_5_), channel_id=1, source_target_pairs={{0,1},{1,0},{2,3},{3,2},{4,5},{5,4},{6,7},{7,6},{8,9},{9,8},{10,11... | collective-permute-start | bytes 1327112 | tf_op jit(solution)/shard_map/ppermute | solution.py:556
  59.1 17.6 %collective-permute-start.21 = (bf16[3,2,144,256]{3,2,1,0:T(8,128)(2,1)}, bf16[3,2,144,256]{3,2,1,0:T(8,128)(2,1)}, u32[]{:S(2)}, u32[]{:S(2)}) collective-permute-start(bf16[3,2,144,256]{3,2,1,0:T(8,128)(2,1)} %copy-done.8), channel_id=1, source_target_pairs={{0,1},{1,0},{2,3},{3,2},{4,5},{5,4},{6,7},{7,6},{8,9},{9,8},{10,11... | collective-permute-start | bytes 1327112 | tf_op jit(solution)/shard_map/ppermute | solution.py:556
  59.6 17.0 %collective-permute-start.22 = (bf16[3,2,144,256]{3,2,1,0:T(8,128)(2,1)}, bf16[3,2,144,256]{3,2,1,0:T(8,128)(2,1)}, u32[]{:S(2)}, u32[]{:S(2)}) collective-permute-start(bf16[3,2,144,256]{3,2,1,0:T(8,128)(2,1)} %collective-permute-done.18.refs_3_), channel_id=1, source_target_pairs={{0,1},{1,0},{2,3},{3,2},{4,5},{5,4},{6,7},{7,6},{8,9},{9,8},{10,11... | collective-permute-start | bytes 1327112 | tf_op jit(solution)/shard_map/ppermute | solution.py:556
  59.7 17.0 %collective-permute-start.23 = (bf16[3,2,144,256]{3,2,1,0:T(8,128)(2,1)}, bf16[3,2,144,256]{3,2,1,0:T(8,128)(2,1)}, u32[]{:S(2)}, u32[]{:S(2)}) collective-permute-start(bf16[3,2,144,256]{3,2,1,0:T(8,128)(2,1)} %copy-done.13), channel_id=1, source_target_pairs={{0,1},{1,0},{2,3},{3,2},{4,5},{5,4},{6,7},{7,6},{8,9},{9,8},{10,11... | collective-permute-start | bytes 1327112 | tf_op jit(solution)/shard_map/ppermute | solution.py:556
  63.8 12.9 %collective-permute-start.24 = (bf16[3,2,144,256]{3,2,1,0:T(8,128)(2,1)}, bf16[3,2,144,256]{3,2,1,0:T(8,128)(2,1)}, u32[]{:S(2)}, u32[]{:S(2)}) collective-permute-start(bf16[3,2,144,256]{3,2,1,0:T(8,128)(2,1)} %collective-permute-done.20.refs_5_), channel_id=1, source_target_pairs={{0,1},{1,0},{2,3},{3,2},{4,5},{5,4},{6,7},{7,6},{8,9},{9,8},{10,11... | collective-permute-start | bytes 1327112 | tf_op jit(solution)/shard_map/ppermute | solution.py:556
  68.1 8.6 %copy-start.9 = (bf16[3,2,144,256]{3,2,1,0:T(8,128)(2,1)S(1)}, bf16[3,2,144,256]{3,2,1,0:T(8,128)(2,1)}, u32[]{:S(2)}) copy-start(bf16[3,2,144,256]{3,2,1,0:T(8,128)(2,1)} %copy-done.8) | copy-start | bytes 1327108
  68.1 8.7 %copy-start.12 = (bf16[256,4096]{1,0:T(8,128)(2,1)S(1)}, bf16[256,4096]{1,0:T(8,128)(2,1)}, u32[]{:S(2)}) copy-start(bf16[256,4096]{1,0:T(8,128)(2,1)} %expand_four.1) | copy-start | bytes 6291460
  68.1 8.7 %copy-start.14 = (bf16[3,2,144,256]{3,2,1,0:T(8,128)(2,1)S(1)}, bf16[3,2,144,256]{3,2,1,0:T(8,128)(2,1)}, u32[]{:S(2)}) copy-start(bf16[3,2,144,256]{3,2,1,0:T(8,128)(2,1)} %copy-done.13) | copy-start | bytes 1327108
  (9 other events, 10.3 us)

commit v5 on v4

--- a/solution.py
+++ b/solution.py
@@ -13,9 +13,10 @@
 LEVELS = 4
 F32 = jnp.float32
 BF16 = jnp.bfloat16
-PROJECT_VMEM = 16 * 1024 * 1024
-COARSE_VMEM = 16 * 1024 * 1024
-FINE_VMEM = 36 * 1024 * 1024
+STACK_VMEM = 4 * 1024 * 1024
+PROJECT_VMEM = 12 * 1024 * 1024
+COARSE_VMEM = 12 * 1024 * 1024
+FINE_VMEM = 32 * 1024 * 1024
 
 
 LANES = 128
@@ -40,7 +41,6 @@
 
 class Plan:
     def __init__(self, phases, channels):
-        self.phases = phases
         self.ch = channels
         self.half = G // 2
         self.block = G // phases
@@ -66,28 +66,20 @@
 
 def project_kernel(plan, phases, where, tokens, weight, shrink, *refs):
     outs, acc_lo, acc_hi = refs[:phases], refs[phases], refs[phases + 1]
-    step = pl.program_id(0)
-    part = dot(tokens[0], weight[0])
     lanes = acc_lo.shape[1]
-
-    @pl.when(step == 0)
-    def _():
-        acc_lo[...] = part[:, :lanes]
-        acc_hi[...] = part[:, lanes:]
-
-    @pl.when(step > 0)
-    def _():
-        acc_lo[...] += part[:, :lanes]
-        acc_hi[...] += part[:, lanes:]
-
-    last = step == pl.num_programs(0) - 1
+    rows = tokens.shape[1] // 2
+    for i in range(2):
+        at = pl.ds(i * rows, rows)
+        value = dot(tokens[0, at, :], weight[0])
+        acc_lo[at, :] = value[:, :lanes]
+        acc_hi[at, :] = value[:, lanes:]
     phase = where[0]
 
     def column(start, size, stride):
         where_rows = pl.ds(start, size, stride=stride)
         return jnp.concatenate([acc_lo[where_rows, :], acc_hi[where_rows, :]], axis=1)
 
-    @pl.when(last & (phase < LEVELS - 1))
+    @pl.when(phase < LEVELS - 1)
     def _():
         for k in range(phases):
             start = plan.sent_start(phase ^ k)
@@ -96,7 +88,7 @@
                     start + j, plan.half, G
                 ).astype(BF16)
 
-    @pl.when(last & (phase == LEVELS - 1))
+    @pl.when(phase == LEVELS - 1)
     def _():
         total = jnp.zeros((plan.half * plan.half // 2, plan.ch), F32)
         for a in range(2):
@@ -117,22 +109,14 @@
 
 def project(plan, phases, where, tokens, weight, shrink):
     rows, depth = tokens.shape[1:]
-    block = min(depth, 512)
     pixels = plan.sent * plan.half
     out = jax.ShapeDtypeStruct((pixels, plan.ch), BF16)
+    vmem = pl.BlockSpec(memory_space=pltpu.VMEM)
     return pl.pallas_call(
         functools.partial(project_kernel, plan, phases),
-        grid_spec=pltpu.PrefetchScalarGridSpec(
-            num_scalar_prefetch=1,
-            grid=(depth // block,),
-            in_specs=[
-                pl.BlockSpec((1, rows, block), lambda i, w: (0, 0, i)),
-                pl.BlockSpec((1, block, plan.ch), lambda i, w: (0, i, 0)),
-                pl.BlockSpec(shrink.shape, lambda i, w: (0, 0)),
-            ],
-            out_specs=[pl.BlockSpec((pixels, plan.ch), lambda i, w: (0, 0))] * phases,
-            scratch_shapes=[pltpu.VMEM((rows, plan.ch // 2), F32)] * 2,
-        ),
+        in_specs=[pl.BlockSpec(memory_space=pltpu.SMEM), vmem, vmem, vmem],
+        out_specs=[vmem] * phases,
+        scratch_shapes=[pltpu.VMEM((rows, plan.ch // 2), F32)] * 2,
         out_shape=[out] * phases,
         compiler_params=pltpu.CompilerParams(vmem_limit_bytes=PROJECT_VMEM),
         cost_estimate=pl.CostEstimate(
@@ -144,6 +128,25 @@
     )(where, tokens, weight, shrink)
 
 
+def stack_kernel(*refs):
+    for i, ref in enumerate(refs[:-1]):
+        refs[-1][i] = ref[...]
+
+
+def stack(values):
+    vmem = pl.BlockSpec(memory_space=pltpu.VMEM)
+    size = len(values) * values[0].size * values[0].dtype.itemsize
+    return pl.pallas_call(
+        stack_kernel,
+        out_shape=jax.ShapeDtypeStruct((len(values),) + values[0].shape, values[0].dtype),
+        in_specs=[vmem] * len(values),
+        out_specs=vmem,
+        compiler_params=pltpu.CompilerParams(vmem_limit_bytes=STACK_VMEM),
+        cost_estimate=pl.CostEstimate(flops=0, bytes_accessed=2 * size, transcendentals=0),
+        name="stack",
+    )(*values)
+
+
 def put_shifted(shifted, col, value):
     count, rows, _ = value.shape
     value = jnp.maximum(value, 0.0)
@@ -179,20 +182,20 @@
         lax.fori_loop(0, count, lambda i, c: (body(i), c)[1], 0)
 
 
-def refine(source, weights, sems, first, second, chunk, out_col, out_count, out_chunk, emit):
+def refine(source, wait, weights, first, second, chunk, out_col, out_count, out_chunk, emit):
     cols, rows = first.shape[1] - 2, first.shape[2]
     clear_edges(first)
     clear_edges(second)
     loop(cols // chunk, lambda i: put_shifted(first, i * chunk, source(i * chunk, chunk)))
 
-    wait_filters(weights, sems, 0)
+    wait(0)
 
     def inner(i):
         put_shifted(second, i * chunk, conv_block(first, weights.at[0], i * chunk, chunk, (0, rows)))
 
     loop(cols // chunk, inner)
 
-    wait_filters(weights, sems, 1)
+    wait(1)
 
     def outer(i):
         col = out_col + i * out_chunk
@@ -202,53 +205,41 @@
     loop(out_count // out_chunk, outer)
 
 
-def start_filters(plan, where, filters, level, weights, sems):
+def start_filters(filters, level, weights, sems):
     if len(filters) == 1:
         for m in range(2):
             pltpu.make_async_copy(filters[0].at[level, m], weights.at[m], sems.at[m]).start()
+
+
+def wait_filters(filters, weights, sems, m):
+    if len(filters) == 1:
+        pltpu.make_async_copy(filters[0].at[0, m], weights.at[m], sems.at[m]).wait()
+
+
+def lay_filters(plan, where, filters, level, weights):
+    if len(filters) == 1:
         return
     phase, side, chip = where[0], where[1], where[2]
     own, swapped = filters[:2]
     rows = own.shape[2]
     part = rows // 2
     slot = plan.slot_of(level)
-    for m in range(2):
-        for ref, core in ((own, side), (swapped, 1 - side)):
-            at = pl.ds(pl.multiple_of((2 * chip + core) * rows, 16), rows)
-            pltpu.make_async_copy(ref.at[level, m], weights.at[m, at], sems.at[m]).start()
-
-    def start_pieces(p):
+    for ref, core in ((own, side), (swapped, 1 - side)):
+        at = pl.ds(pl.multiple_of((2 * chip + core) * rows, 16), rows)
         for m in range(2):
-            for half in range(2):
-                quarter = 2 * m + half
-                for i, away in enumerate(CHIP_ORDER):
-                    for refs, core in ((filters[2:6], side), (filters[6:10], 1 - side)):
-                        start = (2 * (chip ^ away) + core) * rows + half * part
-                        at = pl.ds(pl.multiple_of(start, 16), part)
-                        moved = p ^ quarter
-                        if moved in (0, 3):
-                            pltpu.make_async_copy(
-                                refs[moved].at[i, slot], weights.at[m, at], sems.at[m]
-                            ).start()
-                            continue
-                        for c in range(2):
-                            k = moved if c == 0 else 3 - moved
-
-                            @pl.when(core == c)
-                            def _(ref=refs[k], at=at, i=i, m=m):
-                                pltpu.make_async_copy(
-                                    ref.at[i, slot], weights.at[m, at], sems.at[m]
-                                ).start()
-
-    for p in range(plan.phases):
-
-        @pl.when(phase == p)
-        def _(p=p):
-            start_pieces(p)
-
-
-def wait_filters(weights, sems, m):
-    pltpu.make_async_copy(weights.at[m], weights.at[m], sems.at[m]).wait()
+            weights[m, at, :] = ref[level, m]
+    for refs, core in ((filters[2:6], side), (filters[6:10], 1 - side)):
+        for ref, moved in zip(refs, (0, 1 + core, 2 - core, 3)):
+            quarter = phase ^ moved
+            for i, away in enumerate(CHIP_ORDER):
+                start = (2 * (chip ^ away) + core) * rows + (quarter % 2) * part
+                at = pl.ds(pl.multiple_of(start, 16), part)
+                weights[quarter // 2, at, :] = ref[i, slot]
+
+
+def filter_specs(filters):
+    space = pl.ANY if len(filters) == 1 else pltpu.VMEM
+    return [pl.BlockSpec(memory_space=space)] * len(filters)
 
 
 def load_patches(plan, patch, mine, other, k, side):
@@ -287,7 +278,8 @@
     ch = plan.ch
     phase, side = where[0], where[1]
     for level, weights in ((3, weight3), (2, weight2)):
-        start_filters(plan, where, filters, level, weights, sems.at[level])
+        start_filters(filters, level, weights, sems.at[level])
+        lay_filters(plan, where, filters, level, weights)
 
     row1 = pl.multiple_of(side * (G - plan.rows1), 8)
     load_patches(plan, patch, mine, other, phase, side)
@@ -308,8 +300,8 @@
 
     refine(
         lambda col, n: map3[pl.ds(col, n)],
+        lambda m: wait_filters(filters, weight3, sems.at[3], m),
         weight3,
-        sems.at[3],
         first3,
         second3,
         size3,
@@ -336,7 +328,16 @@
         joined2[pl.ds(col, value.shape[0])] = rounded(value)
 
     refine(
-        source2, weight2, sems.at[2], first2, second2, plan.sent, 0, plan.sent, plan.sent, keep2
+        source2,
+        lambda m: wait_filters(filters, weight2, sems.at[2], m),
+        weight2,
+        first2,
+        second2,
+        plan.sent,
+        0,
+        plan.sent,
+        plan.sent,
+        keep2,
     )
 
     load_patches(plan, patch, mine, other, phase ^ 1, side)
@@ -375,7 +376,7 @@
             jax.ShapeDtypeStruct((plan.cols0 * plan.rows1, ch), BF16),
         ],
         in_specs=[pl.BlockSpec(memory_space=pltpu.SMEM), vmem, vmem, vmem]
-        + [pl.BlockSpec(memory_space=pl.ANY)] * len(filters),
+        + filter_specs(filters),
         out_specs=[vmem, vmem],
         scratch_shapes=[
             weights,
@@ -400,29 +401,28 @@
 FINE_SCRATCH = 12
 
 
-def fine_kernel(plan, where, summed1, patch0, head, vector, expand_four, *refs):
+def fine_kernel(plan, where, summed1, patch0, head, vector, expand_four, matches, *refs):
     count = len(refs) - FINE_SCRATCH
     filters = refs[:count]
     (
-        depth,
+        portions,
         weight1,
         weight0,
         sems,
-        grow,
-        grow_sem,
         joined1,
         map0,
         first1,
         second1,
         first,
         second,
+        by_col,
+        by_row,
     ) = refs[count:]
     ch = plan.ch
     phase, side = where[0], where[1]
-    start_filters(plan, where, filters, 1, weight1, sems.at[1])
-    grow_copy = pltpu.make_async_copy(expand_four, grow, grow_sem)
-    grow_copy.start()
-    start_filters(plan, where, filters, 0, weight0, sems.at[0])
+    for level, weights in ((1, weight1), (0, weight0)):
+        start_filters(filters, level, weights, sems.at[level])
+        lay_filters(plan, where, filters, level, weights)
 
     off0 = 2 * (plan.start0(phase) - plan.start1(phase))
 
@@ -439,8 +439,8 @@
 
     refine(
         source1,
+        lambda m: wait_filters(filters, weight1, sems.at[1], m),
         weight1,
-        sems.at[1],
         first1,
         second1,
         plan.cols1,
@@ -450,11 +450,10 @@
         keep1,
     )
 
-    grow_copy.wait()
     for a in range(4):
         for b in range(4):
             n = 4 * a + b
-            grown = dot(patch0[...], grow[:, n * ch : (n + 1) * ch])
+            grown = dot(patch0[...], expand_four[:, n * ch : (n + 1) * ch])
             below = take(
                 joined1, slice(None), b // 2, pl.ds(a // 2, plan.rows1, stride=2), slice(None)
             )
@@ -481,7 +480,7 @@
     clear_edges(first)
     clear_edges(second)
     loop(9, lambda i: put_shifted(first, i * 4, source0(i * 4, 4, row, rows)))
-    wait_filters(weight0, sems.at[0], 0)
+    wait_filters(filters, weight0, sems.at[0], 0)
 
     def inner(i):
         put_shifted(
@@ -489,8 +488,10 @@
         )
 
     loop(cols // chunk, inner)
-    wait_filters(weight0, sems.at[0], 1)
+    wait_filters(filters, weight0, sems.at[0], 1)
     half_cols = 2 * plan.block
+    hidden_size = head.shape[1]
+    scale = jnp.broadcast_to(vector[...], (hidden_size, hidden_size)).T[:, :1]
 
     def outer(i):
         col = own + i * half_cols
@@ -500,50 +501,69 @@
         hidden = lax.dot_general(
             head[...],
             joined.reshape(half_cols * own_rows, ch),
-            (((1,), (1,)), ((), ())),
+            (((0,), (1,)), ((), ())),
             preferred_element_type=F32,
         )
-        hidden = jnp.maximum(hidden, 0.0) * vector[...]
-        depth[i] = jnp.broadcast_to(hidden.sum(axis=0, keepdims=True), depth.shape[1:])
+        depth = (jnp.maximum(hidden, 0.0) * scale).sum(axis=0, keepdims=True)
+        for j in range(half_cols):
+            by_col[pl.ds(i * half_cols + j, 1), :own_rows] = depth[
+                :, j * own_rows : (j + 1) * own_rows
+            ]
 
     loop(2, outer)
 
-
-def fine(plan, where, summed1, patch0, head, vector, expand_four, filters):
+    by_row[...] = by_col[...].T
+    tile_rows = own_rows // TILES_DEV
+    tiles = jnp.concatenate(
+        [
+            by_row[pl.ds(i, TILES_DEV, stride=tile_rows), :][:, : 2 * half_cols]
+            for i in range(tile_rows)
+        ],
+        axis=1,
+    )
+
+    def add_tiles(d):
+        chosen = matches[d]
+        total = chosen[:, 0:1] * tiles[0:1]
+        for j in range(1, TILES_DEV):
+            total += chosen[:, j : j + 1] * tiles[j : j + 1]
+        portions[d] = total
+
+    for d in range(portions.shape[0]):
+        add_tiles(d)
+
+
+def fine(plan, where, summed1, patch0, head, vector, expand_four, matches, filters):
     ch = plan.ch
     vmem = pl.BlockSpec(memory_space=pltpu.VMEM)
-    any_space = pl.BlockSpec(memory_space=pl.ANY)
-    own_rows = 4 * plan.half
     slabs = ch // LANES
+    pixels = 16 * plan.block * plan.half // TILES_DEV
     weights = pltpu.VMEM((2, 9 * ch, ch), BF16)
     return pl.pallas_call(
         functools.partial(fine_kernel, plan),
-        out_shape=jax.ShapeDtypeStruct((2, 8, 2 * plan.block * own_rows), F32),
-        in_specs=[pl.BlockSpec(memory_space=pltpu.SMEM), vmem, vmem, vmem, vmem, any_space]
-        + [any_space] * len(filters),
+        out_shape=jax.ShapeDtypeStruct(matches.shape[:2] + (pixels,), F32),
+        in_specs=[pl.BlockSpec(memory_space=pltpu.SMEM)] + [vmem] * 6 + filter_specs(filters),
         out_specs=vmem,
         scratch_shapes=[
             weights,
             weights,
             pltpu.SemaphoreType.DMA((LEVELS, 2)),
-            pltpu.VMEM(expand_four.shape, BF16),
-            pltpu.SemaphoreType.DMA,
             pltpu.VMEM((slabs, plan.cols0, 2, 2 * plan.rows1, LANES), F32),
             pltpu.VMEM((slabs, plan.cols0, 4, 4 * plan.rows1, LANES), F32),
         ]
         + shifted_maps(2 * plan.cols1, 2 * plan.rows1, ch)
-        + shifted_maps(plan.conv_cols, plan.conv_rows, ch),
+        + shifted_maps(plan.conv_cols, plan.conv_rows, ch)
+        + [pltpu.VMEM((LANES, LANES), F32)] * 2,
         compiler_params=pltpu.CompilerParams(vmem_limit_bytes=FINE_VMEM),
         cost_estimate=pl.CostEstimate(
             flops=8_000_000_000, bytes_accessed=10_000_000, transcendentals=0
         ),
         name="fine",
-    )(where, summed1, patch0, head.T, vector[:, None], expand_four, *filters)
-
-
-def gather_filters(filters, phases, dp_count):
+    )(where, summed1, patch0, head, vector[None, :], expand_four, matches, *filters)
+
+
+def gather_filters(filters, phase_id, phases, dp_count):
     axes = ("phase", "dp")
-    phase_id = lax.axis_index("phase")
     chips = dp_count // 2
 
     def move(value, to):
@@ -578,7 +598,7 @@
         )[:, 0]
         far = across(own, 2)
         near = across(own, 1)
-        column = jnp.stack([far, near, across(far, 1)])
+        column = stack([far, near, across(far, 1)])
         one = first(column)
         pieces = [column, one, second(column), second(one)]
         gathered.append(pieces + [swap(v) for v in pieces])
@@ -606,8 +626,13 @@
     phase_id = lax.axis_index("phase")
     dp_id = lax.axis_index("dp")
     where = jnp.stack([phase_id, dp_id % 2, dp_id // 2]).astype(jnp.int32)
+    slots = phase_id * dp_count * SLOT_DEV + jnp.arange(dp_count * SLOT_DEV, dtype=jnp.int32)
+    targets = lax.dynamic_slice(tile_slot, (dp_id, phase_id, 0), (1, 1, TILES_DEV))
+    matches = (slots.reshape(dp_count, SLOT_DEV, 1) == targets).astype(F32)
+    where, matches = lax.optimization_barrier((where, matches))
+    phase_id = where[0]
     if by_permutes(phases, dp_count):
-        base, gathered = gather_filters(refine_filters, phases, dp_count)
+        base, gathered = gather_filters(refine_filters, phase_id, phases, dp_count)
         upper, finer = base + gathered[0], base + gathered[1]
     else:
         upper = finer = [lax.all_gather(refine_filters, "dp", axis=2, tiled=True)]
@@ -615,17 +640,12 @@
     arrived = [sent[0]]
     for k in range(1, phases):
         arrived.append(lax.ppermute(sent[k], "phase", [(s, s ^ k) for s in range(phases)]))
-    mine = jnp.stack(arrived)
+    mine = stack(arrived)
     other = lax.ppermute(mine, "dp", [(d, d ^ 1) for d in range(dp_count)])
     summed1, patch0 = coarse(plan, where, mine, other, expand_two, upper)
-    depth = fine(plan, where, summed1, patch0, head_matrix, head_vector, expand_four, finer)
-    depth = depth[:, 0].reshape(4 * plan.block, TILES_DEV, -1)
-    depth_tiles = depth.transpose(1, 2, 0).reshape(TILES_DEV, -1)
-    slots = phase_id * dp_count * SLOT_DEV + jnp.arange(dp_count * SLOT_DEV, dtype=jnp.int32)
-    targets = lax.dynamic_slice(tile_slot, (dp_id, phase_id, 0), (1, 1, TILES_DEV)).reshape(-1)
-    matches = (slots[:, None] == targets[None, :]).astype(F32)
-    partial = jnp.dot(matches, depth_tiles, precision=lax.Precision.HIGHEST)
-    partial = partial.reshape(dp_count, SLOT_DEV, -1)
+    partial = fine(
+        plan, where, summed1, patch0, head_matrix, head_vector, expand_four, matches, finer
+    )
     portions = lax.all_to_all(partial, "dp", split_axis=0, concat_axis=0, tiled=True)
     return portions.sum(axis=0)
 

time: 105 us -> 91.2 us (0.87)
  Pallas kernels: 29.4 us -> 21.3 us
  local copies, waits for them, and re-layouts: 12.7 us -> 6.58 us
  waiting for transfers between devices: 28.7 us -> 33.5 us
  starting transfers between devices: 22.2 us -> 19.8 us
  blocking collectives: 10.2 us -> 8.62 us
    unnamed x33 -> x18, local copies, waits for them, and re-layouts: 11.3 us -> 5.56 us
    ppermute x21, waiting for transfers between devices: 24.9 us -> 29.8 us  [move(): return lax.ppermute(value, axes, route)]
    pallas_call x1, Pallas kernels: 8.58 us -> 5.08 us  [coarse(): pl.pallas_call(functools.partial(coarse_kernel, plan), out_shape=[jax.Sha...]
    pallas_call x1, Pallas kernels: 16.5 us -> 13.7 us  [fine(): pl.pallas_call(functools.partial(fine_kernel, plan), out_shape=jax.ShapeD...]
    ppermute x21, starting transfers between devices: 18.6 us -> 16.2 us  [move(): return lax.ppermute(value, axes, route)]
    pallas_call x1 -> x4, Pallas kernels: 4.35 us -> 2.47 us  [the longest x1 2.37 us: project(): pl.pallas_call(functools.partial(project_kernel, plan, phases), in_specs=...]
    all_to_all x1, blocking collectives: 10.2 us -> 8.62 us  [per_device(): lax.all_to_all(partial, 'dp', split_axis=0, concat_axis=0, tiled=True)]
  transfers between devices with their start and end apart: 25 -> 25, of which waited for: 10 -> 9; matrix products, arithmetic and copies ran while one was open for 1% -> 0% of each run, Pallas kernels for 12% -> 8%
where the time goes in v5:
time: 91.2 us; the launch traced here: 90.9 us
  waiting for transfers between devices  33.5 us (37%)
  Pallas kernels  21.3 us (23%)
  starting transfers between devices  19.8 us (22%)
  blocking collectives  8.62 us (9%)
  local copies, waits for them, and re-layouts  6.58 us (7%)
    ppermute x21, waiting for transfers between devices, move(): return lax.ppermute(value, axes, route)  29.8 us
    ppermute x21, starting transfers between devices, move(): return lax.ppermute(value, axes, route)  16.2 us
    pallas_call x1, Pallas kernels, fine(): pl.pallas_call(functools.partial(fine_kernel, plan), out_shape=jax.ShapeD...  13.7 us
    all_to_all x1, blocking collectives, per_device(): lax.all_to_all(partial, 'dp', split_axis=0, concat_axis=0, tiled=True)  8.62 us
    unnamed x18, local copies, waits for them, and re-layouts  5.56 us
    pallas_call x1, Pallas kernels, coarse(): pl.pallas_call(functools.partial(coarse_kernel, plan), out_shape=[jax.Sha...  5.08 us
    ppermute x3, waiting for transfers between devices, per_device(): lax.ppermute(sent[k], 'phase', [(s, s ^ k) for s in range(phases)])  3.74 us
    ppermute x3, starting transfers between devices, per_device(): lax.ppermute(sent[k], 'phase', [(s, s ^ k) for s in range(phases)])  3.55 us
  transfers between devices with their start and end apart: 25, of which 9 were waited for; matrix products, arithmetic and copies ran while one was open for 0% of the time, Pallas kernels for 8%

profile of v5, /device:TPU:0, one launch (start us, length us, event | category | flops | bytes accessed | tf_op | source)
XLA Modules:
  0.0 90.9 jit_solution(189052545773585660)
XLA Ops:
  0.0 0.7 copy-done
  1.0 1.0 %dynamic-slice_bitcast_fusion = (bf16[2,144,256]{2,1,0:T(8,128)(2,1)S(1)}, bf16[2,144,256]{2,1,0:T(8,128)(2,1)S(1)}) fusion(bf16[4,4,144,256]{3,2,1,0:T(8,128)(2,1)} %bitcast.17, s32[]{:T(128)S(6)} %select_n.25), kind=kLoop, calls=%fused_computation | loop fusion | bytes 589828 | tf_op jit(solution)/shard_map/squeeze | solution.py:596
  2.0 4.1 %collective-permute-start.5 = (bf16[2,144,256]{2,1,0:T(8,128)(2,1)S(1)}, bf16[2,144,256]{2,1,0:T(8,128)(2,1)S(1)}, u32[]{:S(2)}, u32[]{:S(2)}) collective-permute-start(bf16[2,144,256]{2,1,0:T(8,128)(2,1)S(1)} %get-tuple-element.22), channel_id=1, source_target_pairs={{0,4},{1,5},{2,6},{3,7},{4,0},{5,1},{6,2},{7,3},{8,12},{9,13},{10,... | collective-permute-start | bytes 442376 | tf_op jit(solution)/shard_map/ppermute | solution.py:576
  6.1 2.2 %copy-done.1 = bf16[1,512,4096]{2,1,0:T(8,128)(2,1)S(1)} copy-done((bf16[1,512,4096]{2,1,0:T(8,128)(2,1)S(1)}, bf16[1,512,4096]{2,1,0:T(8,128)(2,1)}, u32[]{:S(2)}) %copy-start.1) | copy-done | bytes 4194328
  8.3 1.6 %copy-done.2 = bf16[1,4096,256]{2,1,0:T(8,128)(2,1)S(1)} copy-done((bf16[1,4096,256]{2,1,0:T(8,128)(2,1)S(1)}, bf16[1,4096,256]{2,1,0:T(8,128)(2,1)}, u32[]{:S(2)}) %copy-start.2) | copy-done | bytes 2097176
  9.9 1.0 %copy-done.5 = bf16[1024,256]{1,0:T(8,128)(2,1)S(1)} copy-done((bf16[1024,256]{1,0:T(8,128)(2,1)S(1)}, bf16[1024,256]{1,0:T(8,128)(2,1)}, u32[]{:S(2)}) %copy-start.5) | copy-done | bytes 524312
  11.0 2.4 %project.1 = (bf16[256,256]{1,0:T(8,128)(2,1)S(1)}, bf16[256,256]{1,0:T(8,128)(2,1)S(1)}, bf16[256,256]{1,0:T(8,128)(2,1)S(1)}, bf16[256,256]{1,0:T(8,128)(2,1)S(1)}) custom-call(s32[3]{0:T(128)S(1)} %pad_add_fusion.where, bf16[1,512,4096]{2,1,0:T(8,128)(2,1)S(1)} %copy-done.1, bf16[1,4096,256]{2,1,0:T(8,128)(2,1)S(1)} %copy-done.2, ...), custom_call_target="tpu_custom_call" | custom-call | flops 1073741824 | bytes 6291456 | tf_op jit(solution)/shard_map/project/pallas_call | solution.py:115
  13.4 1.5 %collective-permute-start = (bf16[256,256]{1,0:T(8,128)(2,1)S(1)}, bf16[256,256]{1,0:T(8,128)(2,1)S(1)}, u32[]{:S(2)}, u32[]{:S(2)}) collective-permute-start(bf16[256,256]{1,0:T(8,128)(2,1)S(1)} %get-tuple-element.15), channel_id=1, source_target_pairs={{0,8},{8,0},{16,24},{24,16},{1,9},{9,1},{17,25},{25,17},{2,10},{10... | collective-permute-start | bytes 393224 | tf_op jit(solution)/shard_map/ppermute | solution.py:642
  14.9 1.4 %collective-permute-start.1 = (bf16[256,256]{1,0:T(8,128)(2,1)S(1)}, bf16[256,256]{1,0:T(8,128)(2,1)S(1)}, u32[]{:S(2)}, u32[]{:S(2)}) collective-permute-start(bf16[256,256]{1,0:T(8,128)(2,1)S(1)} %get-tuple-element.16), channel_id=1, source_target_pairs={{0,16},{8,24},{16,0},{24,8},{1,17},{9,25},{17,1},{25,9},{2,18},{10... | collective-permute-start | bytes 393224 | tf_op jit(solution)/shard_map/ppermute | solution.py:642
  16.3 0.7 collective-permute-start.2
  16.9 1.6 %collective-permute-start.6 = (bf16[2,144,256]{2,1,0:T(8,128)(2,1)S(1)}, bf16[2,144,256]{2,1,0:T(8,128)(2,1)S(1)}, u32[]{:S(2)}, u32[]{:S(2)}) collective-permute-start(bf16[2,144,256]{2,1,0:T(8,128)(2,1)S(1)} %get-tuple-element.22), channel_id=1, source_target_pairs={{0,2},{1,3},{2,0},{3,1},{4,6},{5,7},{6,4},{7,5},{8,10},{9,11},{10,... | collective-permute-start | bytes 442376 | tf_op jit(solution)/shard_map/ppermute | solution.py:576
  18.5 0.5 collective-permute-start.7
  18.9 3.7 %collective-permute-done.1.refs_2_ = bf16[256,256]{1,0:T(8,128)(2,1)S(1)} collective-permute-done((bf16[256,256]{1,0:T(8,128)(2,1)S(1)}, bf16[256,256]{1,0:T(8,128)(2,1)S(1)}, u32[]{:S(2)}, u32[]{:S(2)}) %collective-permute-start.1) | collective-permute-done | bytes 131104 | tf_op jit(solution)/shard_map/ppermute | solution.py:642
  22.9 1.6 %collective-permute-done.7.refs_2_ = bf16[2,144,256]{2,1,0:T(8,128)(2,1)S(1)} collective-permute-done((bf16[2,144,256]{2,1,0:T(8,128)(2,1)S(1)}, bf16[2,144,256]{2,1,0:T(8,128)(2,1)S(1)}, u32[]{:S(2)}, u32[]{:S(2)}) %collective-permute-start.7) | collective-permute-done | bytes 147488 | tf_op jit(solution)/shard_map/ppermute | solution.py:576
  24.6 1.6 %collective-permute-start.8 = (bf16[3,2,144,256]{3,2,1,0:T(8,128)(2,1)S(1)}, bf16[3,2,144,256]{3,2,1,0:T(8,128)(2,1)S(1)}, u32[]{:S(2)}, u32[]{:S(2)}) collective-permute-start(bf16[3,2,144,256]{3,2,1,0:T(8,128)(2,1)S(1)} %stack.20.refs_2_), channel_id=1, source_target_pairs={{0,8},{1,17},{2,10},{3,19},{4,12},{5,21},{6,14},{7,23},{8,0},{9,25... | collective-permute-start | bytes 1327112 | tf_op jit(solution)/shard_map/ppermute | solution.py:576
  26.5 1.6 %collective-permute-start.16 = (bf16[2,144,256]{2,1,0:T(8,128)(2,1)S(1)}, bf16[2,144,256]{2,1,0:T(8,128)(2,1)S(1)}, u32[]{:S(2)}, u32[]{:S(2)}) collective-permute-start(bf16[2,144,256]{2,1,0:T(8,128)(2,1)S(1)} %get-tuple-element.21), channel_id=1, source_target_pairs={{0,2},{1,3},{2,0},{3,1},{4,6},{5,7},{6,4},{7,5},{8,10},{9,11},{10,... | collective-permute-start | bytes 442376 | tf_op jit(solution)/shard_map/ppermute | solution.py:576
  28.0 6.1 %collective-permute-done.15.refs_0_ = bf16[2,144,256]{2,1,0:T(8,128)(2,1)S(1)} collective-permute-done((bf16[2,144,256]{2,1,0:T(8,128)(2,1)S(1)}, bf16[2,144,256]{2,1,0:T(8,128)(2,1)S(1)}, u32[]{:S(2)}, u32[]{:S(2)}) %collective-permute-start.15) | collective-permute-done | bytes 147488 | tf_op jit(solution)/shard_map/ppermute | solution.py:576
  34.2 0.9 %collective-permute-start.9 = (bf16[3,2,144,256]{3,2,1,0:T(8,128)(2,1)S(1)}, bf16[3,2,144,256]{3,2,1,0:T(8,128)(2,1)S(1)}, u32[]{:S(2)}, u32[]{:S(2)}) collective-permute-start(bf16[3,2,144,256]{3,2,1,0:T(8,128)(2,1)S(1)} %stack.20.refs_2_), channel_id=1, source_target_pairs={{0,16},{1,9},{2,18},{3,11},{4,20},{5,13},{6,22},{7,15},{8,24},{9,1... | collective-permute-start | bytes 1327112 | tf_op jit(solution)/shard_map/ppermute | solution.py:576
  35.3 5.0 %collective-permute-done.17.refs_2_ = bf16[2,144,256]{2,1,0:T(8,128)(2,1)S(1)} collective-permute-done((bf16[2,144,256]{2,1,0:T(8,128)(2,1)S(1)}, bf16[2,144,256]{2,1,0:T(8,128)(2,1)S(1)}, u32[]{:S(2)}, u32[]{:S(2)}) %collective-permute-start.17) | collective-permute-done | bytes 147488 | tf_op jit(solution)/shard_map/ppermute | solution.py:576
  40.4 0.8 collective-permute-start.18
  41.1 1.1 %collective-permute-start.19 = (bf16[3,2,144,256]{3,2,1,0:T(8,128)(2,1)S(1)}, bf16[3,2,144,256]{3,2,1,0:T(8,128)(2,1)S(1)}, u32[]{:S(2)}, u32[]{:S(2)}) collective-permute-start(bf16[3,2,144,256]{3,2,1,0:T(8,128)(2,1)S(1)} %stack.21.refs_2_), channel_id=1, source_target_pairs={{0,16},{1,9},{2,18},{3,11},{4,20},{5,13},{6,22},{7,15},{8,24},{9,1... | collective-permute-start | bytes 1327112 | tf_op jit(solution)/shard_map/ppermute | solution.py:576
  42.5 0.9 %collective-permute-start.10 = (bf16[3,2,144,256]{3,2,1,0:T(8,128)(2,1)S(1)}, bf16[3,2,144,256]{3,2,1,0:T(8,128)(2,1)S(1)}, u32[]{:S(2)}, u32[]{:S(2)}) collective-permute-start(bf16[3,2,144,256]{3,2,1,0:T(8,128)(2,1)S(1)} %collective-permute-done.8.refs_3_), channel_id=1, source_target_pairs={{0,16},{1,9},{2,18},{3,11},{4,20},{5,13},{6,22},{7,15},{8,24},{9,1... | collective-permute-start | bytes 1327112 | tf_op jit(solution)/shard_map/ppermute | solution.py:576
  43.4 9.7 %collective-permute-done.18.refs_3_ = bf16[3,2,144,256]{3,2,1,0:T(8,128)(2,1)S(1)} collective-permute-done((bf16[3,2,144,256]{3,2,1,0:T(8,128)(2,1)S(1)}, bf16[3,2,144,256]{3,2,1,0:T(8,128)(2,1)S(1)}, u32[]{:S(2)}, u32[]{:S(2)}) %collective-permute-start.18) | collective-permute-done | bytes 442400 | tf_op jit(solution)/shard_map/ppermute | solution.py:576
  53.1 1.2 %collective-permute-start.20 = (bf16[3,2,144,256]{3,2,1,0:T(8,128)(2,1)S(1)}, bf16[3,2,144,256]{3,2,1,0:T(8,128)(2,1)S(1)}, u32[]{:S(2)}, u32[]{:S(2)}) collective-permute-start(bf16[3,2,144,256]{3,2,1,0:T(8,128)(2,1)S(1)} %collective-permute-done.18.refs_3_), channel_id=1, source_target_pairs={{0,16},{1,9},{2,18},{3,11},{4,20},{5,13},{6,22},{7,15},{8,24},{9,1... | collective-permute-start | bytes 1327112 | tf_op jit(solution)/shard_map/ppermute | solution.py:576
  54.4 3.4 %collective-permute-done.10.refs_5_ = bf16[3,2,144,256]{3,2,1,0:T(8,128)(2,1)S(1)} collective-permute-done((bf16[3,2,144,256]{3,2,1,0:T(8,128)(2,1)S(1)}, bf16[3,2,144,256]{3,2,1,0:T(8,128)(2,1)S(1)}, u32[]{:S(2)}, u32[]{:S(2)}) %collective-permute-start.10) | collective-permute-done | bytes 442400 | tf_op jit(solution)/shard_map/ppermute | solution.py:576
  57.7 0.6 collective-permute-start.14
  58.3 0.5 collective-permute-start.22
  58.9 3.6 %collective-permute-done.20.refs_5_ = bf16[3,2,144,256]{3,2,1,0:T(8,128)(2,1)S(1)} collective-permute-done((bf16[3,2,144,256]{3,2,1,0:T(8,128)(2,1)S(1)}, bf16[3,2,144,256]{3,2,1,0:T(8,128)(2,1)S(1)}, u32[]{:S(2)}, u32[]{:S(2)}) %collective-permute-start.20) | collective-permute-done | bytes 442400 | tf_op jit(solution)/shard_map/ppermute | solution.py:576
  62.8 5.1 %coarse.1 = (f32[2,12,2,48,128]{4,3,2,1,0:T(8,128)S(1)}, bf16[240,256]{1,0:T(8,128)(2,1)S(1)}) custom-call(s32[3]{0:T(128)S(1)} %pad_add_fusion.where, bf16[4,256,256]{2,1,0:T(8,128)(2,1)S(1)} %stack.19.mine, bf16[4,256,256]{2,1,0:T(8,128)(2,1)S(1)} %collective-permute-done.3.other, bf16[256,1024]{1,0:T(8,128)(2,1)S(1)} %copy-done.4, ...), custom_call_target="tpu_custom_call" | custom-call | flops 2000000000 | bytes 8000000 | tf_op jit(solution)/shard_map/coarse/pallas_call | solution.py:372
  67.9 13.7 %fine.1 = f32[8,6,256]{2,1,0:T(8,128)S(1)} custom-call(s32[3]{0:T(128)S(1)} %pad_add_fusion.where, f32[2,12,2,48,128]{4,3,2,1,0:T(8,128)S(1)} %get-tuple-element.18.summed1, bf16[240,256]{1,0:T(8,128)(2,1)S(1)} %get-tuple-element.19.patch0, bf16[256,128]{1,0:T(8,128)(2,1)S(1)} %copy-done.7, f32[1,128]{1,0:T(1,128)S(1)} %bitcast.21, ...), custom_call_target="tpu_custom_call" | custom-call | flops 8000000000 | bytes 10000000 | tf_op jit(solution)/shard_map/fine/pallas_call | solution.py:542
  81.7 8.6 %all_to_all.5 = f32[8,6,256]{2,1,0:T(8,128)S(1)} all-to-all(f32[8,6,256]{2,1,0:T(8,128)S(1)} %fine.1), channel_id=1, replica_groups=mesh['phase'=4,'dp'=8] {'dp'}, dimensions={0} | all-to-all | bytes 98304 | tf_op jit(solution)/shard_map/all_to_all | solution.py:649
  90.3 0.6 reduce_sum.9
  (49 shorter events, 1.7 us)
Async XLA Ops:
  2.0 16.5 %collective-permute-start.5 = (bf16[2,144,256]{2,1,0:T(8,128)(2,1)S(1)}, bf16[2,144,256]{2,1,0:T(8,128)(2,1)S(1)}, u32[]{:S(2)}, u32[]{:S(2)}) collective-permute-start(bf16[2,144,256]{2,1,0:T(8,128)(2,1)S(1)} %get-tuple-element.22), channel_id=1, source_target_pairs={{0,4},{1,5},{2,6},{3,7},{4,0},{5,1},{6,2},{7,3},{8,12},{9,13},{10,... | collective-permute-start | bytes 442376 | tf_op jit(solution)/shard_map/ppermute | solution.py:576
  6.1 2.2 %copy-start.1 = (bf16[1,512,4096]{2,1,0:T(8,128)(2,1)S(1)}, bf16[1,512,4096]{2,1,0:T(8,128)(2,1)}, u32[]{:S(2)}) copy-start(bf16[1,512,4096]{2,1,0:T(8,128)(2,1)} %tokens.1) | copy-start | bytes 12582916
  8.3 1.6 %copy-start.2 = (bf16[1,4096,256]{2,1,0:T(8,128)(2,1)S(1)}, bf16[1,4096,256]{2,1,0:T(8,128)(2,1)}, u32[]{:S(2)}) copy-start(bf16[1,4096,256]{2,1,0:T(8,128)(2,1)} %weight.1) | copy-start | bytes 6291460
  13.3 14.7 %copy-start.3 = (bf16[4,2,288,256]{3,2,1,0:T(8,128)(2,1)S(1)}, bf16[4,2,288,256]{3,2,1,0:T(8,128)(2,1)}, u32[]{:S(2)}) copy-start(bf16[4,2,288,256]{3,2,1,0:T(8,128)(2,1)} %refs_0_.3) | copy-start | bytes 3538948
  13.4 5.6 %collective-permute-start = (bf16[256,256]{1,0:T(8,128)(2,1)S(1)}, bf16[256,256]{1,0:T(8,128)(2,1)S(1)}, u32[]{:S(2)}, u32[]{:S(2)}) collective-permute-start(bf16[256,256]{1,0:T(8,128)(2,1)S(1)} %get-tuple-element.15), channel_id=1, source_target_pairs={{0,8},{8,0},{16,24},{24,16},{1,9},{9,1},{17,25},{25,17},{2,10},{10... | collective-permute-start | bytes 393224 | tf_op jit(solution)/shard_map/ppermute | solution.py:642
  14.9 7.8 %collective-permute-start.1 = (bf16[256,256]{1,0:T(8,128)(2,1)S(1)}, bf16[256,256]{1,0:T(8,128)(2,1)S(1)}, u32[]{:S(2)}, u32[]{:S(2)}) collective-permute-start(bf16[256,256]{1,0:T(8,128)(2,1)S(1)} %get-tuple-element.16), channel_id=1, source_target_pairs={{0,16},{8,24},{16,0},{24,8},{1,17},{9,25},{17,1},{25,9},{2,18},{10... | collective-permute-start | bytes 393224 | tf_op jit(solution)/shard_map/ppermute | solution.py:642
  16.3 6.4 %collective-permute-start.2 = (bf16[256,256]{1,0:T(8,128)(2,1)S(1)}, bf16[256,256]{1,0:T(8,128)(2,1)S(1)}, u32[]{:S(2)}, u32[]{:S(2)}) collective-permute-start(bf16[256,256]{1,0:T(8,128)(2,1)S(1)} %get-tuple-element.17), channel_id=1, source_target_pairs={{0,24},{8,16},{16,8},{24,0},{1,25},{9,17},{17,9},{25,1},{2,26},{10... | collective-permute-start | bytes 393224 | tf_op jit(solution)/shard_map/ppermute | solution.py:642
  16.9 6.0 %collective-permute-start.6 = (bf16[2,144,256]{2,1,0:T(8,128)(2,1)S(1)}, bf16[2,144,256]{2,1,0:T(8,128)(2,1)S(1)}, u32[]{:S(2)}, u32[]{:S(2)}) collective-permute-start(bf16[2,144,256]{2,1,0:T(8,128)(2,1)S(1)} %get-tuple-element.22), channel_id=1, source_target_pairs={{0,2},{1,3},{2,0},{3,1},{4,6},{5,7},{6,4},{7,5},{8,10},{9,11},{10,... | collective-permute-start | bytes 442376 | tf_op jit(solution)/shard_map/ppermute | solution.py:576
  18.5 6.0 %collective-permute-start.7 = (bf16[2,144,256]{2,1,0:T(8,128)(2,1)S(1)}, bf16[2,144,256]{2,1,0:T(8,128)(2,1)S(1)}, u32[]{:S(2)}, u32[]{:S(2)}) collective-permute-start(bf16[2,144,256]{2,1,0:T(8,128)(2,1)S(1)} %collective-permute-done.5.refs_0_), channel_id=1, source_target_pairs={{0,2},{1,3},{2,0},{3,1},{4,6},{5,7},{6,4},{7,5},{8,10},{9,11},{10,... | collective-permute-start | bytes 442376 | tf_op jit(solution)/shard_map/ppermute | solution.py:576
  22.7 40.1 %copy-start.4 = (bf16[256,1024]{1,0:T(8,128)(2,1)S(1)}, bf16[256,1024]{1,0:T(8,128)(2,1)}, u32[]{:S(2)}) copy-start(bf16[256,1024]{1,0:T(8,128)(2,1)} %expand_two.1) | copy-start | bytes 1572868
  22.7 17.6 %collective-permute-start.3 = (bf16[4,256,256]{2,1,0:T(8,128)(2,1)S(1)}, bf16[4,256,256]{2,1,0:T(8,128)(2,1)S(1)}, u32[]{:S(2)}, u32[]{:S(2)}) collective-permute-start(bf16[4,256,256]{2,1,0:T(8,128)(2,1)S(1)} %stack.19.mine), channel_id=1, source_target_pairs={{0,1},{1,0},{2,3},{3,2},{4,5},{5,4},{6,7},{7,6},{8,9},{9,8},{10,11... | collective-permute-start | bytes 1572872 | tf_op jit(solution)/shard_map/ppermute | solution.py:644
  24.6 16.6 %collective-permute-start.8 = (bf16[3,2,144,256]{3,2,1,0:T(8,128)(2,1)S(1)}, bf16[3,2,144,256]{3,2,1,0:T(8,128)(2,1)S(1)}, u32[]{:S(2)}, u32[]{:S(2)}) collective-permute-start(bf16[3,2,144,256]{3,2,1,0:T(8,128)(2,1)S(1)} %stack.20.refs_2_), channel_id=1, source_target_pairs={{0,8},{1,17},{2,10},{3,19},{4,12},{5,21},{6,14},{7,23},{8,0},{9,25... | collective-permute-start | bytes 1327112 | tf_op jit(solution)/shard_map/ppermute | solution.py:576
  26.1 8.1 %collective-permute-start.15 = (bf16[2,144,256]{2,1,0:T(8,128)(2,1)S(1)}, bf16[2,144,256]{2,1,0:T(8,128)(2,1)S(1)}, u32[]{:S(2)}, u32[]{:S(2)}) collective-permute-start(bf16[2,144,256]{2,1,0:T(8,128)(2,1)S(1)} %get-tuple-element.21), channel_id=1, source_target_pairs={{0,4},{1,5},{2,6},{3,7},{4,0},{5,1},{6,2},{7,3},{8,12},{9,13},{10,... | collective-permute-start | bytes 442376 | tf_op jit(solution)/shard_map/ppermute | solution.py:576
  26.5 8.7 %collective-permute-start.16 = (bf16[2,144,256]{2,1,0:T(8,128)(2,1)S(1)}, bf16[2,144,256]{2,1,0:T(8,128)(2,1)S(1)}, u32[]{:S(2)}, u32[]{:S(2)}) collective-permute-start(bf16[2,144,256]{2,1,0:T(8,128)(2,1)S(1)} %get-tuple-element.21), channel_id=1, source_target_pairs={{0,2},{1,3},{2,0},{3,1},{4,6},{5,7},{6,4},{7,5},{8,10},{9,11},{10,... | collective-permute-start | bytes 442376 | tf_op jit(solution)/shard_map/ppermute | solution.py:576
  28.0 30.8 %collective-permute-start.4 = (bf16[4,2,288,256]{3,2,1,0:T(8,128)(2,1)S(1)}, bf16[4,2,288,256]{3,2,1,0:T(8,128)(2,1)S(1)}, u32[]{:S(2)}, u32[]{:S(2)}) collective-permute-start(bf16[4,2,288,256]{3,2,1,0:T(8,128)(2,1)S(1)} %copy-done.3), channel_id=1, source_target_pairs={{0,1},{1,0},{2,3},{3,2},{4,5},{5,4},{6,7},{7,6},{8,9},{9,8},{10,11... | collective-permute-start | bytes 3538952 | tf_op jit(solution)/shard_map/ppermute | solution.py:576
  34.2 8.3 %collective-permute-start.9 = (bf16[3,2,144,256]{3,2,1,0:T(8,128)(2,1)S(1)}, bf16[3,2,144,256]{3,2,1,0:T(8,128)(2,1)S(1)}, u32[]{:S(2)}, u32[]{:S(2)}) collective-permute-start(bf16[3,2,144,256]{3,2,1,0:T(8,128)(2,1)S(1)} %stack.20.refs_2_), channel_id=1, source_target_pairs={{0,16},{1,9},{2,18},{3,11},{4,20},{5,13},{6,22},{7,15},{8,24},{9,1... | collective-permute-start | bytes 1327112 | tf_op jit(solution)/shard_map/ppermute | solution.py:576
  35.1 5.1 %collective-permute-start.17 = (bf16[2,144,256]{2,1,0:T(8,128)(2,1)S(1)}, bf16[2,144,256]{2,1,0:T(8,128)(2,1)S(1)}, u32[]{:S(2)}, u32[]{:S(2)}) collective-permute-start(bf16[2,144,256]{2,1,0:T(8,128)(2,1)S(1)} %collective-permute-done.15.refs_0_), channel_id=1, source_target_pairs={{0,2},{1,3},{2,0},{3,1},{4,6},{5,7},{6,4},{7,5},{8,10},{9,11},{10,... | collective-permute-start | bytes 442376 | tf_op jit(solution)/shard_map/ppermute | solution.py:576
  40.3 3.2 %collective-permute-start.11 = (bf16[3,2,144,256]{3,2,1,0:T(8,128)(2,1)S(1)}, bf16[3,2,144,256]{3,2,1,0:T(8,128)(2,1)S(1)}, u32[]{:S(2)}, u32[]{:S(2)}) collective-permute-start(bf16[3,2,144,256]{3,2,1,0:T(8,128)(2,1)S(1)} %stack.20.refs_2_), channel_id=1, source_target_pairs={{0,1},{1,0},{2,3},{3,2},{4,5},{5,4},{6,7},{7,6},{8,9},{9,8},{10,11... | collective-permute-start | bytes 1327112 | tf_op jit(solution)/shard_map/ppermute | solution.py:576
  40.3 27.6 %copy-start.6 = (bf16[256,4096]{1,0:T(8,128)(2,1)S(1)}, bf16[256,4096]{1,0:T(8,128)(2,1)}, u32[]{:S(2)}) copy-start(bf16[256,4096]{1,0:T(8,128)(2,1)} %expand_four.1) | copy-start | bytes 6291460
  40.3 27.6 %copy-start.7 = (bf16[256,128]{1,0:T(8,128)(2,1)S(1)}, bf16[256,128]{1,0:T(8,128)(2,1)}, u32[]{:S(2)}) copy-start(bf16[256,128]{1,0:T(8,128)(2,1)} %head.1) | copy-start | bytes 196612
  40.3 27.6 %copy-start.8 = (f32[128]{0:T(128)S(1)}, f32[128]{0:T(128)}, u32[]{:S(2)}) copy-start(f32[128]{0:T(128)} %param.16) | copy-start | bytes 1540
  40.4 12.8 %collective-permute-start.18 = (bf16[3,2,144,256]{3,2,1,0:T(8,128)(2,1)S(1)}, bf16[3,2,144,256]{3,2,1,0:T(8,128)(2,1)S(1)}, u32[]{:S(2)}, u32[]{:S(2)}) collective-permute-start(bf16[3,2,144,256]{3,2,1,0:T(8,128)(2,1)S(1)} %stack.21.refs_2_), channel_id=1, source_target_pairs={{0,8},{1,17},{2,10},{3,19},{4,12},{5,21},{6,14},{7,23},{8,0},{9,25... | collective-permute-start | bytes 1327112 | tf_op jit(solution)/shard_map/ppermute | solution.py:576
  41.1 12.0 %collective-permute-start.19 = (bf16[3,2,144,256]{3,2,1,0:T(8,128)(2,1)S(1)}, bf16[3,2,144,256]{3,2,1,0:T(8,128)(2,1)S(1)}, u32[]{:S(2)}, u32[]{:S(2)}) collective-permute-start(bf16[3,2,144,256]{3,2,1,0:T(8,128)(2,1)S(1)} %stack.21.refs_2_), channel_id=1, source_target_pairs={{0,16},{1,9},{2,18},{3,11},{4,20},{5,13},{6,22},{7,15},{8,24},{9,1... | collective-permute-start | bytes 1327112 | tf_op jit(solution)/shard_map/ppermute | solution.py:576
  42.5 15.3 %collective-permute-start.10 = (bf16[3,2,144,256]{3,2,1,0:T(8,128)(2,1)S(1)}, bf16[3,2,144,256]{3,2,1,0:T(8,128)(2,1)S(1)}, u32[]{:S(2)}, u32[]{:S(2)}) collective-permute-start(bf16[3,2,144,256]{3,2,1,0:T(8,128)(2,1)S(1)} %collective-permute-done.8.refs_3_), channel_id=1, source_target_pairs={{0,16},{1,9},{2,18},{3,11},{4,20},{5,13},{6,22},{7,15},{8,24},{9,1... | collective-permute-start | bytes 1327112 | tf_op jit(solution)/shard_map/ppermute | solution.py:576
  43.4 14.9 %collective-permute-start.12 = (bf16[3,2,144,256]{3,2,1,0:T(8,128)(2,1)S(1)}, bf16[3,2,144,256]{3,2,1,0:T(8,128)(2,1)S(1)}, u32[]{:S(2)}, u32[]{:S(2)}) collective-permute-start(bf16[3,2,144,256]{3,2,1,0:T(8,128)(2,1)S(1)} %collective-permute-done.8.refs_3_), channel_id=1, source_target_pairs={{0,1},{1,0},{2,3},{3,2},{4,5},{5,4},{6,7},{7,6},{8,9},{9,8},{10,11... | collective-permute-start | bytes 1327112 | tf_op jit(solution)/shard_map/ppermute | solution.py:576
  53.1 5.2 %collective-permute-start.13 = (bf16[3,2,144,256]{3,2,1,0:T(8,128)(2,1)S(1)}, bf16[3,2,144,256]{3,2,1,0:T(8,128)(2,1)S(1)}, u32[]{:S(2)}, u32[]{:S(2)}) collective-permute-start(bf16[3,2,144,256]{3,2,1,0:T(8,128)(2,1)S(1)} %collective-permute-done.9.refs_4_), channel_id=1, source_target_pairs={{0,1},{1,0},{2,3},{3,2},{4,5},{5,4},{6,7},{7,6},{8,9},{9,8},{10,11... | collective-permute-start | bytes 1327112 | tf_op jit(solution)/shard_map/ppermute | solution.py:576
  53.1 9.4 %collective-permute-start.20 = (bf16[3,2,144,256]{3,2,1,0:T(8,128)(2,1)S(1)}, bf16[3,2,144,256]{3,2,1,0:T(8,128)(2,1)S(1)}, u32[]{:S(2)}, u32[]{:S(2)}) collective-permute-start(bf16[3,2,144,256]{3,2,1,0:T(8,128)(2,1)S(1)} %collective-permute-done.18.refs_3_), channel_id=1, source_target_pairs={{0,16},{1,9},{2,18},{3,11},{4,20},{5,13},{6,22},{7,15},{8,24},{9,1... | collective-permute-start | bytes 1327112 | tf_op jit(solution)/shard_map/ppermute | solution.py:576
  57.7 5.0 %collective-permute-start.14 = (bf16[3,2,144,256]{3,2,1,0:T(8,128)(2,1)S(1)}, bf16[3,2,144,256]{3,2,1,0:T(8,128)(2,1)S(1)}, u32[]{:S(2)}, u32[]{:S(2)}) collective-permute-start(bf16[3,2,144,256]{3,2,1,0:T(8,128)(2,1)S(1)} %collective-permute-done.10.refs_5_), channel_id=1, source_target_pairs={{0,1},{1,0},{2,3},{3,2},{4,5},{5,4},{6,7},{7,6},{8,9},{9,8},{10,11... | collective-permute-start | bytes 1327112 | tf_op jit(solution)/shard_map/ppermute | solution.py:576
  58.3 9.5 %collective-permute-start.21 = (bf16[3,2,144,256]{3,2,1,0:T(8,128)(2,1)S(1)}, bf16[3,2,144,256]{3,2,1,0:T(8,128)(2,1)S(1)}, u32[]{:S(2)}, u32[]{:S(2)}) collective-permute-start(bf16[3,2,144,256]{3,2,1,0:T(8,128)(2,1)S(1)} %stack.21.refs_2_), channel_id=1, source_target_pairs={{0,1},{1,0},{2,3},{3,2},{4,5},{5,4},{6,7},{7,6},{8,9},{9,8},{10,11... | collective-permute-start | bytes 1327112 | tf_op jit(solution)/shard_map/ppermute | solution.py:576
  58.3 9.5 %collective-permute-start.22 = (bf16[3,2,144,256]{3,2,1,0:T(8,128)(2,1)S(1)}, bf16[3,2,144,256]{3,2,1,0:T(8,128)(2,1)S(1)}, u32[]{:S(2)}, u32[]{:S(2)}) collective-permute-start(bf16[3,2,144,256]{3,2,1,0:T(8,128)(2,1)S(1)} %collective-permute-done.18.refs_3_), channel_id=1, source_target_pairs={{0,1},{1,0},{2,3},{3,2},{4,5},{5,4},{6,7},{7,6},{8,9},{9,8},{10,11... | collective-permute-start | bytes 1327112 | tf_op jit(solution)/shard_map/ppermute | solution.py:576
  58.8 9.0 %collective-permute-start.23 = (bf16[3,2,144,256]{3,2,1,0:T(8,128)(2,1)S(1)}, bf16[3,2,144,256]{3,2,1,0:T(8,128)(2,1)S(1)}, u32[]{:S(2)}, u32[]{:S(2)}) collective-permute-start(bf16[3,2,144,256]{3,2,1,0:T(8,128)(2,1)S(1)} %collective-permute-done.19.refs_4_), channel_id=1, source_target_pairs={{0,1},{1,0},{2,3},{3,2},{4,5},{5,4},{6,7},{7,6},{8,9},{9,8},{10,11... | collective-permute-start | bytes 1327112 | tf_op jit(solution)/shard_map/ppermute | solution.py:576
  62.5 5.4 %collective-permute-start.24 = (bf16[3,2,144,256]{3,2,1,0:T(8,128)(2,1)S(1)}, bf16[3,2,144,256]{3,2,1,0:T(8,128)(2,1)S(1)}, u32[]{:S(2)}, u32[]{:S(2)}) collective-permute-start(bf16[3,2,144,256]{3,2,1,0:T(8,128)(2,1)S(1)} %collective-permute-done.20.refs_5_), channel_id=1, source_target_pairs={{0,1},{1,0},{2,3},{3,2},{4,5},{5,4},{6,7},{7,6},{8,9},{9,8},{10,11... | collective-permute-start | bytes 1327112 | tf_op jit(solution)/shard_map/ppermute | solution.py:576
  (2 other events, 1.8 us)

commit v6 on v5

--- a/solution.py
+++ b/solution.py
@@ -14,7 +14,8 @@
 F32 = jnp.float32
 BF16 = jnp.bfloat16
 STACK_VMEM = 4 * 1024 * 1024
-PROJECT_VMEM = 12 * 1024 * 1024
+PROJECT_VMEM = 60 * 1024 * 1024
+PROJECT_STEPS = 8
 COARSE_VMEM = 12 * 1024 * 1024
 FINE_VMEM = 32 * 1024 * 1024
 
@@ -64,15 +65,36 @@
         return jnp.clip(s * self.block - 1, 0, G - self.cols0)
 
 
-def project_kernel(plan, phases, where, tokens, weight, shrink, *refs):
-    outs, acc_lo, acc_hi = refs[:phases], refs[phases], refs[phases + 1]
+def project_kernel(plan, phases, where, tokens_hbm, weight_hbm, shrink_hbm, *refs):
+    outs = refs[:phases]
+    acc_lo, acc_hi, tokens, weight, shrink, sems, shrink_sem = refs[phases:]
     lanes = acc_lo.shape[1]
-    rows = tokens.shape[1] // 2
-    for i in range(2):
-        at = pl.ds(i * rows, rows)
-        value = dot(tokens[0, at, :], weight[0])
-        acc_lo[at, :] = value[:, :lanes]
-        acc_hi[at, :] = value[:, lanes:]
+    depth = tokens.shape[1]
+    size = depth // PROJECT_STEPS
+    copies = []
+    for i in range(PROJECT_STEPS):
+        at = pl.ds(i * size, size)
+        pair = (
+            pltpu.make_async_copy(weight_hbm.at[0, at], weight.at[at], sems.at[0, i]),
+            pltpu.make_async_copy(tokens_hbm.at[0, :, at], tokens.at[:, at], sems.at[1, i]),
+        )
+        for copy in pair:
+            copy.start()
+        copies.append(pair)
+    shrink_copy = pltpu.make_async_copy(shrink_hbm, shrink, shrink_sem)
+    shrink_copy.start()
+    for i, pair in enumerate(copies):
+        for copy in pair:
+            copy.wait()
+        at = slice(i * size, (i + 1) * size)
+        part = dot(tokens[:, at], weight[at, :])
+        if i == 0:
+            acc_lo[...] = part[:, :lanes]
+            acc_hi[...] = part[:, lanes:]
+        else:
+            acc_lo[...] += part[:, :lanes]
+            acc_hi[...] += part[:, lanes:]
+    shrink_copy.wait()
     phase = where[0]
 
     def column(start, size, stride):
@@ -110,13 +132,21 @@
 def project(plan, phases, where, tokens, weight, shrink):
     rows, depth = tokens.shape[1:]
     pixels = plan.sent * plan.half
+    hbm = pl.BlockSpec(memory_space=pltpu.HBM)
     out = jax.ShapeDtypeStruct((pixels, plan.ch), BF16)
     vmem = pl.BlockSpec(memory_space=pltpu.VMEM)
     return pl.pallas_call(
         functools.partial(project_kernel, plan, phases),
-        in_specs=[pl.BlockSpec(memory_space=pltpu.SMEM), vmem, vmem, vmem],
+        in_specs=[pl.BlockSpec(memory_space=pltpu.SMEM), hbm, hbm, hbm],
         out_specs=[vmem] * phases,
-        scratch_shapes=[pltpu.VMEM((rows, plan.ch // 2), F32)] * 2,
+        scratch_shapes=[pltpu.VMEM((rows, plan.ch // 2), F32)] * 2
+        + [
+            pltpu.VMEM((rows, depth), BF16),
+            pltpu.VMEM((depth, plan.ch), BF16),
+            pltpu.VMEM(shrink.shape, BF16),
+            pltpu.SemaphoreType.DMA((2, PROJECT_STEPS)),
+            pltpu.SemaphoreType.DMA,
+        ],
         out_shape=[out] * phases,
         compiler_params=pltpu.CompilerParams(vmem_limit_bytes=PROJECT_VMEM),
         cost_estimate=pl.CostEstimate(
@@ -228,6 +258,14 @@
         at = pl.ds(pl.multiple_of((2 * chip + core) * rows, 16), rows)
         for m in range(2):
             weights[m, at, :] = ref[level, m]
+    if len(filters) == 6:
+        for refs, core in ((filters[2:4], side), (filters[4:6], 1 - side)):
+            held = (phase >> core) % 2
+            for ref, m in zip(refs, (held, 1 - held)):
+                for i, away in enumerate(CHIP_ORDER):
+                    start = (2 * (chip ^ away) + core) * rows
+                    weights[m, pl.ds(pl.multiple_of(start, 16), rows), :] = ref[i, slot]
+        return
     for refs, core in ((filters[2:6], side), (filters[6:10], 1 - side)):
         for ref, moved in zip(refs, (0, 1 + core, 2 - core, 3)):
             quarter = phase ^ moved
@@ -562,7 +600,7 @@
     )(where, summed1, patch0, head, vector[None, :], expand_four, matches, *filters)
 
 
-def gather_filters(filters, phase_id, phases, dp_count):
+def gather_filters(filters, phase_id, held, phases, dp_count):
     axes = ("phase", "dp")
     chips = dp_count // 2
 
@@ -592,15 +630,21 @@
     quarters = filters.reshape(levels, phases, part, channels)
     swapped = swap(filters)
     gathered = []
-    for group in GROUPS:
+    for n, group in enumerate(GROUPS):
+        if n == 0:
+            source, chosen = quarters, phase_id
+        else:
+            source, chosen = filters, held
         own = lax.dynamic_slice(
-            quarters, (group[0], phase_id, 0, 0), (len(group), 1, part, channels)
+            source, (group[0], chosen, 0, 0), (len(group), 1) + source.shape[2:]
         )[:, 0]
         far = across(own, 2)
         near = across(own, 1)
         column = stack([far, near, across(far, 1)])
         one = first(column)
-        pieces = [column, one, second(column), second(one)]
+        pieces = [column, one]
+        if n == 0:
+            pieces += [second(column), second(one)]
         gathered.append(pieces + [swap(v) for v in pieces])
     return [filters, swapped], gathered
 
@@ -625,14 +669,14 @@
     plan = Plan(phases, project_weight.shape[2])
     phase_id = lax.axis_index("phase")
     dp_id = lax.axis_index("dp")
-    where = jnp.stack([phase_id, dp_id % 2, dp_id // 2]).astype(jnp.int32)
+    held = (phase_id >> (dp_id & 1)) & 1
+    where = jnp.stack([phase_id, dp_id & 1, dp_id >> 1]).astype(jnp.int32)
     slots = phase_id * dp_count * SLOT_DEV + jnp.arange(dp_count * SLOT_DEV, dtype=jnp.int32)
     targets = lax.dynamic_slice(tile_slot, (dp_id, phase_id, 0), (1, 1, TILES_DEV))
     matches = (slots.reshape(dp_count, SLOT_DEV, 1) == targets).astype(F32)
-    where, matches = lax.optimization_barrier((where, matches))
-    phase_id = where[0]
+    where, matches, phase_id, held = lax.optimization_barrier((where, matches, phase_id, held))
     if by_permutes(phases, dp_count):
-        base, gathered = gather_filters(refine_filters, phase_id, phases, dp_count)
+        base, gathered = gather_filters(refine_filters, phase_id, held, phases, dp_count)
         upper, finer = base + gathered[0], base + gathered[1]
     else:
         upper = finer = [lax.all_gather(refine_filters, "dp", axis=2, tiled=True)]

time: 91.2 us -> 107 us (1.17)
  waiting for transfers between devices: 33.5 us -> 49.6 us
  local copies, waits for them, and re-layouts: 6.58 us -> 2.66 us
  Pallas kernels: 21.3 us -> 25.1 us
  starting transfers between devices: 19.8 us -> 18.6 us
    ppermute x21 -> x17, waiting for transfers between devices: 29.8 us -> 43.6 us  [move(): return lax.ppermute(value, axes, route)]
    unnamed x18 -> x16, local copies, waits for them, and re-layouts: 5.56 us -> 1.65 us
    pallas_call x1, Pallas kernels: 2.37 us -> 6.21 us  [project(): pl.pallas_call(functools.partial(project_kernel, plan, phases), in_specs=...]
    ppermute x3, waiting for transfers between devices: 3.74 us -> 5.99 us  [per_device(): lax.ppermute(sent[k], 'phase', [(s, s ^ k) for s in range(phases)])]
    ppermute x21 -> x17, starting transfers between devices: 16.2 us -> 15 us  [move(): return lax.ppermute(value, axes, route)]
  transfers between devices with their start and end apart: 25 -> 21, of which waited for: 9 -> 10; matrix products, arithmetic and copies ran while one was open for 0% -> 0% of each run, Pallas kernels for 8% -> 11%
where the time goes in v6:
time: 107 us; the launch traced here: 106 us
  waiting for transfers between devices  49.6 us (46%)
  Pallas kernels  25.1 us (23%)
  starting transfers between devices  18.6 us (17%)
  blocking collectives  8.99 us (8%)
  local copies, waits for them, and re-layouts  2.66 us (2%)
  other arithmetic  1.25 us (1%)
    ppermute x17, waiting for transfers between devices, move(): return lax.ppermute(value, axes, route)  43.6 us
    ppermute x17, starting transfers between devices, move(): return lax.ppermute(value, axes, route)  15 us
    pallas_call x1, Pallas kernels, fine(): pl.pallas_call(functools.partial(fine_kernel, plan), out_shape=jax.ShapeD...  13.7 us
    all_to_all x1, blocking collectives, per_device(): lax.all_to_all(partial, 'dp', split_axis=0, concat_axis=0, tiled=True)  8.99 us
    pallas_call x1, Pallas kernels, project(): pl.pallas_call(functools.partial(project_kernel, plan, phases), in_specs=...  6.21 us
    ppermute x3, waiting for transfers between devices, per_device(): lax.ppermute(sent[k], 'phase', [(s, s ^ k) for s in range(phases)])  5.99 us
    pallas_call x1, Pallas kernels, coarse(): pl.pallas_call(functools.partial(coarse_kernel, plan), out_shape=[jax.Sha...  5.09 us
    ppermute x3, starting transfers between devices, per_device(): lax.ppermute(sent[k], 'phase', [(s, s ^ k) for s in range(phases)])  3.55 us
  transfers between devices with their start and end apart: 21, of which 10 were waited for; matrix products, arithmetic and copies ran while one was open for 0% of the time, Pallas kernels for 11%

profile of v6, /device:TPU:0, one launch (start us, length us, event | category | flops | bytes accessed | tf_op | source)
XLA Modules:
  0.0 106.5 jit_solution(10081697674544384596)
XLA Ops:
  0.0 0.7 copy-done
  0.8 0.6 pad_add_fusion.where
  1.4 1.0 dynamic-slice_bitcast_fusion
  2.4 4.1 %collective-permute-start.15 = (bf16[2,288,256]{2,1,0:T(8,128)(2,1)S(1)}, bf16[2,288,256]{2,1,0:T(8,128)(2,1)S(1)}, u32[]{:S(2)}, u32[]{:S(2)}) collective-permute-start(bf16[2,288,256]{2,1,0:T(8,128)(2,1)S(1)} %dynamic-slice_bitcast_fusion), channel_id=1, source_target_pairs={{0,4},{1,5},{2,6},{3,7},{4,0},{5,1},{6,2},{7,3},{8,12},{9,13},{10,... | collective-permute-start | bytes 884744 | tf_op jit(solution)/shard_map/ppermute | solution.py:614
  6.5 1.6 %collective-permute-start.16 = (bf16[2,288,256]{2,1,0:T(8,128)(2,1)S(1)}, bf16[2,288,256]{2,1,0:T(8,128)(2,1)S(1)}, u32[]{:S(2)}, u32[]{:S(2)}) collective-permute-start(bf16[2,288,256]{2,1,0:T(8,128)(2,1)S(1)} %dynamic-slice_bitcast_fusion), channel_id=1, source_target_pairs={{0,2},{1,3},{2,0},{3,1},{4,6},{5,7},{6,4},{7,5},{8,10},{9,11},{10,... | collective-permute-start | bytes 884744 | tf_op jit(solution)/shard_map/ppermute | solution.py:614
  8.1 11.9 %collective-permute-done.15.refs_0_ = bf16[2,288,256]{2,1,0:T(8,128)(2,1)S(1)} collective-permute-done((bf16[2,288,256]{2,1,0:T(8,128)(2,1)S(1)}, bf16[2,288,256]{2,1,0:T(8,128)(2,1)S(1)}, u32[]{:S(2)}, u32[]{:S(2)}) %collective-permute-start.15) | collective-permute-done | bytes 294944 | tf_op jit(solution)/shard_map/ppermute | solution.py:614
  19.9 0.6 collective-permute-start.17
  20.5 6.2 %project.1 = (bf16[256,256]{1,0:T(8,128)(2,1)}, bf16[256,256]{1,0:T(8,128)(2,1)}, bf16[256,256]{1,0:T(8,128)(2,1)}, bf16[256,256]{1,0:T(8,128)(2,1)}) custom-call(s32[3]{0:T(128)} %pad_add_fusion.where, bf16[1,512,4096]{2,1,0:T(8,128)(2,1)} %tokens_hbm.1, bf16[1,4096,256]{2,1,0:T(8,128)(2,1)} %weight_hbm.1, bf16[1024,256]{1,0:T(8,128)(2,1)} %shrink_hbm.1), custom_call_target="tpu_custom_call" | custom-call | flops 1073741824 | bytes 6291456 | tf_op jit(solution)/shard_map/project/pallas_call | solution.py:138
  26.8 1.6 %collective-permute-start = (bf16[256,256]{1,0:T(8,128)(2,1)}, bf16[256,256]{1,0:T(8,128)(2,1)S(1)}, u32[]{:S(2)}, u32[]{:S(2)}) collective-permute-start(bf16[256,256]{1,0:T(8,128)(2,1)} %get-tuple-element.17), channel_id=1, source_target_pairs={{0,8},{8,0},{16,24},{24,16},{1,9},{9,1},{17,25},{25,17},{2,10},{10... | collective-permute-start | bytes 393224 | tf_op jit(solution)/shard_map/ppermute | solution.py:686
  28.3 1.3 %collective-permute-start.1 = (bf16[256,256]{1,0:T(8,128)(2,1)}, bf16[256,256]{1,0:T(8,128)(2,1)S(1)}, u32[]{:S(2)}, u32[]{:S(2)}) collective-permute-start(bf16[256,256]{1,0:T(8,128)(2,1)} %get-tuple-element.18), channel_id=1, source_target_pairs={{0,16},{8,24},{16,0},{24,8},{1,17},{9,25},{17,1},{25,9},{2,18},{10... | collective-permute-start | bytes 393224 | tf_op jit(solution)/shard_map/ppermute | solution.py:686
  29.7 0.7 collective-permute-start.2
  30.3 2.3 %collective-permute-done.refs_1_ = bf16[256,256]{1,0:T(8,128)(2,1)S(1)} collective-permute-done((bf16[256,256]{1,0:T(8,128)(2,1)}, bf16[256,256]{1,0:T(8,128)(2,1)S(1)}, u32[]{:S(2)}, u32[]{:S(2)}) %collective-permute-start) | collective-permute-done | bytes 131104 | tf_op jit(solution)/shard_map/ppermute | solution.py:686
  32.6 3.7 %collective-permute-done.1.refs_2_ = bf16[256,256]{1,0:T(8,128)(2,1)S(1)} collective-permute-done((bf16[256,256]{1,0:T(8,128)(2,1)}, bf16[256,256]{1,0:T(8,128)(2,1)S(1)}, u32[]{:S(2)}, u32[]{:S(2)}) %collective-permute-start.1) | collective-permute-done | bytes 131104 | tf_op jit(solution)/shard_map/ppermute | solution.py:686
  36.3 0.9 copy-done.3
  37.4 3.4 %collective-permute-start.5 = (bf16[2,144,256]{2,1,0:T(8,128)(2,1)S(1)}, bf16[2,144,256]{2,1,0:T(8,128)(2,1)S(1)}, u32[]{:S(2)}, u32[]{:S(2)}) collective-permute-start(bf16[2,144,256]{2,1,0:T(8,128)(2,1)S(1)} %dynamic-slice_bitcast_fusion.1), channel_id=1, source_target_pairs={{0,4},{1,5},{2,6},{3,7},{4,0},{5,1},{6,2},{7,3},{8,12},{9,13},{10,... | collective-permute-start | bytes 442376 | tf_op jit(solution)/shard_map/ppermute | solution.py:614
  40.9 1.0 collective-permute-start.18
  42.2 6.2 %collective-permute-done.5.refs_0_ = bf16[2,144,256]{2,1,0:T(8,128)(2,1)S(1)} collective-permute-done((bf16[2,144,256]{2,1,0:T(8,128)(2,1)S(1)}, bf16[2,144,256]{2,1,0:T(8,128)(2,1)S(1)}, u32[]{:S(2)}, u32[]{:S(2)}) %collective-permute-start.5) | collective-permute-done | bytes 147488 | tf_op jit(solution)/shard_map/ppermute | solution.py:614
  48.4 2.6 %collective-permute-done.6.refs_1_ = bf16[2,144,256]{2,1,0:T(8,128)(2,1)S(1)} collective-permute-done((bf16[2,144,256]{2,1,0:T(8,128)(2,1)S(1)}, bf16[2,144,256]{2,1,0:T(8,128)(2,1)S(1)}, u32[]{:S(2)}, u32[]{:S(2)}) %collective-permute-start.6) | collective-permute-done | bytes 147488 | tf_op jit(solution)/shard_map/ppermute | solution.py:614
  50.9 3.2 %collective-permute-done.7.refs_2_ = bf16[2,144,256]{2,1,0:T(8,128)(2,1)S(1)} collective-permute-done((bf16[2,144,256]{2,1,0:T(8,128)(2,1)S(1)}, bf16[2,144,256]{2,1,0:T(8,128)(2,1)S(1)}, u32[]{:S(2)}, u32[]{:S(2)}) %collective-permute-start.7) | collective-permute-done | bytes 147488 | tf_op jit(solution)/shard_map/ppermute | solution.py:614
  54.2 0.9 collective-permute-start.8
  55.2 1.0 collective-permute-start.9
  56.2 0.5 collective-permute-start.11
  56.7 10.6 %collective-permute-done.8.refs_3_ = bf16[3,2,144,256]{3,2,1,0:T(8,128)(2,1)S(1)} collective-permute-done((bf16[3,2,144,256]{3,2,1,0:T(8,128)(2,1)S(1)}, bf16[3,2,144,256]{3,2,1,0:T(8,128)(2,1)S(1)}, u32[]{:S(2)}, u32[]{:S(2)}) %collective-permute-start.8) | collective-permute-done | bytes 442400 | tf_op jit(solution)/shard_map/ppermute | solution.py:614
  67.7 0.5 collective-permute-start.19
  68.3 7.3 %collective-permute-done.10.refs_5_ = bf16[3,2,144,256]{3,2,1,0:T(8,128)(2,1)S(1)} collective-permute-done((bf16[3,2,144,256]{3,2,1,0:T(8,128)(2,1)S(1)}, bf16[3,2,144,256]{3,2,1,0:T(8,128)(2,1)S(1)}, u32[]{:S(2)}, u32[]{:S(2)}) %collective-permute-start.10) | collective-permute-done | bytes 442400 | tf_op jit(solution)/shard_map/ppermute | solution.py:614
  75.6 0.5 collective-permute-start.14
  76.1 1.3 %collective-permute-done.13.refs_8_ = bf16[3,2,144,256]{3,2,1,0:T(8,128)(2,1)S(1)} collective-permute-done((bf16[3,2,144,256]{3,2,1,0:T(8,128)(2,1)S(1)}, bf16[3,2,144,256]{3,2,1,0:T(8,128)(2,1)S(1)}, u32[]{:S(2)}, u32[]{:S(2)}) %collective-permute-start.13) | collective-permute-done | bytes 442400 | tf_op jit(solution)/shard_map/ppermute | solution.py:614
  77.4 0.6 collective-permute-done.14.refs_9_
  78.0 5.1 %coarse.1 = (f32[2,12,2,48,128]{4,3,2,1,0:T(8,128)S(1)}, bf16[240,256]{1,0:T(8,128)(2,1)S(1)}) custom-call(s32[3]{0:T(128)S(1)} %copy-done.4, bf16[4,256,256]{2,1,0:T(8,128)(2,1)S(1)} %stack.19.mine, bf16[4,256,256]{2,1,0:T(8,128)(2,1)S(1)} %collective-permute-done.3.other, bf16[256,1024]{1,0:T(8,128)(2,1)S(1)} %copy-done.2, ...), custom_call_target="tpu_custom_call" | custom-call | flops 2000000000 | bytes 8000000 | tf_op jit(solution)/shard_map/coarse/pallas_call | solution.py:410
  83.2 13.7 %fine.1 = f32[8,6,256]{2,1,0:T(8,128)S(1)} custom-call(s32[3]{0:T(128)S(1)} %copy-done.4, f32[2,12,2,48,128]{4,3,2,1,0:T(8,128)S(1)} %get-tuple-element.21.summed1, bf16[240,256]{1,0:T(8,128)(2,1)S(1)} %get-tuple-element.22.patch0, bf16[256,128]{1,0:T(8,128)(2,1)S(1)} %copy-done.6, f32[1,128]{1,0:T(1,128)S(1)} %bitcast.14, bf16[256,4096]{1,0:T(8,128)(2,1)S(1)} %copy-done.5, ...), custom_call_target="tpu_custom_call" | custom-call | flops 8000000000 | bytes 10000000 | tf_op jit(solution)/shard_map/fine/pallas_call | solution.py:580
  96.9 9.0 %all_to_all.5 = f32[8,6,256]{2,1,0:T(8,128)S(1)} all-to-all(f32[8,6,256]{2,1,0:T(8,128)S(1)} %fine.1), channel_id=1, replica_groups=mesh['phase'=4,'dp'=8] {'dp'}, dimensions={0} | all-to-all | bytes 98304 | tf_op jit(solution)/shard_map/all_to_all | solution.py:693
  105.9 0.6 reduce_sum.9
  (40 shorter events, 1.1 us)
Async XLA Ops:
  0.0 0.7 copy-start
  2.3 35.0 %copy-start.1 = (bf16[4,2,288,256]{3,2,1,0:T(8,128)(2,1)S(1)}, bf16[4,2,288,256]{3,2,1,0:T(8,128)(2,1)}, u32[]{:S(2)}) copy-start(bf16[4,2,288,256]{3,2,1,0:T(8,128)(2,1)} %refs_0_.3) | copy-start | bytes 3538948
  2.4 17.6 %collective-permute-start.15 = (bf16[2,288,256]{2,1,0:T(8,128)(2,1)S(1)}, bf16[2,288,256]{2,1,0:T(8,128)(2,1)S(1)}, u32[]{:S(2)}, u32[]{:S(2)}) collective-permute-start(bf16[2,288,256]{2,1,0:T(8,128)(2,1)S(1)} %dynamic-slice_bitcast_fusion), channel_id=1, source_target_pairs={{0,4},{1,5},{2,6},{3,7},{4,0},{5,1},{6,2},{7,3},{8,12},{9,13},{10,... | collective-permute-start | bytes 884744 | tf_op jit(solution)/shard_map/ppermute | solution.py:614
  6.5 34.3 %collective-permute-start.16 = (bf16[2,288,256]{2,1,0:T(8,128)(2,1)S(1)}, bf16[2,288,256]{2,1,0:T(8,128)(2,1)S(1)}, u32[]{:S(2)}, u32[]{:S(2)}) collective-permute-start(bf16[2,288,256]{2,1,0:T(8,128)(2,1)S(1)} %dynamic-slice_bitcast_fusion), channel_id=1, source_target_pairs={{0,2},{1,3},{2,0},{3,1},{4,6},{5,7},{6,4},{7,5},{8,10},{9,11},{10,... | collective-permute-start | bytes 884744 | tf_op jit(solution)/shard_map/ppermute | solution.py:614
  19.9 20.9 %collective-permute-start.17 = (bf16[2,288,256]{2,1,0:T(8,128)(2,1)S(1)}, bf16[2,288,256]{2,1,0:T(8,128)(2,1)S(1)}, u32[]{:S(2)}, u32[]{:S(2)}) collective-permute-start(bf16[2,288,256]{2,1,0:T(8,128)(2,1)S(1)} %collective-permute-done.15.refs_0_), channel_id=1, source_target_pairs={{0,2},{1,3},{2,0},{3,1},{4,6},{5,7},{6,4},{7,5},{8,10},{9,11},{10,... | collective-permute-start | bytes 884744 | tf_op jit(solution)/shard_map/ppermute | solution.py:614
  26.8 5.8 %collective-permute-start = (bf16[256,256]{1,0:T(8,128)(2,1)}, bf16[256,256]{1,0:T(8,128)(2,1)S(1)}, u32[]{:S(2)}, u32[]{:S(2)}) collective-permute-start(bf16[256,256]{1,0:T(8,128)(2,1)} %get-tuple-element.17), channel_id=1, source_target_pairs={{0,8},{8,0},{16,24},{24,16},{1,9},{9,1},{17,25},{25,17},{2,10},{10... | collective-permute-start | bytes 393224 | tf_op jit(solution)/shard_map/ppermute | solution.py:686
  28.3 8.0 %collective-permute-start.1 = (bf16[256,256]{1,0:T(8,128)(2,1)}, bf16[256,256]{1,0:T(8,128)(2,1)S(1)}, u32[]{:S(2)}, u32[]{:S(2)}) collective-permute-start(bf16[256,256]{1,0:T(8,128)(2,1)} %get-tuple-element.18), channel_id=1, source_target_pairs={{0,16},{8,24},{16,0},{24,8},{1,17},{9,25},{17,1},{25,9},{2,18},{10... | collective-permute-start | bytes 393224 | tf_op jit(solution)/shard_map/ppermute | solution.py:686
  29.7 6.6 %collective-permute-start.2 = (bf16[256,256]{1,0:T(8,128)(2,1)}, bf16[256,256]{1,0:T(8,128)(2,1)S(1)}, u32[]{:S(2)}, u32[]{:S(2)}) collective-permute-start(bf16[256,256]{1,0:T(8,128)(2,1)} %get-tuple-element.19), channel_id=1, source_target_pairs={{0,24},{8,16},{16,8},{24,0},{1,25},{9,17},{17,9},{25,1},{2,26},{10... | collective-permute-start | bytes 393224 | tf_op jit(solution)/shard_map/ppermute | solution.py:686
  36.3 0.9 copy-start.3
  37.2 18.9 %collective-permute-start.3 = (bf16[4,256,256]{2,1,0:T(8,128)(2,1)S(1)}, bf16[4,256,256]{2,1,0:T(8,128)(2,1)S(1)}, u32[]{:S(2)}, u32[]{:S(2)}) collective-permute-start(bf16[4,256,256]{2,1,0:T(8,128)(2,1)S(1)} %stack.19.mine), channel_id=1, source_target_pairs={{0,1},{1,0},{2,3},{3,2},{4,5},{5,4},{6,7},{7,6},{8,9},{9,8},{10,11... | collective-permute-start | bytes 1572872 | tf_op jit(solution)/shard_map/ppermute | solution.py:688
  37.4 40.6 %copy-start.2 = (bf16[256,1024]{1,0:T(8,128)(2,1)S(1)}, bf16[256,1024]{1,0:T(8,128)(2,1)}, u32[]{:S(2)}) copy-start(bf16[256,1024]{1,0:T(8,128)(2,1)} %expand_two.1) | copy-start | bytes 1572868
  37.4 40.6 %copy-start.4 = (s32[3]{0:T(128)S(1)}, s32[3]{0:T(128)}, u32[]{:S(2)}) copy-start(s32[3]{0:T(128)} %pad_add_fusion.where) | copy-start | bytes 40
  37.4 11.0 %collective-permute-start.5 = (bf16[2,144,256]{2,1,0:T(8,128)(2,1)S(1)}, bf16[2,144,256]{2,1,0:T(8,128)(2,1)S(1)}, u32[]{:S(2)}, u32[]{:S(2)}) collective-permute-start(bf16[2,144,256]{2,1,0:T(8,128)(2,1)S(1)} %dynamic-slice_bitcast_fusion.1), channel_id=1, source_target_pairs={{0,4},{1,5},{2,6},{3,7},{4,0},{5,1},{6,2},{7,3},{8,12},{9,13},{10,... | collective-permute-start | bytes 442376 | tf_op jit(solution)/shard_map/ppermute | solution.py:614
  40.9 27.3 %collective-permute-start.18 = (bf16[3,2,288,256]{3,2,1,0:T(8,128)(2,1)S(1)}, bf16[3,2,288,256]{3,2,1,0:T(8,128)(2,1)S(1)}, u32[]{:S(2)}, u32[]{:S(2)}) collective-permute-start(bf16[3,2,288,256]{3,2,1,0:T(8,128)(2,1)S(1)} %stack.21.refs_2_), channel_id=1, source_target_pairs={{0,8},{1,17},{2,10},{3,19},{4,12},{5,21},{6,14},{7,23},{8,0},{9,25... | collective-permute-start | bytes 2654216 | tf_op jit(solution)/shard_map/ppermute | solution.py:614
  41.9 9.0 %collective-permute-start.6 = (bf16[2,144,256]{2,1,0:T(8,128)(2,1)S(1)}, bf16[2,144,256]{2,1,0:T(8,128)(2,1)S(1)}, u32[]{:S(2)}, u32[]{:S(2)}) collective-permute-start(bf16[2,144,256]{2,1,0:T(8,128)(2,1)S(1)} %dynamic-slice_bitcast_fusion.1), channel_id=1, source_target_pairs={{0,2},{1,3},{2,0},{3,1},{4,6},{5,7},{6,4},{7,5},{8,10},{9,11},{10,... | collective-permute-start | bytes 442376 | tf_op jit(solution)/shard_map/ppermute | solution.py:614
  48.4 5.8 %collective-permute-start.7 = (bf16[2,144,256]{2,1,0:T(8,128)(2,1)S(1)}, bf16[2,144,256]{2,1,0:T(8,128)(2,1)S(1)}, u32[]{:S(2)}, u32[]{:S(2)}) collective-permute-start(bf16[2,144,256]{2,1,0:T(8,128)(2,1)S(1)} %collective-permute-done.5.refs_0_), channel_id=1, source_target_pairs={{0,2},{1,3},{2,0},{3,1},{4,6},{5,7},{6,4},{7,5},{8,10},{9,11},{10,... | collective-permute-start | bytes 442376 | tf_op jit(solution)/shard_map/ppermute | solution.py:614
  54.2 28.9 %copy-start.5 = (bf16[256,4096]{1,0:T(8,128)(2,1)S(1)}, bf16[256,4096]{1,0:T(8,128)(2,1)}, u32[]{:S(2)}) copy-start(bf16[256,4096]{1,0:T(8,128)(2,1)} %expand_four.1) | copy-start | bytes 6291460
  54.2 28.9 %copy-start.6 = (bf16[256,128]{1,0:T(8,128)(2,1)S(1)}, bf16[256,128]{1,0:T(8,128)(2,1)}, u32[]{:S(2)}) copy-start(bf16[256,128]{1,0:T(8,128)(2,1)} %head.1) | copy-start | bytes 196612
  54.2 28.9 %copy-start.7 = (f32[128]{0:T(128)S(1)}, f32[128]{0:T(128)}, u32[]{:S(2)}) copy-start(f32[128]{0:T(128)} %param.16) | copy-start | bytes 1540
  54.2 13.0 %collective-permute-start.8 = (bf16[3,2,144,256]{3,2,1,0:T(8,128)(2,1)S(1)}, bf16[3,2,144,256]{3,2,1,0:T(8,128)(2,1)S(1)}, u32[]{:S(2)}, u32[]{:S(2)}) collective-permute-start(bf16[3,2,144,256]{3,2,1,0:T(8,128)(2,1)S(1)} %stack.20.refs_2_), channel_id=1, source_target_pairs={{0,8},{1,17},{2,10},{3,19},{4,12},{5,21},{6,14},{7,23},{8,0},{9,25... | collective-permute-start | bytes 1327112 | tf_op jit(solution)/shard_map/ppermute | solution.py:614
  55.2 12.5 %collective-permute-start.9 = (bf16[3,2,144,256]{3,2,1,0:T(8,128)(2,1)S(1)}, bf16[3,2,144,256]{3,2,1,0:T(8,128)(2,1)S(1)}, u32[]{:S(2)}, u32[]{:S(2)}) collective-permute-start(bf16[3,2,144,256]{3,2,1,0:T(8,128)(2,1)S(1)} %stack.20.refs_2_), channel_id=1, source_target_pairs={{0,16},{1,9},{2,18},{3,11},{4,20},{5,13},{6,22},{7,15},{8,24},{9,1... | collective-permute-start | bytes 1327112 | tf_op jit(solution)/shard_map/ppermute | solution.py:614
  56.2 21.2 %collective-permute-start.4 = (bf16[4,2,288,256]{3,2,1,0:T(8,128)(2,1)S(1)}, bf16[4,2,288,256]{3,2,1,0:T(8,128)(2,1)S(1)}, u32[]{:S(2)}, u32[]{:S(2)}) collective-permute-start(bf16[4,2,288,256]{3,2,1,0:T(8,128)(2,1)S(1)} %copy-done.1), channel_id=1, source_target_pairs={{0,1},{1,0},{2,3},{3,2},{4,5},{5,4},{6,7},{7,6},{8,9},{9,8},{10,11... | collective-permute-start | bytes 3538952 | tf_op jit(solution)/shard_map/ppermute | solution.py:614
  56.2 11.5 %collective-permute-start.11 = (bf16[3,2,144,256]{3,2,1,0:T(8,128)(2,1)S(1)}, bf16[3,2,144,256]{3,2,1,0:T(8,128)(2,1)S(1)}, u32[]{:S(2)}, u32[]{:S(2)}) collective-permute-start(bf16[3,2,144,256]{3,2,1,0:T(8,128)(2,1)S(1)} %stack.20.refs_2_), channel_id=1, source_target_pairs={{0,1},{1,0},{2,3},{3,2},{4,5},{5,4},{6,7},{7,6},{8,9},{9,8},{10,11... | collective-permute-start | bytes 1327112 | tf_op jit(solution)/shard_map/ppermute | solution.py:614
  67.3 8.3 %collective-permute-start.10 = (bf16[3,2,144,256]{3,2,1,0:T(8,128)(2,1)S(1)}, bf16[3,2,144,256]{3,2,1,0:T(8,128)(2,1)S(1)}, u32[]{:S(2)}, u32[]{:S(2)}) collective-permute-start(bf16[3,2,144,256]{3,2,1,0:T(8,128)(2,1)S(1)} %collective-permute-done.8.refs_3_), channel_id=1, source_target_pairs={{0,16},{1,9},{2,18},{3,11},{4,20},{5,13},{6,22},{7,15},{8,24},{9,1... | collective-permute-start | bytes 1327112 | tf_op jit(solution)/shard_map/ppermute | solution.py:614
  67.7 7.9 %collective-permute-start.12 = (bf16[3,2,144,256]{3,2,1,0:T(8,128)(2,1)S(1)}, bf16[3,2,144,256]{3,2,1,0:T(8,128)(2,1)S(1)}, u32[]{:S(2)}, u32[]{:S(2)}) collective-permute-start(bf16[3,2,144,256]{3,2,1,0:T(8,128)(2,1)S(1)} %collective-permute-done.8.refs_3_), channel_id=1, source_target_pairs={{0,1},{1,0},{2,3},{3,2},{4,5},{5,4},{6,7},{7,6},{8,9},{9,8},{10,11... | collective-permute-start | bytes 1327112 | tf_op jit(solution)/shard_map/ppermute | solution.py:614
  67.7 15.4 %collective-permute-start.19 = (bf16[3,2,288,256]{3,2,1,0:T(8,128)(2,1)S(1)}, bf16[3,2,288,256]{3,2,1,0:T(8,128)(2,1)S(1)}, u32[]{:S(2)}, u32[]{:S(2)}) collective-permute-start(bf16[3,2,288,256]{3,2,1,0:T(8,128)(2,1)S(1)} %stack.21.refs_2_), channel_id=1, source_target_pairs={{0,1},{1,0},{2,3},{3,2},{4,5},{5,4},{6,7},{7,6},{8,9},{9,8},{10,11... | collective-permute-start | bytes 2654216 | tf_op jit(solution)/shard_map/ppermute | solution.py:614
  68.2 14.9 %collective-permute-start.20 = (bf16[3,2,288,256]{3,2,1,0:T(8,128)(2,1)S(1)}, bf16[3,2,288,256]{3,2,1,0:T(8,128)(2,1)S(1)}, u32[]{:S(2)}, u32[]{:S(2)}) collective-permute-start(bf16[3,2,288,256]{3,2,1,0:T(8,128)(2,1)S(1)} %collective-permute-done.18.refs_3_), channel_id=1, source_target_pairs={{0,1},{1,0},{2,3},{3,2},{4,5},{5,4},{6,7},{7,6},{8,9},{9,8},{10,11... | collective-permute-start | bytes 2654216 | tf_op jit(solution)/shard_map/ppermute | solution.py:614
  75.6 1.8 %collective-permute-start.13 = (bf16[3,2,144,256]{3,2,1,0:T(8,128)(2,1)S(1)}, bf16[3,2,144,256]{3,2,1,0:T(8,128)(2,1)S(1)}, u32[]{:S(2)}, u32[]{:S(2)}) collective-permute-start(bf16[3,2,144,256]{3,2,1,0:T(8,128)(2,1)S(1)} %collective-permute-done.9.refs_4_), channel_id=1, source_target_pairs={{0,1},{1,0},{2,3},{3,2},{4,5},{5,4},{6,7},{7,6},{8,9},{9,8},{10,11... | collective-permute-start | bytes 1327112 | tf_op jit(solution)/shard_map/ppermute | solution.py:614
  75.6 2.4 %collective-permute-start.14 = (bf16[3,2,144,256]{3,2,1,0:T(8,128)(2,1)S(1)}, bf16[3,2,144,256]{3,2,1,0:T(8,128)(2,1)S(1)}, u32[]{:S(2)}, u32[]{:S(2)}) collective-permute-start(bf16[3,2,144,256]{3,2,1,0:T(8,128)(2,1)S(1)} %collective-permute-done.10.refs_5_), channel_id=1, source_target_pairs={{0,1},{1,0},{2,3},{3,2},{4,5},{5,4},{6,7},{7,6},{8,9},{9,8},{10,11... | collective-permute-start | bytes 1327112 | tf_op jit(solution)/shard_map/ppermute | solution.py:614

commit v7 on v6

--- a/solution.py
+++ b/solution.py
@@ -17,7 +17,8 @@
 PROJECT_VMEM = 60 * 1024 * 1024
 PROJECT_STEPS = 8
 COARSE_VMEM = 12 * 1024 * 1024
-FINE_VMEM = 32 * 1024 * 1024
+MIDDLE_VMEM = 20 * 1024 * 1024
+FINE_VMEM = 24 * 1024 * 1024
 
 
 LANES = 128
@@ -37,7 +38,7 @@
 
 
 CHIP_ORDER = (2, 1, 3)
-GROUPS = ((2, 3), (0, 1))
+GROUPS = ((2, 3), (1,), (0,))
 
 
 class Plan:
@@ -436,31 +437,17 @@
     )(where, mine, other, expand_two, *filters)
 
 
-FINE_SCRATCH = 12
-
-
-def fine_kernel(plan, where, summed1, patch0, head, vector, expand_four, matches, *refs):
-    count = len(refs) - FINE_SCRATCH
+MIDDLE_SCRATCH = 6
+
+
+def middle_kernel(plan, where, summed1, patch0, expand_four, *refs):
+    count = len(refs) - MIDDLE_SCRATCH
     filters = refs[:count]
-    (
-        portions,
-        weight1,
-        weight0,
-        sems,
-        joined1,
-        map0,
-        first1,
-        second1,
-        first,
-        second,
-        by_col,
-        by_row,
-    ) = refs[count:]
+    summed0, weight1, sems, joined1, first1, second1 = refs[count:]
     ch = plan.ch
-    phase, side = where[0], where[1]
-    for level, weights in ((1, weight1), (0, weight0)):
-        start_filters(filters, level, weights, sems.at[level])
-        lay_filters(plan, where, filters, level, weights)
+    phase = where[0]
+    start_filters(filters, 1, weight1, sems)
+    lay_filters(plan, where, filters, 1, weight1)
 
     off0 = 2 * (plan.start0(phase) - plan.start1(phase))
 
@@ -477,7 +464,7 @@
 
     refine(
         source1,
-        lambda m: wait_filters(filters, weight1, sems.at[1], m),
+        lambda m: wait_filters(filters, weight1, sems, m),
         weight1,
         first1,
         second1,
@@ -496,13 +483,49 @@
                 joined1, slice(None), b // 2, pl.ds(a // 2, plan.rows1, stride=2), slice(None)
             )
             put(
-                map0,
+                summed0,
                 grown.reshape(plan.cols0, plan.rows1, ch) + below,
                 slice(None),
                 b,
                 pl.ds(a, plan.rows1, stride=4),
                 slice(None),
             )
+
+
+def middle(plan, where, summed1, patch0, expand_four, filters):
+    ch = plan.ch
+    vmem = pl.BlockSpec(memory_space=pltpu.VMEM)
+    slabs = ch // LANES
+    return pl.pallas_call(
+        functools.partial(middle_kernel, plan),
+        out_shape=jax.ShapeDtypeStruct((slabs, plan.cols0, 4, 4 * plan.rows1, LANES), F32),
+        in_specs=[pl.BlockSpec(memory_space=pltpu.SMEM)] + [vmem] * 3 + filter_specs(filters),
+        out_specs=vmem,
+        scratch_shapes=[
+            pltpu.VMEM((2, 9 * ch, ch), BF16),
+            pltpu.SemaphoreType.DMA((2,)),
+            pltpu.VMEM((slabs, plan.cols0, 2, 2 * plan.rows1, LANES), F32),
+        ]
+        + shifted_maps(2 * plan.cols1, 2 * plan.rows1, ch),
+        compiler_params=pltpu.CompilerParams(vmem_limit_bytes=MIDDLE_VMEM),
+        cost_estimate=pl.CostEstimate(
+            flops=3_000_000_000, bytes_accessed=6_000_000, transcendentals=0
+        ),
+        name="middle",
+    )(where, summed1, patch0, expand_four, *filters)
+
+
+FINE_SCRATCH = 7
+
+
+def fine_kernel(plan, where, map0, head, vector, matches, *refs):
+    count = len(refs) - FINE_SCRATCH
+    filters = refs[:count]
+    portions, weight0, sems, first, second, by_col, by_row = refs[count:]
+    ch = plan.ch
+    phase, side = where[0], where[1]
+    start_filters(filters, 0, weight0, sems)
+    lay_filters(plan, where, filters, 0, weight0)
     cols, rows, own_rows = plan.conv_cols, plan.conv_rows, 4 * plan.half
     own0 = 4 * (phase * plan.block - plan.start0(phase))
     conv0 = jnp.clip(own0 - 2, 0, 4 * plan.cols0 - cols)
@@ -518,7 +541,7 @@
     clear_edges(first)
     clear_edges(second)
     loop(9, lambda i: put_shifted(first, i * 4, source0(i * 4, 4, row, rows)))
-    wait_filters(filters, weight0, sems.at[0], 0)
+    wait_filters(filters, weight0, sems, 0)
 
     def inner(i):
         put_shifted(
@@ -526,7 +549,7 @@
         )
 
     loop(cols // chunk, inner)
-    wait_filters(filters, weight0, sems.at[0], 1)
+    wait_filters(filters, weight0, sems, 1)
     half_cols = 2 * plan.block
     hidden_size = head.shape[1]
     scale = jnp.broadcast_to(vector[...], (hidden_size, hidden_size)).T[:, :1]
@@ -571,33 +594,24 @@
         add_tiles(d)
 
 
-def fine(plan, where, summed1, patch0, head, vector, expand_four, matches, filters):
+def fine(plan, where, summed0, head, vector, matches, filters):
     ch = plan.ch
     vmem = pl.BlockSpec(memory_space=pltpu.VMEM)
-    slabs = ch // LANES
     pixels = 16 * plan.block * plan.half // TILES_DEV
-    weights = pltpu.VMEM((2, 9 * ch, ch), BF16)
     return pl.pallas_call(
         functools.partial(fine_kernel, plan),
         out_shape=jax.ShapeDtypeStruct(matches.shape[:2] + (pixels,), F32),
-        in_specs=[pl.BlockSpec(memory_space=pltpu.SMEM)] + [vmem] * 6 + filter_specs(filters),
+        in_specs=[pl.BlockSpec(memory_space=pltpu.SMEM)] + [vmem] * 4 + filter_specs(filters),
         out_specs=vmem,
-        scratch_shapes=[
-            weights,
-            weights,
-            pltpu.SemaphoreType.DMA((LEVELS, 2)),
-            pltpu.VMEM((slabs, plan.cols0, 2, 2 * plan.rows1, LANES), F32),
-            pltpu.VMEM((slabs, plan.cols0, 4, 4 * plan.rows1, LANES), F32),
-        ]
-        + shifted_maps(2 * plan.cols1, 2 * plan.rows1, ch)
+        scratch_shapes=[pltpu.VMEM((2, 9 * ch, ch), BF16), pltpu.SemaphoreType.DMA((2,))]
         + shifted_maps(plan.conv_cols, plan.conv_rows, ch)
         + [pltpu.VMEM((LANES, LANES), F32)] * 2,
         compiler_params=pltpu.CompilerParams(vmem_limit_bytes=FINE_VMEM),
         cost_estimate=pl.CostEstimate(
-            flops=8_000_000_000, bytes_accessed=10_000_000, transcendentals=0
+            flops=6_000_000_000, bytes_accessed=8_000_000, transcendentals=0
         ),
         name="fine",
-    )(where, summed1, patch0, head, vector[None, :], expand_four, matches, *filters)
+    )(where, summed0, head, vector[None, :], matches, *filters)
 
 
 def gather_filters(filters, phase_id, held, phases, dp_count):
@@ -674,12 +688,11 @@
     slots = phase_id * dp_count * SLOT_DEV + jnp.arange(dp_count * SLOT_DEV, dtype=jnp.int32)
     targets = lax.dynamic_slice(tile_slot, (dp_id, phase_id, 0), (1, 1, TILES_DEV))
     matches = (slots.reshape(dp_count, SLOT_DEV, 1) == targets).astype(F32)
-    where, matches, phase_id, held = lax.optimization_barrier((where, matches, phase_id, held))
     if by_permutes(phases, dp_count):
         base, gathered = gather_filters(refine_filters, phase_id, held, phases, dp_count)
-        upper, finer = base + gathered[0], base + gathered[1]
+        upper, medium, finer = (base + pieces for pieces in gathered)
     else:
-        upper = finer = [lax.all_gather(refine_filters, "dp", axis=2, tiled=True)]
+        upper = medium = finer = [lax.all_gather(refine_filters, "dp", axis=2, tiled=True)]
     sent = project(plan, phases, where, tap_tokens, project_weight, shrink_weight)
     arrived = [sent[0]]
     for k in range(1, phases):
@@ -687,9 +700,8 @@
     mine = stack(arrived)
     other = lax.ppermute(mine, "dp", [(d, d ^ 1) for d in range(dp_count)])
     summed1, patch0 = coarse(plan, where, mine, other, expand_two, upper)
-    partial = fine(
-        plan, where, summed1, patch0, head_matrix, head_vector, expand_four, matches, finer
-    )
+    summed0 = middle(plan, where, summed1, patch0, expand_four, medium)
+    partial = fine(plan, where, summed0, head_matrix, head_vector, matches, finer)
     portions = lax.all_to_all(partial, "dp", split_axis=0, concat_axis=0, tiled=True)
     return portions.sum(axis=0)
 

time: 107 us -> 96.9 us (0.906)
  waiting for transfers between devices: 49.6 us -> 26.3 us
  starting transfers between devices: 18.6 us -> 23.4 us
  Pallas kernels: 25.1 us -> 29.3 us
  local copies, waits for them, and re-layouts: 2.66 us -> 6.82 us
    ppermute x17 -> x23, waiting for transfers between devices: 43.6 us -> 22.6 us  [move(): return lax.ppermute(value, axes, route)]
    pallas_call x0 -> x1, Pallas kernels: none -> 5.74 us  [middle(): pl.pallas_call(functools.partial(middle_kernel, plan), out_shape=jax.Shap...]
    ppermute x17 -> x23, starting transfers between devices: 15 us -> 19.7 us  [move(): return lax.ppermute(value, axes, route)]
    unnamed x16 -> x28, local copies, waits for them, and re-layouts: 1.65 us -> 5.86 us
    pallas_call x1, Pallas kernels: 13.7 us -> 9.81 us  [fine(): pl.pallas_call(functools.partial(fine_kernel, plan), out_shape=jax.ShapeD...]
    ppermute x3, waiting for transfers between devices: 5.99 us -> 3.68 us  [per_device(): lax.ppermute(sent[k], 'phase', [(s, s ^ k) for s in range(phases)])]
    pallas_call x3 -> x4, Pallas kernels: 0.12 us -> 1.67 us  [stack(): pl.pallas_call(stack_kernel, out_shape=jax.ShapeDtypeStruct((len(values),...]
  transfers between devices with their start and end apart: 21 -> 27, of which waited for: 10 -> 11; matrix products, arithmetic and copies ran while one was open for 0% -> 1% of each run, Pallas kernels for 11% -> 20%
where the time goes in v7:
time: 96.9 us; the launch traced here: 96.5 us
  Pallas kernels  29.3 us (30%)
  waiting for transfers between devices  26.3 us (27%)
  starting transfers between devices  23.4 us (24%)
  blocking collectives  9.12 us (9%)
  local copies, waits for them, and re-layouts  6.82 us (7%)
  other arithmetic  1.33 us (1%)
    ppermute x23, waiting for transfers between devices, move(): return lax.ppermute(value, axes, route)  22.6 us
    ppermute x23, starting transfers between devices, move(): return lax.ppermute(value, axes, route)  19.7 us
    pallas_call x1, Pallas kernels, fine(): pl.pallas_call(functools.partial(fine_kernel, plan), out_shape=jax.ShapeD...  9.81 us
    all_to_all x1, blocking collectives, per_device(): lax.all_to_all(partial, 'dp', split_axis=0, concat_axis=0, tiled=True)  9.12 us
    pallas_call x1, Pallas kernels, project(): pl.pallas_call(functools.partial(project_kernel, plan, phases), in_specs=...  6.3 us
    unnamed x28, local copies, waits for them, and re-layouts  5.86 us
    pallas_call x1, Pallas kernels, coarse(): pl.pallas_call(functools.partial(coarse_kernel, plan), out_shape=[jax.Sha...  5.82 us
    pallas_call x1, Pallas kernels, middle(): pl.pallas_call(functools.partial(middle_kernel, plan), out_shape=jax.Shap...  5.74 us
  transfers between devices with their start and end apart: 27, of which 11 were waited for; matrix products, arithmetic and copies ran while one was open for 1% of the time, Pallas kernels for 20%

profile of v7, /device:TPU:0, one launch (start us, length us, event | category | flops | bytes accessed | tf_op | source)
XLA Modules:
  0.0 96.5 jit_solution(9455859822409981502)
XLA Ops:
  0.0 0.9 dynamic-slice_bitcast_fusion.2
  0.9 4.1 %collective-permute-start.5 = (bf16[2,144,256]{2,1,0:T(8,128)(2,1)S(1)}, bf16[2,144,256]{2,1,0:T(8,128)(2,1)S(1)}, u32[]{:S(2)}, u32[]{:S(2)}) collective-permute-start(bf16[2,144,256]{2,1,0:T(8,128)(2,1)S(1)} %dynamic-slice_bitcast_fusion.2), channel_id=1, source_target_pairs={{0,4},{1,5},{2,6},{3,7},{4,0},{5,1},{6,2},{7,3},{8,12},{9,13},{10,... | collective-permute-start | bytes 442376 | tf_op jit(solution)/shard_map/ppermute | solution.py:628
  5.7 6.3 %project.1 = (bf16[256,256]{1,0:T(8,128)(2,1)}, bf16[256,256]{1,0:T(8,128)(2,1)}, bf16[256,256]{1,0:T(8,128)(2,1)}, bf16[256,256]{1,0:T(8,128)(2,1)}) custom-call(s32[3]{0:T(128)} %pad_add_fusion.where, bf16[1,512,4096]{2,1,0:T(8,128)(2,1)} %tokens_hbm.1, bf16[1,4096,256]{2,1,0:T(8,128)(2,1)} %weight_hbm.1, bf16[1024,256]{1,0:T(8,128)(2,1)} %shrink_hbm.1), custom_call_target="tpu_custom_call" | custom-call | flops 1073741824 | bytes 6291456 | tf_op jit(solution)/shard_map/project/pallas_call | solution.py:139
  12.0 1.6 %collective-permute-start = (bf16[256,256]{1,0:T(8,128)(2,1)}, bf16[256,256]{1,0:T(8,128)(2,1)S(1)}, u32[]{:S(2)}, u32[]{:S(2)}) collective-permute-start(bf16[256,256]{1,0:T(8,128)(2,1)} %get-tuple-element.12), channel_id=1, source_target_pairs={{0,8},{8,0},{16,24},{24,16},{1,9},{9,1},{17,25},{25,17},{2,10},{10... | collective-permute-start | bytes 393224 | tf_op jit(solution)/shard_map/ppermute | solution.py:699
  13.6 1.6 %collective-permute-start.6 = (bf16[2,144,256]{2,1,0:T(8,128)(2,1)S(1)}, bf16[2,144,256]{2,1,0:T(8,128)(2,1)S(1)}, u32[]{:S(2)}, u32[]{:S(2)}) collective-permute-start(bf16[2,144,256]{2,1,0:T(8,128)(2,1)S(1)} %dynamic-slice_bitcast_fusion.2), channel_id=1, source_target_pairs={{0,2},{1,3},{2,0},{3,1},{4,6},{5,7},{6,4},{7,5},{8,10},{9,11},{10,... | collective-permute-start | bytes 442376 | tf_op jit(solution)/shard_map/ppermute | solution.py:628
  15.1 1.3 %collective-permute-start.1 = (bf16[256,256]{1,0:T(8,128)(2,1)}, bf16[256,256]{1,0:T(8,128)(2,1)S(1)}, u32[]{:S(2)}, u32[]{:S(2)}) collective-permute-start(bf16[256,256]{1,0:T(8,128)(2,1)} %get-tuple-element.13), channel_id=1, source_target_pairs={{0,16},{8,24},{16,0},{24,8},{1,17},{9,25},{17,1},{25,9},{2,18},{10... | collective-permute-start | bytes 393224 | tf_op jit(solution)/shard_map/ppermute | solution.py:699
  17.6 1.9 %collective-permute-start.7 = (bf16[2,144,256]{2,1,0:T(8,128)(2,1)S(1)}, bf16[2,144,256]{2,1,0:T(8,128)(2,1)S(1)}, u32[]{:S(2)}, u32[]{:S(2)}) collective-permute-start(bf16[2,144,256]{2,1,0:T(8,128)(2,1)S(1)} %collective-permute-done.5.refs_0_), channel_id=1, source_target_pairs={{0,2},{1,3},{2,0},{3,1},{4,6},{5,7},{6,4},{7,5},{8,10},{9,11},{10,... | collective-permute-start | bytes 442376 | tf_op jit(solution)/shard_map/ppermute | solution.py:628
  19.5 3.6 %collective-permute-done.1.refs_2_ = bf16[256,256]{1,0:T(8,128)(2,1)S(1)} collective-permute-done((bf16[256,256]{1,0:T(8,128)(2,1)}, bf16[256,256]{1,0:T(8,128)(2,1)S(1)}, u32[]{:S(2)}, u32[]{:S(2)}) %collective-permute-start.1) | collective-permute-done | bytes 131104 | tf_op jit(solution)/shard_map/ppermute | solution.py:699
  23.9 0.9 copy-done.10
  25.0 1.2 %collective-permute-done.15.refs_0_ = bf16[1,288,256]{2,1,0:T(8,128)(2,1)S(1)} collective-permute-done((bf16[1,288,256]{2,1,0:T(8,128)(2,1)S(1)}, bf16[1,288,256]{2,1,0:T(8,128)(2,1)S(1)}, u32[]{:S(2)}, u32[]{:S(2)}) %collective-permute-start.15) | collective-permute-done | bytes 147488 | tf_op jit(solution)/shard_map/ppermute | solution.py:628
  26.8 1.2 %collective-permute-done.7.refs_2_ = bf16[2,144,256]{2,1,0:T(8,128)(2,1)S(1)} collective-permute-done((bf16[2,144,256]{2,1,0:T(8,128)(2,1)S(1)}, bf16[2,144,256]{2,1,0:T(8,128)(2,1)S(1)}, u32[]{:S(2)}, u32[]{:S(2)}) %collective-permute-start.7) | collective-permute-done | bytes 147488 | tf_op jit(solution)/shard_map/ppermute | solution.py:628
  28.2 4.5 %collective-permute-done.16.refs_1_ = bf16[1,288,256]{2,1,0:T(8,128)(2,1)S(1)} collective-permute-done((bf16[1,288,256]{2,1,0:T(8,128)(2,1)S(1)}, bf16[1,288,256]{2,1,0:T(8,128)(2,1)S(1)}, u32[]{:S(2)}, u32[]{:S(2)}) %collective-permute-start.16) | collective-permute-done | bytes 147488 | tf_op jit(solution)/shard_map/ppermute | solution.py:628
  32.7 1.4 %collective-permute-start.8 = (bf16[3,2,144,256]{3,2,1,0:T(8,128)(2,1)S(1)}, bf16[3,2,144,256]{3,2,1,0:T(8,128)(2,1)}, u32[]{:S(2)}, u32[]{:S(2)}) collective-permute-start(bf16[3,2,144,256]{3,2,1,0:T(8,128)(2,1)S(1)} %stack.21.refs_2_), channel_id=1, source_target_pairs={{0,8},{1,17},{2,10},{3,19},{4,12},{5,21},{6,14},{7,23},{8,0},{9,25... | collective-permute-start | bytes 1327112 | tf_op jit(solution)/shard_map/ppermute | solution.py:628
  34.1 2.1 %collective-permute-start.23 = (bf16[1,288,256]{2,1,0:T(8,128)(2,1)S(1)}, bf16[1,288,256]{2,1,0:T(8,128)(2,1)S(1)}, u32[]{:S(2)}, u32[]{:S(2)}) collective-permute-start(bf16[1,288,256]{2,1,0:T(8,128)(2,1)S(1)} %collective-permute-done.21.refs_0_), channel_id=1, source_target_pairs={{0,2},{1,3},{2,0},{3,1},{4,6},{5,7},{6,4},{7,5},{8,10},{9,11},{10,... | collective-permute-start | bytes 442376 | tf_op jit(solution)/shard_map/ppermute | solution.py:628
  36.2 1.7 %collective-permute-start.9 = (bf16[3,2,144,256]{3,2,1,0:T(8,128)(2,1)S(1)}, bf16[3,2,144,256]{3,2,1,0:T(8,128)(2,1)S(1)}, u32[]{:S(2)}, u32[]{:S(2)}) collective-permute-start(bf16[3,2,144,256]{3,2,1,0:T(8,128)(2,1)S(1)} %stack.21.refs_2_), channel_id=1, source_target_pairs={{0,16},{1,9},{2,18},{3,11},{4,20},{5,13},{6,22},{7,15},{8,24},{9,1... | collective-permute-start | bytes 1327112 | tf_op jit(solution)/shard_map/ppermute | solution.py:628
  37.9 1.2 %collective-permute-done.17.refs_2_ = bf16[1,288,256]{2,1,0:T(8,128)(2,1)S(1)} collective-permute-done((bf16[1,288,256]{2,1,0:T(8,128)(2,1)S(1)}, bf16[1,288,256]{2,1,0:T(8,128)(2,1)S(1)}, u32[]{:S(2)}, u32[]{:S(2)}) %collective-permute-start.17) | collective-permute-done | bytes 147488 | tf_op jit(solution)/shard_map/ppermute | solution.py:628
  39.1 1.9 %collective-permute-done.23.refs_2_ = bf16[1,288,256]{2,1,0:T(8,128)(2,1)S(1)} collective-permute-done((bf16[1,288,256]{2,1,0:T(8,128)(2,1)S(1)}, bf16[1,288,256]{2,1,0:T(8,128)(2,1)S(1)}, u32[]{:S(2)}, u32[]{:S(2)}) %collective-permute-start.23) | collective-permute-done | bytes 147488 | tf_op jit(solution)/shard_map/ppermute | solution.py:628
  41.8 1.0 %collective-permute-start.18 = (bf16[3,1,288,256]{3,2,1,0:T(8,128)(2,1)}, bf16[3,1,288,256]{3,2,1,0:T(8,128)(2,1)}, u32[]{:S(2)}, u32[]{:S(2)}) collective-permute-start(bf16[3,1,288,256]{3,2,1,0:T(8,128)(2,1)} %stack.22.refs_2_), channel_id=1, source_target_pairs={{0,8},{1,17},{2,10},{3,19},{4,12},{5,21},{6,14},{7,23},{8,0},{9,25... | collective-permute-start | bytes 1327112 | tf_op jit(solution)/shard_map/ppermute | solution.py:628
  42.8 2.9 %collective-permute-done.8.refs_3_ = bf16[3,2,144,256]{3,2,1,0:T(8,128)(2,1)} collective-permute-done((bf16[3,2,144,256]{3,2,1,0:T(8,128)(2,1)S(1)}, bf16[3,2,144,256]{3,2,1,0:T(8,128)(2,1)}, u32[]{:S(2)}, u32[]{:S(2)}) %collective-permute-start.8) | collective-permute-done | bytes 442400 | tf_op jit(solution)/shard_map/ppermute | solution.py:628
  45.7 1.0 %collective-permute-start.10 = (bf16[3,2,144,256]{3,2,1,0:T(8,128)(2,1)}, bf16[3,2,144,256]{3,2,1,0:T(8,128)(2,1)}, u32[]{:S(2)}, u32[]{:S(2)}) collective-permute-start(bf16[3,2,144,256]{3,2,1,0:T(8,128)(2,1)} %collective-permute-done.8.refs_3_), channel_id=1, source_target_pairs={{0,16},{1,9},{2,18},{3,11},{4,20},{5,13},{6,22},{7,15},{8,24},{9,1... | collective-permute-start | bytes 1327112 | tf_op jit(solution)/shard_map/ppermute | solution.py:628
  47.5 1.8 %collective-permute-start.24 = (bf16[3,1,288,256]{3,2,1,0:T(8,128)(2,1)}, bf16[3,1,288,256]{3,2,1,0:T(8,128)(2,1)}, u32[]{:S(2)}, u32[]{:S(2)}) collective-permute-start(bf16[3,1,288,256]{3,2,1,0:T(8,128)(2,1)} %stack.23.refs_2_), channel_id=1, source_target_pairs={{0,8},{1,17},{2,10},{3,19},{4,12},{5,21},{6,14},{7,23},{8,0},{9,25... | collective-permute-start | bytes 1327112 | tf_op jit(solution)/shard_map/ppermute | solution.py:628
  50.2 4.4 %collective-permute-done.18.refs_3_ = bf16[3,1,288,256]{3,2,1,0:T(8,128)(2,1)} collective-permute-done((bf16[3,1,288,256]{3,2,1,0:T(8,128)(2,1)}, bf16[3,1,288,256]{3,2,1,0:T(8,128)(2,1)}, u32[]{:S(2)}, u32[]{:S(2)}) %collective-permute-start.18) | collective-permute-done | bytes 442400 | tf_op jit(solution)/shard_map/ppermute | solution.py:628
  54.6 4.5 %collective-permute-done.10.refs_5_ = bf16[3,2,144,256]{3,2,1,0:T(8,128)(2,1)} collective-permute-done((bf16[3,2,144,256]{3,2,1,0:T(8,128)(2,1)}, bf16[3,2,144,256]{3,2,1,0:T(8,128)(2,1)}, u32[]{:S(2)}, u32[]{:S(2)}) %collective-permute-start.10) | collective-permute-done | bytes 442400 | tf_op jit(solution)/shard_map/ppermute | solution.py:628
  59.1 0.9 collective-permute-done.24.refs_3_
  61.1 1.1 %copy-done.3 = bf16[256,1024]{1,0:T(8,128)(2,1)S(1)} copy-done((bf16[256,1024]{1,0:T(8,128)(2,1)S(1)}, bf16[256,1024]{1,0:T(8,128)(2,1)}, u32[]{:S(2)}) %copy-start.3) | copy-done | bytes 524312
  62.2 1.0 %copy-done.5 = bf16[4,256,256]{2,1,0:T(8,128)(2,1)S(1)} copy-done((bf16[4,256,256]{2,1,0:T(8,128)(2,1)S(1)}, bf16[4,256,256]{2,1,0:T(8,128)(2,1)}, u32[]{:S(2)}) %copy-start.5) | copy-done | bytes 524312
  63.2 1.0 %copy-done.7 = bf16[3,2,144,256]{3,2,1,0:T(8,128)(2,1)S(1)} copy-done((bf16[3,2,144,256]{3,2,1,0:T(8,128)(2,1)S(1)}, bf16[3,2,144,256]{3,2,1,0:T(8,128)(2,1)}, u32[]{:S(2)}) %copy-start.7) | copy-done | bytes 442392
  64.3 1.0 %copy-done.9 = bf16[3,2,144,256]{3,2,1,0:T(8,128)(2,1)S(1)} copy-done((bf16[3,2,144,256]{3,2,1,0:T(8,128)(2,1)S(1)}, bf16[3,2,144,256]{3,2,1,0:T(8,128)(2,1)}, u32[]{:S(2)}) %copy-start.9) | copy-done | bytes 442392
  65.3 5.8 %coarse.1 = (f32[2,12,2,48,128]{4,3,2,1,0:T(8,128)S(1)}, bf16[240,256]{1,0:T(8,128)(2,1)S(1)}) custom-call(s32[3]{0:T(128)S(1)} %copy-done.11, bf16[4,256,256]{2,1,0:T(8,128)(2,1)S(1)} %stack.20.mine, bf16[4,256,256]{2,1,0:T(8,128)(2,1)S(1)} %copy-done.5, bf16[256,1024]{1,0:T(8,128)(2,1)S(1)} %copy-done.3, bf16[4,2,288,256]{3,2,1,0:T(8,128)(2,1)S(1)} %copy-done.1, ...), custom_call_target="tpu_custom_call" | custom-call | flops 2000000000 | bytes 8000000 | tf_op jit(solution)/shard_map/coarse/pallas_call | solution.py:411
  71.1 5.7 %middle.1.map0 = f32[2,10,4,96,128]{4,3,2,1,0:T(8,128)S(1)} custom-call(s32[3]{0:T(128)S(1)} %copy-done.11, f32[2,12,2,48,128]{4,3,2,1,0:T(8,128)S(1)} %get-tuple-element.15.summed1, bf16[240,256]{1,0:T(8,128)(2,1)S(1)} %get-tuple-element.16.patch0, bf16[256,4096]{1,0:T(8,128)(2,1)S(1)} %copy-done.2, bf16[4,2,288,256]{3,2,1,0:T(8,128)(2,1)S(1)} %copy-done.1, ...), custom_call_target="tpu_custom_call" | custom-call | flops 3000000000 | bytes 6000000 | tf_op jit(solution)/shard_map/middle/pallas_call | solution.py:499
  76.9 9.8 %fine.1 = f32[8,6,256]{2,1,0:T(8,128)S(1)} custom-call(s32[3]{0:T(128)S(1)} %copy-done.11, f32[2,10,4,96,128]{4,3,2,1,0:T(8,128)S(1)} %middle.1.map0, bf16[256,128]{1,0:T(8,128)(2,1)S(1)} %copy-done.12, f32[1,128]{1,0:T(1,128)S(1)} %bitcast.16, f32[8,6,8]{2,1,0:T(8,128)S(1)} %compare_convert_fusion.matches, bf16[4,2,288,256]{3,2,1,0:T(8,128)(2,1)S(1)} %copy-done.1, ...), custom_call_target="tpu_custom_call" | custom-call | flops 6000000000 | bytes 8000000 | tf_op jit(solution)/shard_map/fine/pallas_call | solution.py:601
  86.7 9.1 %all_to_all.5 = f32[8,6,256]{2,1,0:T(8,128)S(1)} all-to-all(f32[8,6,256]{2,1,0:T(8,128)S(1)} %fine.1), channel_id=1, replica_groups=mesh['phase'=4,'dp'=8] {'dp'}, dimensions={0} | all-to-all | bytes 98304 | tf_op jit(solution)/shard_map/all_to_all | solution.py:705
  (66 shorter events, 7.7 us)
Async XLA Ops:
  0.0 60.4 %copy-start = (s32[8,4,8]{2,1,0:T(4,128)S(1)}, s32[8,4,8]{2,1,0:T(4,128)}, u32[]{:S(2)}) copy-start(s32[8,4,8]{2,1,0:T(4,128)} %param.17) | copy-start | bytes 3076
  0.9 16.6 %collective-permute-start.5 = (bf16[2,144,256]{2,1,0:T(8,128)(2,1)S(1)}, bf16[2,144,256]{2,1,0:T(8,128)(2,1)S(1)}, u32[]{:S(2)}, u32[]{:S(2)}) collective-permute-start(bf16[2,144,256]{2,1,0:T(8,128)(2,1)S(1)} %dynamic-slice_bitcast_fusion.2), channel_id=1, source_target_pairs={{0,4},{1,5},{2,6},{3,7},{4,0},{5,1},{6,2},{7,3},{8,12},{9,13},{10,... | collective-permute-start | bytes 442376 | tf_op jit(solution)/shard_map/ppermute | solution.py:628
  5.7 11.4 %copy-start.1 = (bf16[4,2,288,256]{3,2,1,0:T(8,128)(2,1)S(1)}, bf16[4,2,288,256]{3,2,1,0:T(8,128)(2,1)}, u32[]{:S(2)}) copy-start(bf16[4,2,288,256]{3,2,1,0:T(8,128)(2,1)} %refs_0_.5) | copy-start | bytes 3538948
  12.0 5.2 %collective-permute-start = (bf16[256,256]{1,0:T(8,128)(2,1)}, bf16[256,256]{1,0:T(8,128)(2,1)S(1)}, u32[]{:S(2)}, u32[]{:S(2)}) collective-permute-start(bf16[256,256]{1,0:T(8,128)(2,1)} %get-tuple-element.12), channel_id=1, source_target_pairs={{0,8},{8,0},{16,24},{24,16},{1,9},{9,1},{17,25},{25,17},{2,10},{10... | collective-permute-start | bytes 393224 | tf_op jit(solution)/shard_map/ppermute | solution.py:699
  13.6 11.3 %collective-permute-start.6 = (bf16[2,144,256]{2,1,0:T(8,128)(2,1)S(1)}, bf16[2,144,256]{2,1,0:T(8,128)(2,1)S(1)}, u32[]{:S(2)}, u32[]{:S(2)}) collective-permute-start(bf16[2,144,256]{2,1,0:T(8,128)(2,1)S(1)} %dynamic-slice_bitcast_fusion.2), channel_id=1, source_target_pairs={{0,2},{1,3},{2,0},{3,1},{4,6},{5,7},{6,4},{7,5},{8,10},{9,11},{10,... | collective-permute-start | bytes 442376 | tf_op jit(solution)/shard_map/ppermute | solution.py:628
  15.1 8.0 %collective-permute-start.1 = (bf16[256,256]{1,0:T(8,128)(2,1)}, bf16[256,256]{1,0:T(8,128)(2,1)S(1)}, u32[]{:S(2)}, u32[]{:S(2)}) collective-permute-start(bf16[256,256]{1,0:T(8,128)(2,1)} %get-tuple-element.13), channel_id=1, source_target_pairs={{0,16},{8,24},{16,0},{24,8},{1,17},{9,25},{17,1},{25,9},{2,18},{10... | collective-permute-start | bytes 393224 | tf_op jit(solution)/shard_map/ppermute | solution.py:699
  16.5 7.1 %collective-permute-start.2 = (bf16[256,256]{1,0:T(8,128)(2,1)}, bf16[256,256]{1,0:T(8,128)(2,1)S(1)}, u32[]{:S(2)}, u32[]{:S(2)}) collective-permute-start(bf16[256,256]{1,0:T(8,128)(2,1)} %get-tuple-element.14), channel_id=1, source_target_pairs={{0,24},{8,16},{16,8},{24,0},{1,25},{9,17},{17,9},{25,1},{2,26},{10... | collective-permute-start | bytes 393224 | tf_op jit(solution)/shard_map/ppermute | solution.py:699
  17.3 8.9 %collective-permute-start.15 = (bf16[1,288,256]{2,1,0:T(8,128)(2,1)S(1)}, bf16[1,288,256]{2,1,0:T(8,128)(2,1)S(1)}, u32[]{:S(2)}, u32[]{:S(2)}) collective-permute-start(bf16[1,288,256]{2,1,0:T(8,128)(2,1)S(1)} %get-tuple-element.18), channel_id=1, source_target_pairs={{0,4},{1,5},{2,6},{3,7},{4,0},{5,1},{6,2},{7,3},{8,12},{9,13},{10,... | collective-permute-start | bytes 442376 | tf_op jit(solution)/shard_map/ppermute | solution.py:628
  17.6 10.4 %collective-permute-start.7 = (bf16[2,144,256]{2,1,0:T(8,128)(2,1)S(1)}, bf16[2,144,256]{2,1,0:T(8,128)(2,1)S(1)}, u32[]{:S(2)}, u32[]{:S(2)}) collective-permute-start(bf16[2,144,256]{2,1,0:T(8,128)(2,1)S(1)} %collective-permute-done.5.refs_0_), channel_id=1, source_target_pairs={{0,2},{1,3},{2,0},{3,1},{4,6},{5,7},{6,4},{7,5},{8,10},{9,11},{10,... | collective-permute-start | bytes 442376 | tf_op jit(solution)/shard_map/ppermute | solution.py:628
  23.1 9.6 %collective-permute-start.16 = (bf16[1,288,256]{2,1,0:T(8,128)(2,1)S(1)}, bf16[1,288,256]{2,1,0:T(8,128)(2,1)S(1)}, u32[]{:S(2)}, u32[]{:S(2)}) collective-permute-start(bf16[1,288,256]{2,1,0:T(8,128)(2,1)S(1)} %get-tuple-element.18), channel_id=1, source_target_pairs={{0,2},{1,3},{2,0},{3,1},{4,6},{5,7},{6,4},{7,5},{8,10},{9,11},{10,... | collective-permute-start | bytes 442376 | tf_op jit(solution)/shard_map/ppermute | solution.py:628
  23.6 10.5 %collective-permute-start.21 = (bf16[1,288,256]{2,1,0:T(8,128)(2,1)S(1)}, bf16[1,288,256]{2,1,0:T(8,128)(2,1)S(1)}, u32[]{:S(2)}, u32[]{:S(2)}) collective-permute-start(bf16[1,288,256]{2,1,0:T(8,128)(2,1)S(1)} %get-tuple-element.17), channel_id=1, source_target_pairs={{0,4},{1,5},{2,6},{3,7},{4,0},{5,1},{6,2},{7,3},{8,12},{9,13},{10,... | collective-permute-start | bytes 442376 | tf_op jit(solution)/shard_map/ppermute | solution.py:628
  24.9 36.3 %copy-start.11 = (s32[3]{0:T(128)S(1)}, s32[3]{0:T(128)}, u32[]{:S(2)}) copy-start(s32[3]{0:T(128)} %pad_add_fusion.where) | copy-start | bytes 40
  24.9 16.9 %collective-permute-start.3 = (bf16[4,256,256]{2,1,0:T(8,128)(2,1)S(1)}, bf16[4,256,256]{2,1,0:T(8,128)(2,1)S(1)}, u32[]{:S(2)}, u32[]{:S(2)}) collective-permute-start(bf16[4,256,256]{2,1,0:T(8,128)(2,1)S(1)} %stack.20.mine), channel_id=1, source_target_pairs={{0,1},{1,0},{2,3},{3,2},{4,5},{5,4},{6,7},{7,6},{8,9},{9,8},{10,11... | collective-permute-start | bytes 1572872 | tf_op jit(solution)/shard_map/ppermute | solution.py:701
  26.1 10.1 %collective-permute-start.22 = (bf16[1,288,256]{2,1,0:T(8,128)(2,1)S(1)}, bf16[1,288,256]{2,1,0:T(8,128)(2,1)S(1)}, u32[]{:S(2)}, u32[]{:S(2)}) collective-permute-start(bf16[1,288,256]{2,1,0:T(8,128)(2,1)S(1)} %get-tuple-element.17), channel_id=1, source_target_pairs={{0,2},{1,3},{2,0},{3,1},{4,6},{5,7},{6,4},{7,5},{8,10},{9,11},{10,... | collective-permute-start | bytes 442376 | tf_op jit(solution)/shard_map/ppermute | solution.py:628
  28.0 11.1 %collective-permute-start.17 = (bf16[1,288,256]{2,1,0:T(8,128)(2,1)S(1)}, bf16[1,288,256]{2,1,0:T(8,128)(2,1)S(1)}, u32[]{:S(2)}, u32[]{:S(2)}) collective-permute-start(bf16[1,288,256]{2,1,0:T(8,128)(2,1)S(1)} %collective-permute-done.15.refs_0_), channel_id=1, source_target_pairs={{0,2},{1,3},{2,0},{3,1},{4,6},{5,7},{6,4},{7,5},{8,10},{9,11},{10,... | collective-permute-start | bytes 442376 | tf_op jit(solution)/shard_map/ppermute | solution.py:628
  32.7 13.0 %collective-permute-start.8 = (bf16[3,2,144,256]{3,2,1,0:T(8,128)(2,1)S(1)}, bf16[3,2,144,256]{3,2,1,0:T(8,128)(2,1)}, u32[]{:S(2)}, u32[]{:S(2)}) collective-permute-start(bf16[3,2,144,256]{3,2,1,0:T(8,128)(2,1)S(1)} %stack.21.refs_2_), channel_id=1, source_target_pairs={{0,8},{1,17},{2,10},{3,19},{4,12},{5,21},{6,14},{7,23},{8,0},{9,25... | collective-permute-start | bytes 1327112 | tf_op jit(solution)/shard_map/ppermute | solution.py:628
  34.1 6.9 %collective-permute-start.23 = (bf16[1,288,256]{2,1,0:T(8,128)(2,1)S(1)}, bf16[1,288,256]{2,1,0:T(8,128)(2,1)S(1)}, u32[]{:S(2)}, u32[]{:S(2)}) collective-permute-start(bf16[1,288,256]{2,1,0:T(8,128)(2,1)S(1)} %collective-permute-done.21.refs_0_), channel_id=1, source_target_pairs={{0,2},{1,3},{2,0},{3,1},{4,6},{5,7},{6,4},{7,5},{8,10},{9,11},{10,... | collective-permute-start | bytes 442376 | tf_op jit(solution)/shard_map/ppermute | solution.py:628
  36.2 11.3 %collective-permute-start.9 = (bf16[3,2,144,256]{3,2,1,0:T(8,128)(2,1)S(1)}, bf16[3,2,144,256]{3,2,1,0:T(8,128)(2,1)S(1)}, u32[]{:S(2)}, u32[]{:S(2)}) collective-permute-start(bf16[3,2,144,256]{3,2,1,0:T(8,128)(2,1)S(1)} %stack.21.refs_2_), channel_id=1, source_target_pairs={{0,16},{1,9},{2,18},{3,11},{4,20},{5,13},{6,22},{7,15},{8,24},{9,1... | collective-permute-start | bytes 1327112 | tf_op jit(solution)/shard_map/ppermute | solution.py:628
  39.0 10.3 %collective-permute-start.11 = (bf16[3,2,144,256]{3,2,1,0:T(8,128)(2,1)S(1)}, bf16[3,2,144,256]{3,2,1,0:T(8,128)(2,1)S(1)}, u32[]{:S(2)}, u32[]{:S(2)}) collective-permute-start(bf16[3,2,144,256]{3,2,1,0:T(8,128)(2,1)S(1)} %stack.21.refs_2_), channel_id=1, source_target_pairs={{0,1},{1,0},{2,3},{3,2},{4,5},{5,4},{6,7},{7,6},{8,9},{9,8},{10,11... | collective-permute-start | bytes 1327112 | tf_op jit(solution)/shard_map/ppermute | solution.py:628
  41.0 19.7 %collective-permute-start.4 = (bf16[4,2,288,256]{3,2,1,0:T(8,128)(2,1)S(1)}, bf16[4,2,288,256]{3,2,1,0:T(8,128)(2,1)S(1)}, u32[]{:S(2)}, u32[]{:S(2)}) collective-permute-start(bf16[4,2,288,256]{3,2,1,0:T(8,128)(2,1)S(1)} %copy-done.1), channel_id=1, source_target_pairs={{0,1},{1,0},{2,3},{3,2},{4,5},{5,4},{6,7},{7,6},{8,9},{9,8},{10,11... | collective-permute-start | bytes 3538952 | tf_op jit(solution)/shard_map/ppermute | solution.py:628
  41.8 7.6 %copy-start.4 = (bf16[4,256,256]{2,1,0:T(8,128)(2,1)}, bf16[4,256,256]{2,1,0:T(8,128)(2,1)S(1)}, u32[]{:S(2)}) copy-start(bf16[4,256,256]{2,1,0:T(8,128)(2,1)S(1)} %collective-permute-done.3.other) | copy-start | bytes 1572868
  41.8 12.8 %collective-permute-start.18 = (bf16[3,1,288,256]{3,2,1,0:T(8,128)(2,1)}, bf16[3,1,288,256]{3,2,1,0:T(8,128)(2,1)}, u32[]{:S(2)}, u32[]{:S(2)}) collective-permute-start(bf16[3,1,288,256]{3,2,1,0:T(8,128)(2,1)} %stack.22.refs_2_), channel_id=1, source_target_pairs={{0,8},{1,17},{2,10},{3,19},{4,12},{5,21},{6,14},{7,23},{8,0},{9,25... | collective-permute-start | bytes 1327112 | tf_op jit(solution)/shard_map/ppermute | solution.py:628
  45.7 13.4 %collective-permute-start.10 = (bf16[3,2,144,256]{3,2,1,0:T(8,128)(2,1)}, bf16[3,2,144,256]{3,2,1,0:T(8,128)(2,1)}, u32[]{:S(2)}, u32[]{:S(2)}) collective-permute-start(bf16[3,2,144,256]{3,2,1,0:T(8,128)(2,1)} %collective-permute-done.8.refs_3_), channel_id=1, source_target_pairs={{0,16},{1,9},{2,18},{3,11},{4,20},{5,13},{6,22},{7,15},{8,24},{9,1... | collective-permute-start | bytes 1327112 | tf_op jit(solution)/shard_map/ppermute | solution.py:628
  47.5 12.4 %collective-permute-start.24 = (bf16[3,1,288,256]{3,2,1,0:T(8,128)(2,1)}, bf16[3,1,288,256]{3,2,1,0:T(8,128)(2,1)}, u32[]{:S(2)}, u32[]{:S(2)}) collective-permute-start(bf16[3,1,288,256]{3,2,1,0:T(8,128)(2,1)} %stack.23.refs_2_), channel_id=1, source_target_pairs={{0,8},{1,17},{2,10},{3,19},{4,12},{5,21},{6,14},{7,23},{8,0},{9,25... | collective-permute-start | bytes 1327112 | tf_op jit(solution)/shard_map/ppermute | solution.py:628
  50.2 9.7 %collective-permute-start.12 = (bf16[3,2,144,256]{3,2,1,0:T(8,128)(2,1)}, bf16[3,2,144,256]{3,2,1,0:T(8,128)(2,1)}, u32[]{:S(2)}, u32[]{:S(2)}) collective-permute-start(bf16[3,2,144,256]{3,2,1,0:T(8,128)(2,1)} %collective-permute-done.8.refs_3_), channel_id=1, source_target_pairs={{0,1},{1,0},{2,3},{3,2},{4,5},{5,4},{6,7},{7,6},{8,9},{9,8},{10,11... | collective-permute-start | bytes 1327112 | tf_op jit(solution)/shard_map/ppermute | solution.py:628
  54.6 5.9 %collective-permute-start.13 = (bf16[3,2,144,256]{3,2,1,0:T(8,128)(2,1)}, bf16[3,2,144,256]{3,2,1,0:T(8,128)(2,1)S(1)}, u32[]{:S(2)}, u32[]{:S(2)}) collective-permute-start(bf16[3,2,144,256]{3,2,1,0:T(8,128)(2,1)} %copy-done.6), channel_id=1, source_target_pairs={{0,1},{1,0},{2,3},{3,2},{4,5},{5,4},{6,7},{7,6},{8,9},{9,8},{10,11... | collective-permute-start | bytes 1327112 | tf_op jit(solution)/shard_map/ppermute | solution.py:628
  59.1 2.1 %collective-permute-start.14 = (bf16[3,2,144,256]{3,2,1,0:T(8,128)(2,1)}, bf16[3,2,144,256]{3,2,1,0:T(8,128)(2,1)S(1)}, u32[]{:S(2)}, u32[]{:S(2)}) collective-permute-start(bf16[3,2,144,256]{3,2,1,0:T(8,128)(2,1)} %collective-permute-done.10.refs_5_), channel_id=1, source_target_pairs={{0,1},{1,0},{2,3},{3,2},{4,5},{5,4},{6,7},{7,6},{8,9},{9,8},{10,11... | collective-permute-start | bytes 1327112 | tf_op jit(solution)/shard_map/ppermute | solution.py:628
  59.9 11.2 %collective-permute-start.19 = (bf16[3,1,288,256]{3,2,1,0:T(8,128)(2,1)}, bf16[3,1,288,256]{3,2,1,0:T(8,128)(2,1)S(1)}, u32[]{:S(2)}, u32[]{:S(2)}) collective-permute-start(bf16[3,1,288,256]{3,2,1,0:T(8,128)(2,1)} %stack.22.refs_2_), channel_id=1, source_target_pairs={{0,1},{1,0},{2,3},{3,2},{4,5},{5,4},{6,7},{7,6},{8,9},{9,8},{10,11... | collective-permute-start | bytes 1327112 | tf_op jit(solution)/shard_map/ppermute | solution.py:628
  59.9 11.2 %collective-permute-start.20 = (bf16[3,1,288,256]{3,2,1,0:T(8,128)(2,1)}, bf16[3,1,288,256]{3,2,1,0:T(8,128)(2,1)S(1)}, u32[]{:S(2)}, u32[]{:S(2)}) collective-permute-start(bf16[3,1,288,256]{3,2,1,0:T(8,128)(2,1)} %collective-permute-done.18.refs_3_), channel_id=1, source_target_pairs={{0,1},{1,0},{2,3},{3,2},{4,5},{5,4},{6,7},{7,6},{8,9},{9,8},{10,11... | collective-permute-start | bytes 1327112 | tf_op jit(solution)/shard_map/ppermute | solution.py:628
  60.5 10.6 %copy-start.2 = (bf16[256,4096]{1,0:T(8,128)(2,1)S(1)}, bf16[256,4096]{1,0:T(8,128)(2,1)}, u32[]{:S(2)}) copy-start(bf16[256,4096]{1,0:T(8,128)(2,1)} %expand_four.1) | copy-start | bytes 6291460
  60.5 16.4 %collective-permute-start.25 = (bf16[3,1,288,256]{3,2,1,0:T(8,128)(2,1)}, bf16[3,1,288,256]{3,2,1,0:T(8,128)(2,1)S(1)}, u32[]{:S(2)}, u32[]{:S(2)}) collective-permute-start(bf16[3,1,288,256]{3,2,1,0:T(8,128)(2,1)} %stack.23.refs_2_), channel_id=1, source_target_pairs={{0,1},{1,0},{2,3},{3,2},{4,5},{5,4},{6,7},{7,6},{8,9},{9,8},{10,11... | collective-permute-start | bytes 1327112 | tf_op jit(solution)/shard_map/ppermute | solution.py:628
  60.6 16.3 %collective-permute-start.26 = (bf16[3,1,288,256]{3,2,1,0:T(8,128)(2,1)}, bf16[3,1,288,256]{3,2,1,0:T(8,128)(2,1)S(1)}, u32[]{:S(2)}, u32[]{:S(2)}) collective-permute-start(bf16[3,1,288,256]{3,2,1,0:T(8,128)(2,1)} %collective-permute-done.24.refs_3_), channel_id=1, source_target_pairs={{0,1},{1,0},{2,3},{3,2},{4,5},{5,4},{6,7},{7,6},{8,9},{9,8},{10,11... | collective-permute-start | bytes 1327112 | tf_op jit(solution)/shard_map/ppermute | solution.py:628
  (9 other events, 19.3 us)

commit v8 on v7

--- a/solution.py
+++ b/solution.py
@@ -207,24 +207,26 @@
 
 
 def loop(count, body):
-    if count == 1:
-        body(0)
-    else:
-        lax.fori_loop(0, count, lambda i, c: (body(i), c)[1], 0)
+    lax.fori_loop(0, count, lambda i, c: (body(i), c)[1], 0)
+
+
+def steps(count, body):
+    for i in range(count):
+        body(i)
 
 
 def refine(source, wait, weights, first, second, chunk, out_col, out_count, out_chunk, emit):
     cols, rows = first.shape[1] - 2, first.shape[2]
     clear_edges(first)
     clear_edges(second)
-    loop(cols // chunk, lambda i: put_shifted(first, i * chunk, source(i * chunk, chunk)))
+    steps(cols // chunk, lambda i: put_shifted(first, i * chunk, source(i * chunk, chunk)))
 
     wait(0)
 
     def inner(i):
         put_shifted(second, i * chunk, conv_block(first, weights.at[0], i * chunk, chunk, (0, rows)))
 
-    loop(cols // chunk, inner)
+    steps(cols // chunk, inner)
 
     wait(1)
 
@@ -233,7 +235,7 @@
         branch = conv_block(second, weights.at[1], col, out_chunk, (0, rows))
         emit(i * out_chunk, source(col, out_chunk) + branch)
 
-    loop(out_count // out_chunk, outer)
+    steps(out_count // out_chunk, outer)
 
 
 def start_filters(filters, level, weights, sems):
@@ -518,7 +520,7 @@
 FINE_SCRATCH = 7
 
 
-def fine_kernel(plan, where, map0, head, vector, matches, *refs):
+def fine_kernel(plan, where, map0, head, vector, tile_slot, *refs):
     count = len(refs) - FINE_SCRATCH
     filters = refs[:count]
     portions, weight0, sems, first, second, by_col, by_row = refs[count:]
@@ -583,24 +585,24 @@
         axis=1,
     )
 
-    def add_tiles(d):
-        chosen = matches[d]
+    count = portions.shape[0]
+    targets = tile_slot[2 * where[2] + side, pl.ds(phase, 1), :]
+    slot = lax.broadcasted_iota(jnp.int32, (SLOT_DEV, TILES_DEV), 0) + phase * count * SLOT_DEV
+    for d in range(count):
+        chosen = (slot + d * SLOT_DEV == targets).astype(F32)
         total = chosen[:, 0:1] * tiles[0:1]
         for j in range(1, TILES_DEV):
             total += chosen[:, j : j + 1] * tiles[j : j + 1]
         portions[d] = total
 
-    for d in range(portions.shape[0]):
-        add_tiles(d)
-
-
-def fine(plan, where, summed0, head, vector, matches, filters):
+
+def fine(plan, dp_count, where, summed0, head, vector, tile_slot, filters):
     ch = plan.ch
     vmem = pl.BlockSpec(memory_space=pltpu.VMEM)
     pixels = 16 * plan.block * plan.half // TILES_DEV
     return pl.pallas_call(
         functools.partial(fine_kernel, plan),
-        out_shape=jax.ShapeDtypeStruct(matches.shape[:2] + (pixels,), F32),
+        out_shape=jax.ShapeDtypeStruct((dp_count, SLOT_DEV, pixels), F32),
         in_specs=[pl.BlockSpec(memory_space=pltpu.SMEM)] + [vmem] * 4 + filter_specs(filters),
         out_specs=vmem,
         scratch_shapes=[pltpu.VMEM((2, 9 * ch, ch), BF16), pltpu.SemaphoreType.DMA((2,))]
@@ -611,7 +613,7 @@
             flops=6_000_000_000, bytes_accessed=8_000_000, transcendentals=0
         ),
         name="fine",
-    )(where, summed0, head, vector[None, :], matches, *filters)
+    )(where, summed0, head, vector[None, :], tile_slot, *filters)
 
 
 def gather_filters(filters, phase_id, held, phases, dp_count):
@@ -685,9 +687,6 @@
     dp_id = lax.axis_index("dp")
     held = (phase_id >> (dp_id & 1)) & 1
     where = jnp.stack([phase_id, dp_id & 1, dp_id >> 1]).astype(jnp.int32)
-    slots = phase_id * dp_count * SLOT_DEV + jnp.arange(dp_count * SLOT_DEV, dtype=jnp.int32)
-    targets = lax.dynamic_slice(tile_slot, (dp_id, phase_id, 0), (1, 1, TILES_DEV))
-    matches = (slots.reshape(dp_count, SLOT_DEV, 1) == targets).astype(F32)
     if by_permutes(phases, dp_count):
         base, gathered = gather_filters(refine_filters, phase_id, held, phases, dp_count)
         upper, medium, finer = (base + pieces for pieces in gathered)
@@ -701,7 +700,7 @@
     other = lax.ppermute(mine, "dp", [(d, d ^ 1) for d in range(dp_count)])
     summed1, patch0 = coarse(plan, where, mine, other, expand_two, upper)
     summed0 = middle(plan, where, summed1, patch0, expand_four, medium)
-    partial = fine(plan, where, summed0, head_matrix, head_vector, matches, finer)
+    partial = fine(plan, dp_count, where, summed0, head_matrix, head_vector, tile_slot, finer)
     portions = lax.all_to_all(partial, "dp", split_axis=0, concat_axis=0, tiled=True)
     return portions.sum(axis=0)
 

time: 96.9 us -> 90.5 us (0.934)
  local copies, waits for them, and re-layouts: 6.82 us -> 1.88 us
  waiting for transfers between devices: 26.3 us -> 30.5 us
  Pallas kernels: 29.3 us -> 25.2 us
    unnamed x28 -> x16, local copies, waits for them, and re-layouts: 5.86 us -> 0.94 us
    ppermute x23, waiting for transfers between devices: 22.6 us -> 25 us  [move(): return lax.ppermute(value, axes, route)]
    ppermute x3, waiting for transfers between devices: 3.68 us -> 5.41 us  [per_device(): lax.ppermute(sent[k], 'phase', [(s, s ^ k) for s in range(phases)])]
    pallas_call x4, Pallas kernels: 1.67 us -> 0.12 us  [stack(): pl.pallas_call(stack_kernel, out_shape=jax.ShapeDtypeStruct((len(values),...]
    pallas_call x1, Pallas kernels: 5.74 us -> 4.4 us  [middle(): pl.pallas_call(functools.partial(middle_kernel, plan), out_shape=jax.Shap...]
  transfers between devices with their start and end apart: 27 -> 27, of which waited for: 11 -> 9; matrix products, arithmetic and copies ran while one was open for 1% -> 1% of each run, Pallas kernels for 20% -> 18%
where the time goes in v8:
time: 90.5 us; the launch traced here: 90.3 us
  waiting for transfers between devices  30.5 us (34%)
  Pallas kernels  25.2 us (28%)
  starting transfers between devices  22.5 us (25%)
  blocking collectives  8.82 us (10%)
  local copies, waits for them, and re-layouts  1.88 us (2%)
  other arithmetic  1.17 us (1%)
    ppermute x23, waiting for transfers between devices, move(): return lax.ppermute(value, axes, route)  25 us
    ppermute x23, starting transfers between devices, move(): return lax.ppermute(value, axes, route)  18.9 us
    pallas_call x1, Pallas kernels, fine(): pl.pallas_call(functools.partial(fine_kernel, plan), out_shape=jax.ShapeD...  9.26 us
    all_to_all x1, blocking collectives, per_device(): lax.all_to_all(partial, 'dp', split_axis=0, concat_axis=0, tiled=True)  8.82 us
    pallas_call x1, Pallas kernels, project(): pl.pallas_call(functools.partial(project_kernel, plan, phases), in_specs=...  6.3 us
    ppermute x3, waiting for transfers between devices, per_device(): lax.ppermute(sent[k], 'phase', [(s, s ^ k) for s in range(phases)])  5.41 us
    pallas_call x1, Pallas kernels, coarse(): pl.pallas_call(functools.partial(coarse_kernel, plan), out_shape=[jax.Sha...  5.1 us
    pallas_call x1, Pallas kernels, middle(): pl.pallas_call(functools.partial(middle_kernel, plan), out_shape=jax.Shap...  4.4 us
  transfers between devices with their start and end apart: 27, of which 9 were waited for; matrix products, arithmetic and copies ran while one was open for 1% of the time, Pallas kernels for 18%

profile of v8, /device:TPU:0, one launch (start us, length us, event | category | flops | bytes accessed | tf_op | source)
XLA Modules:
  0.0 90.3 jit_solution(3920594322958787950)
XLA Ops:
  0.0 0.9 %dynamic-slice_bitcast_fusion.2 = bf16[2,144,256]{2,1,0:T(8,128)(2,1)S(1)} fusion(bf16[4,4,144,256]{3,2,1,0:T(8,128)(2,1)} %bitcast.13, s32[]{:T(128)S(6)} %select_n.7), kind=kLoop, calls=%fused_computation.2 | loop fusion | bytes 294916 | tf_op jit(solution)/shard_map/squeeze | solution.py:654
  0.9 4.1 %collective-permute-start.5 = (bf16[2,144,256]{2,1,0:T(8,128)(2,1)S(1)}, bf16[2,144,256]{2,1,0:T(8,128)(2,1)S(1)}, u32[]{:S(2)}, u32[]{:S(2)}) collective-permute-start(bf16[2,144,256]{2,1,0:T(8,128)(2,1)S(1)} %dynamic-slice_bitcast_fusion.2), channel_id=1, source_target_pairs={{0,4},{1,5},{2,6},{3,7},{4,0},{5,1},{6,2},{7,3},{8,12},{9,13},{10,... | collective-permute-start | bytes 442376 | tf_op jit(solution)/shard_map/ppermute | solution.py:630
  5.1 0.6 pad_add_fusion.where
  5.6 6.3 %project.1 = (bf16[256,256]{1,0:T(8,128)(2,1)}, bf16[256,256]{1,0:T(8,128)(2,1)}, bf16[256,256]{1,0:T(8,128)(2,1)}, bf16[256,256]{1,0:T(8,128)(2,1)}) custom-call(s32[3]{0:T(128)} %pad_add_fusion.where, bf16[1,512,4096]{2,1,0:T(8,128)(2,1)} %tokens_hbm.1, bf16[1,4096,256]{2,1,0:T(8,128)(2,1)} %weight_hbm.1, bf16[1024,256]{1,0:T(8,128)(2,1)} %shrink_hbm.1), custom_call_target="tpu_custom_call" | custom-call | flops 1073741824 | bytes 6291456 | tf_op jit(solution)/shard_map/project/pallas_call | solution.py:139
  11.9 1.6 %collective-permute-start = (bf16[256,256]{1,0:T(8,128)(2,1)}, bf16[256,256]{1,0:T(8,128)(2,1)S(1)}, u32[]{:S(2)}, u32[]{:S(2)}) collective-permute-start(bf16[256,256]{1,0:T(8,128)(2,1)} %get-tuple-element.12), channel_id=1, source_target_pairs={{0,8},{8,0},{16,24},{24,16},{1,9},{9,1},{17,25},{25,17},{2,10},{10... | collective-permute-start | bytes 393224 | tf_op jit(solution)/shard_map/ppermute | solution.py:698
  13.5 1.6 %collective-permute-start.6 = (bf16[2,144,256]{2,1,0:T(8,128)(2,1)S(1)}, bf16[2,144,256]{2,1,0:T(8,128)(2,1)S(1)}, u32[]{:S(2)}, u32[]{:S(2)}) collective-permute-start(bf16[2,144,256]{2,1,0:T(8,128)(2,1)S(1)} %dynamic-slice_bitcast_fusion.2), channel_id=1, source_target_pairs={{0,2},{1,3},{2,0},{3,1},{4,6},{5,7},{6,4},{7,5},{8,10},{9,11},{10,... | collective-permute-start | bytes 442376 | tf_op jit(solution)/shard_map/ppermute | solution.py:630
  15.1 1.3 %collective-permute-start.1 = (bf16[256,256]{1,0:T(8,128)(2,1)}, bf16[256,256]{1,0:T(8,128)(2,1)S(1)}, u32[]{:S(2)}, u32[]{:S(2)}) collective-permute-start(bf16[256,256]{1,0:T(8,128)(2,1)} %get-tuple-element.13), channel_id=1, source_target_pairs={{0,16},{8,24},{16,0},{24,8},{1,17},{9,25},{17,1},{25,9},{2,18},{10... | collective-permute-start | bytes 393224 | tf_op jit(solution)/shard_map/ppermute | solution.py:698
  16.4 0.7 collective-permute-start.2
  17.1 0.5 collective-permute-start.7
  17.6 5.4 %collective-permute-done.1.refs_2_ = bf16[256,256]{1,0:T(8,128)(2,1)S(1)} collective-permute-done((bf16[256,256]{1,0:T(8,128)(2,1)}, bf16[256,256]{1,0:T(8,128)(2,1)S(1)}, u32[]{:S(2)}, u32[]{:S(2)}) %collective-permute-start.1) | collective-permute-done | bytes 131104 | tf_op jit(solution)/shard_map/ppermute | solution.py:698
  23.0 0.5 collective-permute-start.16
  23.8 0.9 copy-done.3
  24.9 2.0 %collective-permute-done.7.refs_2_ = bf16[2,144,256]{2,1,0:T(8,128)(2,1)S(1)} collective-permute-done((bf16[2,144,256]{2,1,0:T(8,128)(2,1)S(1)}, bf16[2,144,256]{2,1,0:T(8,128)(2,1)S(1)}, u32[]{:S(2)}, u32[]{:S(2)}) %collective-permute-start.7) | collective-permute-done | bytes 147488 | tf_op jit(solution)/shard_map/ppermute | solution.py:630
  26.9 2.4 %collective-permute-start.8 = (bf16[3,2,144,256]{3,2,1,0:T(8,128)(2,1)S(1)}, bf16[3,2,144,256]{3,2,1,0:T(8,128)(2,1)S(1)}, u32[]{:S(2)}, u32[]{:S(2)}) collective-permute-start(bf16[3,2,144,256]{3,2,1,0:T(8,128)(2,1)S(1)} %stack.21.refs_2_), channel_id=1, source_target_pairs={{0,8},{1,17},{2,10},{3,19},{4,12},{5,21},{6,14},{7,23},{8,0},{9,25... | collective-permute-start | bytes 1327112 | tf_op jit(solution)/shard_map/ppermute | solution.py:630
  29.3 3.0 %collective-permute-done.16.refs_1_ = bf16[1,288,256]{2,1,0:T(8,128)(2,1)S(1)} collective-permute-done((bf16[1,288,256]{2,1,0:T(8,128)(2,1)S(1)}, bf16[1,288,256]{2,1,0:T(8,128)(2,1)S(1)}, u32[]{:S(2)}, u32[]{:S(2)}) %collective-permute-start.16) | collective-permute-done | bytes 147488 | tf_op jit(solution)/shard_map/ppermute | solution.py:630
  32.3 2.0 %collective-permute-start.23 = (bf16[1,288,256]{2,1,0:T(8,128)(2,1)S(1)}, bf16[1,288,256]{2,1,0:T(8,128)(2,1)S(1)}, u32[]{:S(2)}, u32[]{:S(2)}) collective-permute-start(bf16[1,288,256]{2,1,0:T(8,128)(2,1)S(1)} %collective-permute-done.21.refs_0_), channel_id=1, source_target_pairs={{0,2},{1,3},{2,0},{3,1},{4,6},{5,7},{6,4},{7,5},{8,10},{9,11},{10,... | collective-permute-start | bytes 442376 | tf_op jit(solution)/shard_map/ppermute | solution.py:630
  34.3 1.1 %collective-permute-done.22.refs_1_ = bf16[1,288,256]{2,1,0:T(8,128)(2,1)S(1)} collective-permute-done((bf16[1,288,256]{2,1,0:T(8,128)(2,1)S(1)}, bf16[1,288,256]{2,1,0:T(8,128)(2,1)S(1)}, u32[]{:S(2)}, u32[]{:S(2)}) %collective-permute-start.22) | collective-permute-done | bytes 147488 | tf_op jit(solution)/shard_map/ppermute | solution.py:630
  35.4 3.6 %collective-permute-done.17.refs_2_ = bf16[1,288,256]{2,1,0:T(8,128)(2,1)S(1)} collective-permute-done((bf16[1,288,256]{2,1,0:T(8,128)(2,1)S(1)}, bf16[1,288,256]{2,1,0:T(8,128)(2,1)S(1)}, u32[]{:S(2)}, u32[]{:S(2)}) %collective-permute-start.17) | collective-permute-done | bytes 147488 | tf_op jit(solution)/shard_map/ppermute | solution.py:630
  39.0 1.5 %collective-permute-start.9 = (bf16[3,2,144,256]{3,2,1,0:T(8,128)(2,1)S(1)}, bf16[3,2,144,256]{3,2,1,0:T(8,128)(2,1)S(1)}, u32[]{:S(2)}, u32[]{:S(2)}) collective-permute-start(bf16[3,2,144,256]{3,2,1,0:T(8,128)(2,1)S(1)} %stack.21.refs_2_), channel_id=1, source_target_pairs={{0,16},{1,9},{2,18},{3,11},{4,20},{5,13},{6,22},{7,15},{8,24},{9,1... | collective-permute-start | bytes 1327112 | tf_op jit(solution)/shard_map/ppermute | solution.py:630
  40.8 1.1 %collective-permute-start.18 = (bf16[3,1,288,256]{3,2,1,0:T(8,128)(2,1)S(1)}, bf16[3,1,288,256]{3,2,1,0:T(8,128)(2,1)S(1)}, u32[]{:S(2)}, u32[]{:S(2)}) collective-permute-start(bf16[3,1,288,256]{3,2,1,0:T(8,128)(2,1)S(1)} %stack.22.refs_2_), channel_id=1, source_target_pairs={{0,8},{1,17},{2,10},{3,19},{4,12},{5,21},{6,14},{7,23},{8,0},{9,25... | collective-permute-start | bytes 1327112 | tf_op jit(solution)/shard_map/ppermute | solution.py:630
  41.9 1.3 %collective-permute-start.10 = (bf16[3,2,144,256]{3,2,1,0:T(8,128)(2,1)S(1)}, bf16[3,2,144,256]{3,2,1,0:T(8,128)(2,1)S(1)}, u32[]{:S(2)}, u32[]{:S(2)}) collective-permute-start(bf16[3,2,144,256]{3,2,1,0:T(8,128)(2,1)S(1)} %collective-permute-done.8.refs_3_), channel_id=1, source_target_pairs={{0,16},{1,9},{2,18},{3,11},{4,20},{5,13},{6,22},{7,15},{8,24},{9,1... | collective-permute-start | bytes 1327112 | tf_op jit(solution)/shard_map/ppermute | solution.py:630
  43.3 7.3 %collective-permute-done.9.refs_4_ = bf16[3,2,144,256]{3,2,1,0:T(8,128)(2,1)S(1)} collective-permute-done((bf16[3,2,144,256]{3,2,1,0:T(8,128)(2,1)S(1)}, bf16[3,2,144,256]{3,2,1,0:T(8,128)(2,1)S(1)}, u32[]{:S(2)}, u32[]{:S(2)}) %collective-permute-start.9) | collective-permute-done | bytes 442400 | tf_op jit(solution)/shard_map/ppermute | solution.py:630
  50.6 1.4 %collective-permute-start.24 = (bf16[3,1,288,256]{3,2,1,0:T(8,128)(2,1)S(1)}, bf16[3,1,288,256]{3,2,1,0:T(8,128)(2,1)S(1)}, u32[]{:S(2)}, u32[]{:S(2)}) collective-permute-start(bf16[3,1,288,256]{3,2,1,0:T(8,128)(2,1)S(1)} %stack.23.refs_2_), channel_id=1, source_target_pairs={{0,8},{1,17},{2,10},{3,19},{4,12},{5,21},{6,14},{7,23},{8,0},{9,25... | collective-permute-start | bytes 1327112 | tf_op jit(solution)/shard_map/ppermute | solution.py:630
  52.0 1.3 %collective-permute-done.18.refs_3_ = bf16[3,1,288,256]{3,2,1,0:T(8,128)(2,1)S(1)} collective-permute-done((bf16[3,1,288,256]{3,2,1,0:T(8,128)(2,1)S(1)}, bf16[3,1,288,256]{3,2,1,0:T(8,128)(2,1)S(1)}, u32[]{:S(2)}, u32[]{:S(2)}) %collective-permute-start.18) | collective-permute-done | bytes 442400 | tf_op jit(solution)/shard_map/ppermute | solution.py:630
  53.6 6.6 %collective-permute-done.10.refs_5_ = bf16[3,2,144,256]{3,2,1,0:T(8,128)(2,1)S(1)} collective-permute-done((bf16[3,2,144,256]{3,2,1,0:T(8,128)(2,1)S(1)}, bf16[3,2,144,256]{3,2,1,0:T(8,128)(2,1)S(1)}, u32[]{:S(2)}, u32[]{:S(2)}) %collective-permute-start.10) | collective-permute-done | bytes 442400 | tf_op jit(solution)/shard_map/ppermute | solution.py:630
  60.1 1.2 %collective-permute-start.19 = (bf16[3,1,288,256]{3,2,1,0:T(8,128)(2,1)S(1)}, bf16[3,1,288,256]{3,2,1,0:T(8,128)(2,1)S(1)}, u32[]{:S(2)}, u32[]{:S(2)}) collective-permute-start(bf16[3,1,288,256]{3,2,1,0:T(8,128)(2,1)S(1)} %stack.22.refs_2_), channel_id=1, source_target_pairs={{0,1},{1,0},{2,3},{3,2},{4,5},{5,4},{6,7},{7,6},{8,9},{9,8},{10,11... | collective-permute-start | bytes 1327112 | tf_op jit(solution)/shard_map/ppermute | solution.py:630
  61.4 0.5 collective-permute-start.25
  61.9 5.1 %coarse.1 = (f32[2,12,2,48,128]{4,3,2,1,0:T(8,128)S(1)}, bf16[240,256]{1,0:T(8,128)(2,1)S(1)}) custom-call(s32[3]{0:T(128)S(1)} %copy-done.4, bf16[4,256,256]{2,1,0:T(8,128)(2,1)S(1)} %stack.20.mine, bf16[4,256,256]{2,1,0:T(8,128)(2,1)S(1)} %collective-permute-done.3.other, bf16[256,1024]{1,0:T(8,128)(2,1)S(1)} %copy-done.2, ...), custom_call_target="tpu_custom_call" | custom-call | flops 2000000000 | bytes 8000000 | tf_op jit(solution)/shard_map/coarse/pallas_call | solution.py:413
  67.1 4.4 %middle.1.map0 = f32[2,10,4,96,128]{4,3,2,1,0:T(8,128)S(1)} custom-call(s32[3]{0:T(128)S(1)} %copy-done.4, f32[2,12,2,48,128]{4,3,2,1,0:T(8,128)S(1)} %get-tuple-element.15.summed1, bf16[240,256]{1,0:T(8,128)(2,1)S(1)} %get-tuple-element.16.patch0, bf16[256,4096]{1,0:T(8,128)(2,1)S(1)} %copy-done.1, bf16[4,2,288,256]{3,2,1,0:T(8,128)(2,1)S(1)} %copy-done, ...), custom_call_target="tpu_custom_call" | custom-call | flops 3000000000 | bytes 6000000 | tf_op jit(solution)/shard_map/middle/pallas_call | solution.py:501
  71.6 9.3 %fine.1 = f32[8,6,256]{2,1,0:T(8,128)S(1)} custom-call(s32[3]{0:T(128)S(1)} %copy-done.4, f32[2,10,4,96,128]{4,3,2,1,0:T(8,128)S(1)} %middle.1.map0, bf16[256,128]{1,0:T(8,128)(2,1)S(1)} %copy-done.5, f32[1,128]{1,0:T(1,128)S(1)} %bitcast.14, s32[8,4,8]{2,1,0:T(4,128)S(1)} %copy-done.6, bf16[4,2,288,256]{3,2,1,0:T(8,128)(2,1)S(1)} %copy-done, ...), custom_call_target="tpu_custom_call" | custom-call | flops 6000000000 | bytes 8000000 | tf_op jit(solution)/shard_map/fine/pallas_call | solution.py:603
  80.9 8.8 %all_to_all.5 = f32[8,6,256]{2,1,0:T(8,128)S(1)} all-to-all(f32[8,6,256]{2,1,0:T(8,128)S(1)} %fine.1), channel_id=1, replica_groups=mesh['phase'=4,'dp'=8] {'dp'}, dimensions={0} | all-to-all | bytes 98304 | tf_op jit(solution)/shard_map/all_to_all | solution.py:704
  89.7 0.6 reduce_sum.9
  (51 shorter events, 1.2 us)
Async XLA Ops:
  0.9 16.2 %collective-permute-start.5 = (bf16[2,144,256]{2,1,0:T(8,128)(2,1)S(1)}, bf16[2,144,256]{2,1,0:T(8,128)(2,1)S(1)}, u32[]{:S(2)}, u32[]{:S(2)}) collective-permute-start(bf16[2,144,256]{2,1,0:T(8,128)(2,1)S(1)} %dynamic-slice_bitcast_fusion.2), channel_id=1, source_target_pairs={{0,4},{1,5},{2,6},{3,7},{4,0},{5,1},{6,2},{7,3},{8,12},{9,13},{10,... | collective-permute-start | bytes 442376 | tf_op jit(solution)/shard_map/ppermute | solution.py:630
  5.6 11.4 %copy-start = (bf16[4,2,288,256]{3,2,1,0:T(8,128)(2,1)S(1)}, bf16[4,2,288,256]{3,2,1,0:T(8,128)(2,1)}, u32[]{:S(2)}) copy-start(bf16[4,2,288,256]{3,2,1,0:T(8,128)(2,1)} %refs_0_.5) | copy-start | bytes 3538948
  11.9 5.7 %collective-permute-start = (bf16[256,256]{1,0:T(8,128)(2,1)}, bf16[256,256]{1,0:T(8,128)(2,1)S(1)}, u32[]{:S(2)}, u32[]{:S(2)}) collective-permute-start(bf16[256,256]{1,0:T(8,128)(2,1)} %get-tuple-element.12), channel_id=1, source_target_pairs={{0,8},{8,0},{16,24},{24,16},{1,9},{9,1},{17,25},{25,17},{2,10},{10... | collective-permute-start | bytes 393224 | tf_op jit(solution)/shard_map/ppermute | solution.py:698
  13.5 11.3 %collective-permute-start.6 = (bf16[2,144,256]{2,1,0:T(8,128)(2,1)S(1)}, bf16[2,144,256]{2,1,0:T(8,128)(2,1)S(1)}, u32[]{:S(2)}, u32[]{:S(2)}) collective-permute-start(bf16[2,144,256]{2,1,0:T(8,128)(2,1)S(1)} %dynamic-slice_bitcast_fusion.2), channel_id=1, source_target_pairs={{0,2},{1,3},{2,0},{3,1},{4,6},{5,7},{6,4},{7,5},{8,10},{9,11},{10,... | collective-permute-start | bytes 442376 | tf_op jit(solution)/shard_map/ppermute | solution.py:630
  15.1 8.0 %collective-permute-start.1 = (bf16[256,256]{1,0:T(8,128)(2,1)}, bf16[256,256]{1,0:T(8,128)(2,1)S(1)}, u32[]{:S(2)}, u32[]{:S(2)}) collective-permute-start(bf16[256,256]{1,0:T(8,128)(2,1)} %get-tuple-element.13), channel_id=1, source_target_pairs={{0,16},{8,24},{16,0},{24,8},{1,17},{9,25},{17,1},{25,9},{2,18},{10... | collective-permute-start | bytes 393224 | tf_op jit(solution)/shard_map/ppermute | solution.py:698
  16.4 7.1 %collective-permute-start.2 = (bf16[256,256]{1,0:T(8,128)(2,1)}, bf16[256,256]{1,0:T(8,128)(2,1)S(1)}, u32[]{:S(2)}, u32[]{:S(2)}) collective-permute-start(bf16[256,256]{1,0:T(8,128)(2,1)} %get-tuple-element.14), channel_id=1, source_target_pairs={{0,24},{8,16},{16,8},{24,0},{1,25},{9,17},{17,9},{25,1},{2,26},{10... | collective-permute-start | bytes 393224 | tf_op jit(solution)/shard_map/ppermute | solution.py:698
  17.1 9.8 %collective-permute-start.7 = (bf16[2,144,256]{2,1,0:T(8,128)(2,1)S(1)}, bf16[2,144,256]{2,1,0:T(8,128)(2,1)S(1)}, u32[]{:S(2)}, u32[]{:S(2)}) collective-permute-start(bf16[2,144,256]{2,1,0:T(8,128)(2,1)S(1)} %collective-permute-done.5.refs_0_), channel_id=1, source_target_pairs={{0,2},{1,3},{2,0},{3,1},{4,6},{5,7},{6,4},{7,5},{8,10},{9,11},{10,... | collective-permute-start | bytes 442376 | tf_op jit(solution)/shard_map/ppermute | solution.py:630
  17.6 9.3 %collective-permute-start.15 = (bf16[1,288,256]{2,1,0:T(8,128)(2,1)S(1)}, bf16[1,288,256]{2,1,0:T(8,128)(2,1)S(1)}, u32[]{:S(2)}, u32[]{:S(2)}) collective-permute-start(bf16[1,288,256]{2,1,0:T(8,128)(2,1)S(1)} %get-tuple-element.18), channel_id=1, source_target_pairs={{0,4},{1,5},{2,6},{3,7},{4,0},{5,1},{6,2},{7,3},{8,12},{9,13},{10,... | collective-permute-start | bytes 442376 | tf_op jit(solution)/shard_map/ppermute | solution.py:630
  23.0 9.2 %collective-permute-start.16 = (bf16[1,288,256]{2,1,0:T(8,128)(2,1)S(1)}, bf16[1,288,256]{2,1,0:T(8,128)(2,1)S(1)}, u32[]{:S(2)}, u32[]{:S(2)}) collective-permute-start(bf16[1,288,256]{2,1,0:T(8,128)(2,1)S(1)} %get-tuple-element.18), channel_id=1, source_target_pairs={{0,2},{1,3},{2,0},{3,1},{4,6},{5,7},{6,4},{7,5},{8,10},{9,11},{10,... | collective-permute-start | bytes 442376 | tf_op jit(solution)/shard_map/ppermute | solution.py:630
  23.5 8.8 %collective-permute-start.21 = (bf16[1,288,256]{2,1,0:T(8,128)(2,1)S(1)}, bf16[1,288,256]{2,1,0:T(8,128)(2,1)S(1)}, u32[]{:S(2)}, u32[]{:S(2)}) collective-permute-start(bf16[1,288,256]{2,1,0:T(8,128)(2,1)S(1)} %get-tuple-element.17), channel_id=1, source_target_pairs={{0,4},{1,5},{2,6},{3,7},{4,0},{5,1},{6,2},{7,3},{8,12},{9,13},{10,... | collective-permute-start | bytes 442376 | tf_op jit(solution)/shard_map/ppermute | solution.py:630
  24.8 37.2 %copy-start.2 = (bf16[256,1024]{1,0:T(8,128)(2,1)S(1)}, bf16[256,1024]{1,0:T(8,128)(2,1)}, u32[]{:S(2)}) copy-start(bf16[256,1024]{1,0:T(8,128)(2,1)} %expand_two.1) | copy-start | bytes 1572868
  24.8 37.2 %copy-start.4 = (s32[3]{0:T(128)S(1)}, s32[3]{0:T(128)}, u32[]{:S(2)}) copy-start(s32[3]{0:T(128)} %pad_add_fusion.where) | copy-start | bytes 40
  24.8 16.0 %collective-permute-start.3 = (bf16[4,256,256]{2,1,0:T(8,128)(2,1)S(1)}, bf16[4,256,256]{2,1,0:T(8,128)(2,1)S(1)}, u32[]{:S(2)}, u32[]{:S(2)}) collective-permute-start(bf16[4,256,256]{2,1,0:T(8,128)(2,1)S(1)} %stack.20.mine), channel_id=1, source_target_pairs={{0,1},{1,0},{2,3},{3,2},{4,5},{5,4},{6,7},{7,6},{8,9},{9,8},{10,11... | collective-permute-start | bytes 1572872 | tf_op jit(solution)/shard_map/ppermute | solution.py:700
  26.8 8.6 %collective-permute-start.22 = (bf16[1,288,256]{2,1,0:T(8,128)(2,1)S(1)}, bf16[1,288,256]{2,1,0:T(8,128)(2,1)S(1)}, u32[]{:S(2)}, u32[]{:S(2)}) collective-permute-start(bf16[1,288,256]{2,1,0:T(8,128)(2,1)S(1)} %get-tuple-element.17), channel_id=1, source_target_pairs={{0,2},{1,3},{2,0},{3,1},{4,6},{5,7},{6,4},{7,5},{8,10},{9,11},{10,... | collective-permute-start | bytes 442376 | tf_op jit(solution)/shard_map/ppermute | solution.py:630
  26.9 15.0 %collective-permute-start.8 = (bf16[3,2,144,256]{3,2,1,0:T(8,128)(2,1)S(1)}, bf16[3,2,144,256]{3,2,1,0:T(8,128)(2,1)S(1)}, u32[]{:S(2)}, u32[]{:S(2)}) collective-permute-start(bf16[3,2,144,256]{3,2,1,0:T(8,128)(2,1)S(1)} %stack.21.refs_2_), channel_id=1, source_target_pairs={{0,8},{1,17},{2,10},{3,19},{4,12},{5,21},{6,14},{7,23},{8,0},{9,25... | collective-permute-start | bytes 1327112 | tf_op jit(solution)/shard_map/ppermute | solution.py:630
  32.3 6.7 %collective-permute-start.17 = (bf16[1,288,256]{2,1,0:T(8,128)(2,1)S(1)}, bf16[1,288,256]{2,1,0:T(8,128)(2,1)S(1)}, u32[]{:S(2)}, u32[]{:S(2)}) collective-permute-start(bf16[1,288,256]{2,1,0:T(8,128)(2,1)S(1)} %collective-permute-done.15.refs_0_), channel_id=1, source_target_pairs={{0,2},{1,3},{2,0},{3,1},{4,6},{5,7},{6,4},{7,5},{8,10},{9,11},{10,... | collective-permute-start | bytes 442376 | tf_op jit(solution)/shard_map/ppermute | solution.py:630
  32.3 8.5 %collective-permute-start.23 = (bf16[1,288,256]{2,1,0:T(8,128)(2,1)S(1)}, bf16[1,288,256]{2,1,0:T(8,128)(2,1)S(1)}, u32[]{:S(2)}, u32[]{:S(2)}) collective-permute-start(bf16[1,288,256]{2,1,0:T(8,128)(2,1)S(1)} %collective-permute-done.21.refs_0_), channel_id=1, source_target_pairs={{0,2},{1,3},{2,0},{3,1},{4,6},{5,7},{6,4},{7,5},{8,10},{9,11},{10,... | collective-permute-start | bytes 442376 | tf_op jit(solution)/shard_map/ppermute | solution.py:630
  35.4 26.4 %collective-permute-start.4 = (bf16[4,2,288,256]{3,2,1,0:T(8,128)(2,1)S(1)}, bf16[4,2,288,256]{3,2,1,0:T(8,128)(2,1)S(1)}, u32[]{:S(2)}, u32[]{:S(2)}) collective-permute-start(bf16[4,2,288,256]{3,2,1,0:T(8,128)(2,1)S(1)} %copy-done), channel_id=1, source_target_pairs={{0,1},{1,0},{2,3},{3,2},{4,5},{5,4},{6,7},{7,6},{8,9},{9,8},{10,11... | collective-permute-start | bytes 3538952 | tf_op jit(solution)/shard_map/ppermute | solution.py:630
  39.0 11.6 %collective-permute-start.9 = (bf16[3,2,144,256]{3,2,1,0:T(8,128)(2,1)S(1)}, bf16[3,2,144,256]{3,2,1,0:T(8,128)(2,1)S(1)}, u32[]{:S(2)}, u32[]{:S(2)}) collective-permute-start(bf16[3,2,144,256]{3,2,1,0:T(8,128)(2,1)S(1)} %stack.21.refs_2_), channel_id=1, source_target_pairs={{0,16},{1,9},{2,18},{3,11},{4,20},{5,13},{6,22},{7,15},{8,24},{9,1... | collective-permute-start | bytes 1327112 | tf_op jit(solution)/shard_map/ppermute | solution.py:630
  40.7 11.3 %collective-permute-start.11 = (bf16[3,2,144,256]{3,2,1,0:T(8,128)(2,1)S(1)}, bf16[3,2,144,256]{3,2,1,0:T(8,128)(2,1)S(1)}, u32[]{:S(2)}, u32[]{:S(2)}) collective-permute-start(bf16[3,2,144,256]{3,2,1,0:T(8,128)(2,1)S(1)} %stack.21.refs_2_), channel_id=1, source_target_pairs={{0,1},{1,0},{2,3},{3,2},{4,5},{5,4},{6,7},{7,6},{8,9},{9,8},{10,11... | collective-permute-start | bytes 1327112 | tf_op jit(solution)/shard_map/ppermute | solution.py:630
  40.8 12.5 %collective-permute-start.18 = (bf16[3,1,288,256]{3,2,1,0:T(8,128)(2,1)S(1)}, bf16[3,1,288,256]{3,2,1,0:T(8,128)(2,1)S(1)}, u32[]{:S(2)}, u32[]{:S(2)}) collective-permute-start(bf16[3,1,288,256]{3,2,1,0:T(8,128)(2,1)S(1)} %stack.22.refs_2_), channel_id=1, source_target_pairs={{0,8},{1,17},{2,10},{3,19},{4,12},{5,21},{6,14},{7,23},{8,0},{9,25... | collective-permute-start | bytes 1327112 | tf_op jit(solution)/shard_map/ppermute | solution.py:630
  41.9 18.2 %collective-permute-start.10 = (bf16[3,2,144,256]{3,2,1,0:T(8,128)(2,1)S(1)}, bf16[3,2,144,256]{3,2,1,0:T(8,128)(2,1)S(1)}, u32[]{:S(2)}, u32[]{:S(2)}) collective-permute-start(bf16[3,2,144,256]{3,2,1,0:T(8,128)(2,1)S(1)} %collective-permute-done.8.refs_3_), channel_id=1, source_target_pairs={{0,16},{1,9},{2,18},{3,11},{4,20},{5,13},{6,22},{7,15},{8,24},{9,1... | collective-permute-start | bytes 1327112 | tf_op jit(solution)/shard_map/ppermute | solution.py:630
  43.3 23.8 %copy-start.1 = (bf16[256,4096]{1,0:T(8,128)(2,1)S(1)}, bf16[256,4096]{1,0:T(8,128)(2,1)}, u32[]{:S(2)}) copy-start(bf16[256,4096]{1,0:T(8,128)(2,1)} %expand_four.1) | copy-start | bytes 6291460
  50.6 9.5 %collective-permute-start.24 = (bf16[3,1,288,256]{3,2,1,0:T(8,128)(2,1)S(1)}, bf16[3,1,288,256]{3,2,1,0:T(8,128)(2,1)S(1)}, u32[]{:S(2)}, u32[]{:S(2)}) collective-permute-start(bf16[3,1,288,256]{3,2,1,0:T(8,128)(2,1)S(1)} %stack.23.refs_2_), channel_id=1, source_target_pairs={{0,8},{1,17},{2,10},{3,19},{4,12},{5,21},{6,14},{7,23},{8,0},{9,25... | collective-permute-start | bytes 1327112 | tf_op jit(solution)/shard_map/ppermute | solution.py:630
  52.0 9.3 %collective-permute-start.12 = (bf16[3,2,144,256]{3,2,1,0:T(8,128)(2,1)S(1)}, bf16[3,2,144,256]{3,2,1,0:T(8,128)(2,1)S(1)}, u32[]{:S(2)}, u32[]{:S(2)}) collective-permute-start(bf16[3,2,144,256]{3,2,1,0:T(8,128)(2,1)S(1)} %collective-permute-done.8.refs_3_), channel_id=1, source_target_pairs={{0,1},{1,0},{2,3},{3,2},{4,5},{5,4},{6,7},{7,6},{8,9},{9,8},{10,11... | collective-permute-start | bytes 1327112 | tf_op jit(solution)/shard_map/ppermute | solution.py:630
  53.3 8.1 %collective-permute-start.13 = (bf16[3,2,144,256]{3,2,1,0:T(8,128)(2,1)S(1)}, bf16[3,2,144,256]{3,2,1,0:T(8,128)(2,1)S(1)}, u32[]{:S(2)}, u32[]{:S(2)}) collective-permute-start(bf16[3,2,144,256]{3,2,1,0:T(8,128)(2,1)S(1)} %collective-permute-done.9.refs_4_), channel_id=1, source_target_pairs={{0,1},{1,0},{2,3},{3,2},{4,5},{5,4},{6,7},{7,6},{8,9},{9,8},{10,11... | collective-permute-start | bytes 1327112 | tf_op jit(solution)/shard_map/ppermute | solution.py:630
  60.1 1.8 %collective-permute-start.14 = (bf16[3,2,144,256]{3,2,1,0:T(8,128)(2,1)S(1)}, bf16[3,2,144,256]{3,2,1,0:T(8,128)(2,1)S(1)}, u32[]{:S(2)}, u32[]{:S(2)}) collective-permute-start(bf16[3,2,144,256]{3,2,1,0:T(8,128)(2,1)S(1)} %collective-permute-done.10.refs_5_), channel_id=1, source_target_pairs={{0,1},{1,0},{2,3},{3,2},{4,5},{5,4},{6,7},{7,6},{8,9},{9,8},{10,11... | collective-permute-start | bytes 1327112 | tf_op jit(solution)/shard_map/ppermute | solution.py:630
  60.1 6.9 %collective-permute-start.19 = (bf16[3,1,288,256]{3,2,1,0:T(8,128)(2,1)S(1)}, bf16[3,1,288,256]{3,2,1,0:T(8,128)(2,1)S(1)}, u32[]{:S(2)}, u32[]{:S(2)}) collective-permute-start(bf16[3,1,288,256]{3,2,1,0:T(8,128)(2,1)S(1)} %stack.22.refs_2_), channel_id=1, source_target_pairs={{0,1},{1,0},{2,3},{3,2},{4,5},{5,4},{6,7},{7,6},{8,9},{9,8},{10,11... | collective-permute-start | bytes 1327112 | tf_op jit(solution)/shard_map/ppermute | solution.py:630
  61.3 5.7 %collective-permute-start.20 = (bf16[3,1,288,256]{3,2,1,0:T(8,128)(2,1)S(1)}, bf16[3,1,288,256]{3,2,1,0:T(8,128)(2,1)S(1)}, u32[]{:S(2)}, u32[]{:S(2)}) collective-permute-start(bf16[3,1,288,256]{3,2,1,0:T(8,128)(2,1)S(1)} %collective-permute-done.18.refs_3_), channel_id=1, source_target_pairs={{0,1},{1,0},{2,3},{3,2},{4,5},{5,4},{6,7},{7,6},{8,9},{9,8},{10,11... | collective-permute-start | bytes 1327112 | tf_op jit(solution)/shard_map/ppermute | solution.py:630
  61.4 10.2 %collective-permute-start.25 = (bf16[3,1,288,256]{3,2,1,0:T(8,128)(2,1)S(1)}, bf16[3,1,288,256]{3,2,1,0:T(8,128)(2,1)S(1)}, u32[]{:S(2)}, u32[]{:S(2)}) collective-permute-start(bf16[3,1,288,256]{3,2,1,0:T(8,128)(2,1)S(1)} %stack.23.refs_2_), channel_id=1, source_target_pairs={{0,1},{1,0},{2,3},{3,2},{4,5},{5,4},{6,7},{7,6},{8,9},{9,8},{10,11... | collective-permute-start | bytes 1327112 | tf_op jit(solution)/shard_map/ppermute | solution.py:630
  61.9 9.7 %collective-permute-start.26 = (bf16[3,1,288,256]{3,2,1,0:T(8,128)(2,1)S(1)}, bf16[3,1,288,256]{3,2,1,0:T(8,128)(2,1)S(1)}, u32[]{:S(2)}, u32[]{:S(2)}) collective-permute-start(bf16[3,1,288,256]{3,2,1,0:T(8,128)(2,1)S(1)} %collective-permute-done.24.refs_3_), channel_id=1, source_target_pairs={{0,1},{1,0},{2,3},{3,2},{4,5},{5,4},{6,7},{7,6},{8,9},{9,8},{10,11... | collective-permute-start | bytes 1327112 | tf_op jit(solution)/shard_map/ppermute | solution.py:630
  67.1 4.5 %copy-start.5 = (bf16[256,128]{1,0:T(8,128)(2,1)S(1)}, bf16[256,128]{1,0:T(8,128)(2,1)}, u32[]{:S(2)}) copy-start(bf16[256,128]{1,0:T(8,128)(2,1)} %head.1) | copy-start | bytes 196612
  (3 other events, 9.8 us)

commit v9 on v8

--- a/solution.py
+++ b/solution.py
@@ -517,13 +517,13 @@
     )(where, summed1, patch0, expand_four, *filters)
 
 
-FINE_SCRATCH = 7
-
-
-def fine_kernel(plan, where, map0, head, vector, tile_slot, *refs):
-    count = len(refs) - FINE_SCRATCH
-    filters = refs[:count]
-    portions, weight0, sems, first, second, by_col, by_row = refs[count:]
+FINE_SCRATCH = 6
+
+
+def fine_kernel(plan, dp_count, outputs, where, map0, head, vector, tile_slot, *refs):
+    count = len(refs) - FINE_SCRATCH - outputs
+    filters, portions = refs[:count], refs[count : count + outputs]
+    weight0, sems, first, second, by_col, by_row = refs[count + outputs :]
     ch = plan.ch
     phase, side = where[0], where[1]
     start_filters(filters, 0, weight0, sems)
@@ -585,26 +585,35 @@
         axis=1,
     )
 
-    count = portions.shape[0]
-    targets = tile_slot[2 * where[2] + side, pl.ds(phase, 1), :]
-    slot = lax.broadcasted_iota(jnp.int32, (SLOT_DEV, TILES_DEV), 0) + phase * count * SLOT_DEV
-    for d in range(count):
-        chosen = (slot + d * SLOT_DEV == targets).astype(F32)
+    chip = where[2]
+    targets = tile_slot[2 * chip + side, pl.ds(phase, 1), :]
+    slot = lax.broadcasted_iota(jnp.int32, (SLOT_DEV, TILES_DEV), 0)
+
+    def tile_sums(d):
+        chosen = (slot + (phase * dp_count + d) * SLOT_DEV == targets).astype(F32)
         total = chosen[:, 0:1] * tiles[0:1]
         for j in range(1, TILES_DEV):
             total += chosen[:, j : j + 1] * tiles[j : j + 1]
-        portions[d] = total
-
-
-def fine(plan, dp_count, where, summed0, head, vector, tile_slot, filters):
+        return total
+
+    if outputs == 1:
+        for d in range(dp_count):
+            portions[0][d] = tile_sums(d)
+    else:
+        for i in range(dp_count // 2):
+            for ref, core in zip(portions, (side, 1 - side)):
+                ref[i] = tile_sums(2 * (chip ^ i) + core)
+
+
+def fine(plan, dp_count, outputs, where, summed0, head, vector, tile_slot, filters):
     ch = plan.ch
     vmem = pl.BlockSpec(memory_space=pltpu.VMEM)
     pixels = 16 * plan.block * plan.half // TILES_DEV
     return pl.pallas_call(
-        functools.partial(fine_kernel, plan),
-        out_shape=jax.ShapeDtypeStruct((dp_count, SLOT_DEV, pixels), F32),
+        functools.partial(fine_kernel, plan, dp_count, outputs),
+        out_shape=[jax.ShapeDtypeStruct((dp_count // outputs, SLOT_DEV, pixels), F32)] * outputs,
         in_specs=[pl.BlockSpec(memory_space=pltpu.SMEM)] + [vmem] * 4 + filter_specs(filters),
-        out_specs=vmem,
+        out_specs=[vmem] * outputs,
         scratch_shapes=[pltpu.VMEM((2, 9 * ch, ch), BF16), pltpu.SemaphoreType.DMA((2,))]
         + shifted_maps(plan.conv_cols, plan.conv_rows, ch)
         + [pltpu.VMEM((LANES, LANES), F32)] * 2,
@@ -663,6 +672,34 @@
             pieces += [second(column), second(one)]
         gathered.append(pieces + [swap(v) for v in pieces])
     return [filters, swapped], gathered
+
+
+def merge_kernel(kept, given, *outs):
+    for i, out in enumerate(outs):
+        out[...] = kept[i] + given[i]
+
+
+def gather_tiles(kept, given, dp_count):
+    def move(value, bits):
+        return lax.ppermute(value, "dp", [(d, d ^ bits) for d in range(dp_count)])
+
+    vmem = pl.BlockSpec(memory_space=pltpu.VMEM)
+    chips = dp_count // 2
+    sums = pl.pallas_call(
+        merge_kernel,
+        out_shape=[jax.ShapeDtypeStruct(kept.shape[1:], F32)] * chips,
+        in_specs=[vmem] * 2,
+        out_specs=[vmem] * chips,
+        compiler_params=pltpu.CompilerParams(vmem_limit_bytes=STACK_VMEM),
+        cost_estimate=pl.CostEstimate(
+            flops=kept.size, bytes_accessed=12 * kept.size, transcendentals=0
+        ),
+        name="merge",
+    )(kept, move(given, 1))
+    total = sums[0]
+    for i in CHIP_ORDER:
+        total += move(sums[i], 2 * i)
+    return total
 
 
 def by_permutes(phases, dp_count):
@@ -700,9 +737,13 @@
     other = lax.ppermute(mine, "dp", [(d, d ^ 1) for d in range(dp_count)])
     summed1, patch0 = coarse(plan, where, mine, other, expand_two, upper)
     summed0 = middle(plan, where, summed1, patch0, expand_four, medium)
-    partial = fine(plan, dp_count, where, summed0, head_matrix, head_vector, tile_slot, finer)
-    portions = lax.all_to_all(partial, "dp", split_axis=0, concat_axis=0, tiled=True)
-    return portions.sum(axis=0)
+    outputs = 2 if by_permutes(phases, dp_count) else 1
+    portions = fine(
+        plan, dp_count, outputs, where, summed0, head_matrix, head_vector, tile_slot, finer
+    )
+    if outputs == 2:
+        return gather_tiles(*portions, dp_count)
+    return lax.all_to_all(portions[0], "dp", split_axis=0, concat_axis=0, tiled=True).sum(axis=0)
 
 
 def solution(mesh):

time: 90.5 us -> 90.3 us (level)
  blocking collectives: 8.82 us -> 0 us
  starting transfers between devices: 22.5 us -> 27.4 us
  waiting for transfers between devices: 30.5 us -> 34.2 us
    all_to_all x1 -> x0, blocking collectives: 8.82 us -> none  [per_device(): lax.all_to_all(partial, 'dp', split_axis=0, concat_axis=0, tiled=True)]
    ppermute x0 -> x4, starting transfers between devices: none -> 4.9 us  [move(): return lax.ppermute(value, 'dp', [(d, d ^ bits) for d in range(dp_count)])]
    ppermute x0 -> x4, waiting for transfers between devices: none -> 3.75 us  [move(): return lax.ppermute(value, 'dp', [(d, d ^ bits) for d in range(dp_count)])]
    pallas_call x1 -> x2, Pallas kernels: 9.26 us -> 9.26 us  [the longest x1 9.26 us: fine(): pl.pallas_call(functools.partial(fine_kernel, plan, dp_count, outputs), o...]
  transfers between devices with their start and end apart: 27 -> 31, of which waited for: 9 -> 12; matrix products, arithmetic and copies ran while one was open for 1% -> 1% of each run, Pallas kernels for 18% -> 18%
where the time goes in v9:
time: 90.3 us; the launch traced here: 90.1 us
  waiting for transfers between devices  34.2 us (38%)
  starting transfers between devices  27.4 us (30%)
  Pallas kernels  25.2 us (28%)
  local copies, waits for them, and re-layouts  1.88 us (2%)
  other arithmetic  1.18 us (1%)
    ppermute x23, waiting for transfers between devices, move(): return lax.ppermute(value, axes, route)  25 us
    ppermute x23, starting transfers between devices, move(): return lax.ppermute(value, axes, route)  18.9 us
    pallas_call x1, Pallas kernels, fine(): pl.pallas_call(functools.partial(fine_kernel, plan, dp_count, outputs), o...  9.26 us
    pallas_call x1, Pallas kernels, project(): pl.pallas_call(functools.partial(project_kernel, plan, phases), in_specs=...  6.3 us
    ppermute x3, waiting for transfers between devices, per_device(): lax.ppermute(sent[k], 'phase', [(s, s ^ k) for s in range(phases)])  5.41 us
    pallas_call x1, Pallas kernels, coarse(): pl.pallas_call(functools.partial(coarse_kernel, plan), out_shape=[jax.Sha...  5.1 us
    ppermute x4, starting transfers between devices, move(): return lax.ppermute(value, 'dp', [(d, d ^ bits) for d in range(dp_count)])  4.9 us
    pallas_call x1, Pallas kernels, middle(): pl.pallas_call(functools.partial(middle_kernel, plan), out_shape=jax.Shap...  4.4 us
  transfers between devices with their start and end apart: 31, of which 12 were waited for; matrix products, arithmetic and copies ran while one was open for 1% of the time, Pallas kernels for 18%

profile of v9, /device:TPU:0, one launch (start us, length us, event | category | flops | bytes accessed | tf_op | source)
XLA Modules:
  0.0 90.1 jit_solution(5098161001664383076)
XLA Ops:
  0.0 0.9 %dynamic-slice_bitcast_fusion.2 = bf16[2,144,256]{2,1,0:T(8,128)(2,1)S(1)} fusion(bf16[4,4,144,256]{3,2,1,0:T(8,128)(2,1)} %bitcast.13, s32[]{:T(128)S(6)} %select_n.7), kind=kLoop, calls=%fused_computation.2 | loop fusion | bytes 294916 | tf_op jit(solution)/shard_map/squeeze | solution.py:663
  0.9 4.1 %collective-permute-start.5 = (bf16[2,144,256]{2,1,0:T(8,128)(2,1)S(1)}, bf16[2,144,256]{2,1,0:T(8,128)(2,1)S(1)}, u32[]{:S(2)}, u32[]{:S(2)}) collective-permute-start(bf16[2,144,256]{2,1,0:T(8,128)(2,1)S(1)} %dynamic-slice_bitcast_fusion.2), channel_id=1, source_target_pairs={{0,4},{1,5},{2,6},{3,7},{4,0},{5,1},{6,2},{7,3},{8,12},{9,13},{10,... | collective-permute-start | bytes 442376 | tf_op jit(solution)/shard_map/ppermute | solution.py:639
  5.1 0.6 pad_add_fusion.where
  5.6 6.3 %project.1 = (bf16[256,256]{1,0:T(8,128)(2,1)}, bf16[256,256]{1,0:T(8,128)(2,1)}, bf16[256,256]{1,0:T(8,128)(2,1)}, bf16[256,256]{1,0:T(8,128)(2,1)}) custom-call(s32[3]{0:T(128)} %pad_add_fusion.where, bf16[1,512,4096]{2,1,0:T(8,128)(2,1)} %tokens_hbm.1, bf16[1,4096,256]{2,1,0:T(8,128)(2,1)} %weight_hbm.1, bf16[1024,256]{1,0:T(8,128)(2,1)} %shrink_hbm.1), custom_call_target="tpu_custom_call" | custom-call | flops 1073741824 | bytes 6291456 | tf_op jit(solution)/shard_map/project/pallas_call | solution.py:139
  11.9 1.6 %collective-permute-start = (bf16[256,256]{1,0:T(8,128)(2,1)}, bf16[256,256]{1,0:T(8,128)(2,1)S(1)}, u32[]{:S(2)}, u32[]{:S(2)}) collective-permute-start(bf16[256,256]{1,0:T(8,128)(2,1)} %get-tuple-element.18), channel_id=1, source_target_pairs={{0,8},{8,0},{16,24},{24,16},{1,9},{9,1},{17,25},{25,17},{2,10},{10... | collective-permute-start | bytes 393224 | tf_op jit(solution)/shard_map/ppermute | solution.py:735
  13.5 1.6 %collective-permute-start.6 = (bf16[2,144,256]{2,1,0:T(8,128)(2,1)S(1)}, bf16[2,144,256]{2,1,0:T(8,128)(2,1)S(1)}, u32[]{:S(2)}, u32[]{:S(2)}) collective-permute-start(bf16[2,144,256]{2,1,0:T(8,128)(2,1)S(1)} %dynamic-slice_bitcast_fusion.2), channel_id=1, source_target_pairs={{0,2},{1,3},{2,0},{3,1},{4,6},{5,7},{6,4},{7,5},{8,10},{9,11},{10,... | collective-permute-start | bytes 442376 | tf_op jit(solution)/shard_map/ppermute | solution.py:639
  15.1 1.3 %collective-permute-start.1 = (bf16[256,256]{1,0:T(8,128)(2,1)}, bf16[256,256]{1,0:T(8,128)(2,1)S(1)}, u32[]{:S(2)}, u32[]{:S(2)}) collective-permute-start(bf16[256,256]{1,0:T(8,128)(2,1)} %get-tuple-element.19), channel_id=1, source_target_pairs={{0,16},{8,24},{16,0},{24,8},{1,17},{9,25},{17,1},{25,9},{2,18},{10... | collective-permute-start | bytes 393224 | tf_op jit(solution)/shard_map/ppermute | solution.py:735
  16.4 0.7 collective-permute-start.2
  17.7 5.4 %collective-permute-done.1.refs_2_ = bf16[256,256]{1,0:T(8,128)(2,1)S(1)} collective-permute-done((bf16[256,256]{1,0:T(8,128)(2,1)}, bf16[256,256]{1,0:T(8,128)(2,1)S(1)}, u32[]{:S(2)}, u32[]{:S(2)}) %collective-permute-start.1) | collective-permute-done | bytes 131104 | tf_op jit(solution)/shard_map/ppermute | solution.py:735
  23.8 0.9 %copy-done.3 = bf16[256,256]{1,0:T(8,128)(2,1)S(1)} copy-done((bf16[256,256]{1,0:T(8,128)(2,1)S(1)}, bf16[256,256]{1,0:T(8,128)(2,1)}, u32[]{:S(2)}) %copy-start.3) | copy-done | bytes 131096
  24.9 2.0 %collective-permute-done.7.refs_2_ = bf16[2,144,256]{2,1,0:T(8,128)(2,1)S(1)} collective-permute-done((bf16[2,144,256]{2,1,0:T(8,128)(2,1)S(1)}, bf16[2,144,256]{2,1,0:T(8,128)(2,1)S(1)}, u32[]{:S(2)}, u32[]{:S(2)}) %collective-permute-start.7) | collective-permute-done | bytes 147488 | tf_op jit(solution)/shard_map/ppermute | solution.py:639
  26.9 2.4 %collective-permute-start.8 = (bf16[3,2,144,256]{3,2,1,0:T(8,128)(2,1)S(1)}, bf16[3,2,144,256]{3,2,1,0:T(8,128)(2,1)S(1)}, u32[]{:S(2)}, u32[]{:S(2)}) collective-permute-start(bf16[3,2,144,256]{3,2,1,0:T(8,128)(2,1)S(1)} %stack.21.refs_2_), channel_id=1, source_target_pairs={{0,8},{1,17},{2,10},{3,19},{4,12},{5,21},{6,14},{7,23},{8,0},{9,25... | collective-permute-start | bytes 1327112 | tf_op jit(solution)/shard_map/ppermute | solution.py:639
  29.3 3.0 %collective-permute-done.16.refs_1_ = bf16[1,288,256]{2,1,0:T(8,128)(2,1)S(1)} collective-permute-done((bf16[1,288,256]{2,1,0:T(8,128)(2,1)S(1)}, bf16[1,288,256]{2,1,0:T(8,128)(2,1)S(1)}, u32[]{:S(2)}, u32[]{:S(2)}) %collective-permute-start.16) | collective-permute-done | bytes 147488 | tf_op jit(solution)/shard_map/ppermute | solution.py:639
  32.3 2.0 %collective-permute-start.23 = (bf16[1,288,256]{2,1,0:T(8,128)(2,1)S(1)}, bf16[1,288,256]{2,1,0:T(8,128)(2,1)S(1)}, u32[]{:S(2)}, u32[]{:S(2)}) collective-permute-start(bf16[1,288,256]{2,1,0:T(8,128)(2,1)S(1)} %collective-permute-done.21.refs_0_), channel_id=1, source_target_pairs={{0,2},{1,3},{2,0},{3,1},{4,6},{5,7},{6,4},{7,5},{8,10},{9,11},{10,... | collective-permute-start | bytes 442376 | tf_op jit(solution)/shard_map/ppermute | solution.py:639
  34.3 1.1 %collective-permute-done.22.refs_1_ = bf16[1,288,256]{2,1,0:T(8,128)(2,1)S(1)} collective-permute-done((bf16[1,288,256]{2,1,0:T(8,128)(2,1)S(1)}, bf16[1,288,256]{2,1,0:T(8,128)(2,1)S(1)}, u32[]{:S(2)}, u32[]{:S(2)}) %collective-permute-start.22) | collective-permute-done | bytes 147488 | tf_op jit(solution)/shard_map/ppermute | solution.py:639
  35.5 3.6 %collective-permute-done.17.refs_2_ = bf16[1,288,256]{2,1,0:T(8,128)(2,1)S(1)} collective-permute-done((bf16[1,288,256]{2,1,0:T(8,128)(2,1)S(1)}, bf16[1,288,256]{2,1,0:T(8,128)(2,1)S(1)}, u32[]{:S(2)}, u32[]{:S(2)}) %collective-permute-start.17) | collective-permute-done | bytes 147488 | tf_op jit(solution)/shard_map/ppermute | solution.py:639
  39.0 1.5 %collective-permute-start.9 = (bf16[3,2,144,256]{3,2,1,0:T(8,128)(2,1)S(1)}, bf16[3,2,144,256]{3,2,1,0:T(8,128)(2,1)S(1)}, u32[]{:S(2)}, u32[]{:S(2)}) collective-permute-start(bf16[3,2,144,256]{3,2,1,0:T(8,128)(2,1)S(1)} %stack.21.refs_2_), channel_id=1, source_target_pairs={{0,16},{1,9},{2,18},{3,11},{4,20},{5,13},{6,22},{7,15},{8,24},{9,1... | collective-permute-start | bytes 1327112 | tf_op jit(solution)/shard_map/ppermute | solution.py:639
  40.8 1.1 %collective-permute-start.18 = (bf16[3,1,288,256]{3,2,1,0:T(8,128)(2,1)S(1)}, bf16[3,1,288,256]{3,2,1,0:T(8,128)(2,1)S(1)}, u32[]{:S(2)}, u32[]{:S(2)}) collective-permute-start(bf16[3,1,288,256]{3,2,1,0:T(8,128)(2,1)S(1)} %stack.22.refs_2_), channel_id=1, source_target_pairs={{0,8},{1,17},{2,10},{3,19},{4,12},{5,21},{6,14},{7,23},{8,0},{9,25... | collective-permute-start | bytes 1327112 | tf_op jit(solution)/shard_map/ppermute | solution.py:639
  41.9 1.3 %collective-permute-start.10 = (bf16[3,2,144,256]{3,2,1,0:T(8,128)(2,1)S(1)}, bf16[3,2,144,256]{3,2,1,0:T(8,128)(2,1)S(1)}, u32[]{:S(2)}, u32[]{:S(2)}) collective-permute-start(bf16[3,2,144,256]{3,2,1,0:T(8,128)(2,1)S(1)} %collective-permute-done.8.refs_3_), channel_id=1, source_target_pairs={{0,16},{1,9},{2,18},{3,11},{4,20},{5,13},{6,22},{7,15},{8,24},{9,1... | collective-permute-start | bytes 1327112 | tf_op jit(solution)/shard_map/ppermute | solution.py:639
  43.3 7.3 %collective-permute-done.9.refs_4_ = bf16[3,2,144,256]{3,2,1,0:T(8,128)(2,1)S(1)} collective-permute-done((bf16[3,2,144,256]{3,2,1,0:T(8,128)(2,1)S(1)}, bf16[3,2,144,256]{3,2,1,0:T(8,128)(2,1)S(1)}, u32[]{:S(2)}, u32[]{:S(2)}) %collective-permute-start.9) | collective-permute-done | bytes 442400 | tf_op jit(solution)/shard_map/ppermute | solution.py:639
  50.7 1.4 %collective-permute-start.24 = (bf16[3,1,288,256]{3,2,1,0:T(8,128)(2,1)S(1)}, bf16[3,1,288,256]{3,2,1,0:T(8,128)(2,1)S(1)}, u32[]{:S(2)}, u32[]{:S(2)}) collective-permute-start(bf16[3,1,288,256]{3,2,1,0:T(8,128)(2,1)S(1)} %stack.23.refs_2_), channel_id=1, source_target_pairs={{0,8},{1,17},{2,10},{3,19},{4,12},{5,21},{6,14},{7,23},{8,0},{9,25... | collective-permute-start | bytes 1327112 | tf_op jit(solution)/shard_map/ppermute | solution.py:639
  52.1 1.3 %collective-permute-done.18.refs_3_ = bf16[3,1,288,256]{3,2,1,0:T(8,128)(2,1)S(1)} collective-permute-done((bf16[3,1,288,256]{3,2,1,0:T(8,128)(2,1)S(1)}, bf16[3,1,288,256]{3,2,1,0:T(8,128)(2,1)S(1)}, u32[]{:S(2)}, u32[]{:S(2)}) %collective-permute-start.18) | collective-permute-done | bytes 442400 | tf_op jit(solution)/shard_map/ppermute | solution.py:639
  53.6 6.6 %collective-permute-done.10.refs_5_ = bf16[3,2,144,256]{3,2,1,0:T(8,128)(2,1)S(1)} collective-permute-done((bf16[3,2,144,256]{3,2,1,0:T(8,128)(2,1)S(1)}, bf16[3,2,144,256]{3,2,1,0:T(8,128)(2,1)S(1)}, u32[]{:S(2)}, u32[]{:S(2)}) %collective-permute-start.10) | collective-permute-done | bytes 442400 | tf_op jit(solution)/shard_map/ppermute | solution.py:639
  60.1 1.2 %collective-permute-start.19 = (bf16[3,1,288,256]{3,2,1,0:T(8,128)(2,1)S(1)}, bf16[3,1,288,256]{3,2,1,0:T(8,128)(2,1)S(1)}, u32[]{:S(2)}, u32[]{:S(2)}) collective-permute-start(bf16[3,1,288,256]{3,2,1,0:T(8,128)(2,1)S(1)} %stack.22.refs_2_), channel_id=1, source_target_pairs={{0,1},{1,0},{2,3},{3,2},{4,5},{5,4},{6,7},{7,6},{8,9},{9,8},{10,11... | collective-permute-start | bytes 1327112 | tf_op jit(solution)/shard_map/ppermute | solution.py:639
  62.0 5.1 %coarse.1 = (f32[2,12,2,48,128]{4,3,2,1,0:T(8,128)S(1)}, bf16[240,256]{1,0:T(8,128)(2,1)S(1)}) custom-call(s32[3]{0:T(128)S(1)} %copy-done.4, bf16[4,256,256]{2,1,0:T(8,128)(2,1)S(1)} %stack.20.mine, bf16[4,256,256]{2,1,0:T(8,128)(2,1)S(1)} %collective-permute-done.3.other, bf16[256,1024]{1,0:T(8,128)(2,1)S(1)} %copy-done.2, ...), custom_call_target="tpu_custom_call" | custom-call | flops 2000000000 | bytes 8000000 | tf_op jit(solution)/shard_map/coarse/pallas_call | solution.py:413
  67.1 4.4 %middle.1.map0 = f32[2,10,4,96,128]{4,3,2,1,0:T(8,128)S(1)} custom-call(s32[3]{0:T(128)S(1)} %copy-done.4, f32[2,12,2,48,128]{4,3,2,1,0:T(8,128)S(1)} %get-tuple-element.21.summed1, bf16[240,256]{1,0:T(8,128)(2,1)S(1)} %get-tuple-element.22.patch0, bf16[256,4096]{1,0:T(8,128)(2,1)S(1)} %copy-done.1, bf16[4,2,288,256]{3,2,1,0:T(8,128)(2,1)S(1)} %copy-done, ...), custom_call_target="tpu_custom_call" | custom-call | flops 3000000000 | bytes 6000000 | tf_op jit(solution)/shard_map/middle/pallas_call | solution.py:501
  71.6 9.3 %fine.1 = (f32[4,6,256]{2,1,0:T(8,128)S(1)}, f32[4,6,256]{2,1,0:T(8,128)S(1)}) custom-call(s32[3]{0:T(128)S(1)} %copy-done.4, f32[2,10,4,96,128]{4,3,2,1,0:T(8,128)S(1)} %middle.1.map0, bf16[256,128]{1,0:T(8,128)(2,1)S(1)} %copy-done.5, f32[1,128]{1,0:T(1,128)S(1)} %bitcast.14, s32[8,4,8]{2,1,0:T(4,128)S(1)} %copy-done.6, ...), custom_call_target="tpu_custom_call" | custom-call | flops 6000000000 | bytes 8000000 | tf_op jit(solution)/shard_map/fine/pallas_call | solution.py:612
  81.4 0.9 collective-permute-done.27.given
  82.8 1.3 %collective-permute-start.29 = (f32[6,256]{1,0:T(8,128)S(1)}, f32[6,256]{1,0:T(8,128)S(1)}, u32[]{:S(2)}, u32[]{:S(2)}) collective-permute-start(f32[6,256]{1,0:T(8,128)S(1)} %get-tuple-element.27), channel_id=1, source_target_pairs={{0,2},{1,3},{2,0},{3,1},{4,6},{5,7},{6,4},{7,5},{8,10},{9,11},{10,... | collective-permute-start | bytes 18440 | tf_op jit(solution)/shard_map/ppermute | solution.py:684
  84.1 2.6 %collective-permute-start.30 = (f32[6,256]{1,0:T(8,128)S(1)}, f32[6,256]{1,0:T(8,128)S(1)}, u32[]{:S(2)}, u32[]{:S(2)}) collective-permute-start(f32[6,256]{1,0:T(8,128)S(1)} %get-tuple-element.28), channel_id=1, source_target_pairs={{0,6},{1,7},{2,4},{3,5},{4,2},{5,3},{6,0},{7,1},{8,14},{9,15},{10,... | collective-permute-start | bytes 18440 | tf_op jit(solution)/shard_map/ppermute | solution.py:684
  86.8 2.7 %collective-permute-done.30 = f32[6,256]{1,0:T(8,128)S(1)} collective-permute-done((f32[6,256]{1,0:T(8,128)S(1)}, f32[6,256]{1,0:T(8,128)S(1)}, u32[]{:S(2)}, u32[]{:S(2)}) %collective-permute-start.30) | collective-permute-done | bytes 6176 | tf_op jit(solution)/shard_map/ppermute | solution.py:684
  89.5 0.6 add_add_fusion
  (59 shorter events, 4.0 us)
Async XLA Ops:
  0.9 16.2 %collective-permute-start.5 = (bf16[2,144,256]{2,1,0:T(8,128)(2,1)S(1)}, bf16[2,144,256]{2,1,0:T(8,128)(2,1)S(1)}, u32[]{:S(2)}, u32[]{:S(2)}) collective-permute-start(bf16[2,144,256]{2,1,0:T(8,128)(2,1)S(1)} %dynamic-slice_bitcast_fusion.2), channel_id=1, source_target_pairs={{0,4},{1,5},{2,6},{3,7},{4,0},{5,1},{6,2},{7,3},{8,12},{9,13},{10,... | collective-permute-start | bytes 442376 | tf_op jit(solution)/shard_map/ppermute | solution.py:639
  11.9 5.7 %collective-permute-start = (bf16[256,256]{1,0:T(8,128)(2,1)}, bf16[256,256]{1,0:T(8,128)(2,1)S(1)}, u32[]{:S(2)}, u32[]{:S(2)}) collective-permute-start(bf16[256,256]{1,0:T(8,128)(2,1)} %get-tuple-element.18), channel_id=1, source_target_pairs={{0,8},{8,0},{16,24},{24,16},{1,9},{9,1},{17,25},{25,17},{2,10},{10... | collective-permute-start | bytes 393224 | tf_op jit(solution)/shard_map/ppermute | solution.py:735
  13.5 11.3 %collective-permute-start.6 = (bf16[2,144,256]{2,1,0:T(8,128)(2,1)S(1)}, bf16[2,144,256]{2,1,0:T(8,128)(2,1)S(1)}, u32[]{:S(2)}, u32[]{:S(2)}) collective-permute-start(bf16[2,144,256]{2,1,0:T(8,128)(2,1)S(1)} %dynamic-slice_bitcast_fusion.2), channel_id=1, source_target_pairs={{0,2},{1,3},{2,0},{3,1},{4,6},{5,7},{6,4},{7,5},{8,10},{9,11},{10,... | collective-permute-start | bytes 442376 | tf_op jit(solution)/shard_map/ppermute | solution.py:639
  15.1 8.0 %collective-permute-start.1 = (bf16[256,256]{1,0:T(8,128)(2,1)}, bf16[256,256]{1,0:T(8,128)(2,1)S(1)}, u32[]{:S(2)}, u32[]{:S(2)}) collective-permute-start(bf16[256,256]{1,0:T(8,128)(2,1)} %get-tuple-element.19), channel_id=1, source_target_pairs={{0,16},{8,24},{16,0},{24,8},{1,17},{9,25},{17,1},{25,9},{2,18},{10... | collective-permute-start | bytes 393224 | tf_op jit(solution)/shard_map/ppermute | solution.py:735
  16.4 7.1 %collective-permute-start.2 = (bf16[256,256]{1,0:T(8,128)(2,1)}, bf16[256,256]{1,0:T(8,128)(2,1)S(1)}, u32[]{:S(2)}, u32[]{:S(2)}) collective-permute-start(bf16[256,256]{1,0:T(8,128)(2,1)} %get-tuple-element.20), channel_id=1, source_target_pairs={{0,24},{8,16},{16,8},{24,0},{1,25},{9,17},{17,9},{25,1},{2,26},{10... | collective-permute-start | bytes 393224 | tf_op jit(solution)/shard_map/ppermute | solution.py:735
  17.1 9.7 %collective-permute-start.7 = (bf16[2,144,256]{2,1,0:T(8,128)(2,1)S(1)}, bf16[2,144,256]{2,1,0:T(8,128)(2,1)S(1)}, u32[]{:S(2)}, u32[]{:S(2)}) collective-permute-start(bf16[2,144,256]{2,1,0:T(8,128)(2,1)S(1)} %collective-permute-done.5.refs_0_), channel_id=1, source_target_pairs={{0,2},{1,3},{2,0},{3,1},{4,6},{5,7},{6,4},{7,5},{8,10},{9,11},{10,... | collective-permute-start | bytes 442376 | tf_op jit(solution)/shard_map/ppermute | solution.py:639
  17.6 9.3 %collective-permute-start.15 = (bf16[1,288,256]{2,1,0:T(8,128)(2,1)S(1)}, bf16[1,288,256]{2,1,0:T(8,128)(2,1)S(1)}, u32[]{:S(2)}, u32[]{:S(2)}) collective-permute-start(bf16[1,288,256]{2,1,0:T(8,128)(2,1)S(1)} %get-tuple-element.30), channel_id=1, source_target_pairs={{0,4},{1,5},{2,6},{3,7},{4,0},{5,1},{6,2},{7,3},{8,12},{9,13},{10,... | collective-permute-start | bytes 442376 | tf_op jit(solution)/shard_map/ppermute | solution.py:639
  23.1 9.2 %collective-permute-start.16 = (bf16[1,288,256]{2,1,0:T(8,128)(2,1)S(1)}, bf16[1,288,256]{2,1,0:T(8,128)(2,1)S(1)}, u32[]{:S(2)}, u32[]{:S(2)}) collective-permute-start(bf16[1,288,256]{2,1,0:T(8,128)(2,1)S(1)} %get-tuple-element.30), channel_id=1, source_target_pairs={{0,2},{1,3},{2,0},{3,1},{4,6},{5,7},{6,4},{7,5},{8,10},{9,11},{10,... | collective-permute-start | bytes 442376 | tf_op jit(solution)/shard_map/ppermute | solution.py:639
  23.5 8.8 %collective-permute-start.21 = (bf16[1,288,256]{2,1,0:T(8,128)(2,1)S(1)}, bf16[1,288,256]{2,1,0:T(8,128)(2,1)S(1)}, u32[]{:S(2)}, u32[]{:S(2)}) collective-permute-start(bf16[1,288,256]{2,1,0:T(8,128)(2,1)S(1)} %get-tuple-element.29), channel_id=1, source_target_pairs={{0,4},{1,5},{2,6},{3,7},{4,0},{5,1},{6,2},{7,3},{8,12},{9,13},{10,... | collective-permute-start | bytes 442376 | tf_op jit(solution)/shard_map/ppermute | solution.py:639
  24.8 37.2 %copy-start.2 = (bf16[256,1024]{1,0:T(8,128)(2,1)S(1)}, bf16[256,1024]{1,0:T(8,128)(2,1)}, u32[]{:S(2)}) copy-start(bf16[256,1024]{1,0:T(8,128)(2,1)} %expand_two.1) | copy-start | bytes 1572868
  24.8 16.0 %collective-permute-start.3 = (bf16[4,256,256]{2,1,0:T(8,128)(2,1)S(1)}, bf16[4,256,256]{2,1,0:T(8,128)(2,1)S(1)}, u32[]{:S(2)}, u32[]{:S(2)}) collective-permute-start(bf16[4,256,256]{2,1,0:T(8,128)(2,1)S(1)} %stack.20.mine), channel_id=1, source_target_pairs={{0,1},{1,0},{2,3},{3,2},{4,5},{5,4},{6,7},{7,6},{8,9},{9,8},{10,11... | collective-permute-start | bytes 1572872 | tf_op jit(solution)/shard_map/ppermute | solution.py:737
  26.9 8.6 %collective-permute-start.22 = (bf16[1,288,256]{2,1,0:T(8,128)(2,1)S(1)}, bf16[1,288,256]{2,1,0:T(8,128)(2,1)S(1)}, u32[]{:S(2)}, u32[]{:S(2)}) collective-permute-start(bf16[1,288,256]{2,1,0:T(8,128)(2,1)S(1)} %get-tuple-element.29), channel_id=1, source_target_pairs={{0,2},{1,3},{2,0},{3,1},{4,6},{5,7},{6,4},{7,5},{8,10},{9,11},{10,... | collective-permute-start | bytes 442376 | tf_op jit(solution)/shard_map/ppermute | solution.py:639
  26.9 15.0 %collective-permute-start.8 = (bf16[3,2,144,256]{3,2,1,0:T(8,128)(2,1)S(1)}, bf16[3,2,144,256]{3,2,1,0:T(8,128)(2,1)S(1)}, u32[]{:S(2)}, u32[]{:S(2)}) collective-permute-start(bf16[3,2,144,256]{3,2,1,0:T(8,128)(2,1)S(1)} %stack.21.refs_2_), channel_id=1, source_target_pairs={{0,8},{1,17},{2,10},{3,19},{4,12},{5,21},{6,14},{7,23},{8,0},{9,25... | collective-permute-start | bytes 1327112 | tf_op jit(solution)/shard_map/ppermute | solution.py:639
  32.3 6.7 %collective-permute-start.17 = (bf16[1,288,256]{2,1,0:T(8,128)(2,1)S(1)}, bf16[1,288,256]{2,1,0:T(8,128)(2,1)S(1)}, u32[]{:S(2)}, u32[]{:S(2)}) collective-permute-start(bf16[1,288,256]{2,1,0:T(8,128)(2,1)S(1)} %collective-permute-done.15.refs_0_), channel_id=1, source_target_pairs={{0,2},{1,3},{2,0},{3,1},{4,6},{5,7},{6,4},{7,5},{8,10},{9,11},{10,... | collective-permute-start | bytes 442376 | tf_op jit(solution)/shard_map/ppermute | solution.py:639
  32.3 8.5 %collective-permute-start.23 = (bf16[1,288,256]{2,1,0:T(8,128)(2,1)S(1)}, bf16[1,288,256]{2,1,0:T(8,128)(2,1)S(1)}, u32[]{:S(2)}, u32[]{:S(2)}) collective-permute-start(bf16[1,288,256]{2,1,0:T(8,128)(2,1)S(1)} %collective-permute-done.21.refs_0_), channel_id=1, source_target_pairs={{0,2},{1,3},{2,0},{3,1},{4,6},{5,7},{6,4},{7,5},{8,10},{9,11},{10,... | collective-permute-start | bytes 442376 | tf_op jit(solution)/shard_map/ppermute | solution.py:639
  35.5 26.4 %collective-permute-start.4 = (bf16[4,2,288,256]{3,2,1,0:T(8,128)(2,1)S(1)}, bf16[4,2,288,256]{3,2,1,0:T(8,128)(2,1)S(1)}, u32[]{:S(2)}, u32[]{:S(2)}) collective-permute-start(bf16[4,2,288,256]{3,2,1,0:T(8,128)(2,1)S(1)} %copy-done), channel_id=1, source_target_pairs={{0,1},{1,0},{2,3},{3,2},{4,5},{5,4},{6,7},{7,6},{8,9},{9,8},{10,11... | collective-permute-start | bytes 3538952 | tf_op jit(solution)/shard_map/ppermute | solution.py:639
  39.0 11.6 %collective-permute-start.9 = (bf16[3,2,144,256]{3,2,1,0:T(8,128)(2,1)S(1)}, bf16[3,2,144,256]{3,2,1,0:T(8,128)(2,1)S(1)}, u32[]{:S(2)}, u32[]{:S(2)}) collective-permute-start(bf16[3,2,144,256]{3,2,1,0:T(8,128)(2,1)S(1)} %stack.21.refs_2_), channel_id=1, source_target_pairs={{0,16},{1,9},{2,18},{3,11},{4,20},{5,13},{6,22},{7,15},{8,24},{9,1... | collective-permute-start | bytes 1327112 | tf_op jit(solution)/shard_map/ppermute | solution.py:639
  40.8 11.3 %collective-permute-start.11 = (bf16[3,2,144,256]{3,2,1,0:T(8,128)(2,1)S(1)}, bf16[3,2,144,256]{3,2,1,0:T(8,128)(2,1)S(1)}, u32[]{:S(2)}, u32[]{:S(2)}) collective-permute-start(bf16[3,2,144,256]{3,2,1,0:T(8,128)(2,1)S(1)} %stack.21.refs_2_), channel_id=1, source_target_pairs={{0,1},{1,0},{2,3},{3,2},{4,5},{5,4},{6,7},{7,6},{8,9},{9,8},{10,11... | collective-permute-start | bytes 1327112 | tf_op jit(solution)/shard_map/ppermute | solution.py:639
  40.8 12.5 %collective-permute-start.18 = (bf16[3,1,288,256]{3,2,1,0:T(8,128)(2,1)S(1)}, bf16[3,1,288,256]{3,2,1,0:T(8,128)(2,1)S(1)}, u32[]{:S(2)}, u32[]{:S(2)}) collective-permute-start(bf16[3,1,288,256]{3,2,1,0:T(8,128)(2,1)S(1)} %stack.22.refs_2_), channel_id=1, source_target_pairs={{0,8},{1,17},{2,10},{3,19},{4,12},{5,21},{6,14},{7,23},{8,0},{9,25... | collective-permute-start | bytes 1327112 | tf_op jit(solution)/shard_map/ppermute | solution.py:639
  41.9 18.2 %collective-permute-start.10 = (bf16[3,2,144,256]{3,2,1,0:T(8,128)(2,1)S(1)}, bf16[3,2,144,256]{3,2,1,0:T(8,128)(2,1)S(1)}, u32[]{:S(2)}, u32[]{:S(2)}) collective-permute-start(bf16[3,2,144,256]{3,2,1,0:T(8,128)(2,1)S(1)} %collective-permute-done.8.refs_3_), channel_id=1, source_target_pairs={{0,16},{1,9},{2,18},{3,11},{4,20},{5,13},{6,22},{7,15},{8,24},{9,1... | collective-permute-start | bytes 1327112 | tf_op jit(solution)/shard_map/ppermute | solution.py:639
  50.7 9.5 %collective-permute-start.24 = (bf16[3,1,288,256]{3,2,1,0:T(8,128)(2,1)S(1)}, bf16[3,1,288,256]{3,2,1,0:T(8,128)(2,1)S(1)}, u32[]{:S(2)}, u32[]{:S(2)}) collective-permute-start(bf16[3,1,288,256]{3,2,1,0:T(8,128)(2,1)S(1)} %stack.23.refs_2_), channel_id=1, source_target_pairs={{0,8},{1,17},{2,10},{3,19},{4,12},{5,21},{6,14},{7,23},{8,0},{9,25... | collective-permute-start | bytes 1327112 | tf_op jit(solution)/shard_map/ppermute | solution.py:639
  52.0 9.3 %collective-permute-start.12 = (bf16[3,2,144,256]{3,2,1,0:T(8,128)(2,1)S(1)}, bf16[3,2,144,256]{3,2,1,0:T(8,128)(2,1)S(1)}, u32[]{:S(2)}, u32[]{:S(2)}) collective-permute-start(bf16[3,2,144,256]{3,2,1,0:T(8,128)(2,1)S(1)} %collective-permute-done.8.refs_3_), channel_id=1, source_target_pairs={{0,1},{1,0},{2,3},{3,2},{4,5},{5,4},{6,7},{7,6},{8,9},{9,8},{10,11... | collective-permute-start | bytes 1327112 | tf_op jit(solution)/shard_map/ppermute | solution.py:639
  53.3 8.1 %collective-permute-start.13 = (bf16[3,2,144,256]{3,2,1,0:T(8,128)(2,1)S(1)}, bf16[3,2,144,256]{3,2,1,0:T(8,128)(2,1)S(1)}, u32[]{:S(2)}, u32[]{:S(2)}) collective-permute-start(bf16[3,2,144,256]{3,2,1,0:T(8,128)(2,1)S(1)} %collective-permute-done.9.refs_4_), channel_id=1, source_target_pairs={{0,1},{1,0},{2,3},{3,2},{4,5},{5,4},{6,7},{7,6},{8,9},{9,8},{10,11... | collective-permute-start | bytes 1327112 | tf_op jit(solution)/shard_map/ppermute | solution.py:639
  60.1 1.8 %collective-permute-start.14 = (bf16[3,2,144,256]{3,2,1,0:T(8,128)(2,1)S(1)}, bf16[3,2,144,256]{3,2,1,0:T(8,128)(2,1)S(1)}, u32[]{:S(2)}, u32[]{:S(2)}) collective-permute-start(bf16[3,2,144,256]{3,2,1,0:T(8,128)(2,1)S(1)} %collective-permute-done.10.refs_5_), channel_id=1, source_target_pairs={{0,1},{1,0},{2,3},{3,2},{4,5},{5,4},{6,7},{7,6},{8,9},{9,8},{10,11... | collective-permute-start | bytes 1327112 | tf_op jit(solution)/shard_map/ppermute | solution.py:639
  60.1 6.9 %collective-permute-start.19 = (bf16[3,1,288,256]{3,2,1,0:T(8,128)(2,1)S(1)}, bf16[3,1,288,256]{3,2,1,0:T(8,128)(2,1)S(1)}, u32[]{:S(2)}, u32[]{:S(2)}) collective-permute-start(bf16[3,1,288,256]{3,2,1,0:T(8,128)(2,1)S(1)} %stack.22.refs_2_), channel_id=1, source_target_pairs={{0,1},{1,0},{2,3},{3,2},{4,5},{5,4},{6,7},{7,6},{8,9},{9,8},{10,11... | collective-permute-start | bytes 1327112 | tf_op jit(solution)/shard_map/ppermute | solution.py:639
  61.4 5.7 %collective-permute-start.20 = (bf16[3,1,288,256]{3,2,1,0:T(8,128)(2,1)S(1)}, bf16[3,1,288,256]{3,2,1,0:T(8,128)(2,1)S(1)}, u32[]{:S(2)}, u32[]{:S(2)}) collective-permute-start(bf16[3,1,288,256]{3,2,1,0:T(8,128)(2,1)S(1)} %collective-permute-done.18.refs_3_), channel_id=1, source_target_pairs={{0,1},{1,0},{2,3},{3,2},{4,5},{5,4},{6,7},{7,6},{8,9},{9,8},{10,11... | collective-permute-start | bytes 1327112 | tf_op jit(solution)/shard_map/ppermute | solution.py:639
  61.4 10.2 %collective-permute-start.25 = (bf16[3,1,288,256]{3,2,1,0:T(8,128)(2,1)S(1)}, bf16[3,1,288,256]{3,2,1,0:T(8,128)(2,1)S(1)}, u32[]{:S(2)}, u32[]{:S(2)}) collective-permute-start(bf16[3,1,288,256]{3,2,1,0:T(8,128)(2,1)S(1)} %stack.23.refs_2_), channel_id=1, source_target_pairs={{0,1},{1,0},{2,3},{3,2},{4,5},{5,4},{6,7},{7,6},{8,9},{9,8},{10,11... | collective-permute-start | bytes 1327112 | tf_op jit(solution)/shard_map/ppermute | solution.py:639
  61.9 9.7 %collective-permute-start.26 = (bf16[3,1,288,256]{3,2,1,0:T(8,128)(2,1)S(1)}, bf16[3,1,288,256]{3,2,1,0:T(8,128)(2,1)S(1)}, u32[]{:S(2)}, u32[]{:S(2)}) collective-permute-start(bf16[3,1,288,256]{3,2,1,0:T(8,128)(2,1)S(1)} %collective-permute-done.24.refs_3_), channel_id=1, source_target_pairs={{0,1},{1,0},{2,3},{3,2},{4,5},{5,4},{6,7},{7,6},{8,9},{9,8},{10,11... | collective-permute-start | bytes 1327112 | tf_op jit(solution)/shard_map/ppermute | solution.py:639
  80.9 1.4 %collective-permute-start.27 = (f32[4,6,256]{2,1,0:T(8,128)S(1)}, f32[4,6,256]{2,1,0:T(8,128)S(1)}, u32[]{:S(2)}, u32[]{:S(2)}) collective-permute-start(f32[4,6,256]{2,1,0:T(8,128)S(1)} %get-tuple-element.24), channel_id=1, source_target_pairs={{0,1},{1,0},{2,3},{3,2},{4,5},{5,4},{6,7},{7,6},{8,9},{9,8},{10,11... | collective-permute-start | bytes 73736 | tf_op jit(solution)/shard_map/ppermute | solution.py:684
  82.2 4.5 %collective-permute-start.28 = (f32[6,256]{1,0:T(8,128)S(1)}, f32[6,256]{1,0:T(8,128)S(1)}, u32[]{:S(2)}, u32[]{:S(2)}) collective-permute-start(f32[6,256]{1,0:T(8,128)S(1)} %get-tuple-element.26), channel_id=1, source_target_pairs={{0,4},{1,5},{2,6},{3,7},{4,0},{5,1},{6,2},{7,3},{8,12},{9,13},{10,... | collective-permute-start | bytes 18440 | tf_op jit(solution)/shard_map/ppermute | solution.py:684
  82.8 4.0 %collective-permute-start.29 = (f32[6,256]{1,0:T(8,128)S(1)}, f32[6,256]{1,0:T(8,128)S(1)}, u32[]{:S(2)}, u32[]{:S(2)}) collective-permute-start(f32[6,256]{1,0:T(8,128)S(1)} %get-tuple-element.27), channel_id=1, source_target_pairs={{0,2},{1,3},{2,0},{3,1},{4,6},{5,7},{6,4},{7,5},{8,10},{9,11},{10,... | collective-permute-start | bytes 18440 | tf_op jit(solution)/shard_map/ppermute | solution.py:684
  84.1 5.4 %collective-permute-start.30 = (f32[6,256]{1,0:T(8,128)S(1)}, f32[6,256]{1,0:T(8,128)S(1)}, u32[]{:S(2)}, u32[]{:S(2)}) collective-permute-start(f32[6,256]{1,0:T(8,128)S(1)} %get-tuple-element.28), channel_id=1, source_target_pairs={{0,6},{1,7},{2,4},{3,5},{4,2},{5,3},{6,0},{7,1},{8,14},{9,15},{10,... | collective-permute-start | bytes 18440 | tf_op jit(solution)/shard_map/ppermute | solution.py:684
  (7 other events, 86.7 us)
